TPU v7x, 32 devices: a whole 2x2x4 slice. The times are simulated.
32 devices in a mesh: fsdp: 4 (over y, x), ctx: 2 (over core), tp: 4 (over z).
Axes of the slice: x: 2, y: 2, z: 4, core: 2. Of those that a mesh axis runs over, the one named last changes fastest.
Arguments:
- tokens: bfloat16 [2, 4, 1024, 768], P(None, 'fsdp', 'ctx'), may hold values from -6 to 6
- cotangent: bfloat16 [2, 4, 1024, 768], P(None, 'fsdp', 'ctx'), may hold values from -6 to 6
- lengths: int32 [2, 4], P(None, 'fsdp'), may hold values from 513 to 1024
- routes: int32 [2, 2, 4, 1024, 2], P(None, None, 'fsdp', 'ctx'), may hold values from 0 to 11, all different within a row; in each aligned block of 512 rows (0 to 511, 512 to 1023, ..., all dimensions but the last counted through in order) at most 128 rows name the same one
- norm_attn: bfloat16 [2, 768], P(None, ('fsdp', 'ctx')), may hold values from 0.5 to 1.5
- w_qkv: bfloat16 [2, 768, 2304], P(None, ('fsdp', 'ctx'), 'tp'), may hold values from -0.21875 to 0.21875
- w_out: bfloat16 [2, 768, 768], P(None, 'tp', ('fsdp', 'ctx')), may hold values from -1.25 to 1.25
- norm_moe: bfloat16 [2, 768], P(None, ('fsdp', 'ctx')), may hold values from 0.5 to 1.5
- w_router: bfloat16 [2, 768, 12], P(None, ('fsdp', 'ctx')), may hold values from -0.15625 to 0.15625
- w_resid: bfloat16 [12, 12], replicated, may hold values from -1.75 to 1.75
- w_const: bfloat16 [2, 2, 768, 2], P(None, None, ('fsdp', 'ctx')), may hold values from -0.21875 to 0.21875
- v_const: bfloat16 [2, 2, 768], P(None, None, ('fsdp', 'ctx')), may hold values from -6 to 6
- w_gate_up: bfloat16 [2, 8, 768, 2, 2048], P(None, None, ('fsdp', 'ctx'), None, 'tp'), may hold values from -0.21875 to 0.21875
- w_down: bfloat16 [2, 8, 2048, 768], P(None, None, 'tp', ('fsdp', 'ctx')), may hold values from -0.1875 to 0.1875
Outputs:
- mixed: bfloat16 [2, 4, 1024, 768], P(None, 'fsdp', 'ctx')
- grad_tokens: float32 [2, 4, 1024, 768], P(None, 'fsdp', 'ctx')
- grad_norm_attn: float32 [2, 768], P(None, ('fsdp', 'ctx'))
- grad_w_qkv: float32 [2, 768, 2304], P(None, ('fsdp', 'ctx'), 'tp')
- grad_w_out: float32 [2, 768, 768], P(None, 'tp', ('fsdp', 'ctx'))
- grad_norm_moe: float32 [2, 768], P(None, ('fsdp', 'ctx'))
- grad_w_router: float32 [2, 768, 12], P(None, ('fsdp', 'ctx'))
- grad_w_resid: float32 [12, 12], replicated
- grad_w_const: float32 [2, 2, 768, 2], P(None, None, ('fsdp', 'ctx'))
- grad_v_const: float32 [2, 2, 768], P(None, None, ('fsdp', 'ctx'))
- grad_w_gate_up: float32 [2, 8, 768, 2, 2048], P(None, None, ('fsdp', 'ctx'), None, 'tp')
- grad_w_down: float32 [2, 8, 2048, 768], P(None, None, 'tp', ('fsdp', 'ctx'))
Inputs may be any that keep to these rules, and one draw needn't show every extreme that they name: In each aligned block of 512 slots of routes (one context block of one sequence in one layer and micro-batch), no expert is named by more than 128 of the block's routes, a bound that some block reaches; the two routes of a slot name different experts; every expert is named somewhere.
All inputs are finite; a program needn't handle non-finite values.
Results may differ from a plain program's by a relative error of at most 0.025.
Values may be sent and summed in bfloat16 or wider, within the bound.
No kernel may reach another device: no remote copies, remote signals or barrier semaphores. Data moves between devices by JAX's collectives and lax.ppermute only.
A program may use at most 384 MiB of HBM per device.

v0:
```python
import jax
import jax.numpy as jnp
from jax import lax
from jax.sharding import PartitionSpec as P

HD = 64
NF = 8
NE = 12


PRECISE = lax.Precision.HIGHEST
EPSILON = 1e-06
MASKED = -1e30


def rms_norm(operand, norm_gain):
    return (
        operand
        * lax.rsqrt(jnp.mean(operand * operand, axis=-1, keepdims=True) + EPSILON)
        * norm_gain
    )


def pair_softmax(operand):
    row_max = jnp.max(operand, axis=-1, keepdims=True)
    exp_terms = jnp.exp(operand - row_max)
    return exp_terms / jnp.sum(exp_terms, axis=-1, keepdims=True)


def gate_terms(xm_wide, normed, logits_prev, w_router, w_resid, w_const, v_const, route_flat):
    logits = jnp.dot(xm_wide, w_router, precision=PRECISE) + jnp.dot(
        logits_prev, w_resid, precision=PRECISE
    )
    expert_ids = jnp.arange(NE, dtype=jnp.int32)
    one_hot = (route_flat[:, :, None] == expert_ids[None, None, :]).astype(jnp.float32)
    chosen = jnp.sum(one_hot * logits[:, None, :], axis=-1)
    gate_vals = pair_softmax(chosen)
    const_terms = []
    for const_idx in range(2):
        alpha_pair = pair_softmax(jnp.dot(xm_wide, w_const[const_idx], precision=PRECISE))
        const_terms.append(
            alpha_pair[:, 0:1] * normed + alpha_pair[:, 1:2] * v_const[const_idx][None, :]
        )
    slot_terms = (
        one_hot[:, :, NF + 1 : NF + 2] * normed[:, None, :]
        + one_hot[:, :, NF + 2 : NF + 3] * const_terms[0][:, None, :]
        + one_hot[:, :, NF + 3 : NF + 4] * const_terms[1][:, None, :]
    )
    fixed_terms = jnp.sum(gate_vals[:, :, None] * slot_terms, axis=1)
    return (gate_vals, fixed_terms, logits)


def dispatch_tables(route_ids, block_len):
    seq_count = route_ids.shape[0]
    capacity = block_len // 4
    row_count = seq_count * block_len
    block_ids = jnp.arange(seq_count, dtype=jnp.int32)

    def one_block(route_block):
        slot_routes = route_block.reshape(-1)
        slot_count = slot_routes.shape[0]
        expert_hits = (slot_routes[:, None] == jnp.arange(NF, dtype=jnp.int32)[None, :]).astype(
            jnp.int32
        )
        slot_place = jnp.sum((jnp.cumsum(expert_hits, axis=0) - expert_hits) * expert_hits, axis=1)
        is_ffn = slot_routes < NF
        slot_table = (
            jnp.full((NF, capacity), slot_count, jnp.int32)
            .at[jnp.where(is_ffn, slot_routes, NF), slot_place]
            .set(jnp.arange(slot_count, dtype=jnp.int32), mode="drop")
        )
        return (slot_table, slot_place, is_ffn)

    slot_table, slot_place, is_ffn = jax.vmap(one_block)(route_ids)
    filled = slot_table < 2 * block_len
    slot_index = jnp.where(
        filled, slot_table + 2 * block_len * block_ids[:, None, None], 2 * row_count
    )
    row_index = jnp.where(filled, slot_table // 2 + block_len * block_ids[:, None, None], row_count)
    slot_index = jnp.transpose(slot_index, (1, 0, 2)).reshape(NF, seq_count * capacity)
    row_index = jnp.transpose(row_index, (1, 0, 2)).reshape(NF, seq_count * capacity)
    slot_routes = route_ids.reshape(seq_count, 2 * block_len)
    target = jnp.where(
        is_ffn,
        slot_routes * (seq_count * capacity) + block_ids[:, None] * capacity + slot_place,
        NF * seq_count * capacity,
    )
    return (row_index, slot_index, target.reshape(-1))


def slot_outputs(result, target, row_count):
    feature_dim = result.shape[-1]
    flat_result = jnp.concatenate(
        [result.reshape(-1, feature_dim), jnp.zeros((1, feature_dim), jnp.float32)], axis=0
    )
    return flat_result[target].reshape(row_count, 2, feature_dim)


def masked_scores(query_part, keyval, query_pos, seq_length):
    key_pos = jnp.arange(keyval.shape[0], dtype=jnp.int32)
    scores = jnp.einsum(
        "qhe,khe->hqk", query_part, keyval[:, :, 0], preferred_element_type=jnp.float32
    ) * HD ** (-0.5)
    allowed = (key_pos[None, :] <= query_pos[:, None]) & (key_pos[None, :] < seq_length)
    return jnp.where(allowed[None], scores, MASKED)


def attend_forward(query_part, keyval, query_pos, seq_length):
    masked = masked_scores(query_part, keyval, query_pos, seq_length)
    row_max = jnp.max(masked, axis=-1, keepdims=True)
    exp_terms = jnp.exp(masked - row_max)
    row_total = jnp.sum(exp_terms, axis=-1, keepdims=True)
    prob_low = (exp_terms / row_total).astype(jnp.bfloat16)
    context = jnp.einsum(
        "hqk,khe->qhe", prob_low, keyval[:, :, 1], preferred_element_type=jnp.float32
    )
    return (context.astype(jnp.bfloat16), row_max + jnp.log(row_total))


def attend_backward(query_part, keyval, query_pos, seq_length, log_total, grad_context):
    masked = masked_scores(query_part, keyval, query_pos, seq_length)
    prob_full = jnp.exp(masked - log_total)
    prob_low = prob_full.astype(jnp.bfloat16)
    grad_prob = jnp.einsum(
        "qhe,khe->hqk", grad_context, keyval[:, :, 1], preferred_element_type=jnp.float32
    )
    row_inner = jnp.sum(prob_full * grad_prob, axis=-1, keepdims=True)
    grad_scores = (prob_full * (grad_prob - row_inner)).astype(jnp.bfloat16)
    score_scale = HD ** (-0.5)
    grad_query = (
        jnp.einsum("hqk,khe->qhe", grad_scores, keyval[:, :, 0], preferred_element_type=jnp.float32)
        * score_scale
    )
    grad_key = (
        jnp.einsum("hqk,qhe->khe", grad_scores, query_part, preferred_element_type=jnp.float32)
        * score_scale
    )
    grad_value = jnp.einsum(
        "hqk,qhe->khe", prob_low, grad_context, preferred_element_type=jnp.float32
    )
    return (grad_query, jnp.stack([grad_key, grad_value], axis=2))


def layer_forward(residual, weights, route_ids, seq_lengths, query_pos, logits_prev, w_resid):
    gain_attn, w_qkv, w_out, gain_moe, w_router, w_const, v_const, w_gate_up, w_down = weights
    seq_count, block_len = (route_ids.shape[0], route_ids.shape[1])
    row_count = seq_count * block_len
    heads_local = w_qkv.shape[1] // (3 * HD)
    attn_in = rms_norm(residual, gain_attn.astype(jnp.float32)).astype(jnp.bfloat16)
    qkv_low = jnp.dot(attn_in, w_qkv, preferred_element_type=jnp.float32).astype(jnp.bfloat16)
    qkv_heads = qkv_low.reshape(seq_count, block_len, heads_local, 3, HD)
    keyval_own = qkv_heads[:, :, :, 1:3].reshape(seq_count, block_len, heads_local * 2 * HD)
    keyval_all = lax.all_gather(keyval_own, "ctx", axis=1, tiled=True).reshape(
        seq_count, -1, heads_local, 2, HD
    )

    def one_sequence(seq_items):
        return attend_forward(seq_items[0], seq_items[1], query_pos, seq_items[2])

    context, log_total = lax.map(one_sequence, (qkv_heads[:, :, :, 0], keyval_all, seq_lengths))
    context_flat = context.reshape(row_count, heads_local * HD)
    attn_part = jnp.dot(context_flat, w_out, preferred_element_type=jnp.float32)
    middle = residual + lax.psum(attn_part, "tp")
    normed = rms_norm(middle, gain_moe.astype(jnp.float32))
    xm_low = normed.astype(jnp.bfloat16)
    feature_dim = xm_low.shape[1]
    route_flat = route_ids.reshape(row_count, 2)
    gate_vals, fixed_terms, logits = gate_terms(
        xm_low.astype(jnp.float32),
        normed,
        logits_prev,
        w_router.astype(jnp.float32),
        w_resid,
        w_const.astype(jnp.float32),
        v_const.astype(jnp.float32),
        route_flat,
    )
    row_index, slot_index, target = dispatch_tables(route_ids, block_len)
    padded = jnp.concatenate([xm_low, jnp.zeros((1, feature_dim), jnp.bfloat16)], axis=0)
    picked = padded[row_index]
    gate_up = jnp.einsum("ecd,edkf->eckf", picked, w_gate_up, preferred_element_type=jnp.float32)
    hidden = (gate_up[:, :, 0] * lax.logistic(gate_up[:, :, 0]) * gate_up[:, :, 1]).astype(
        jnp.bfloat16
    )
    result = jnp.einsum("ecf,efd->ecd", hidden, w_down, preferred_element_type=jnp.float32)
    per_slot = slot_outputs(result, target, row_count)
    ffn_part = jnp.sum(gate_vals[:, :, None] * per_slot, axis=1)
    layer_out = (
        middle + lax.psum(ffn_part.astype(jnp.bfloat16), "tp").astype(jnp.float32) + fixed_terms
    )
    saved_state = (
        residual,
        attn_in,
        qkv_heads,
        keyval_all,
        context_flat,
        log_total,
        middle,
        xm_low,
        logits_prev,
        gate_vals,
        row_index,
        slot_index,
        target,
        picked,
        gate_up,
        hidden,
        result,
        route_flat,
    )
    return (layer_out, logits, saved_state)


def layer_backward(grad_out, grad_logits, saved_state, weights, w_resid, query_pos, seq_lengths):
    (
        residual,
        attn_in,
        qkv_heads,
        keyval_all,
        context_flat,
        log_total,
        middle,
        xm_low,
        logits_prev,
        gate_vals,
        row_index,
        slot_index,
        target,
        expert_input,
        gate_up,
        hidden,
        result,
        route_flat,
    ) = saved_state
    gain_attn, w_qkv, w_out, gain_moe, w_router, w_const, v_const, w_gate_up, w_down = weights
    row_count, feature_dim = grad_out.shape
    seq_count = qkv_heads.shape[0]
    heads_local = qkv_heads.shape[2]
    per_slot = slot_outputs(result, target, row_count)
    grad_gate_part = jnp.sum(per_slot * grad_out[:, None, :], axis=-1)
    gate_flat = jnp.concatenate([gate_vals.reshape(-1), jnp.zeros((1,), jnp.float32)])
    grad_padded = jnp.concatenate([grad_out, jnp.zeros((1, feature_dim), jnp.float32)], axis=0)
    grad_result = (gate_flat[slot_index][:, :, None] * grad_padded[row_index]).astype(jnp.bfloat16)
    grad_hidden = jnp.einsum(
        "ecd,efd->ecf", grad_result, w_down, preferred_element_type=jnp.float32
    )
    grad_w_down = jnp.einsum(
        "ecf,ecd->efd", hidden, grad_result, preferred_element_type=jnp.float32
    )
    gate_in = gate_up[:, :, 0]
    sigmoid_gate = lax.logistic(gate_in)
    grad_gate_in = (
        grad_hidden * gate_up[:, :, 1] * sigmoid_gate * (1.0 + gate_in * (1.0 - sigmoid_gate))
    )
    grad_up_in = grad_hidden * gate_in * sigmoid_gate
    grad_gate_up = jnp.stack([grad_gate_in, grad_up_in], axis=2).astype(jnp.bfloat16)
    grad_picked = jnp.einsum(
        "eckf,edkf->ecd", grad_gate_up, w_gate_up, preferred_element_type=jnp.float32
    )
    grad_w_gate_up = jnp.einsum(
        "ecd,eckf->edkf", expert_input, grad_gate_up, preferred_element_type=jnp.float32
    )
    grad_xm_part = jax.ops.segment_sum(
        grad_picked.reshape(-1, feature_dim), row_index.reshape(-1), num_segments=row_count + 1
    )[:row_count]
    grad_xm_ffn, grad_gates = (
        lax.psum(grad_xm_part.astype(jnp.bfloat16), "tp").astype(jnp.float32),
        lax.psum(grad_gate_part.astype(jnp.bfloat16), "tp").astype(jnp.float32),
    )
    normed = rms_norm(middle, gain_moe.astype(jnp.float32))

    def gate_piece(xm_wide, normed_in, prev_in, router_in, resid_in, const_in, vector_in):
        return gate_terms(
            xm_wide, normed_in, prev_in, router_in, resid_in, const_in, vector_in, route_flat
        )

    unused_out, gate_pull = jax.vjp(
        gate_piece,
        xm_low.astype(jnp.float32),
        normed,
        logits_prev,
        w_router.astype(jnp.float32),
        w_resid,
        w_const.astype(jnp.float32),
        v_const.astype(jnp.float32),
    )
    grad_xm_wide, grad_normed, grad_prev, grad_router, grad_resid_w, grad_const_w, grad_const_v = (
        gate_pull((grad_gates, grad_out, grad_logits))
    )
    unused_norm, norm_pull = jax.vjp(rms_norm, middle, gain_moe.astype(jnp.float32))
    grad_mid_norm, grad_gain_moe = norm_pull(grad_normed + grad_xm_wide + grad_xm_ffn)
    grad_middle = grad_out + grad_mid_norm
    grad_attn = grad_middle.astype(jnp.bfloat16)
    grad_context = jnp.einsum(
        "rd,cd->rc", grad_attn, w_out, preferred_element_type=jnp.float32
    ).astype(jnp.bfloat16)
    grad_w_out = jnp.einsum(
        "rc,rd->cd", context_flat, grad_attn, preferred_element_type=jnp.float32
    )

    def one_sequence(seq_items):
        return attend_backward(
            seq_items[0], seq_items[1], query_pos, seq_items[2], seq_items[3], seq_items[4]
        )

    grad_query, grad_keyval = lax.map(
        one_sequence,
        (
            qkv_heads[:, :, :, 0],
            keyval_all,
            seq_lengths,
            log_total,
            grad_context.reshape(seq_count, -1, heads_local, HD),
        ),
    )
    key_count = keyval_all.shape[1]
    grad_keyval_own = lax.psum_scatter(
        grad_keyval.reshape(seq_count, key_count, heads_local * 2 * HD).astype(jnp.bfloat16),
        "ctx",
        scatter_dimension=1,
        tiled=True,
    ).astype(jnp.float32)
    grad_qkv = jnp.concatenate(
        [grad_query[:, :, :, None, :], grad_keyval_own.reshape(seq_count, -1, heads_local, 2, HD)],
        axis=3,
    )
    grad_qkv = grad_qkv.reshape(row_count, heads_local * 3 * HD).astype(jnp.bfloat16)
    grad_attn_part = jnp.einsum("rc,dc->rd", grad_qkv, w_qkv, preferred_element_type=jnp.float32)
    grad_w_qkv = jnp.einsum("rd,rc->dc", attn_in, grad_qkv, preferred_element_type=jnp.float32)
    grad_attn_in = lax.psum(grad_attn_part.astype(jnp.bfloat16), "tp").astype(jnp.float32)
    unused_first, first_pull = jax.vjp(rms_norm, residual, gain_attn.astype(jnp.float32))
    grad_res_norm, grad_gain_attn = first_pull(grad_attn_in)
    layer_grads = (
        grad_gain_attn,
        grad_w_qkv,
        grad_w_out,
        grad_gain_moe,
        grad_router,
        grad_const_w,
        grad_const_v,
        grad_w_gate_up,
        grad_w_down,
    )
    return (grad_middle + grad_res_norm, grad_prev, layer_grads, grad_resid_w)


def add_up(current, extra):
    if current is None:
        return extra
    return tuple((first_term + second_term for first_term, second_term in zip(current, extra)))


def per_device(
    tokens,
    cotangent,
    lengths,
    routes,
    norm_attn,
    w_qkv,
    w_out,
    norm_moe,
    w_router,
    w_resid,
    w_const,
    v_const,
    w_gate_up,
    w_down,
):
    micro_count, seq_count, block_len, feature_dim = tokens.shape
    row_count = seq_count * block_len
    layer_count = w_qkv.shape[0]
    query_pos = lax.axis_index("ctx") * block_len + jnp.arange(block_len, dtype=jnp.int32)
    resid_weight = w_resid.astype(jnp.float32)

    def fetch_layer(layer_idx):
        return (
            lax.all_gather(norm_attn[layer_idx], ("fsdp", "ctx"), axis=0, tiled=True),
            lax.all_gather(w_qkv[layer_idx], ("fsdp", "ctx"), axis=0, tiled=True),
            lax.all_gather(w_out[layer_idx], ("fsdp", "ctx"), axis=1, tiled=True),
            lax.all_gather(norm_moe[layer_idx], ("fsdp", "ctx"), axis=0, tiled=True),
            lax.all_gather(w_router[layer_idx], ("fsdp", "ctx"), axis=0, tiled=True),
            lax.all_gather(w_const[layer_idx], ("fsdp", "ctx"), axis=1, tiled=True),
            lax.all_gather(v_const[layer_idx], ("fsdp", "ctx"), axis=1, tiled=True),
            lax.all_gather(w_gate_up[layer_idx], ("fsdp", "ctx"), axis=1, tiled=True),
            lax.all_gather(w_down[layer_idx], ("fsdp", "ctx"), axis=2, tiled=True),
        )

    shard_totals = [None] * layer_count
    resid_total = jnp.zeros_like(resid_weight)
    outputs = []
    input_grads = []
    for micro_idx in range(micro_count):
        residual = tokens[micro_idx].reshape(row_count, feature_dim).astype(jnp.float32)
        logits_prev = jnp.zeros((row_count, NE), jnp.float32)
        seq_lengths = lengths[micro_idx]
        saved_layers = []
        for layer_idx in range(layer_count):
            weights = fetch_layer(layer_idx)
            residual, logits_next, saved_state = layer_forward(
                residual,
                weights,
                routes[layer_idx, micro_idx],
                seq_lengths,
                query_pos,
                logits_prev,
                resid_weight,
            )
            saved_layers.append(saved_state)
            logits_prev = logits_next
        outputs.append(residual.astype(jnp.bfloat16).reshape(seq_count, block_len, feature_dim))
        valid_mask = (query_pos[None, :] < seq_lengths[:, None]).astype(jnp.float32)
        grad_residual = (cotangent[micro_idx].astype(jnp.float32) * valid_mask[:, :, None]).reshape(
            row_count, feature_dim
        )
        grad_logits = jnp.zeros((row_count, NE), jnp.float32)
        for layer_idx in reversed(range(layer_count)):
            weights = fetch_layer(layer_idx)
            grad_residual, grad_logits, layer_grads, grad_resid_w = layer_backward(
                grad_residual,
                grad_logits,
                saved_layers[layer_idx],
                weights,
                resid_weight,
                query_pos,
                seq_lengths,
            )
            resid_total = resid_total + grad_resid_w
            shard_totals[layer_idx] = add_up(
                shard_totals[layer_idx],
                (
                    lax.psum_scatter(
                        layer_grads[0].astype(jnp.bfloat16),
                        ("fsdp", "ctx"),
                        scatter_dimension=0,
                        tiled=True,
                    ).astype(jnp.float32),
                    lax.psum_scatter(
                        layer_grads[1].astype(jnp.bfloat16),
                        ("fsdp", "ctx"),
                        scatter_dimension=0,
                        tiled=True,
                    ).astype(jnp.float32),
                    lax.psum_scatter(
                        layer_grads[2].astype(jnp.bfloat16),
                        ("fsdp", "ctx"),
                        scatter_dimension=1,
                        tiled=True,
                    ).astype(jnp.float32),
                    lax.psum_scatter(
                        layer_grads[3].astype(jnp.bfloat16),
                        ("fsdp", "ctx"),
                        scatter_dimension=0,
                        tiled=True,
                    ).astype(jnp.float32),
                    lax.psum_scatter(
                        layer_grads[4].astype(jnp.bfloat16),
                        ("fsdp", "ctx"),
                        scatter_dimension=0,
                        tiled=True,
                    ).astype(jnp.float32),
                    lax.psum_scatter(
                        layer_grads[5].astype(jnp.bfloat16),
                        ("fsdp", "ctx"),
                        scatter_dimension=1,
                        tiled=True,
                    ).astype(jnp.float32),
                    lax.psum_scatter(
                        layer_grads[6].astype(jnp.bfloat16),
                        ("fsdp", "ctx"),
                        scatter_dimension=1,
                        tiled=True,
                    ).astype(jnp.float32),
                    lax.psum_scatter(
                        layer_grads[7].astype(jnp.bfloat16),
                        ("fsdp", "ctx"),
                        scatter_dimension=1,
                        tiled=True,
                    ).astype(jnp.float32),
                    lax.psum_scatter(
                        layer_grads[8].astype(jnp.bfloat16),
                        ("fsdp", "ctx"),
                        scatter_dimension=2,
                        tiled=True,
                    ).astype(jnp.float32),
                ),
            )
        input_grads.append(grad_residual.reshape(seq_count, block_len, feature_dim))
    stacked = [
        jnp.stack([shard_totals[layer_idx][member] for layer_idx in range(layer_count)])
        for member in range(9)
    ]
    resid_grad = lax.psum(resid_total, ("fsdp", "ctx"))
    return (
        jnp.stack(outputs),
        jnp.stack(input_grads),
        stacked[0],
        stacked[1],
        stacked[2],
        stacked[3],
        stacked[4],
        resid_grad,
        stacked[5],
        stacked[6],
        stacked[7],
        stacked[8],
    )


def solution(mesh):
    in_specs = (
        P(None, "fsdp", "ctx", None),
        P(None, "fsdp", "ctx", None),
        P(None, "fsdp"),
        P(None, None, "fsdp", "ctx", None),
        P(None, ("fsdp", "ctx")),
        P(None, ("fsdp", "ctx"), "tp"),
        P(None, "tp", ("fsdp", "ctx")),
        P(None, ("fsdp", "ctx")),
        P(None, ("fsdp", "ctx"), None),
        P(),
        P(None, None, ("fsdp", "ctx"), None),
        P(None, None, ("fsdp", "ctx")),
        P(None, None, ("fsdp", "ctx"), None, "tp"),
        P(None, None, "tp", ("fsdp", "ctx")),
    )
    out_specs = (
        P(None, "fsdp", "ctx", None),
        P(None, "fsdp", "ctx", None),
        P(None, ("fsdp", "ctx")),
        P(None, ("fsdp", "ctx"), "tp"),
        P(None, "tp", ("fsdp", "ctx")),
        P(None, ("fsdp", "ctx")),
        P(None, ("fsdp", "ctx"), None),
        P(),
        P(None, None, ("fsdp", "ctx"), None),
        P(None, None, ("fsdp", "ctx")),
        P(None, None, ("fsdp", "ctx"), None, "tp"),
        P(None, None, "tp", ("fsdp", "ctx")),
    )
    return jax.shard_map(
        per_device, mesh=mesh, in_specs=in_specs, out_specs=out_specs, check_vma=False
    )
```

profile of v0, /device:TPU:0, one launch (start us, length us, event | category | flops | bytes accessed | tf_op | source)
XLA Modules:
  0.0 2754.1 jit_solution(12539515553021089263)
XLA Ops:
  15.2 16.0 all-reduce.59
  44.7 11.1 all-gather.1
  166.8 32.5 %all-reduce.77.cloned.1.call-done = (f32[512,768]{1,0:T(8,128)}, f32[512,768]{1,0:T(8,128)}) async-done(((f32[512,768]{1,0:T(8,128)}, f32[512,768]{1,0:T(8,128)}), (f32[512,768]{1,0:T(8,128)}, f32[512,768]{1,0:T(8,128)})) %all-reduce.77.cloned.1.call-update) | async-done | bytes 3145744 | tf_op jit(solution)/shard_map/psum | solution.py:163
  281.4 17.9 multiply_reduce_fusion.15
  299.3 15.2 multiply_reduce_fusion.19
  317.3 11.7 all-gather.11
  329.5 13.7 all-gather.10
  343.2 39.9 %all-reduce.87.cloned.1.call-done = (bf16[512,768]{1,0:T(8,128)(2,1)}, bf16[512,768]{1,0:T(8,128)(2,1)}) async-done(((bf16[512,768]{1,0:T(8,128)(2,1)}, bf16[512,768]{1,0:T(8,128)(2,1)}), (bf16[512,768]{1,0:T(8,128)(2,1)}, bf16[512,768]{1,0:T(8,128)(2,1)})) %all-reduce.87.cloned.1.call-update) | async-done | bytes 1572880 | tf_op jit(solution)/shard_map/psum | solution.py:189
  416.9 10.9 all-gather.17
  428.9 12.2 all-gather.13
  510.0 19.7 all-reduce.75.cloned.1.call-done
  671.9 31.1 %multiply_reduce_fusion.10 = (f32[512,2]{1,0:T(8,128)}, f32[512,768]{1,0:T(8,128)}, bf16[512,768]{1,0:T(8,128)(2,1)}, bf16[512,2]{1,0:T(8,128)(2,1)}, f32[512,76...) fusion(f32[512,768]{1,0:T(8,128)S(1)} %copy-done.66, f32[512,2]{1,0:T(8,128)} %copy-done.150, ...), kind=kLoop, calls=%fused_computation.145 | loop fusion | flops 13760512 | bytes 16537600 | tf_op jit(solution)/shard_map/transpose(jvp())/reduce_sum | solution.py:49
  711.7 30.7 %multiply_reduce_fusion.6 = (f32[512,2]{1,0:T(8,128)}, f32[512,768]{1,0:T(8,128)}, bf16[512,768]{1,0:T(8,128)(2,1)}, bf16[512,2]{1,0:T(8,128)(2,1)}, f32[512,768...) fusion(f32[512,768]{1,0:T(8,128)S(1)} %copy-done.64, f32[512,2]{1,0:T(8,128)} %copy-done.149, ...), kind=kLoop, calls=%fused_computation.135 | loop fusion | flops 13760512 | bytes 16537600 | tf_op jit(solution)/shard_map/transpose(jvp())/reduce_sum | solution.py:49
  769.0 59.6 %all-reduce.85.cloned.1.call-done = (bf16[512,768]{1,0:T(8,128)(2,1)}, bf16[512,768]{1,0:T(8,128)(2,1)}) async-done(((bf16[512,768]{1,0:T(8,128)(2,1)}, bf16[512,768]{1,0:T(8,128)(2,1)}), (bf16[512,768]{1,0:T(8,128)(2,1)}, bf16[512,768]{1,0:T(8,128)(2,1)})) %all-reduce.85.cloned.1.call-update) | async-done | bytes 1572880 | tf_op jit(solution)/shard_map/psum | solution.py:267
  898.6 44.5 %all-reduce.83.cloned.1.call-done = (bf16[512,768]{1,0:T(8,128)(2,1)}, bf16[512,768]{1,0:T(8,128)(2,1)}) async-done(((bf16[512,768]{1,0:T(8,128)(2,1)}, bf16[512,768]{1,0:T(8,128)(2,1)}), (bf16[512,768]{1,0:T(8,128)(2,1)}, bf16[512,768]{1,0:T(8,128)(2,1)})) %all-reduce.83.cloned.1.call-update) | async-done | bytes 1572880 | tf_op jit(solution)/shard_map/psum | solution.py:330
  951.0 21.6 multiply_reduce_fusion.5
  975.7 21.6 multiply_reduce_fusion.9
  1058.4 11.2 fusion.4
  1088.2 11.2 fusion
  1121.5 57.1 %all-reduce.81.cloned.1.call-done = (bf16[512,768]{1,0:T(8,128)(2,1)}, bf16[512,768]{1,0:T(8,128)(2,1)}) async-done(((bf16[512,768]{1,0:T(8,128)(2,1)}, bf16[512,768]{1,0:T(8,128)(2,1)}), (bf16[512,768]{1,0:T(8,128)(2,1)}, bf16[512,768]{1,0:T(8,128)(2,1)})) %all-reduce.81.cloned.1.call-update) | async-done | bytes 1572880 | tf_op jit(solution)/shard_map/psum | solution.py:267
  1336.6 30.9 %reduce-scatter.119.cloned.1.call-done = bf16[96,4]{1,0:T(8,128)(2,1)} async-done(((bf16[768,4]{1,0:T(8,128)(2,1)}), bf16[96,4]{1,0:T(8,128)(2,1)}) %reduce-scatter.119.cloned.1.call-update) | async-done | bytes 784
  1368.5 35.5 %reduce-scatter.109.cloned.1.call-done = bf16[96,12]{1,0:T(8,128)(2,1)} async-done(((bf16[768,12]{1,0:T(8,128)(2,1)}), bf16[96,12]{1,0:T(8,128)(2,1)}) %reduce-scatter.109.cloned.1.call-update) | async-done | bytes 2320
  1404.8 35.9 %reduce-scatter.111.cloned.1.call-done = bf16[96,12]{1,0:T(8,128)(2,1)} async-done(((bf16[768,12]{1,0:T(8,128)(2,1)}), bf16[96,12]{1,0:T(8,128)(2,1)}) %reduce-scatter.111.cloned.1.call-update) | async-done | bytes 2320
  1441.5 36.0 %reduce-scatter.101.cloned.1.call-done = bf16[96,192]{1,0:T(8,128)(2,1)} async-done(((bf16[768,192]{1,0:T(8,128)(2,1)}), bf16[96,192]{1,0:T(8,128)(2,1)}) %reduce-scatter.101.cloned.1.call-update) | async-done | bytes 36880
  1478.4 36.4 %reduce-scatter.103.cloned.1.call-done = bf16[96,192]{1,0:T(8,128)(2,1)} async-done(((bf16[768,192]{1,0:T(8,128)(2,1)}), bf16[96,192]{1,0:T(8,128)(2,1)}) %reduce-scatter.103.cloned.1.call-update) | async-done | bytes 36880
  1515.8 38.0 %reduce-scatter.79.cloned.1.call-done = bf16[96,576]{1,0:T(8,128)(2,1)} async-done(((bf16[768,576]{1,0:T(8,128)(2,1)}), bf16[96,576]{1,0:T(8,128)(2,1)}) %reduce-scatter.79.cloned.1.call-update) | async-done | bytes 110608 | tf_op jit(solution)/shard_map/reduce_scatter | solution.py:437
  1553.8 39.1 %reduce-scatter.77.cloned.1.call-done = bf16[96,576]{1,0:T(8,128)(2,1)} async-done(((bf16[768,576]{1,0:T(8,128)(2,1)}), bf16[96,576]{1,0:T(8,128)(2,1)}) %reduce-scatter.77.cloned.1.call-update) | async-done | bytes 110608 | tf_op jit(solution)/shard_map/reduce_scatter | solution.py:437
  1594.5 13.5 psum.167
  1608.0 21.5 reduce-scatter.123.cloned.1.call-done
  1630.3 36.1 %reduce-scatter.121.cloned.1.call-done = bf16[96,2]{1,0:T(8,128)(2,1)} async-done(((bf16[768,2]{1,0:T(8,128)(2,1)}), bf16[96,2]{1,0:T(8,128)(2,1)}) %reduce-scatter.121.cloned.1.call-update) | async-done | bytes 400
  1667.8 35.1 %reduce-scatter.115.cloned.1.call-done = bf16[96,4]{1,0:T(8,128)(2,1)} async-done(((bf16[768,4]{1,0:T(8,128)(2,1)}), bf16[96,4]{1,0:T(8,128)(2,1)}) %reduce-scatter.115.cloned.1.call-update) | async-done | bytes 784
  1703.9 35.8 %reduce-scatter.113.cloned.1.call-done = bf16[96,4]{1,0:T(8,128)(2,1)} async-done(((bf16[768,4]{1,0:T(8,128)(2,1)}), bf16[96,4]{1,0:T(8,128)(2,1)}) %reduce-scatter.113.cloned.1.call-update) | async-done | bytes 784
  1741.2 35.0 %reduce-scatter.105.cloned.1.call-done = bf16[96,12]{1,0:T(8,128)(2,1)} async-done(((bf16[768,12]{1,0:T(8,128)(2,1)}), bf16[96,12]{1,0:T(8,128)(2,1)}) %reduce-scatter.105.cloned.1.call-update) | async-done | bytes 2320
  1777.1 36.5 %reduce-scatter.107.cloned.1.call-done = bf16[96,12]{1,0:T(8,128)(2,1)} async-done(((bf16[768,12]{1,0:T(8,128)(2,1)}), bf16[96,12]{1,0:T(8,128)(2,1)}) %reduce-scatter.107.cloned.1.call-update) | async-done | bytes 2320
  1815.0 35.3 %reduce-scatter.97.cloned.1.call-done = bf16[96,192]{1,0:T(8,128)(2,1)} async-done(((bf16[768,192]{1,0:T(8,128)(2,1)}), bf16[96,192]{1,0:T(8,128)(2,1)}) %reduce-scatter.97.cloned.1.call-update) | async-done | bytes 36880
  1851.2 36.0 %reduce-scatter.99.cloned.1.call-done = bf16[96,192]{1,0:T(8,128)(2,1)} async-done(((bf16[768,192]{1,0:T(8,128)(2,1)}), bf16[96,192]{1,0:T(8,128)(2,1)}) %reduce-scatter.99.cloned.1.call-update) | async-done | bytes 36880
  1888.9 37.9 %reduce-scatter.75.cloned.1.call-done = bf16[96,576]{1,0:T(8,128)(2,1)} async-done(((bf16[768,576]{1,0:T(8,128)(2,1)}), bf16[96,576]{1,0:T(8,128)(2,1)}) %reduce-scatter.75.cloned.1.call-update) | async-done | bytes 110608 | tf_op jit(solution)/shard_map/reduce_scatter | solution.py:437
  1926.8 39.1 %reduce-scatter.73.cloned.1.call-done = bf16[96,576]{1,0:T(8,128)(2,1)} async-done(((bf16[768,576]{1,0:T(8,128)(2,1)}), bf16[96,576]{1,0:T(8,128)(2,1)}) %reduce-scatter.73.cloned.1.call-update) | async-done | bytes 110608 | tf_op jit(solution)/shard_map/reduce_scatter | solution.py:437
  1967.8 63.9 %reduce-scatter.95.cloned.1.call-done = bf16[8,512,96]{1,2,0:T(8,128)(2,1)} async-done(((bf16[8,512,768]{1,2,0:T(8,128)(2,1)}), bf16[8,512,96]{1,2,0:T(8,128)(2,1)}) %reduce-scatter.95.cloned.1.call-update) | async-done | bytes 786448 | tf_op jit(solution)/shard_map/reduce_scatter | solution.py:479
  2031.7 65.5 %reduce-scatter.93.cloned.1.call-done = bf16[8,512,96]{1,2,0:T(8,128)(2,1)} async-done(((bf16[8,512,768]{1,2,0:T(8,128)(2,1)}), bf16[8,512,96]{1,2,0:T(8,128)(2,1)}) %reduce-scatter.93.cloned.1.call-update) | async-done | bytes 786448 | tf_op jit(solution)/shard_map/reduce_scatter | solution.py:479
  2100.0 121.8 %all-reduce.79.cloned.1.call-done = (bf16[512,768]{1,0:T(8,128)(2,1)}, bf16[512,768]{1,0:T(8,128)(2,1)}, bf16[512,768]{1,0:T(8,128)(2,1)}, bf16[512,768]{1,0:T(8,128)(2,1)}) async-done(((bf16[512,768]{1,0:T(8,128)(2,1)}, bf16[512,768]{1,0:T(8,128)(2,1)}, bf16[512,768]{1,0:T(8,128)(2,1)}, bf16[512,768]{1,0:T(8,128)(2,1)}), (bf16[512,768]{1,0:T(8,128)(2,1)}, bf16[512,768]{1,0:T(8,128)(2,1)}, ...) | async-done | bytes 3145744 | tf_op jit(solution)/shard_map/psum | solution.py:189
  2224.8 24.0 all-reduce.58
  2258.9 27.1 reduce-scatter.91.cloned.1.call-done
  2285.9 65.5 %reduce-scatter.89.cloned.1.call-done = bf16[8,512,96]{1,2,0:T(8,128)(2,1)} async-done(((bf16[8,512,768]{1,2,0:T(8,128)(2,1)}), bf16[8,512,96]{1,2,0:T(8,128)(2,1)}) %reduce-scatter.89.cloned.1.call-update) | async-done | bytes 786448 | tf_op jit(solution)/shard_map/reduce_scatter | solution.py:479
  2355.2 92.1 %reduce-scatter.85.cloned.1.call-done = bf16[8,96,2,512]{3,1,2,0:T(8,128)(2,1)} async-done(((bf16[8,768,2,512]{3,1,2,0:T(8,128)(2,1)}), bf16[8,96,2,512]{3,1,2,0:T(8,128)(2,1)}) %reduce-scatter.85.cloned.1.call-update) | async-done | bytes 1572880 | tf_op jit(solution)/shard_map/reduce_scatter | solution.py:473
  2447.2 95.8 %reduce-scatter.87.cloned.1.call-done = bf16[8,96,2,512]{3,1,2,0:T(8,128)(2,1)} async-done(((bf16[8,768,2,512]{3,1,2,0:T(8,128)(2,1)}), bf16[8,96,2,512]{3,1,2,0:T(8,128)(2,1)}) %reduce-scatter.87.cloned.1.call-update) | async-done | bytes 1572880 | tf_op jit(solution)/shard_map/reduce_scatter | solution.py:473
  2547.1 91.9 %reduce-scatter.81.cloned.1.call-done = bf16[8,96,2,512]{3,1,2,0:T(8,128)(2,1)} async-done(((bf16[8,768,2,512]{3,1,2,0:T(8,128)(2,1)}), bf16[8,96,2,512]{3,1,2,0:T(8,128)(2,1)}) %reduce-scatter.81.cloned.1.call-update) | async-done | bytes 1572880 | tf_op jit(solution)/shard_map/reduce_scatter | solution.py:473
  2638.9 95.8 %reduce-scatter.83.cloned.1.call-done = bf16[8,96,2,512]{3,1,2,0:T(8,128)(2,1)} async-done(((bf16[8,768,2,512]{3,1,2,0:T(8,128)(2,1)}), bf16[8,96,2,512]{3,1,2,0:T(8,128)(2,1)}) %reduce-scatter.83.cloned.1.call-update) | async-done | bytes 1572880 | tf_op jit(solution)/shard_map/reduce_scatter | solution.py:473
  (1763 shorter events, 882.7 us)
Async XLA Ops:
  8.0 191.3 %all-reduce.77.cloned.1.call-start = ((), (), s32[]{:S(2)}) async-start(), calls=%async_computation.69 | async-start | bytes 6291456 | tf_op jit(solution)/shard_map/psum | solution.py:163
  77.4 153.9 %all-gather.25.cloned.1.call-start = ((), (), s32[]{:S(2)}) async-start(), calls=%async_computation.49 | async-start | bytes 7077888 | tf_op jit(solution)/shard_map/all_gather | solution.py:385
  79.8 160.7 %all-gather.23.cloned.1.call-start = ((), (), s32[]{:S(2)}) async-start(), calls=%async_computation.48 | async-start | bytes 14155776 | tf_op jit(solution)/shard_map/all_gather | solution.py:384
  86.3 296.8 %all-reduce.87.cloned.1.call-start = ((), (), s32[]{:S(2)}) async-start(), calls=%async_computation.74 | async-start | bytes 3145728 | tf_op jit(solution)/shard_map/psum | solution.py:189
  204.8 330.5 %copy-start.202 = (f32[512,12]{0,1:T(8,128)}, f32[512,12]{0,1:T(8,128)S(1)}, u32[]{:S(2)}) copy-start(f32[512,12]{0,1:T(8,128)S(1)} %convolution_add_fusion.3) | copy-start | bytes 73732
  314.5 185.5 %all-gather.29.cloned.1.call-start = ((), (), s32[]{:S(2)}) async-start(), calls=%async_computation.51 | async-start | bytes 7077888 | tf_op jit(solution)/shard_map/all_gather | solution.py:385
  317.0 212.7 %all-reduce.75.cloned.1.call-start = ((), (), s32[]{:S(2)}) async-start(), calls=%async_computation.68 | async-start | bytes 6291456 | tf_op jit(solution)/shard_map/psum | solution.py:163
  409.1 160.0 %all-gather.27.cloned.1.call-start = ((), (), s32[]{:S(2)}) async-start(), calls=%async_computation.50 | async-start | bytes 14155776 | tf_op jit(solution)/shard_map/all_gather | solution.py:384
  410.7 417.9 %all-reduce.85.cloned.1.call-start = ((), (), s32[]{:S(2)}) async-start(), calls=%async_computation.73 | async-start | bytes 3145728 | tf_op jit(solution)/shard_map/psum | solution.py:267
  759.3 353.0 %copy-start.173 = (f32[512,12]{0,1:T(8,128)}, f32[512,12]{0,1:T(8,128)S(1)}, u32[]{:S(2)}) copy-start(f32[512,12]{0,1:T(8,128)S(1)} %select_reduce_fusion.3) | copy-start | bytes 73732
  760.4 352.0 %copy-start.171 = (f32[512,12]{0,1:T(8,128)}, f32[512,12]{0,1:T(8,128)S(1)}, u32[]{:S(2)}) copy-start(f32[512,12]{0,1:T(8,128)S(1)} %select_reduce_fusion.1) | copy-start | bytes 73732
  760.4 105.5 %reduce-scatter.69.cloned.1.call-start = ((), (), s32[]{:S(2)}) async-start(), calls=%async_computation.34 | async-start | bytes 1179648 | tf_op jit(solution)/shard_map/reduce_scatter | solution.py:317
  850.3 19.3 reduce-scatter.65.cloned.1.call-start
  860.6 82.4 %all-reduce.83.cloned.1.call-start = ((), (), s32[]{:S(2)}) async-start(), calls=%async_computation.72 | async-start | bytes 3145728 | tf_op jit(solution)/shard_map/psum | solution.py:330
  872.4 306.2 %all-reduce.81.cloned.1.call-start = ((), (), s32[]{:S(2)}) async-start(), calls=%async_computation.71 | async-start | bytes 3145728 | tf_op jit(solution)/shard_map/psum | solution.py:267
  1110.8 139.2 %reduce-scatter.71.cloned.1.call-start = ((), (), s32[]{:S(2)}) async-start(), calls=%async_computation.35 | async-start | bytes 1179648 | tf_op jit(solution)/shard_map/reduce_scatter | solution.py:317
  1200.7 56.6 %reduce-scatter.67.cloned.1.call-start = ((), (), s32[]{:S(2)}) async-start(), calls=%async_computation.33 | async-start | bytes 1179648 | tf_op jit(solution)/shard_map/reduce_scatter | solution.py:317
  1211.3 122.7 %reduce-scatter.125.cloned.1.call-start = ((), (), s32[]{:S(2)}) async-start(), calls=%async_computation.66 | async-start | bytes 221184
  1214.1 120.8 %reduce-scatter.127.cloned.1.call-start = ((), (), s32[]{:S(2)}) async-start(), calls=%async_computation.67 | async-start | bytes 221184
  1215.0 120.7 %reduce-scatter.117.cloned.1.call-start = ((), (), s32[]{:S(2)}) async-start(), calls=%async_computation.62 | async-start | bytes 221184
  1216.4 151.2 %reduce-scatter.119.cloned.1.call-start = ((), (), s32[]{:S(2)}) async-start(), calls=%async_computation.63 | async-start | bytes 221184
  1217.8 186.2 %reduce-scatter.109.cloned.1.call-start = ((), (), s32[]{:S(2)}) async-start(), calls=%async_computation.58 | async-start | bytes 221184
  1219.9 220.8 %reduce-scatter.111.cloned.1.call-start = ((), (), s32[]{:S(2)}) async-start(), calls=%async_computation.59 | async-start | bytes 221184
  1222.1 255.4 %reduce-scatter.101.cloned.1.call-start = ((), (), s32[]{:S(2)}) async-start(), calls=%async_computation.54 | async-start | bytes 442368
  1223.4 291.4 %reduce-scatter.103.cloned.1.call-start = ((), (), s32[]{:S(2)}) async-start(), calls=%async_computation.55 | async-start | bytes 442368
  1226.2 327.6 %reduce-scatter.79.cloned.1.call-start = ((), (), s32[]{:S(2)}) async-start(), calls=%async_computation.39 | async-start | bytes 1105920 | tf_op jit(solution)/shard_map/reduce_scatter | solution.py:437
  1229.5 363.5 %reduce-scatter.77.cloned.1.call-start = ((), (), s32[]{:S(2)}) async-start(), calls=%async_computation.38 | async-start | bytes 1105920 | tf_op jit(solution)/shard_map/reduce_scatter | solution.py:437
  1232.7 396.9 %reduce-scatter.123.cloned.1.call-start = ((), (), s32[]{:S(2)}) async-start(), calls=%async_computation.65 | async-start | bytes 221184
  1235.5 430.9 %reduce-scatter.121.cloned.1.call-start = ((), (), s32[]{:S(2)}) async-start(), calls=%async_computation.64 | async-start | bytes 221184
  1236.4 466.6 %reduce-scatter.115.cloned.1.call-start = ((), (), s32[]{:S(2)}) async-start(), calls=%async_computation.61 | async-start | bytes 221184
  1237.8 501.9 %reduce-scatter.113.cloned.1.call-start = ((), (), s32[]{:S(2)}) async-start(), calls=%async_computation.60 | async-start | bytes 221184
  1239.3 537.0 %reduce-scatter.105.cloned.1.call-start = ((), (), s32[]{:S(2)}) async-start(), calls=%async_computation.56 | async-start | bytes 221184
  1240.8 572.7 %reduce-scatter.107.cloned.1.call-start = ((), (), s32[]{:S(2)}) async-start(), calls=%async_computation.57 | async-start | bytes 221184
  1242.2 608.1 %reduce-scatter.97.cloned.1.call-start = ((), (), s32[]{:S(2)}) async-start(), calls=%async_computation.52 | async-start | bytes 442368
  1245.0 642.3 %reduce-scatter.99.cloned.1.call-start = ((), (), s32[]{:S(2)}) async-start(), calls=%async_computation.53 | async-start | bytes 442368
  1247.9 678.9 %reduce-scatter.75.cloned.1.call-start = ((), (), s32[]{:S(2)}) async-start(), calls=%async_computation.37 | async-start | bytes 1105920 | tf_op jit(solution)/shard_map/reduce_scatter | solution.py:437
  1255.2 710.8 %reduce-scatter.73.cloned.1.call-start = ((), (), s32[]{:S(2)}) async-start(), calls=%async_computation.36 | async-start | bytes 1105920 | tf_op jit(solution)/shard_map/reduce_scatter | solution.py:437
  1262.4 769.3 %reduce-scatter.95.cloned.1.call-start = ((), (), s32[]{:S(2)}) async-start(), calls=%async_computation.47 | async-start | bytes 7077888 | tf_op jit(solution)/shard_map/reduce_scatter | solution.py:479
  1268.3 829.0 %reduce-scatter.93.cloned.1.call-start = ((), (), s32[]{:S(2)}) async-start(), calls=%async_computation.46 | async-start | bytes 7077888 | tf_op jit(solution)/shard_map/reduce_scatter | solution.py:479
  1275.9 945.9 %all-reduce.79.cloned.1.call-start = ((), (), s32[]{:S(2)}) async-start(), calls=%async_computation.70 | async-start | bytes 6291456 | tf_op jit(solution)/shard_map/psum | solution.py:189
  1280.7 1005.2 %reduce-scatter.91.cloned.1.call-start = ((), (), s32[]{:S(2)}) async-start(), calls=%async_computation.45 | async-start | bytes 7077888 | tf_op jit(solution)/shard_map/reduce_scatter | solution.py:479
  1288.4 1063.1 %reduce-scatter.89.cloned.1.call-start = ((), (), s32[]{:S(2)}) async-start(), calls=%async_computation.44 | async-start | bytes 7077888 | tf_op jit(solution)/shard_map/reduce_scatter | solution.py:479
  1295.9 1151.3 %reduce-scatter.85.cloned.1.call-start = ((), (), s32[]{:S(2)}) async-start(), calls=%async_computation.42 | async-start | bytes 14155776 | tf_op jit(solution)/shard_map/reduce_scatter | solution.py:473
  1305.2 1237.8 %reduce-scatter.87.cloned.1.call-start = ((), (), s32[]{:S(2)}) async-start(), calls=%async_computation.43 | async-start | bytes 14155776 | tf_op jit(solution)/shard_map/reduce_scatter | solution.py:473
  1314.5 1324.4 %reduce-scatter.81.cloned.1.call-start = ((), (), s32[]{:S(2)}) async-start(), calls=%async_computation.40 | async-start | bytes 14155776 | tf_op jit(solution)/shard_map/reduce_scatter | solution.py:473
  1323.9 1410.9 %reduce-scatter.83.cloned.1.call-start = ((), (), s32[]{:S(2)}) async-start(), calls=%async_computation.41 | async-start | bytes 14155776 | tf_op jit(solution)/shard_map/reduce_scatter | solution.py:473
  1333.1 261.0 %copy-start.172 = (f32[512,12]{0,1:T(8,128)S(1)}, f32[512,12]{0,1:T(8,128)}, u32[]{:S(2)}) copy-start(f32[512,12]{0,1:T(8,128)} %copy-done.171) | copy-start | bytes 73732
  1333.1 261.0 %copy-start.203 = (f32[512,12]{0,1:T(8,128)S(1)}, f32[512,12]{0,1:T(8,128)}, u32[]{:S(2)}) copy-start(f32[512,12]{0,1:T(8,128)} %copy-done.202) | copy-start | bytes 73732
  (510 other events, 7293.1 us)
Sparse Core Ops, SparseCore 0:
  77.5 121.7 all-reduce.76
  314.7 68.4 all-reduce.86
  409.2 120.4 all-reduce.74
  760.5 67.9 all-reduce.84
  850.4 7.3 reduce-scatter.68
  860.8 8.6 reduce-scatter.64
  872.5 70.4 all-reduce.82
  1110.9 67.6 all-reduce.80
  1200.8 7.3 reduce-scatter.70
  1211.4 8.3 reduce-scatter.66
  1222.8 34.7 reduce-scatter.124
  1260.8 33.4 reduce-scatter.126
  1297.3 33.4 reduce-scatter.116
  1334.0 33.5 reduce-scatter.118
  1370.4 33.4 reduce-scatter.108
  1407.1 33.5 reduce-scatter.110
  1443.6 33.8 reduce-scatter.100
  1481.0 33.8 reduce-scatter.102
  1518.1 35.7 reduce-scatter.78
  1557.2 35.7 reduce-scatter.76
  1596.0 33.4 reduce-scatter.122
  1632.9 33.5 reduce-scatter.120
  1669.4 33.4 reduce-scatter.114
  1706.1 33.5 reduce-scatter.112
  1742.7 33.4 reduce-scatter.104
  1780.0 33.5 reduce-scatter.106
  1816.5 33.8 reduce-scatter.96
  1853.4 33.8 reduce-scatter.98
  1891.0 35.7 reduce-scatter.74
  1930.2 35.7 reduce-scatter.72
  1969.9 61.7 reduce-scatter.94
  2035.5 61.7 reduce-scatter.92
  2099.7 122.1 all-reduce.78
  2225.2 60.6 reduce-scatter.90
  2289.7 61.7 reduce-scatter.88
  2354.8 92.3 reduce-scatter.84
  2450.6 92.3 reduce-scatter.86
  2546.5 92.3 reduce-scatter.80
  2642.3 92.3 reduce-scatter.82
Sparse Core Ops, SparseCore 1:
  80.3 47.3 all-gather.24
  130.0 71.9 all-gather.22
  317.1 46.6 all-gather.28
  411.7 74.2 all-gather.26
where the time goes:
time: 2760 us; the launch traced here: 2750 us
  waiting for transfers between devices  1570 us (57%)
  local copies, waits for them, and re-layouts  352 us (13%)
  other arithmetic  329 us (12%)
  matrix products  279 us (10%)
  blocking collectives  191 us (7%)
    unnamed x59, waiting for transfers between devices  447 us
    reduce_scatter x4, waiting for transfers between devices, per_device(): lax.psum_scatter(layer_grads[7].astype(jnp.bfloat16), ('fsdp', 'ctx'), sc...  375 us
    reduce_scatter x4, waiting for transfers between devices, per_device(): lax.psum_scatter(layer_grads[8].astype(jnp.bfloat16), ('fsdp', 'ctx'), sc...  222 us
    psum x2, waiting for transfers between devices, layer_forward(): lax.psum(ffn_part.astype(jnp.bfloat16), 'tp').astype(jnp.float32)  162 us
    reduce_scatter x4, waiting for transfers between devices, per_device(): lax.psum_scatter(layer_grads[1].astype(jnp.bfloat16), ('fsdp', 'ctx'), sc...  154 us
    unnamed x1103, local copies, waits for them, and re-layouts  120 us
    psum x2, waiting for transfers between devices, layer_backward(): lax.psum(grad_xm_part.astype(jnp.bfloat16), 'tp').astype(jnp.float32)  117 us
    reduce_sum x2, other arithmetic, gate_terms(): fixed_terms = jnp.sum(gate_vals[:, :, None] * slot_terms, axis=1)  61.7 us
  transfers between devices with their start and end apart: 43, of which 32 were waited for; matrix products, arithmetic and copies ran while one was open for 16% of the time, Pallas kernels for 0%

commit v1 on v0

v1 whole, which is shorter than its diff:
```python
import functools

import jax
import jax.numpy as jnp
from jax import lax
from jax.experimental import pallas as pl
from jax.experimental.pallas import tpu as pltpu
from jax.sharding import PartitionSpec as P

HD = 64
NF = 8
NE = 12
BLOCK = 512
CAP = 128
TILE = 256
EPSILON = 1e-06
MASKED = -1e30
F32 = jnp.float32
BF16 = jnp.bfloat16
HIGH = lax.Precision.HIGHEST
ROW_CONST, ROW_VEC, ROW_GA, ROW_GM = 16, 20, 22, 23
VMEM_LIMIT = 58 * 1024 * 1024

NN = (((1,), (0,)), ((), ()))
NT = (((1,), (1,)), ((), ()))
TN = (((0,), (0,)), ((), ()))


def mm(left, right, dims=NN, precision=None):
    return lax.dot_general(left, right, dims, precision=precision, preferred_element_type=F32)


def kernel_params():
    return pltpu.CompilerParams(vmem_limit_bytes=VMEM_LIMIT)


def cost(flops, nbytes, trans=0):
    return pl.CostEstimate(flops=int(flops), bytes_accessed=int(nbytes), transcendentals=int(trans))


def iota(shape, dim):
    return lax.broadcasted_iota(jnp.int32, shape, dim)


def full_spec(shape):
    zeros = (0,) * len(shape)
    return pl.BlockSpec(shape, lambda *idx: zeros)


SMEM_SPEC = pl.BlockSpec(memory_space=pltpu.SMEM)


def pad_rows(rows, count, width):
    row_id = iota((count, width), 0)
    out = jnp.zeros((count, width), F32)
    for place, row in rows:
        out = jnp.where(row_id == place, row, out)
    return out


def prep_kernel(count, rows, offs_ref, *refs):
    in_a, in_w = refs[:count], refs[count : 2 * count]
    qkv_ref, wo_ref, vec_ref = refs[2 * count :]
    cols = qkv_ref.shape[1]
    vec_cols = []
    for piece in range(count):
        start = pl.multiple_of(offs_ref[piece] * rows, rows)
        block = in_a[piece][...]
        qkv_ref[pl.ds(start, rows), :] = block[:, :cols]
        vec_ref[pl.ds(start, rows), :] = block[:, cols:]
        for rank in range(wo_ref.shape[0]):
            wo_ref[rank, pl.ds(start, rows), :] = in_w[piece][rank]
    del vec_cols


def prep_weights(pieces_a, pieces_w, offs, feature_dim, qkv_cols):
    count = len(pieces_a)
    rows = feature_dim // count
    tp_count, _, out_cols = pieces_w[0].shape
    vec_cols = pieces_a[0].shape[1] - qkv_cols
    return pl.pallas_call(
        functools.partial(prep_kernel, count, rows),
        out_shape=(
            jax.ShapeDtypeStruct((feature_dim, qkv_cols), BF16),
            jax.ShapeDtypeStruct((tp_count, feature_dim, out_cols), BF16),
            jax.ShapeDtypeStruct((feature_dim, vec_cols), BF16),
        ),
        in_specs=[SMEM_SPEC] + [pl.BlockSpec(memory_space=pltpu.VMEM)] * (2 * count),
        out_specs=tuple([pl.BlockSpec(memory_space=pltpu.VMEM)] * 3),
        compiler_params=kernel_params(),
        cost_estimate=cost(1e6, 5e6),
        name="prep",
    )(offs, *pieces_a, *pieces_w)


def qkv_kernel(with_ffn, *refs):
    if with_ffn:
        base_ref, ffn_ref, vec_ref, w_ref, h_ref, qkv_ref = refs
        hidden = base_ref[...] + ffn_ref[...].astype(F32)
        h_ref[...] = hidden
    else:
        base_ref, vec_ref, w_ref, qkv_ref = refs
        hidden = base_ref[...].astype(F32)
    gain = vec_ref[ROW_GA : ROW_GA + 1, :]
    scale = lax.rsqrt(jnp.mean(hidden * hidden, axis=-1, keepdims=True) + EPSILON)
    attn_in = (hidden * scale * gain).astype(BF16)
    qkv_ref[...] = mm(attn_in, w_ref[...]).astype(BF16)


def qkv_part(base, ffn, vecs, w_qkv):
    rows, feature_dim = base.shape
    cols = w_qkv.shape[1]
    row_spec = pl.BlockSpec((TILE, feature_dim), lambda i: (i, 0))
    with_ffn = ffn is not None
    out_shape = [jax.ShapeDtypeStruct((rows, cols), BF16)]
    out_specs = [pl.BlockSpec((TILE, cols), lambda i: (i, 0))]
    if with_ffn:
        out_shape = [jax.ShapeDtypeStruct((rows, feature_dim), F32)] + out_shape
        out_specs = [row_spec] + out_specs
    ins = [base] + ([ffn] if with_ffn else []) + [vecs, w_qkv]
    in_specs = [row_spec] * (2 if with_ffn else 1) + [full_spec(vecs.shape), full_spec(w_qkv.shape)]
    return pl.pallas_call(
        functools.partial(qkv_kernel, with_ffn),
        grid=(rows // TILE,),
        out_shape=tuple(out_shape),
        in_specs=in_specs,
        out_specs=tuple(out_specs),
        compiler_params=kernel_params(),
        cost_estimate=cost(2 * rows * feature_dim * cols, rows * feature_dim * 10),
        name="qkv_part",
    )(*ins)


def attn_masks(ctx, length, tile, width):
    row = iota((TILE, width), 0) + tile * TILE
    col = iota((TILE, width), 1)
    return (col <= row) & (col + ctx * BLOCK < length)


def attn_fwd_kernel(heads, info_ref, own_ref, other_ref, ctx_ref, lse_ref):
    ctx = info_ref[0]
    length = info_ref[1 + pl.program_id(0)]
    own = own_ref[...]
    other = other_ref[...]
    for head in range(heads):
        col = head * 3 * HD
        k_own = own[:, col + HD : col + 2 * HD]
        v_own = own[:, col + 2 * HD : col + 3 * HD]
        k_oth = other[:, col + HD : col + 2 * HD]
        v_oth = other[:, col + 2 * HD : col + 3 * HD]
        for tile in range(BLOCK // TILE):
            width = (tile + 1) * TILE
            query = own[tile * TILE : (tile + 1) * TILE, col : col + HD] * BF16(HD**-0.5)
            s_own = mm(query, k_own[:width], NT)
            s_own = jnp.where(attn_masks(ctx, length, tile, width), s_own, MASKED)
            s_oth = jnp.where(ctx > 0, mm(query, k_oth, NT), MASKED)
            top = jnp.maximum(
                jnp.max(s_own, axis=-1, keepdims=True), jnp.max(s_oth, axis=-1, keepdims=True)
            )
            p_own = jnp.exp(s_own - top)
            p_oth = jnp.exp(s_oth - top)
            total = jnp.sum(p_own, axis=-1, keepdims=True) + jnp.sum(p_oth, axis=-1, keepdims=True)
            out = mm(p_own.astype(BF16), v_own[:width]) + mm(p_oth.astype(BF16), v_oth)
            out = out / total
            rows = slice(tile * TILE, (tile + 1) * TILE)
            ctx_ref[rows, head * HD : (head + 1) * HD] = out.astype(BF16)
            lse_ref[rows, head : head + 1] = top + jnp.log(total)


def attend_forward(qkv, other, info, heads):
    rows, cols = qkv.shape
    count = rows // BLOCK
    spec = pl.BlockSpec((BLOCK, cols), lambda i: (i, 0))
    return pl.pallas_call(
        functools.partial(attn_fwd_kernel, heads),
        grid=(count,),
        out_shape=(
            jax.ShapeDtypeStruct((rows, heads * HD), BF16),
            jax.ShapeDtypeStruct((rows, 8), F32),
        ),
        in_specs=[SMEM_SPEC, spec, spec],
        out_specs=(
            pl.BlockSpec((BLOCK, heads * HD), lambda i: (i, 0)),
            pl.BlockSpec((BLOCK, 8), lambda i: (i, 0)),
        ),
        compiler_params=kernel_params(),
        cost_estimate=cost(rows * 1024 * heads * HD * 16, rows * cols * 6, rows * heads * 1024),
        name="attend_forward",
    )(info, qkv, other)


def attn_bwd_kernel(heads, info_ref, own_ref, other_ref, lse_ref, gctx_ref, gown_ref, goth_ref):
    ctx = info_ref[0]
    length = info_ref[1 + pl.program_id(0)]
    own = own_ref[...]
    other = other_ref[...]
    scale = BF16(HD**-0.5)
    for head in range(heads):
        col = head * 3 * HD
        k_own = own[:, col + HD : col + 2 * HD]
        v_own = own[:, col + 2 * HD : col + 3 * HD]
        k_oth = other[:, col + HD : col + 2 * HD]
        v_oth = other[:, col + 2 * HD : col + 3 * HD]
        goth_ref[:, col : col + HD] = jnp.zeros((BLOCK, HD), BF16)
        gk_own, gv_own, gk_oth, gv_oth = [], [], [], []
        for tile in range(BLOCK // TILE):
            width = (tile + 1) * TILE
            rows = slice(tile * TILE, (tile + 1) * TILE)
            query = own[rows, col : col + HD] * scale
            gout = gctx_ref[rows, head * HD : (head + 1) * HD]
            lse = lse_ref[rows, head : head + 1]
            s_own = mm(query, k_own[:width], NT)
            s_own = jnp.where(attn_masks(ctx, length, tile, width), s_own, MASKED)
            s_oth = jnp.where(ctx > 0, mm(query, k_oth, NT), MASKED)
            p_own = jnp.exp(s_own - lse)
            p_oth = jnp.exp(s_oth - lse)
            d_own = mm(gout, v_own[:width], NT)
            d_oth = mm(gout, v_oth, NT)
            inner = jnp.sum(p_own * d_own, axis=-1, keepdims=True) + jnp.sum(
                p_oth * d_oth, axis=-1, keepdims=True
            )
            ds_own = (p_own * (d_own - inner)).astype(BF16)
            ds_oth = (p_oth * (d_oth - inner)).astype(BF16)
            p_own = p_own.astype(BF16)
            p_oth = p_oth.astype(BF16)
            gown_ref[rows, col : col + HD] = (mm(ds_own, k_own[:width]) + mm(ds_oth, k_oth)) * (
                HD**-0.5
            )
            gk_own.append(mm(ds_own, query, TN))
            gv_own.append(mm(p_own, gout, TN))
            gk_oth.append(mm(ds_oth, query, TN))
            gv_oth.append(mm(p_oth, gout, TN))
        gown_ref[:TILE, col + HD : col + 2 * HD] = gk_own[0] + gk_own[1][:TILE]
        gown_ref[TILE:, col + HD : col + 2 * HD] = gk_own[1][TILE:]
        gown_ref[:TILE, col + 2 * HD : col + 3 * HD] = gv_own[0] + gv_own[1][:TILE]
        gown_ref[TILE:, col + 2 * HD : col + 3 * HD] = gv_own[1][TILE:]
        goth_ref[:, col + HD : col + 2 * HD] = (gk_oth[0] + gk_oth[1]).astype(BF16)
        goth_ref[:, col + 2 * HD : col + 3 * HD] = (gv_oth[0] + gv_oth[1]).astype(BF16)


def attend_backward(qkv, other, lse, grad_context, info, heads):
    rows, cols = qkv.shape
    spec = pl.BlockSpec((BLOCK, cols), lambda i: (i, 0))
    return pl.pallas_call(
        functools.partial(attn_bwd_kernel, heads),
        grid=(rows // BLOCK,),
        out_shape=(
            jax.ShapeDtypeStruct((rows, cols), F32),
            jax.ShapeDtypeStruct((rows, cols), BF16),
        ),
        in_specs=[
            SMEM_SPEC,
            spec,
            spec,
            pl.BlockSpec((BLOCK, 8), lambda i: (i, 0)),
            pl.BlockSpec((BLOCK, heads * HD), lambda i: (i, 0)),
        ],
        out_specs=(spec, spec),
        compiler_params=kernel_params(),
        cost_estimate=cost(rows * 1024 * heads * HD * 40, rows * cols * 12, rows * heads * 1024),
        name="attend_backward",
    )(info, qkv, other, lse, grad_context)


def alpha_rows(gate_in, const_idx):
    first = gate_in[ROW_CONST + 2 * const_idx : ROW_CONST + 2 * const_idx + 1]
    second = gate_in[ROW_CONST + 2 * const_idx + 1 : ROW_CONST + 2 * const_idx + 2]
    return pair(first, second)


def pair(first, second):
    top = jnp.maximum(first, second)
    exp_first = jnp.exp(first - top)
    exp_second = jnp.exp(second - top)
    total = exp_first + exp_second
    return exp_first / total, exp_second / total


def picks(route, value):
    return (route == value).astype(F32)


def gate_coefs(routes, gates, alphas):
    copy = picks(routes[0], NF + 1) * gates[0] + picks(routes[1], NF + 1) * gates[1]
    const = [
        picks(routes[0], NF + 2 + j) * gates[0] + picks(routes[1], NF + 2 + j) * gates[1]
        for j in range(2)
    ]
    on_normed = copy + const[0] * alphas[0][0] + const[1] * alphas[1][0]
    on_vec = [const[j] * alphas[j][1] for j in range(2)]
    return const, on_normed, on_vec


def to_columns(rows):
    width = rows[0].shape[1]
    return pad_rows(list(enumerate(rows)), 128, width).T


def middle_kernel(with_prev, *refs):
    if with_prev:
        h_ref, ctx_ref, wo_ref, vec_ref, route_ref, prev_ref, resid_ref = refs[:7]
        refs = refs[7:]
    else:
        h_ref, ctx_ref, wo_ref, vec_ref, route_ref = refs[:5]
        refs = refs[5:]
    mid_ref, base_ref, xm_ref, gate_ref, logit_ref = refs
    attn_out = mm(ctx_ref[0], wo_ref[0], NT)
    for rank in range(1, ctx_ref.shape[0]):
        attn_out += mm(ctx_ref[rank], wo_ref[rank], NT)
    middle = h_ref[...].astype(F32) + attn_out
    mid_ref[...] = middle
    vecs = vec_ref[...]
    scale = lax.rsqrt(jnp.mean(middle * middle, axis=-1, keepdims=True) + EPSILON)
    normed = middle * scale * vecs[ROW_GM : ROW_GM + 1]
    xm_low = normed.astype(BF16)
    xm_ref[...] = xm_low
    gate_in = mm(vecs[:32].astype(BF16), xm_low, NT)
    logits = gate_in[:16]
    if with_prev:
        logits = logits + mm(resid_ref[...], prev_ref[...], TN, HIGH)
    logit_ref[...] = logits
    routes = (route_ref[0:1], route_ref[1:2])
    expert = iota(logits.shape, 0)
    chosen = [
        jnp.sum(jnp.where(expert == route, logits, 0.0), axis=0, keepdims=True) for route in routes
    ]
    gates = pair(chosen[0], chosen[1])
    gate_ref[...] = pad_rows(list(enumerate(gates)), 8, logits.shape[1])
    alphas = [alpha_rows(gate_in, j) for j in range(2)]
    const, on_normed, on_vec = gate_coefs(routes, gates, alphas)
    cols = to_columns([on_normed, on_vec[0], on_vec[1]])
    base_ref[...] = (
        middle
        + cols[:, 0:1] * normed
        + cols[:, 1:2] * vecs[ROW_VEC : ROW_VEC + 1]
        + cols[:, 2:3] * vecs[ROW_VEC + 1 : ROW_VEC + 2]
    )


def middle_part(h, ctx_all, wo_all, vecs, routes_t, prev_t, resid):
    rows, feature_dim = h.shape
    tp_count, _, out_cols = ctx_all.shape
    row_spec = pl.BlockSpec((TILE, feature_dim), lambda i: (i, 0))
    lane8 = pl.BlockSpec((8, TILE), lambda i: (0, i))
    lane16 = pl.BlockSpec((16, TILE), lambda i: (0, i))
    ins = [h, ctx_all, wo_all, vecs, routes_t]
    in_specs = [
        row_spec,
        pl.BlockSpec((tp_count, TILE, out_cols), lambda i: (0, i, 0)),
        full_spec(wo_all.shape),
        full_spec(vecs.shape),
        lane8,
    ]
    with_prev = prev_t is not None
    if with_prev:
        ins += [prev_t, resid]
        in_specs += [lane16, full_spec(resid.shape)]
    return pl.pallas_call(
        functools.partial(middle_kernel, with_prev),
        grid=(rows // TILE,),
        out_shape=(
            jax.ShapeDtypeStruct((rows, feature_dim), F32),
            jax.ShapeDtypeStruct((rows, feature_dim), F32),
            jax.ShapeDtypeStruct((rows, feature_dim), BF16),
            jax.ShapeDtypeStruct((8, rows), F32),
            jax.ShapeDtypeStruct((16, rows), F32),
        ),
        in_specs=in_specs,
        out_specs=(row_spec, row_spec, row_spec, lane8, lane16),
        compiler_params=kernel_params(),
        cost_estimate=cost(2 * rows * feature_dim * feature_dim, rows * feature_dim * 16),
        name="middle_part",
    )(*ins)


def split(value):
    high = value.astype(BF16)
    return high, (value - high.astype(F32)).astype(BF16)


def gate_bwd_kernel(with_prev, rank_ref, *refs):
    del rank_ref
    gh_ref, mid_ref, gxm_ref, vec_ref, route_ref, gate_ref, gg_ref, ctx_ref, wo_ref = refs[:9]
    refs = refs[9:]
    if with_prev:
        prev_ref, resid_ref = refs[:2]
        gmid_ref, gctx_ref, dwo_ref, dvec_ref, gprev_ref, dres_ref = refs[2:]
    else:
        gl_ref = refs[0]
        gmid_ref, gctx_ref, dwo_ref, dvec_ref = refs[1:]
    step = pl.program_id(0)
    grad = gh_ref[...].astype(F32)
    middle = mid_ref[...]
    vecs = vec_ref[...]
    gain = vecs[ROW_GM : ROW_GM + 1]
    scale = lax.rsqrt(jnp.mean(middle * middle, axis=-1, keepdims=True) + EPSILON)
    unit = middle * scale
    normed = unit * gain
    xm_low = normed.astype(BF16)
    low_vecs = vecs[:32].astype(BF16)
    gate_in = mm(low_vecs, xm_low, NT)
    alphas = [alpha_rows(gate_in, j) for j in range(2)]
    routes = (route_ref[0:1], route_ref[1:2])
    gates = (gate_ref[0:1], gate_ref[1:2])
    const, on_normed, on_vec = gate_coefs(routes, gates, alphas)
    grad_hi, grad_lo = split(grad)
    vec_dots = mm(low_vecs[16:32], grad_hi, NT) + mm(low_vecs[16:32], grad_lo, NT)
    dot_vec = [vec_dots[ROW_VEC - 16 + j : ROW_VEC - 15 + j] for j in range(2)]
    dot_col = jnp.sum(grad * normed, axis=-1, keepdims=True)
    dot_normed = jnp.broadcast_to(dot_col, (dot_col.shape[0], 128)).T[0:1]
    term = [alphas[j][0] * dot_normed + alphas[j][1] * dot_vec[j] for j in range(2)]
    gate_grads = []
    for slot in range(2):
        fixed = (
            picks(routes[slot], NF + 1) * dot_normed
            + picks(routes[slot], NF + 2) * term[0]
            + picks(routes[slot], NF + 3) * term[1]
        )
        gate_grads.append(jnp.where(routes[slot] < NF, gg_ref[slot : slot + 1], fixed))
    inner = gates[0] * gate_grads[0] + gates[1] * gate_grads[1]
    chosen_grads = [gates[slot] * (gate_grads[slot] - inner) for slot in range(2)]
    expert = iota((16, TILE), 0)
    grad_logits = jnp.where(expert == routes[0], chosen_grads[0], 0.0) + jnp.where(
        expert == routes[1], chosen_grads[1], 0.0
    )
    if not with_prev:
        grad_logits = grad_logits + gl_ref[...]
    alpha_grads = []
    for j in range(2):
        grad_first = const[j] * dot_normed
        grad_second = const[j] * dot_vec[j]
        mean = alphas[j][0] * grad_first + alphas[j][1] * grad_second
        alpha_grads.append((2 * j, alphas[j][0] * (grad_first - mean)))
        alpha_grads.append((2 * j + 1, alphas[j][1] * (grad_second - mean)))
    grad_in = jnp.concatenate([grad_logits, pad_rows(alpha_grads, 16, TILE)], axis=0)
    in_hi, in_lo = split(grad_in)
    low_gate = jnp.where(iota(low_vecs.shape, 0) < ROW_VEC, low_vecs, 0)
    grad_xm = mm(in_hi, low_gate, TN) + mm(in_lo, low_gate, TN)
    cols = to_columns([on_normed])
    grad_y = cols[:, 0:1] * grad + grad_xm + gxm_ref[...].astype(F32)
    weighted = grad_y * gain
    mean = jnp.mean(weighted * unit, axis=-1, keepdims=True)
    grad_mid = grad + scale * (weighted - unit * mean)
    gmid_ref[...] = grad_mid
    low_mid = grad_mid.astype(BF16)
    gctx_ref[...] = mm(low_mid, wo_ref[...]).astype(BF16)
    dwo = mm(low_mid, ctx_ref[...], TN)
    vec_rows = pad_rows([(ROW_VEC - 16 + j, on_vec[j]) for j in range(2)], 16, TILE)
    vec_hi, vec_lo = split(vec_rows)
    dvec_low = mm(vec_hi, grad_hi) + mm(vec_lo, grad_hi)
    dvec_gate = mm(in_hi, xm_low) + mm(in_lo, xm_low)
    dgain = jnp.sum(grad_y * unit, axis=0, keepdims=True)
    row_id = iota(dvec_gate.shape, 0)
    dvec = dvec_gate + jnp.concatenate([jnp.zeros_like(dvec_low), dvec_low], axis=0)
    dvec = jnp.where(row_id == ROW_GM, dgain, dvec)

    @pl.when(step == 0)
    def _():
        dwo_ref[...] = dwo
        dvec_ref[...] = dvec

    @pl.when(step > 0)
    def _():
        dwo_ref[...] += dwo
        dvec_ref[...] += dvec

    if with_prev:
        gprev_ref[...] = mm(resid_ref[...], grad_logits, NN, HIGH)
        dres = mm(prev_ref[...], grad_logits, NT, HIGH)

        @pl.when(step == 0)
        def _():
            dres_ref[...] = dres

        @pl.when(step > 0)
        def _():
            dres_ref[...] += dres


def gate_backward(grad, middle, gxm, vecs, routes_t, gates_t, gg_t, context, wo_all, rank, extra):
    rows, feature_dim = middle.shape
    out_cols = context.shape[1]
    with_prev = len(extra) == 2
    row_spec = pl.BlockSpec((TILE, feature_dim), lambda i, r: (i, 0))
    lane8 = pl.BlockSpec((8, TILE), lambda i, r: (0, i))
    lane16 = pl.BlockSpec((16, TILE), lambda i, r: (0, i))
    ctx_spec = pl.BlockSpec((TILE, out_cols), lambda i, r: (i, 0))
    wo_spec = pl.BlockSpec((pl.Squeezed(), feature_dim, out_cols), lambda i, r: (r[0], 0, 0))
    in_specs = [row_spec, row_spec, row_spec, full_spec(vecs.shape), lane8, lane8, lane8]
    in_specs += [ctx_spec, wo_spec, lane16]
    out_shape = [
        jax.ShapeDtypeStruct((rows, feature_dim), F32),
        jax.ShapeDtypeStruct((rows, out_cols), BF16),
        jax.ShapeDtypeStruct((feature_dim, out_cols), F32),
        jax.ShapeDtypeStruct((32, feature_dim), F32),
    ]
    out_specs = [row_spec, ctx_spec, full_spec((feature_dim, out_cols)), full_spec((32, feature_dim))]
    if with_prev:
        in_specs.append(full_spec(extra[1].shape))
        out_shape += [jax.ShapeDtypeStruct((16, rows), F32), jax.ShapeDtypeStruct((16, 16), F32)]
        out_specs += [lane16, full_spec((16, 16))]
    return pl.pallas_call(
        functools.partial(gate_bwd_kernel, with_prev),
        grid_spec=pltpu.PrefetchScalarGridSpec(
            num_scalar_prefetch=1,
            grid=(rows // TILE,),
            in_specs=in_specs,
            out_specs=tuple(out_specs),
        ),
        out_shape=tuple(out_shape),
        compiler_params=kernel_params(),
        cost_estimate=cost(4 * rows * feature_dim * out_cols, rows * feature_dim * 18),
        name="gate_backward",
    )(rank, grad, middle, gxm, vecs, routes_t, gates_t, gg_t, context, wo_all, *extra)


def qkv_bwd_kernel(gown_ref, goth_ref, h_ref, vec_ref, w_ref, part_ref, dw_ref):
    step = pl.program_id(0)
    grad = (gown_ref[...] + goth_ref[...].astype(F32)).astype(BF16)
    part_ref[...] = mm(grad, w_ref[...], NT).astype(BF16)
    hidden = h_ref[...].astype(F32)
    gain = vec_ref[ROW_GA : ROW_GA + 1, :]
    scale = lax.rsqrt(jnp.mean(hidden * hidden, axis=-1, keepdims=True) + EPSILON)
    attn_in = (hidden * scale * gain).astype(BF16)
    dw = mm(attn_in, grad, TN)

    @pl.when(step == 0)
    def _():
        dw_ref[...] = dw

    @pl.when(step > 0)
    def _():
        dw_ref[...] += dw


def qkv_backward(gown, goth, h, vecs, w_qkv):
    rows, feature_dim = h.shape
    cols = w_qkv.shape[1]
    row_spec = pl.BlockSpec((TILE, feature_dim), lambda i: (i, 0))
    col_spec = pl.BlockSpec((TILE, cols), lambda i: (i, 0))
    return pl.pallas_call(
        qkv_bwd_kernel,
        grid=(rows // TILE,),
        out_shape=(
            jax.ShapeDtypeStruct((rows, feature_dim), BF16),
            jax.ShapeDtypeStruct((feature_dim, cols), F32),
        ),
        in_specs=[col_spec, col_spec, row_spec, full_spec(vecs.shape), full_spec(w_qkv.shape)],
        out_specs=(row_spec, full_spec((feature_dim, cols))),
        compiler_params=kernel_params(),
        cost_estimate=cost(4 * rows * feature_dim * cols, rows * feature_dim * 10),
        name="qkv_backward",
    )(gown, goth, h, vecs, w_qkv)


def norm_bwd_kernel(with_low, gmid_ref, ga_ref, h_ref, vec_ref, out_ref, *rest):
    step = pl.program_id(0)
    hidden = h_ref[...].astype(F32)
    gain = vec_ref[ROW_GA : ROW_GA + 1, :]
    scale = lax.rsqrt(jnp.mean(hidden * hidden, axis=-1, keepdims=True) + EPSILON)
    unit = hidden * scale
    grad_y = ga_ref[...].astype(F32)
    weighted = grad_y * gain
    mean = jnp.mean(weighted * unit, axis=-1, keepdims=True)
    grad = gmid_ref[...] + scale * (weighted - unit * mean)
    out_ref[...] = grad
    if with_low:
        rest[0][...] = grad.astype(BF16)
    dgain_ref = rest[-1]
    dgain = jnp.broadcast_to(jnp.sum(grad_y * unit, axis=0, keepdims=True), dgain_ref.shape)

    @pl.when(step == 0)
    def _():
        dgain_ref[...] = dgain

    @pl.when(step > 0)
    def _():
        dgain_ref[...] += dgain


def norm_backward(gmid, ga, h, vecs, with_low):
    rows, feature_dim = gmid.shape
    row_spec = pl.BlockSpec((TILE, feature_dim), lambda i: (i, 0))
    out_shape = [jax.ShapeDtypeStruct((rows, feature_dim), F32)]
    out_specs = [row_spec]
    if with_low:
        out_shape.append(jax.ShapeDtypeStruct((rows, feature_dim), BF16))
        out_specs.append(row_spec)
    out_shape.append(jax.ShapeDtypeStruct((8, feature_dim), F32))
    out_specs.append(full_spec((8, feature_dim)))
    return pl.pallas_call(
        functools.partial(norm_bwd_kernel, with_low),
        grid=(rows // TILE,),
        out_shape=tuple(out_shape),
        in_specs=[row_spec, row_spec, row_spec, full_spec(vecs.shape)],
        out_specs=tuple(out_specs),
        compiler_params=kernel_params(),
        cost_estimate=cost(rows * feature_dim * 10, rows * feature_dim * 16),
        name="norm_backward",
    )(gmid, ga, h, vecs)


def experts_kernel(fwd, bwd, blocks, count, halves, rows, offs_ref, *refs):
    refs = list(refs)
    xm_ref = refs.pop(0)
    gh_ref = refs.pop(0) if bwd else None
    route_ref, gate_ref = refs.pop(0), refs.pop(0)
    w_refs = [refs.pop(0) for _ in range(count * halves)]
    ffn_ref = refs.pop(0) if fwd else None
    if bwd:
        gx_ref = refs.pop(0)
        dw_refs = [refs.pop(0) for _ in range(count * halves)]
    w_scr, place_scr, pick_scr = refs.pop(0), refs.pop(0), refs.pop(0)
    acc_ref = refs.pop(0) if fwd else None
    if bwd:
        gacc_ref, raw_scr, gg_scr, dw_scr = refs
    expert = pl.program_id(0)
    last = pl.num_programs(0) - 1
    width = w_scr.shape[1]
    units = width // 3
    half = NF // halves

    @pl.when(expert == 0)
    def _():
        order = (iota((BLOCK, BLOCK), 0) < iota((BLOCK, BLOCK), 1)).astype(BF16)
        for block in range(blocks):
            lanes = slice(block * BLOCK, (block + 1) * BLOCK)
            ids = iota((8, BLOCK), 0)
            hits = (ids == route_ref[0:1, lanes]) | (ids == route_ref[1:2, lanes])
            earlier = mm(hits.astype(BF16), order)
            place_scr[block] = jnp.where(hits, earlier, -1.0)
        if fwd:
            acc_ref[...] = jnp.zeros_like(acc_ref)
        if bwd:
            gacc_ref[...] = jnp.zeros_like(gacc_ref)
            gg_scr[...] = jnp.zeros_like(gg_scr)

    for part in range(halves):

        @pl.when((expert >= part * half) & (expert < (part + 1) * half))
        def _(part=part):
            for piece in range(count):
                start = pl.multiple_of(offs_ref[piece] * rows, rows)
                w_scr[pl.ds(start, rows), :] = w_refs[part * count + piece][0]

    hot, gate_cols, masks = [], [], []
    for block in range(blocks):
        lanes = slice(block * BLOCK, (block + 1) * BLOCK)
        place = place_scr[block, pl.ds(expert, 1), :]
        one_hot = (iota((CAP, BLOCK), 0).astype(F32) == place).astype(F32)
        mask = [route_ref[slot : slot + 1, lanes] == expert for slot in range(2)]
        gate_row = jnp.where(mask[0], gate_ref[0:1, lanes], 0.0) + jnp.where(
            mask[1], gate_ref[1:2, lanes], 0.0
        )
        gate_cols.append(jnp.sum(one_hot * gate_row, axis=1, keepdims=True))
        one_hot = one_hot.astype(BF16)
        pick_scr[block * CAP : (block + 1) * CAP, :] = mm(one_hot, xm_ref[lanes, :]).astype(BF16)
        if bwd:
            raw_scr[block * CAP : (block + 1) * CAP, :] = mm(one_hot, gh_ref[lanes, :]).astype(BF16)
        hot.append(one_hot)
        masks.append(mask)
    gate_col = jnp.concatenate(gate_cols, axis=0)
    picked = pick_scr[...]
    gate_up = mm(picked, w_scr[:, : 2 * units])
    gate_in, up_in = gate_up[:, :units], gate_up[:, units:]
    sigmoid = lax.logistic(gate_in)
    silu = gate_in * sigmoid
    hidden = (silu * up_in).astype(BF16)
    if fwd:
        scaled = (mm(hidden, w_scr[:, 2 * units :], NT) * gate_col).astype(BF16)
        for block in range(blocks):
            acc_ref[block * BLOCK : (block + 1) * BLOCK, :] += mm(
                hot[block], scaled[block * CAP : (block + 1) * CAP], TN
            )

        @pl.when(expert == last)
        def _():
            ffn_ref[...] = acc_ref[...].astype(BF16)

    if bwd:
        raw = raw_scr[...]
        grad_raw = mm(raw, w_scr[:, 2 * units :])
        gate_dot = jnp.sum(hidden.astype(F32) * grad_raw, axis=1, keepdims=True)
        for block in range(blocks):
            row = jnp.sum(
                hot[block].astype(F32) * gate_dot[block * CAP : (block + 1) * CAP],
                axis=0,
                keepdims=True,
            )
            for slot in range(2):
                gg_scr[8 * block + slot : 8 * block + slot + 1, :] += jnp.where(
                    masks[block][slot], row, 0.0
                )
        grad_hidden = grad_raw * gate_col
        grad_gate = grad_hidden * up_in * sigmoid * (1.0 + gate_in * (1.0 - sigmoid))
        grad_up = grad_hidden * silu
        grad_gu = jnp.concatenate([grad_gate.astype(BF16), grad_up.astype(BF16)], axis=1)
        grad_pick = mm(grad_gu, w_scr[:, : 2 * units], NT).astype(BF16)
        for block in range(blocks):
            gacc_ref[block * BLOCK : (block + 1) * BLOCK, :] += mm(
                hot[block], grad_pick[block * CAP : (block + 1) * CAP], TN
            )
        grad_result = (raw.astype(F32) * gate_col).astype(BF16)
        dw_scr[:, : 2 * units] = mm(picked, grad_gu, TN).astype(BF16)
        dw_scr[:, 2 * units :] = mm(grad_result, hidden, TN).astype(BF16)
        for part in range(halves):

            @pl.when((expert >= part * half) & (expert < (part + 1) * half))
            def _(part=part):
                for piece in range(count):
                    start = pl.multiple_of(offs_ref[piece] * rows, rows)
                    dw_refs[part * count + piece][0] = dw_scr[pl.ds(start, rows), :]

        @pl.when(expert == last)
        def _():
            total = blocks * BLOCK
            gx_ref[:total, :] = gacc_ref[...].astype(BF16)
            gx_ref[total:, :] = jnp.zeros((gx_ref.shape[0] - total, gx_ref.shape[1]), BF16)
            gx_ref[total : total + gg_scr.shape[0], :BLOCK] = gg_scr[...].astype(BF16)


def experts(fwd, bwd, xm, gh, routes_t, gates_t, pieces, offs):
    rows, feature_dim = xm.shape
    blocks = rows // BLOCK
    halves, count = len(pieces), len(pieces[0])
    half = NF // halves
    piece_rows = pieces[0][0].shape[1]
    width = pieces[0][0].shape[2]
    units = width // 3

    def piece_specs():
        specs = []
        for part in range(halves):
            for _ in range(count):
                specs.append(
                    pl.BlockSpec(
                        (1, piece_rows, width),
                        lambda e, part=part: (jnp.clip(e - part * half, 0, half - 1), 0, 0),
                    )
                )
        return specs

    ins = [xm] + ([gh] if bwd else []) + [routes_t, gates_t]
    in_specs = [SMEM_SPEC] + [full_spec(item.shape) for item in ins] + piece_specs()
    flat = [piece for part in pieces for piece in part]
    out_shape, out_specs, scratch = [], [], []
    scratch += [
        pltpu.VMEM((feature_dim, width), BF16),
        pltpu.VMEM((blocks, 8, BLOCK), F32),
        pltpu.VMEM((blocks * CAP, feature_dim), BF16),
    ]
    flops = 0
    if fwd:
        out_shape.append(jax.ShapeDtypeStruct((rows, feature_dim), BF16))
        out_specs.append(full_spec((rows, feature_dim)))
        scratch.append(pltpu.VMEM((rows, feature_dim), F32))
        flops += 1.0e9 * NF * blocks / 2
    if bwd:
        out_shape.append(jax.ShapeDtypeStruct((rows + 16, feature_dim), BF16))
        out_specs.append(full_spec((rows + 16, feature_dim)))
        for piece in flat:
            out_shape.append(jax.ShapeDtypeStruct(piece.shape, BF16))
        out_specs += piece_specs()
        scratch += [
            pltpu.VMEM((rows, feature_dim), F32),
            pltpu.VMEM((blocks * CAP, feature_dim), BF16),
            pltpu.VMEM((blocks * 8, BLOCK), F32),
            pltpu.VMEM((feature_dim, width), BF16),
        ]
        flops += 2.2e9 * NF * blocks / 2
    outs = pl.pallas_call(
        functools.partial(experts_kernel, fwd, bwd, blocks, count, halves, piece_rows),
        grid=(NF,),
        out_shape=tuple(out_shape),
        in_specs=in_specs,
        out_specs=tuple(out_specs),
        scratch_shapes=scratch,
        compiler_params=kernel_params(),
        cost_estimate=cost(flops, 20e6 * (2 if bwd else 1), rows * units * 8),
        name="experts",
    )(offs, *ins, *flat)
    outs = list(outs)
    ffn = outs.pop(0) if fwd else None
    if not bwd:
        return ffn
    gx = outs.pop(0)
    grads = [outs[part * count : (part + 1) * count] for part in range(halves)]
    return ffn, gx, grads


def hop(value, step):
    return lax.ppermute(value, "fsdp", [(i, i ^ step) for i in range(4)])


def swap(value):
    return lax.ppermute(value, "ctx", [(0, 1), (1, 0)])


def gather_small(value):
    by_x, by_y = hop(value, 1), hop(value, 2)
    by_d = hop(value, 3)
    out = []
    for item in (value, by_x, by_y, by_d):
        out += [item, swap(item)]
    return out


def gather_halves(low, high):
    x_low, y_high = hop(low, 1), hop(high, 2)
    x_high, y_low = hop(high, 1), hop(low, 2)
    d_low, d_high = hop(y_low, 1), hop(x_high, 2)
    lows, highs = [], []
    for item in (low, x_low, y_low, d_low):
        lows += [item, swap(item)]
    for item in (high, x_high, y_high, d_high):
        highs += [item, swap(item)]
    return lows, highs


def add_low(first, second):
    return (first.astype(F32) + second.astype(F32)).astype(BF16)


def sum_cores(pieces):
    return [add_low(pieces[2 * chip], swap(pieces[2 * chip + 1])) for chip in range(4)]


def sum_chips(sums, first):
    second = 3 - first
    mine = add_low(sums[0], hop(sums[first], first))
    beside = add_low(sums[second], hop(sums[3], first))
    return mine.astype(F32) + hop(beside, second).astype(F32)


def per_device(
    hyper,
    axes,
    tokens,
    cotangent,
    lengths,
    routes,
    norm_attn,
    w_qkv,
    w_out,
    norm_moe,
    w_router,
    w_resid,
    w_const,
    v_const,
    w_gate_up,
    w_down,
):
    micro_count, seq_count, block_len, feature_dim = tokens.shape
    rows = micro_count * seq_count * block_len
    layer_count, shard_rows, qkv_cols = w_qkv.shape
    heads = qkv_cols // (3 * HD)
    units = w_gate_up.shape[-1]
    groups = ("fsdp", "ctx")
    shard_count = feature_dim // shard_rows
    ctx = lax.axis_index("ctx")
    me = lax.axis_index("fsdp") * axes["ctx"] + ctx
    rank = lax.axis_index("tp").reshape(1)
    if hyper:
        offs = me ^ jnp.arange(shard_count, dtype=jnp.int32)
    else:
        offs = jnp.zeros((1,), jnp.int32)
    info = jnp.concatenate([ctx.reshape(1), lengths.reshape(-1)]).astype(jnp.int32)
    resid = jnp.zeros((16, 16), F32).at[:NE, :NE].set(w_resid.astype(F32))

    small, wide, outer = [], [], []
    for layer in range(layer_count):
        vec = jnp.concatenate(
            [
                w_router[layer],
                jnp.zeros((shard_rows, ROW_CONST - NE), BF16),
                w_const[layer, 0],
                w_const[layer, 1],
                v_const[layer].T,
                norm_attn[layer][:, None],
                norm_moe[layer][:, None],
                jnp.zeros((shard_rows, 128 - ROW_GM - 1), BF16),
            ],
            axis=1,
        )
        small.append(jnp.concatenate([w_qkv[layer], vec], axis=1))
        wide.append(
            jnp.concatenate(
                [
                    w_gate_up[layer].reshape(NF, shard_rows, 2 * units),
                    jnp.transpose(w_down[layer], (0, 2, 1)),
                ],
                axis=2,
            )
        )
    outer = lax.all_gather(jnp.transpose(w_out, (0, 2, 1)), "tp", axis=1)

    weights = []
    token = None
    for layer in range(layer_count):
        if hyper:
            low, high = wide[layer][: NF // 2], wide[layer][NF // 2 :]
            own_small, own_outer = small[layer], outer[layer]
            if token is not None:
                own_small, low, high, _ = lax.optimization_barrier((own_small, low, high, token))
            pieces_small = gather_small(own_small)
            pieces_outer = gather_small(own_outer)
            pieces = gather_halves(low, high)
            token = (pieces[0][6], pieces[1][6])
        else:
            pieces_small = [lax.all_gather(small[layer], groups, axis=0, tiled=True)]
            pieces_outer = [lax.all_gather(outer[layer], groups, axis=1, tiled=True)]
            pieces = [[lax.all_gather(wide[layer], groups, axis=1, tiled=True)]]
        qkv_full, wo_all, vec_cols = prep_weights(
            pieces_small, pieces_outer, offs, feature_dim, qkv_cols
        )
        weights.append((qkv_full, wo_all, vec_cols[:, :32].T.astype(F32), pieces))

    routes_t = jnp.moveaxis(routes.reshape(layer_count, rows, 2), 2, 1)
    routes_t = jnp.concatenate(
        [routes_t, jnp.full((layer_count, 6, rows), -1, jnp.int32)], axis=1
    )
    position = ctx * block_len + jnp.arange(block_len, dtype=jnp.int32)
    valid = position[None, None, :] < lengths[:, :, None]
    cot = jnp.where(valid[..., None], cotangent, 0).reshape(rows, feature_dim)

    base, ffn, prev_t = tokens.reshape(rows, feature_dim), None, None
    saved = []
    for layer in range(layer_count):
        qkv_full, wo_all, vecs, pieces = weights[layer]
        outs = qkv_part(base, ffn, vecs, qkv_full)
        h_in, qkv = outs if ffn is not None else (base, outs[0])
        other = swap(qkv)
        context, lse = attend_forward(qkv, other, info, heads)
        ctx_all = lax.all_gather(context, "tp", axis=0)
        middle, base, xm_low, gates_t, logits_t = middle_part(
            h_in, ctx_all, wo_all, vecs, routes_t[layer], prev_t, resid
        )
        saved.append((h_in, qkv, other, context, lse, middle, xm_low, gates_t, prev_t))
        prev_t = logits_t
        if layer < layer_count - 1:
            part = experts(True, False, xm_low, None, routes_t[layer], gates_t, pieces, offs)
            ffn = lax.psum(part, "tp")

    grad, grad_low = cot, cot
    grad_logits = None
    finals = [None] * layer_count
    for layer in reversed(range(layer_count)):
        qkv_full, wo_all, vecs, pieces = weights[layer]
        h_in, qkv, other, context, lse, middle, xm_low, gates_t, prev_t = saved[layer]
        top = layer == layer_count - 1
        part, gx, grads = experts(
            top, True, xm_low, grad_low, routes_t[layer], gates_t, pieces, offs
        )
        gx = lax.psum(gx, "tp")
        if top:
            ffn = lax.psum(part, "tp")
            mixed = (base + ffn.astype(F32)).astype(BF16)
        gg_t = gx[rows : rows + 16, :block_len].astype(F32)
        gg_t = jnp.moveaxis(gg_t.reshape(2, 8, block_len)[: rows // BLOCK], 0, 1).reshape(8, rows)
        extra = (prev_t, resid) if prev_t is not None else (grad_logits,)
        outs = gate_backward(
            grad, middle, gx, vecs, routes_t[layer], gates_t, gg_t, context, wo_all, rank, extra
        )
        gmid, gctx, dwo, dvec = outs[:4]
        if prev_t is not None:
            grad_logits, dres = outs[4:]
        gown, goth = attend_backward(qkv, other, lse, gctx, info, heads)
        ga_part, dqkv = qkv_backward(gown, swap(goth), h_in, vecs, qkv_full)
        ga = lax.psum(ga_part, "tp")
        outs = norm_backward(gmid, ga, h_in, vecs, layer > 0)
        grad, dgain = outs[0], outs[-1]
        grad_low = outs[1]
        finals[layer] = (grads, dqkv, dwo, dvec, dgain)

    results = []
    gain_rows = jnp.concatenate([item[4][:1] for item in finals] + [dres[:NE + 4].reshape(1, -1)], axis=1)
    if hyper:
        total = gain_rows + swap(gain_rows)
        total = total + hop(total, 1)
        total = total + hop(total, 2)
    else:
        total = lax.psum(gain_rows, groups)
    gain_total = total[0, : layer_count * feature_dim].reshape(layer_count, feature_dim)
    resid_total = total[0, layer_count * feature_dim :].reshape(16, 16)[:NE, :NE]
    gain_own = lax.dynamic_slice(gain_total, (0, me * shard_rows), (layer_count, shard_rows))
    for layer in range(layer_count):
        grads, dqkv, dwo, dvec, _ = finals[layer]
        packed = jnp.concatenate([dqkv, dwo, dvec.T], axis=1).astype(BF16)
        if hyper:
            packed = packed.reshape(shard_count, shard_rows, -1)
            packed = [
                lax.dynamic_index_in_dim(packed, me ^ off, 0, keepdims=False)
                for off in range(shard_count)
            ]
            own = sum_chips(sum_cores(packed), 1)
            low = sum_chips(sum_cores(grads[0]), 1)
            high = sum_chips(sum_cores(grads[1]), 2)
            wide_own = jnp.concatenate([low, high], axis=0)
        else:
            own = lax.psum_scatter(packed, groups, scatter_dimension=0, tiled=True).astype(F32)
            wide_own = lax.psum_scatter(
                grads[0][0], groups, scatter_dimension=1, tiled=True
            ).astype(F32)
        out_cols = dwo.shape[1]
        vec = own[:, qkv_cols + out_cols :]
        results.append(
            (
                own[:, :qkv_cols],
                own[:, qkv_cols : qkv_cols + out_cols].T,
                vec[:, ROW_GM],
                vec[:, :NE],
                jnp.stack([vec[:, ROW_CONST : ROW_CONST + 2], vec[:, ROW_CONST + 2 : ROW_CONST + 4]]),
                vec[:, ROW_VEC : ROW_VEC + 2].T,
                wide_own[:, :, : 2 * units].reshape(NF, shard_rows, 2, units),
                jnp.transpose(wide_own[:, :, 2 * units :], (0, 2, 1)),
            )
        )
    stacked = [jnp.stack([item[member] for item in results]) for member in range(8)]
    return (
        mixed.reshape(tokens.shape),
        grad.reshape(tokens.shape),
        gain_own,
        stacked[0],
        stacked[1],
        stacked[2],
        stacked[3],
        resid_total,
        stacked[4],
        stacked[5],
        stacked[6],
        stacked[7],
    )


def solution(mesh):
    axes = dict(mesh.shape)
    hyper = axes["fsdp"] == 4 and axes["ctx"] == 2
    in_specs = (
        P(None, "fsdp", "ctx", None),
        P(None, "fsdp", "ctx", None),
        P(None, "fsdp"),
        P(None, None, "fsdp", "ctx", None),
        P(None, ("fsdp", "ctx")),
        P(None, ("fsdp", "ctx"), "tp"),
        P(None, "tp", ("fsdp", "ctx")),
        P(None, ("fsdp", "ctx")),
        P(None, ("fsdp", "ctx"), None),
        P(),
        P(None, None, ("fsdp", "ctx"), None),
        P(None, None, ("fsdp", "ctx")),
        P(None, None, ("fsdp", "ctx"), None, "tp"),
        P(None, None, "tp", ("fsdp", "ctx")),
    )
    out_specs = (
        P(None, "fsdp", "ctx", None),
        P(None, "fsdp", "ctx", None),
        P(None, ("fsdp", "ctx")),
        P(None, ("fsdp", "ctx"), "tp"),
        P(None, "tp", ("fsdp", "ctx")),
        P(None, ("fsdp", "ctx")),
        P(None, ("fsdp", "ctx"), None),
        P(),
        P(None, None, ("fsdp", "ctx"), None),
        P(None, None, ("fsdp", "ctx")),
        P(None, None, ("fsdp", "ctx"), None, "tp"),
        P(None, None, "tp", ("fsdp", "ctx")),
    )
    return jax.shard_map(
        functools.partial(per_device, hyper, axes),
        mesh=mesh,
        in_specs=in_specs,
        out_specs=out_specs,
        check_vma=False,
    )
```

time: 2760 us -> 958 us (0.35)
  waiting for transfers between devices: 1570 us -> 466 us
  matrix products: 279 us -> 0 us
  local copies, waits for them, and re-layouts: 352 us -> 77.2 us
  other arithmetic: 329 us -> 82.1 us
  Pallas kernels: 0 us -> 229 us
  blocking collectives: 191 us -> 15.5 us
  starting transfers between devices: 3.97 us -> 63.8 us
    reduce_scatter x16 -> x0, waiting for transfers between devices: 752 us -> none  [the longest x4 375 us: per_device(): lax.psum_scatter(layer_grads[7].astype(jnp.bfloat16), ('fsdp', 'ctx'), sc...]
    unnamed x59 -> x7, waiting for transfers between devices: 447 us -> 0.12 us
    dot_general x117 -> x0, matrix products: 279 us -> none  [the longest x4 43.2 us: layer_backward(): jnp.einsum('eckf,edkf->ecd', grad_gate_up, w_gate_up, preferred_element_t...]
    ppermute x0 -> x105, waiting for transfers between devices: none -> 241 us  [the longest x44 239 us: hop(): return lax.ppermute(value, 'fsdp', [(i, i ^ step) for i in range(4)])]
    pallas_call x0 -> x19, Pallas kernels: none -> 229 us  [the longest x3 95.5 us: experts(): pl.pallas_call(functools.partial(experts_kernel, fwd, bwd, blocks, count,...]
    reduce_sum x73 -> x0, other arithmetic: 195 us -> none  [the longest x2 61.7 us: gate_terms(): fixed_terms = jnp.sum(gate_vals[:, :, None] * slot_terms, axis=1)]
    psum x7 -> x5, waiting for transfers between devices: 375 us -> 225 us  [the longest x2 116 us: per_device(): gx = lax.psum(gx, 'tp')]
    gather x20 -> x0, local copies, waits for them, and re-layouts: 112 us -> none  [the longest x8 35.8 us: layer_backward(): grad_padded[row_index]]
  transfers between devices with their start and end apart: 43 -> 112, of which waited for: 32 -> 36; matrix products, arithmetic and copies ran while one was open for 16% -> 14% of each run, Pallas kernels for 0% -> 16%
where the time goes in v1:
time: 958 us; the launch traced here: 949 us
  waiting for transfers between devices  466 us (49%)
  Pallas kernels  229 us (24%)
  other arithmetic  82.1 us (9%)
  local copies, waits for them, and re-layouts  77.2 us (8%)
  starting transfers between devices  63.8 us (7%)
  between operations  15.9 us (2%)
  blocking collectives  15.5 us (2%)
    ppermute x44, waiting for transfers between devices, hop(): return lax.ppermute(value, 'fsdp', [(i, i ^ step) for i in range(4)])  239 us
    psum x2, waiting for transfers between devices, per_device(): gx = lax.psum(gx, 'tp')  116 us
    pallas_call x3, Pallas kernels, experts(): pl.pallas_call(functools.partial(experts_kernel, fwd, bwd, blocks, count,...  95.5 us
    psum x2, waiting for transfers between devices, per_device(): ffn = lax.psum(part, 'tp')  73.6 us
    ppermute x44, starting transfers between devices, hop(): return lax.ppermute(value, 'fsdp', [(i, i ^ step) for i in range(4)])  52.4 us
    psum x1, waiting for transfers between devices, per_device(): ga = lax.psum(ga_part, 'tp')  35.6 us
    convert_element_type x16, other arithmetic, add_low(): return (first.astype(F32) + second.astype(F32)).astype(BF16)  30.7 us
    pallas_call x2, Pallas kernels, attend_backward(): pl.pallas_call(functools.partial(attn_bwd_kernel, heads), grid=(rows // B...  28.9 us
  transfers between devices with their start and end apart: 112, of which 36 were waited for; matrix products, arithmetic and copies ran while one was open for 14% of the time, Pallas kernels for 16%

profile of v1, /device:TPU:0, one launch (start us, length us, event | category | flops | bytes accessed | tf_op | source)
XLA Modules:
  0.0 949.5 jit_solution(15630480511379107311)
XLA Ops:
  14.5 3.0 collective-permute-start.1
  20.0 15.5 %all-gather = bf16[2,384,192]{2,0,1:T(2,128)(2,1)S(1)} all-gather(bf16[2,96,192]{2,0,1:T(2,128)(2,1)S(1)} %bitcast.194), channel_id=2, replica_groups=mesh['fsdp'=4,'ctx'=2,'tp'=4] {'tp'}, dimensions={1}, use_global_device_ids=true | all-gather | bytes 368640 | tf_op jit(solution)/shard_map/all_gather | solution.py:895
  40.3 5.2 collective-permute-done.10.refs_12_
  49.1 4.0 fusion.18
  53.6 3.6 prep.2
  60.4 5.0 qkv_part.2.own_ref
  82.6 8.2 attend_forward.2
  91.2 13.5 %collective-permute-done.18.refs_7_.refs_8_ = bf16[4,96,1536]{2,1,0:T(8,128)(2,1)} collective-permute-done((bf16[4,96,1536]{2,1,0:T(8,128)(2,1)}, bf16[4,96,1536]{2,1,0:T(8,128)(2,1)}, u32[]{:S(2)}, u32[]{:S(2)}) %collective-permute-start.18) | collective-permute-done | bytes 1179680 | tf_op jit(solution)/shard_map/ppermute | solution.py:792
  107.5 23.8 %collective-permute-done.16.refs_5_.refs_6_ = bf16[4,96,1536]{2,1,0:T(8,128)(2,1)} collective-permute-done((bf16[4,96,1536]{2,1,0:T(8,128)(2,1)}, bf16[4,96,1536]{2,1,0:T(8,128)(2,1)}, u32[]{:S(2)}, u32[]{:S(2)}) %collective-permute-start.16) | collective-permute-done | bytes 1179680 | tf_op jit(solution)/shard_map/ppermute | solution.py:792
  133.8 22.0 %collective-permute-done.20.refs_9_.refs_10_ = bf16[4,96,1536]{2,1,0:T(8,128)(2,1)} collective-permute-done((bf16[4,96,1536]{2,1,0:T(8,128)(2,1)}, bf16[4,96,1536]{2,1,0:T(8,128)(2,1)}, u32[]{:S(2)}, u32[]{:S(2)}) %collective-permute-start.20) | collective-permute-done | bytes 1179680 | tf_op jit(solution)/shard_map/ppermute | solution.py:792
  159.3 8.5 middle_part.2
  168.9 18.9 %experts.3 = bf16[1024,768]{1,0:T(8,128)(2,1)} custom-call(s32[8]{0:T(128)} %iota_xor_fusion.offs_ref, bf16[1024,768]{1,0:T(8,128)(2,1)} %get-tuple-element.111.refs_0_, s32[8,1024]{1,0:T(8,128)} %get-tuple-element.257.refs_4_.refs_1_.refs_2_, f32[8,1024]{1,0:T(8,128)} %get-tuple-element.112.refs_2_.refs_3_.refs_5_, ...), custom_call_target="tpu_custom_call" | custom-call | flops 8000000000 | bytes 20000000 | tf_op jit(solution)/shard_map/experts/pallas_call | solution.py:771
  193.2 3.4 collective-permute-done.37.refs_10_
  196.6 4.5 collective-permute-done.39.refs_12_
  205.6 2.9 collective-permute-start.34
  217.3 3.6 prep.3
  222.6 34.1 %all-reduce.9.cloned.1.call-done.refs_1_ = bf16[1024,768]{1,0:T(8,128)(2,1)} async-done(((bf16[1024,768]{1,0:T(8,128)(2,1)}), bf16[1024,768]{1,0:T(8,128)(2,1)}) %all-reduce.9.cloned.1.call-update) | async-done | bytes 1572880 | tf_op jit(solution)/shard_map/psum | solution.py:942
  256.7 5.9 qkv_part.3
  270.0 8.4 attend_forward.3
  278.7 14.8 %collective-permute-done.47.refs_8_ = bf16[4,96,1536]{2,1,0:T(8,128)(2,1)} collective-permute-done((bf16[4,96,1536]{2,1,0:T(8,128)(2,1)}, bf16[4,96,1536]{2,1,0:T(8,128)(2,1)}, u32[]{:S(2)}, u32[]{:S(2)}) %collective-permute-start.47) | collective-permute-done | bytes 1179680 | tf_op jit(solution)/shard_map/ppermute | solution.py:792
  296.3 23.8 %collective-permute-done.45.refs_6_ = bf16[4,96,1536]{2,1,0:T(8,128)(2,1)} collective-permute-done((bf16[4,96,1536]{2,1,0:T(8,128)(2,1)}, bf16[4,96,1536]{2,1,0:T(8,128)(2,1)}, u32[]{:S(2)}, u32[]{:S(2)}) %collective-permute-start.45) | collective-permute-done | bytes 1179680 | tf_op jit(solution)/shard_map/ppermute | solution.py:792
  322.8 21.9 %collective-permute-done.49.refs_10_ = bf16[4,96,1536]{2,1,0:T(8,128)(2,1)} collective-permute-done((bf16[4,96,1536]{2,1,0:T(8,128)(2,1)}, bf16[4,96,1536]{2,1,0:T(8,128)(2,1)}, u32[]{:S(2)}, u32[]{:S(2)}) %collective-permute-start.49) | collective-permute-done | bytes 1179680 | tf_op jit(solution)/shard_map/ppermute | solution.py:792
  349.5 9.3 middle_part.3
  359.8 42.1 %experts.4 = (bf16[1024,768]{1,0:T(8,128)(2,1)}, bf16[1040,768]{1,0:T(8,128)(2,1)}, bf16[4,96,1536]{2,1,0:T(8,128)(2,1)}, bf16[4,96,1536]{2,1,0:T(8,128)(2,1)}, ...) custom-call(s32[8]{0:T(128)} %iota_xor_fusion.offs_ref, ...), custom_call_target="tpu_custom_call" | custom-call | flops 25600000000 | bytes 40000000 | tf_op jit(solution)/shard_map/experts/pallas_call | solution.py:771
  403.6 66.8 %all-reduce.11.cloned.1.call-done.refs_2_ = bf16[1040,768]{1,0:T(8,128)(2,1)} async-done(((bf16[1040,768]{1,0:T(8,128)(2,1)}), bf16[1040,768]{1,0:T(8,128)(2,1)}) %all-reduce.11.cloned.1.call-update) | async-done | bytes 1597456 | tf_op jit(solution)/shard_map/psum | solution.py:954
  471.7 12.1 %gate_backward.2 = (f32[1024,768]{1,0:T(8,128)}, bf16[1024,192]{1,0:T(8,128)(2,1)}, f32[768,192]{1,0:T(8,128)}, f32[32,768]{1,0:T(8,128)}, f32[16,1024]{1,0:T(8,128)}, /*index=5*/f32[16,16]{1,0:T(8,128)}) custom-call(s32[1]{0:T(128)} %bitcast.35.rank_ref, bf16[1024,768]{1,0:T(8,128)(2,1)} %bitcast.181, f32[1024,768]{1,0:T(8,128)} %get-tuple-element.127.refs_1_, ...), custom_call_target="tpu_custom_call" | custom-call | flops 603979776 | bytes 14155776 | tf_op jit(solution)/shard_map/gate_backward/pallas_call | solution.py:502
  483.8 14.5 %attend_backward.2 = (f32[1024,576]{1,0:T(8,128)}, bf16[1024,576]{1,0:T(8,128)(2,1)}) custom-call(s32[3]{0:T(128)} %pad_add_fusion.info_ref, bf16[1024,576]{1,0:T(8,128)(2,1)} %get-tuple-element.117.own_ref, bf16[1024,576]{1,0:T(8,128)(2,1)} %copy.120.other_ref, f32[1024,8]{1,0:T(8,128)} %get-tuple-element.130.lse_ref, ...), custom_call_target="tpu_custom_call" | custom-call | flops 8053063680 | bytes 7077888 | tf_op jit(solution)/shard_map/attend_backward/pallas_call | solution.py:244
  509.0 7.9 qkv_backward.2
  534.8 3.4 add_convert_fusion.1
  538.4 17.7 %collective-permute-done.75 = bf16[96,800]{0,1:T(8,128)(2,1)} collective-permute-done((bf16[96,800]{0,1:T(8,128)(2,1)}, bf16[96,800]{0,1:T(8,128)(2,1)}, u32[]{:S(2)}, u32[]{:S(2)}) %collective-permute-start.75) | collective-permute-done | bytes 153632 | tf_op jit(solution)/shard_map/ppermute | solution.py:792
  559.3 3.4 add_convert_fusion.7
  570.1 35.6 %all-reduce.13.cloned.1.call-done.ga_ref = bf16[1024,768]{1,0:T(8,128)(2,1)} async-done(((bf16[1024,768]{1,0:T(8,128)(2,1)}), bf16[1024,768]{1,0:T(8,128)(2,1)}) %all-reduce.13.cloned.1.call-update) | async-done | bytes 1572880 | tf_op jit(solution)/shard_map/psum | solution.py:969
  605.7 6.4 norm_backward.2
  613.7 34.5 %experts.5 = (bf16[1040,768]{1,0:T(8,128)(2,1)}, bf16[4,96,1536]{2,1,0:T(8,128)(2,1)}, bf16[4,96,1536]{2,1,0:T(8,128)(2,1)}, bf16[4,96,1536]{2,1,0:T(8,128)(2,1)...) custom-call(s32[8]{0:T(128)} %iota_xor_fusion.offs_ref, ...), custom_call_target="tpu_custom_call" | custom-call | flops 17600000000 | bytes 40000000 | tf_op jit(solution)/shard_map/experts/pallas_call | solution.py:771
  658.2 5.8 stack_reshape.7
  668.2 48.8 %all-reduce.15.cloned.1.call-done.refs_2_ = bf16[1040,768]{1,0:T(8,128)(2,1)} async-done(((bf16[1040,768]{1,0:T(8,128)(2,1)}), bf16[1040,768]{1,0:T(8,128)(2,1)}) %all-reduce.15.cloned.1.call-update) | async-done | bytes 1597456 | tf_op jit(solution)/shard_map/psum | solution.py:954
  718.3 11.7 %gate_backward.3 = (f32[1024,768]{1,0:T(8,128)}, bf16[1024,192]{1,0:T(8,128)(2,1)}, f32[768,192]{1,0:T(8,128)}, f32[32,768]{1,0:T(8,128)}) custom-call(s32[1]{0:T(128)} %bitcast.35.rank_ref, f32[1024,768]{1,0:T(8,128)} %get-tuple-element.135.refs_0_, f32[1024,768]{1,0:T(8,128)} %get-tuple-element.136.refs_1_, ...), custom_call_target="tpu_custom_call" | custom-call | flops 603979776 | bytes 14155776 | tf_op jit(solution)/shard_map/gate_backward/pallas_call | solution.py:502
  730.0 14.5 %attend_backward.3 = (f32[1024,576]{1,0:T(8,128)}, bf16[1024,576]{1,0:T(8,128)(2,1)}) custom-call(s32[3]{0:T(128)} %pad_add_fusion.info_ref, bf16[1024,576]{1,0:T(8,128)(2,1)} %qkv_part.2.own_ref, bf16[1024,576]{1,0:T(8,128)(2,1)} %copy.104.other_ref, f32[1024,8]{1,0:T(8,128)} %get-tuple-element.141.lse_ref, bf16[1024,192]{1,0:T(8,128)(2,1)} %get-tuple-element.142.gctx_ref), custom_call_target="tpu_custom_call" | custom-call | flops 8053063680 | bytes 7077888 | tf_op jit(solution)/shard_map/attend_backward/pallas_call | solution.py:244
  755.2 7.7 qkv_backward.3
  773.8 5.8 collective-permute-done.89
  781.0 3.2 add_convert_fusion.13
  784.2 16.7 %collective-permute-done.68 = bf16[96,800]{0,1:T(8,128)(2,1)S(1)} collective-permute-done((bf16[96,800]{0,1:T(8,128)(2,1)S(1)}, bf16[96,800]{0,1:T(8,128)(2,1)S(1)}, u32[]{:S(2)}, u32[]{:S(2)}) %collective-permute-start.68) | collective-permute-done | bytes 153632 | tf_op jit(solution)/shard_map/ppermute | solution.py:792
  815.6 20.3 %collective-permute-done.86 = bf16[4,96,1536]{2,1,0:T(8,128)(2,1)} collective-permute-done((bf16[4,96,1536]{2,1,0:T(8,128)(2,1)}, bf16[4,96,1536]{2,1,0:T(8,128)(2,1)}, u32[]{:S(2)}, u32[]{:S(2)}) %collective-permute-start.86) | collective-permute-done | bytes 1179680 | tf_op jit(solution)/shard_map/ppermute | solution.py:792
  835.8 25.9 %collective-permute-done.90 = bf16[4,96,1536]{2,1,0:T(8,128)(2,1)} collective-permute-done((bf16[4,96,1536]{2,1,0:T(8,128)(2,1)}, bf16[4,96,1536]{2,1,0:T(8,128)(2,1)}, u32[]{:S(2)}, u32[]{:S(2)}) %collective-permute-start.90) | collective-permute-done | bytes 1179680 | tf_op jit(solution)/shard_map/ppermute | solution.py:792
  870.4 5.7 stack_reshape.6
  876.1 10.0 %pad_maximum_fusion = f32[2,8,96,2,512]{4,3,2,1,0:T(2,128)} fusion(f32[1,8,96,2,512]{4,3,2,1,0:T(2,128)} %stack_reshape.7, f32[1,8,96,2,512]{4,3,2,1,0:T(2,128)} %stack_reshape.6), kind=kLoop, calls=%fused_computation | loop fusion | flops 1572864 | bytes 12582912 | tf_op jit(solution)/shard_map/stack | solution.py:1018
  886.1 39.5 %all-reduce.17.cloned.1.call-done = (bf16[1024,768]{1,0:T(8,128)(2,1)}, bf16[1024,768]{1,0:T(8,128)(2,1)}) async-done(((bf16[1024,768]{1,0:T(8,128)(2,1)}, bf16[1024,768]{1,0:T(8,128)(2,1)}), (bf16[1024,768]{1,0:T(8,128)(2,1)}, bf16[1024,768]{1,0:T(8,128)(2,1)})) %all-reduce.17.cloned.1.call-update) | async-done | bytes 3145744 | tf_op jit(solution)/shard_map/psum | solution.py:956
  925.6 5.8 norm_backward.3
  (481 shorter events, 204.1 us)
Async XLA Ops:
  7.2 152.2 %all-gather.6.cloned.1.call-start = ((), (), s32[]{:S(2)}) async-start(), calls=%async_computation.4 | async-start | bytes 2621440 | tf_op jit(solution)/shard_map/all_gather | solution.py:934
  75.6 29.1 %collective-permute-start.18 = (bf16[4,96,1536]{2,1,0:T(8,128)(2,1)}, bf16[4,96,1536]{2,1,0:T(8,128)(2,1)}, u32[]{:S(2)}, u32[]{:S(2)}) collective-permute-start(bf16[4,96,1536]{2,1,0:T(8,128)(2,1)} %get-tuple-element.231.refs_3_.refs_4_), channel_id=1, source_target_pairs={{0,16},{8,24},{16,0},{24,8},{1,17},{9,25},{17,1},{25,9},{2,18},{10... | collective-permute-start | bytes 3538952 | tf_op jit(solution)/shard_map/ppermute | solution.py:792
  78.6 52.7 %collective-permute-start.16 = (bf16[4,96,1536]{2,1,0:T(8,128)(2,1)}, bf16[4,96,1536]{2,1,0:T(8,128)(2,1)}, u32[]{:S(2)}, u32[]{:S(2)}) collective-permute-start(bf16[4,96,1536]{2,1,0:T(8,128)(2,1)} %get-tuple-element.231.refs_3_.refs_4_), channel_id=1, source_target_pairs={{0,8},{8,0},{16,24},{24,16},{1,9},{9,1},{17,25},{25,17},{2,10},{10... | collective-permute-start | bytes 3538952 | tf_op jit(solution)/shard_map/ppermute | solution.py:792
  79.1 52.7 %collective-permute-start.25 = (bf16[4,96,1536]{2,1,0:T(8,128)(2,1)S(1)}, bf16[4,96,1536]{2,1,0:T(8,128)(2,1)}, u32[]{:S(2)}, u32[]{:S(2)}) collective-permute-start(bf16[4,96,1536]{2,1,0:T(8,128)(2,1)S(1)} %get-tuple-element.230.refs_11_.refs_12_), channel_id=1, source_target_pairs={{0,16},{8,24},{16,0},{24,8},{1,17},{9,25},{17,1},{25,9},{2,18},{10... | collective-permute-start | bytes 3538952 | tf_op jit(solution)/shard_map/ppermute | solution.py:792
  90.9 165.8 %all-reduce.9.cloned.1.call-start = ((), (), s32[]{:S(2)}) async-start(), calls=%async_computation | async-start | bytes 3145728 | tf_op jit(solution)/shard_map/psum | solution.py:942
  91.1 40.7 %collective-permute-start.15 = (bf16[4,96,1536]{2,1,0:T(8,128)(2,1)}, bf16[4,96,1536]{2,1,0:T(8,128)(2,1)S(1)}, u32[]{:S(2)}, u32[]{:S(2)}) collective-permute-start(bf16[4,96,1536]{2,1,0:T(8,128)(2,1)} %get-tuple-element.231.refs_3_.refs_4_), channel_id=1, source_target_pairs={{0,4},{4,0},{1,5},{5,1},{2,6},{6,2},{3,7},{7,3},{8,12},{12,8},{9,1... | collective-permute-start | bytes 3538952 | tf_op jit(solution)/shard_map/ppermute | solution.py:796
  106.0 49.9 %collective-permute-start.20 = (bf16[4,96,1536]{2,1,0:T(8,128)(2,1)}, bf16[4,96,1536]{2,1,0:T(8,128)(2,1)}, u32[]{:S(2)}, u32[]{:S(2)}) collective-permute-start(bf16[4,96,1536]{2,1,0:T(8,128)(2,1)} %collective-permute-done.18.refs_7_.refs_8_), channel_id=1, source_target_pairs={{0,8},{8,0},{16,24},{24,16},{1,9},{9,1},{17,25},{25,17},{2,10},{10... | collective-permute-start | bytes 3538952 | tf_op jit(solution)/shard_map/ppermute | solution.py:792
  131.8 36.1 %collective-permute-start.24 = (bf16[4,96,1536]{2,1,0:T(8,128)(2,1)}, bf16[4,96,1536]{2,1,0:T(8,128)(2,1)}, u32[]{:S(2)}, u32[]{:S(2)}) collective-permute-start(bf16[4,96,1536]{2,1,0:T(8,128)(2,1)} %collective-permute-done.23.refs_13_.refs_14_), channel_id=1, source_target_pairs={{0,4},{4,0},{1,5},{5,1},{2,6},{6,2},{3,7},{7,3},{8,12},{12,8},{9,1... | collective-permute-start | bytes 3538952 | tf_op jit(solution)/shard_map/ppermute | solution.py:796
  132.8 35.1 %collective-permute-start.17 = (bf16[4,96,1536]{2,1,0:T(8,128)(2,1)}, bf16[4,96,1536]{2,1,0:T(8,128)(2,1)S(1)}, u32[]{:S(2)}, u32[]{:S(2)}) collective-permute-start(bf16[4,96,1536]{2,1,0:T(8,128)(2,1)} %collective-permute-done.16.refs_5_.refs_6_), channel_id=1, source_target_pairs={{0,4},{4,0},{1,5},{5,1},{2,6},{6,2},{3,7},{7,3},{8,12},{12,8},{9,1... | collective-permute-start | bytes 3538952 | tf_op jit(solution)/shard_map/ppermute | solution.py:796
  187.8 161.6 %all-gather.8.cloned.1.call-start = ((), (), s32[]{:S(2)}) async-start(), calls=%async_computation.5 | async-start | bytes 2621440 | tf_op jit(solution)/shard_map/all_gather | solution.py:934
  264.4 29.1 %collective-permute-start.47 = (bf16[4,96,1536]{2,1,0:T(8,128)(2,1)}, bf16[4,96,1536]{2,1,0:T(8,128)(2,1)}, u32[]{:S(2)}, u32[]{:S(2)}) collective-permute-start(bf16[4,96,1536]{2,1,0:T(8,128)(2,1)} %get-tuple-element.124.refs_4_), channel_id=1, source_target_pairs={{0,16},{8,24},{16,0},{24,8},{1,17},{9,25},{17,1},{25,9},{2,18},{10... | collective-permute-start | bytes 3538952 | tf_op jit(solution)/shard_map/ppermute | solution.py:792
  265.9 28.9 %collective-permute-start.52 = (bf16[4,96,1536]{2,1,0:T(8,128)(2,1)S(1)}, bf16[4,96,1536]{2,1,0:T(8,128)(2,1)}, u32[]{:S(2)}, u32[]{:S(2)}) collective-permute-start(bf16[4,96,1536]{2,1,0:T(8,128)(2,1)S(1)} %copy-done.22), channel_id=1, source_target_pairs={{0,8},{8,0},{16,24},{24,16},{1,9},{9,1},{17,25},{25,17},{2,10},{10... | collective-permute-start | bytes 3538952 | tf_op jit(solution)/shard_map/ppermute | solution.py:792
  267.4 52.7 %collective-permute-start.45 = (bf16[4,96,1536]{2,1,0:T(8,128)(2,1)}, bf16[4,96,1536]{2,1,0:T(8,128)(2,1)}, u32[]{:S(2)}, u32[]{:S(2)}) collective-permute-start(bf16[4,96,1536]{2,1,0:T(8,128)(2,1)} %get-tuple-element.124.refs_4_), channel_id=1, source_target_pairs={{0,8},{8,0},{16,24},{24,16},{1,9},{9,1},{17,25},{25,17},{2,10},{10... | collective-permute-start | bytes 3538952 | tf_op jit(solution)/shard_map/ppermute | solution.py:792
  268.0 52.7 %collective-permute-start.54 = (bf16[4,96,1536]{2,1,0:T(8,128)(2,1)S(1)}, bf16[4,96,1536]{2,1,0:T(8,128)(2,1)}, u32[]{:S(2)}, u32[]{:S(2)}) collective-permute-start(bf16[4,96,1536]{2,1,0:T(8,128)(2,1)S(1)} %copy-done.22), channel_id=1, source_target_pairs={{0,16},{8,24},{16,0},{24,8},{1,17},{9,25},{17,1},{25,9},{2,18},{10... | collective-permute-start | bytes 3538952 | tf_op jit(solution)/shard_map/ppermute | solution.py:792
  278.4 192.0 %all-reduce.11.cloned.1.call-start = ((), (), s32[]{:S(2)}) async-start(), calls=%async_computation.1 | async-start | bytes 3194880 | tf_op jit(solution)/shard_map/psum | solution.py:954
  278.7 42.0 %collective-permute-start.44 = (bf16[4,96,1536]{2,1,0:T(8,128)(2,1)}, bf16[4,96,1536]{2,1,0:T(8,128)(2,1)S(1)}, u32[]{:S(2)}, u32[]{:S(2)}) collective-permute-start(bf16[4,96,1536]{2,1,0:T(8,128)(2,1)} %get-tuple-element.124.refs_4_), channel_id=1, source_target_pairs={{0,4},{4,0},{1,5},{5,1},{2,6},{6,2},{3,7},{7,3},{8,12},{12,8},{9,1... | collective-permute-start | bytes 3538952 | tf_op jit(solution)/shard_map/ppermute | solution.py:796
  294.8 49.8 %collective-permute-start.49 = (bf16[4,96,1536]{2,1,0:T(8,128)(2,1)}, bf16[4,96,1536]{2,1,0:T(8,128)(2,1)}, u32[]{:S(2)}, u32[]{:S(2)}) collective-permute-start(bf16[4,96,1536]{2,1,0:T(8,128)(2,1)} %collective-permute-done.47.refs_8_), channel_id=1, source_target_pairs={{0,8},{8,0},{16,24},{24,16},{1,9},{9,1},{17,25},{25,17},{2,10},{10... | collective-permute-start | bytes 3538952 | tf_op jit(solution)/shard_map/ppermute | solution.py:792
  320.7 38.0 %collective-permute-start.53 = (bf16[4,96,1536]{2,1,0:T(8,128)(2,1)}, bf16[4,96,1536]{2,1,0:T(8,128)(2,1)}, u32[]{:S(2)}, u32[]{:S(2)}) collective-permute-start(bf16[4,96,1536]{2,1,0:T(8,128)(2,1)} %collective-permute-done.52.refs_14_), channel_id=1, source_target_pairs={{0,4},{4,0},{1,5},{5,1},{2,6},{6,2},{3,7},{7,3},{8,12},{12,8},{9,1... | collective-permute-start | bytes 3538952 | tf_op jit(solution)/shard_map/ppermute | solution.py:796
  321.7 37.0 %collective-permute-start.46 = (bf16[4,96,1536]{2,1,0:T(8,128)(2,1)}, bf16[4,96,1536]{2,1,0:T(8,128)(2,1)S(1)}, u32[]{:S(2)}, u32[]{:S(2)}) collective-permute-start(bf16[4,96,1536]{2,1,0:T(8,128)(2,1)} %collective-permute-done.45.refs_6_), channel_id=1, source_target_pairs={{0,4},{4,0},{1,5},{5,1},{2,6},{6,2},{3,7},{7,3},{8,12},{12,8},{9,1... | collective-permute-start | bytes 3538952 | tf_op jit(solution)/shard_map/ppermute | solution.py:796
  402.0 203.7 %all-reduce.13.cloned.1.call-start = ((), (), s32[]{:S(2)}) async-start(), calls=%async_computation.2 | async-start | bytes 3145728 | tf_op jit(solution)/shard_map/psum | solution.py:969
  402.4 98.4 %collective-permute-start.99 = (bf16[4,96,1536]{2,1,0:T(8,128)(2,1)}, bf16[4,96,1536]{2,1,0:T(8,128)(2,1)S(1)}, u32[]{:S(2)}, u32[]{:S(2)}) collective-permute-start(bf16[4,96,1536]{2,1,0:T(8,128)(2,1)} %get-tuple-element.183), channel_id=1, source_target_pairs={{0,4},{4,0},{1,5},{5,1},{2,6},{6,2},{3,7},{7,3},{8,12},{12,8},{9,1... | collective-permute-start | bytes 3538952 | tf_op jit(solution)/shard_map/ppermute | solution.py:796
  402.5 99.7 %collective-permute-start.102 = (bf16[4,96,1536]{2,1,0:T(8,128)(2,1)}, bf16[4,96,1536]{2,1,0:T(8,128)(2,1)S(1)}, u32[]{:S(2)}, u32[]{:S(2)}) collective-permute-start(bf16[4,96,1536]{2,1,0:T(8,128)(2,1)} %get-tuple-element.187), channel_id=1, source_target_pairs={{0,4},{4,0},{1,5},{5,1},{2,6},{6,2},{3,7},{7,3},{8,12},{12,8},{9,1... | collective-permute-start | bytes 3538952 | tf_op jit(solution)/shard_map/ppermute | solution.py:796
  403.0 128.0 %collective-permute-start.101 = (bf16[4,96,1536]{2,1,0:T(8,128)(2,1)}, bf16[4,96,1536]{2,1,0:T(8,128)(2,1)}, u32[]{:S(2)}, u32[]{:S(2)}) collective-permute-start(bf16[4,96,1536]{2,1,0:T(8,128)(2,1)} %get-tuple-element.185), channel_id=1, source_target_pairs={{0,4},{4,0},{1,5},{5,1},{2,6},{6,2},{3,7},{7,3},{8,12},{12,8},{9,1... | collective-permute-start | bytes 3538952 | tf_op jit(solution)/shard_map/ppermute | solution.py:796
  403.1 120.7 %collective-permute-start.92 = (bf16[4,96,1536]{2,1,0:T(8,128)(2,1)}, bf16[4,96,1536]{2,1,0:T(8,128)(2,1)}, u32[]{:S(2)}, u32[]{:S(2)}) collective-permute-start(bf16[4,96,1536]{2,1,0:T(8,128)(2,1)} %get-tuple-element.175), channel_id=1, source_target_pairs={{0,4},{4,0},{1,5},{5,1},{2,6},{6,2},{3,7},{7,3},{8,12},{12,8},{9,1... | collective-permute-start | bytes 3538952 | tf_op jit(solution)/shard_map/ppermute | solution.py:796
  403.5 116.4 %collective-permute-start.95 = (bf16[4,96,1536]{2,1,0:T(8,128)(2,1)}, bf16[4,96,1536]{2,1,0:T(8,128)(2,1)}, u32[]{:S(2)}, u32[]{:S(2)}) collective-permute-start(bf16[4,96,1536]{2,1,0:T(8,128)(2,1)} %get-tuple-element.179), channel_id=1, source_target_pairs={{0,4},{4,0},{1,5},{5,1},{2,6},{6,2},{3,7},{7,3},{8,12},{12,8},{9,1... | collective-permute-start | bytes 3538952 | tf_op jit(solution)/shard_map/ppermute | solution.py:796
  502.2 55.0 %collective-permute-start.94 = (bf16[4,96,1536]{2,1,0:T(8,128)(2,1)}, bf16[4,96,1536]{2,1,0:T(8,128)(2,1)}, u32[]{:S(2)}, u32[]{:S(2)}) collective-permute-start(bf16[4,96,1536]{2,1,0:T(8,128)(2,1)} %get-tuple-element.177), channel_id=1, source_target_pairs={{0,4},{4,0},{1,5},{5,1},{2,6},{6,2},{3,7},{7,3},{8,12},{12,8},{9,1... | collective-permute-start | bytes 3538952 | tf_op jit(solution)/shard_map/ppermute | solution.py:796
  523.8 34.9 %collective-permute-start.96 = (bf16[4,96,1536]{2,1,0:T(8,128)(2,1)}, bf16[4,96,1536]{2,1,0:T(8,128)(2,1)}, u32[]{:S(2)}, u32[]{:S(2)}) collective-permute-start(bf16[4,96,1536]{2,1,0:T(8,128)(2,1)} %add_convert_fusion.8), channel_id=1, source_target_pairs={{0,8},{8,0},{16,24},{24,16},{1,9},{9,1},{17,25},{25,17},{2,10},{10... | collective-permute-start | bytes 3538952 | tf_op jit(solution)/shard_map/ppermute | solution.py:792
  528.7 83.4 %collective-permute-start.98 = (bf16[4,96,1536]{2,1,0:T(8,128)(2,1)}, bf16[4,96,1536]{2,1,0:T(8,128)(2,1)S(1)}, u32[]{:S(2)}, u32[]{:S(2)}) collective-permute-start(bf16[4,96,1536]{2,1,0:T(8,128)(2,1)} %get-tuple-element.181), channel_id=1, source_target_pairs={{0,4},{4,0},{1,5},{5,1},{2,6},{6,2},{3,7},{7,3},{8,12},{12,8},{9,1... | collective-permute-start | bytes 3538952 | tf_op jit(solution)/shard_map/ppermute | solution.py:796
  538.3 178.7 %all-reduce.15.cloned.1.call-start = ((), (), s32[]{:S(2)}) async-start(), calls=%async_computation.3 | async-start | bytes 3194880 | tf_op jit(solution)/shard_map/psum | solution.py:954
  538.3 113.7 %collective-permute-start.91 = (bf16[4,96,1536]{2,1,0:T(8,128)(2,1)}, bf16[4,96,1536]{2,1,0:T(8,128)(2,1)}, u32[]{:S(2)}, u32[]{:S(2)}) collective-permute-start(bf16[4,96,1536]{2,1,0:T(8,128)(2,1)} %get-tuple-element.173), channel_id=1, source_target_pairs={{0,4},{4,0},{1,5},{5,1},{2,6},{6,2},{3,7},{7,3},{8,12},{12,8},{9,1... | collective-permute-start | bytes 3538952 | tf_op jit(solution)/shard_map/ppermute | solution.py:796
  562.7 85.5 %collective-permute-start.100 = (bf16[4,96,1536]{2,1,0:T(8,128)(2,1)}, bf16[4,96,1536]{2,1,0:T(8,128)(2,1)}, u32[]{:S(2)}, u32[]{:S(2)}) collective-permute-start(bf16[4,96,1536]{2,1,0:T(8,128)(2,1)} %add_convert_fusion.5), channel_id=1, source_target_pairs={{0,16},{8,24},{16,0},{24,8},{1,17},{9,25},{17,1},{25,9},{2,18},{10... | collective-permute-start | bytes 3538952 | tf_op jit(solution)/shard_map/ppermute | solution.py:792
  565.0 87.1 %collective-permute-start.93 = (bf16[4,96,1536]{2,1,0:T(8,128)(2,1)}, bf16[4,96,1536]{2,1,0:T(8,128)(2,1)}, u32[]{:S(2)}, u32[]{:S(2)}) collective-permute-start(bf16[4,96,1536]{2,1,0:T(8,128)(2,1)} %add_convert_fusion.11), channel_id=1, source_target_pairs={{0,8},{8,0},{16,24},{24,16},{1,9},{9,1},{17,25},{25,17},{2,10},{10... | collective-permute-start | bytes 3538952 | tf_op jit(solution)/shard_map/ppermute | solution.py:792
  566.4 81.8 %collective-permute-start.104 = (bf16[4,96,1536]{2,1,0:T(8,128)(2,1)}, bf16[4,96,1536]{2,1,0:T(8,128)(2,1)}, u32[]{:S(2)}, u32[]{:S(2)}) collective-permute-start(bf16[4,96,1536]{2,1,0:T(8,128)(2,1)} %add_convert_fusion.1), channel_id=1, source_target_pairs={{0,8},{8,0},{16,24},{24,16},{1,9},{9,1},{17,25},{25,17},{2,10},{10... | collective-permute-start | bytes 3538952 | tf_op jit(solution)/shard_map/ppermute | solution.py:792
  612.1 40.0 %collective-permute-start.97 = (bf16[4,96,1536]{2,1,0:T(8,128)(2,1)}, bf16[4,96,1536]{2,1,0:T(8,128)(2,1)}, u32[]{:S(2)}, u32[]{:S(2)}) collective-permute-start(bf16[4,96,1536]{2,1,0:T(8,128)(2,1)} %add_convert_fusion.7), channel_id=1, source_target_pairs={{0,16},{8,24},{16,0},{24,8},{1,17},{9,25},{17,1},{25,9},{2,18},{10... | collective-permute-start | bytes 3538952 | tf_op jit(solution)/shard_map/ppermute | solution.py:792
  648.2 277.4 %all-reduce.17.cloned.1.call-start = ((), (), s32[]{:S(2)}) async-start(), calls=%async_computation.6 | async-start | bytes 6291456 | tf_op jit(solution)/shard_map/psum | solution.py:956
  664.0 83.0 %collective-permute-start.85 = (bf16[4,96,1536]{2,1,0:T(8,128)(2,1)}, bf16[4,96,1536]{2,1,0:T(8,128)(2,1)S(1)}, u32[]{:S(2)}, u32[]{:S(2)}) collective-permute-start(bf16[4,96,1536]{2,1,0:T(8,128)(2,1)} %get-tuple-element.167), channel_id=1, source_target_pairs={{0,4},{4,0},{1,5},{5,1},{2,6},{6,2},{3,7},{7,3},{8,12},{12,8},{9,1... | collective-permute-start | bytes 3538952 | tf_op jit(solution)/shard_map/ppermute | solution.py:796
  666.4 81.9 %collective-permute-start.88 = (bf16[4,96,1536]{2,1,0:T(8,128)(2,1)}, bf16[4,96,1536]{2,1,0:T(8,128)(2,1)S(1)}, u32[]{:S(2)}, u32[]{:S(2)}) collective-permute-start(bf16[4,96,1536]{2,1,0:T(8,128)(2,1)} %get-tuple-element.171), channel_id=1, source_target_pairs={{0,4},{4,0},{1,5},{5,1},{2,6},{6,2},{3,7},{7,3},{8,12},{12,8},{9,1... | collective-permute-start | bytes 3538952 | tf_op jit(solution)/shard_map/ppermute | solution.py:796
  666.9 106.7 %collective-permute-start.87 = (bf16[4,96,1536]{2,1,0:T(8,128)(2,1)}, bf16[4,96,1536]{2,1,0:T(8,128)(2,1)}, u32[]{:S(2)}, u32[]{:S(2)}) collective-permute-start(bf16[4,96,1536]{2,1,0:T(8,128)(2,1)} %get-tuple-element.169), channel_id=1, source_target_pairs={{0,4},{4,0},{1,5},{5,1},{2,6},{6,2},{3,7},{7,3},{8,12},{12,8},{9,1... | collective-permute-start | bytes 3538952 | tf_op jit(solution)/shard_map/ppermute | solution.py:796
  666.9 101.9 %collective-permute-start.78 = (bf16[4,96,1536]{2,1,0:T(8,128)(2,1)}, bf16[4,96,1536]{2,1,0:T(8,128)(2,1)}, u32[]{:S(2)}, u32[]{:S(2)}) collective-permute-start(bf16[4,96,1536]{2,1,0:T(8,128)(2,1)} %get-tuple-element.159), channel_id=1, source_target_pairs={{0,4},{4,0},{1,5},{5,1},{2,6},{6,2},{3,7},{7,3},{8,12},{12,8},{9,1... | collective-permute-start | bytes 3538952 | tf_op jit(solution)/shard_map/ppermute | solution.py:796
  667.5 98.5 %collective-permute-start.81 = (bf16[4,96,1536]{2,1,0:T(8,128)(2,1)}, bf16[4,96,1536]{2,1,0:T(8,128)(2,1)}, u32[]{:S(2)}, u32[]{:S(2)}) collective-permute-start(bf16[4,96,1536]{2,1,0:T(8,128)(2,1)} %get-tuple-element.163), channel_id=1, source_target_pairs={{0,4},{4,0},{1,5},{5,1},{2,6},{6,2},{3,7},{7,3},{8,12},{12,8},{9,1... | collective-permute-start | bytes 3538952 | tf_op jit(solution)/shard_map/ppermute | solution.py:796
  748.3 52.7 %collective-permute-start.80 = (bf16[4,96,1536]{2,1,0:T(8,128)(2,1)}, bf16[4,96,1536]{2,1,0:T(8,128)(2,1)}, u32[]{:S(2)}, u32[]{:S(2)}) collective-permute-start(bf16[4,96,1536]{2,1,0:T(8,128)(2,1)} %get-tuple-element.161), channel_id=1, source_target_pairs={{0,4},{4,0},{1,5},{5,1},{2,6},{6,2},{3,7},{7,3},{8,12},{12,8},{9,1... | collective-permute-start | bytes 3538952 | tf_op jit(solution)/shard_map/ppermute | solution.py:796
  768.8 33.7 %collective-permute-start.82 = (bf16[4,96,1536]{2,1,0:T(8,128)(2,1)S(1)}, bf16[4,96,1536]{2,1,0:T(8,128)(2,1)S(1)}, u32[]{:S(2)}, u32[]{:S(2)}) collective-permute-start(bf16[4,96,1536]{2,1,0:T(8,128)(2,1)S(1)} %add_convert_fusion.20), channel_id=1, source_target_pairs={{0,8},{8,0},{16,24},{24,16},{1,9},{9,1},{17,25},{25,17},{2,10},{10... | collective-permute-start | bytes 3538952 | tf_op jit(solution)/shard_map/ppermute | solution.py:792
  773.1 38.8 %collective-permute-start.84 = (bf16[4,96,1536]{2,1,0:T(8,128)(2,1)}, bf16[4,96,1536]{2,1,0:T(8,128)(2,1)}, u32[]{:S(2)}, u32[]{:S(2)}) collective-permute-start(bf16[4,96,1536]{2,1,0:T(8,128)(2,1)} %get-tuple-element.165), channel_id=1, source_target_pairs={{0,4},{4,0},{1,5},{5,1},{2,6},{6,2},{3,7},{7,3},{8,12},{12,8},{9,1... | collective-permute-start | bytes 3538952 | tf_op jit(solution)/shard_map/ppermute | solution.py:796
  784.2 80.2 %collective-permute-start.77 = (bf16[4,96,1536]{2,1,0:T(8,128)(2,1)}, bf16[4,96,1536]{2,1,0:T(8,128)(2,1)}, u32[]{:S(2)}, u32[]{:S(2)}) collective-permute-start(bf16[4,96,1536]{2,1,0:T(8,128)(2,1)} %get-tuple-element.157), channel_id=1, source_target_pairs={{0,4},{4,0},{1,5},{5,1},{2,6},{6,2},{3,7},{7,3},{8,12},{12,8},{9,1... | collective-permute-start | bytes 3538952 | tf_op jit(solution)/shard_map/ppermute | solution.py:796
  805.9 29.9 %collective-permute-start.86 = (bf16[4,96,1536]{2,1,0:T(8,128)(2,1)}, bf16[4,96,1536]{2,1,0:T(8,128)(2,1)}, u32[]{:S(2)}, u32[]{:S(2)}) collective-permute-start(bf16[4,96,1536]{2,1,0:T(8,128)(2,1)} %add_convert_fusion.17), channel_id=1, source_target_pairs={{0,16},{8,24},{16,0},{24,8},{1,17},{9,25},{17,1},{25,9},{2,18},{10... | collective-permute-start | bytes 3538952 | tf_op jit(solution)/shard_map/ppermute | solution.py:792
  808.6 55.8 %collective-permute-start.79 = (bf16[4,96,1536]{2,1,0:T(8,128)(2,1)}, bf16[4,96,1536]{2,1,0:T(8,128)(2,1)}, u32[]{:S(2)}, u32[]{:S(2)}) collective-permute-start(bf16[4,96,1536]{2,1,0:T(8,128)(2,1)} %add_convert_fusion.23), channel_id=1, source_target_pairs={{0,8},{8,0},{16,24},{24,16},{1,9},{9,1},{17,25},{25,17},{2,10},{10... | collective-permute-start | bytes 3538952 | tf_op jit(solution)/shard_map/ppermute | solution.py:792
  810.5 51.3 %collective-permute-start.90 = (bf16[4,96,1536]{2,1,0:T(8,128)(2,1)}, bf16[4,96,1536]{2,1,0:T(8,128)(2,1)}, u32[]{:S(2)}, u32[]{:S(2)}) collective-permute-start(bf16[4,96,1536]{2,1,0:T(8,128)(2,1)} %add_convert_fusion.13), channel_id=1, source_target_pairs={{0,8},{8,0},{16,24},{24,16},{1,9},{9,1},{17,25},{25,17},{2,10},{10... | collective-permute-start | bytes 3538952 | tf_op jit(solution)/shard_map/ppermute | solution.py:792
  811.9 52.5 %collective-permute-start.83 = (bf16[4,96,1536]{2,1,0:T(8,128)(2,1)}, bf16[4,96,1536]{2,1,0:T(8,128)(2,1)}, u32[]{:S(2)}, u32[]{:S(2)}) collective-permute-start(bf16[4,96,1536]{2,1,0:T(8,128)(2,1)} %add_convert_fusion.19), channel_id=1, source_target_pairs={{0,16},{8,24},{16,0},{24,8},{1,17},{9,25},{17,1},{25,9},{2,18},{10... | collective-permute-start | bytes 3538952 | tf_op jit(solution)/shard_map/ppermute | solution.py:792
  (136 other events, 1437.6 us)
Sparse Core Ops, SparseCore 0:
  91.0 46.4 all-gather.5
  188.0 68.6 all-reduce.8
  278.5 44.9 all-gather.7
  402.1 68.2 all-reduce.10
  538.4 67.2 all-reduce.12
  648.3 68.6 all-reduce.14
  806.0 119.5 all-reduce.16

commit v2 on v1

--- a/solution.py
+++ b/solution.py
@@ -18,8 +18,11 @@
 F32 = jnp.float32
 BF16 = jnp.bfloat16
 HIGH = lax.Precision.HIGHEST
-ROW_CONST, ROW_VEC, ROW_GA, ROW_GM = 16, 20, 22, 23
+ROW_CONST, ROW_VEC, ROW_GA, ROW_GM, ROW_UP = 16, 20, 22, 23, 24
 VMEM_LIMIT = 58 * 1024 * 1024
+SCALE = 0.05
+PACK = 128
+LATE = 512
 
 NN = (((1,), (0,)), ((), ()))
 NT = (((1,), (1,)), ((), ()))
@@ -35,7 +38,9 @@
 
 
 def cost(flops, nbytes, trans=0):
-    return pl.CostEstimate(flops=int(flops), bytes_accessed=int(nbytes), transcendentals=int(trans))
+    return pl.CostEstimate(
+        flops=int(flops * SCALE), bytes_accessed=int(nbytes * SCALE), transcendentals=int(trans * SCALE)
+    )
 
 
 def iota(shape, dim):
@@ -58,39 +63,120 @@
     return out
 
 
+def round_up(value, unit):
+    return -(-value // unit) * unit
+
+
 def prep_kernel(count, rows, offs_ref, *refs):
-    in_a, in_w = refs[:count], refs[count : 2 * count]
-    qkv_ref, wo_ref, vec_ref = refs[2 * count :]
-    cols = qkv_ref.shape[1]
-    vec_cols = []
+    qkv_ref, wo_ref, vec_ref, scr_ref = refs[count:]
+    cols, out_cols = qkv_ref.shape[1], wo_ref.shape[2]
     for piece in range(count):
         start = pl.multiple_of(offs_ref[piece] * rows, rows)
-        block = in_a[piece][...]
+        block = refs[piece][...]
         qkv_ref[pl.ds(start, rows), :] = block[:, :cols]
-        vec_ref[pl.ds(start, rows), :] = block[:, cols:]
+        scr_ref[pl.ds(start, rows), :] = block[:, cols : cols + PACK].astype(F32)
         for rank in range(wo_ref.shape[0]):
-            wo_ref[rank, pl.ds(start, rows), :] = in_w[piece][rank]
-    del vec_cols
-
-
-def prep_weights(pieces_a, pieces_w, offs, feature_dim, qkv_cols):
-    count = len(pieces_a)
+            first = cols + PACK + rank * out_cols
+            wo_ref[rank, pl.ds(start, rows), :] = block[:, first : first + out_cols]
+    vec_ref[...] = scr_ref[...].T[:32]
+
+
+def prep_weights(pieces, offs, feature_dim, qkv_cols, tp_count):
+    count = len(pieces)
+    cols = round_up(qkv_cols, 128)
+    out_cols = (pieces[0].shape[1] - cols - PACK) // tp_count
+    vmem = pl.BlockSpec(memory_space=pltpu.VMEM)
+    return pl.pallas_call(
+        functools.partial(prep_kernel, count, feature_dim // count),
+        out_shape=(
+            jax.ShapeDtypeStruct((feature_dim, cols), BF16),
+            jax.ShapeDtypeStruct((tp_count, feature_dim, out_cols), BF16),
+            jax.ShapeDtypeStruct((32, feature_dim), F32),
+        ),
+        in_specs=[SMEM_SPEC] + [vmem] * count,
+        out_specs=(vmem, vmem, vmem),
+        scratch_shapes=[pltpu.VMEM((feature_dim, PACK), F32)],
+        compiler_params=kernel_params(),
+        cost_estimate=cost(1e6, 3e6),
+        name="prep",
+    )(offs, *pieces)
+
+
+def pack_kernel(count, rows, offs_ref, dqkv_ref, dwo_ref, dvec_ref, *refs):
+    outs, scr_ref = refs[:-1], refs[-1]
+    cols, out_cols = dqkv_ref.shape[1], dwo_ref.shape[1]
+    scr_ref[:, :cols] = dqkv_ref[...]
+    scr_ref[:, cols : cols + out_cols] = dwo_ref[...]
+    wide = jnp.concatenate([dvec_ref[...], jnp.zeros((96, dvec_ref.shape[1]), F32)], axis=0).T
+    scr_ref[:, cols + out_cols :] = wide
+    for piece in range(count):
+        start = pl.multiple_of(offs_ref[piece] * rows, rows)
+        block = scr_ref[pl.ds(start, rows), :].astype(BF16)
+        if count > 1:
+            outs[piece % 2][piece // 2] = block
+        else:
+            outs[0][...] = block
+
+
+def pack_grads(dqkv, dwo, dvec, offs):
+    feature_dim = dqkv.shape[0]
+    count = offs.shape[0]
     rows = feature_dim // count
-    tp_count, _, out_cols = pieces_w[0].shape
-    vec_cols = pieces_a[0].shape[1] - qkv_cols
+    width = dqkv.shape[1] + dwo.shape[1] + PACK
+    shape = (count // 2, rows, width) if count > 1 else (feature_dim, width)
+    vmem = pl.BlockSpec(memory_space=pltpu.VMEM)
+    outs = 2 if count > 1 else 1
     return pl.pallas_call(
-        functools.partial(prep_kernel, count, rows),
-        out_shape=(
-            jax.ShapeDtypeStruct((feature_dim, qkv_cols), BF16),
-            jax.ShapeDtypeStruct((tp_count, feature_dim, out_cols), BF16),
-            jax.ShapeDtypeStruct((feature_dim, vec_cols), BF16),
-        ),
-        in_specs=[SMEM_SPEC] + [pl.BlockSpec(memory_space=pltpu.VMEM)] * (2 * count),
-        out_specs=tuple([pl.BlockSpec(memory_space=pltpu.VMEM)] * 3),
+        functools.partial(pack_kernel, count, rows),
+        out_shape=tuple([jax.ShapeDtypeStruct(shape, BF16)] * outs),
+        in_specs=[SMEM_SPEC, vmem, vmem, vmem],
+        out_specs=tuple([vmem] * outs),
+        scratch_shapes=[pltpu.VMEM((feature_dim, width), F32)],
+        compiler_params=kernel_params(),
+        cost_estimate=cost(1e6, 6e6),
+        name="pack_grads",
+    )(offs, dqkv, dwo, dvec)
+
+
+def pack_wide_kernel(gu_ref, down_ref, low_ref, high_ref):
+    units = down_ref.shape[-1]
+
+    def write(ref):
+        ref[0, :, :units] = gu_ref[0, 0, :, 0, :]
+        ref[0, :, units : 2 * units] = gu_ref[0, 0, :, 1, :]
+        ref[0, :, 2 * units :] = down_ref[0, 0]
+
+    @pl.when(pl.program_id(0) < NF // 2)
+    def _():
+        write(low_ref)
+
+    @pl.when(pl.program_id(0) >= NF // 2)
+    def _():
+        write(high_ref)
+
+
+def pack_wide(w_gate_up, w_down_t, layer):
+    _, _, rows, _, units = w_gate_up.shape
+    half = NF // 2
+    specs = [
+        pl.BlockSpec(
+            (1, rows, 3 * units), lambda e, part=part: (jnp.clip(e - part * half, 0, half - 1), 0, 0)
+        )
+        for part in range(2)
+    ]
+    return pl.pallas_call(
+        pack_wide_kernel,
+        grid=(NF,),
+        out_shape=tuple([jax.ShapeDtypeStruct((half, rows, 3 * units), BF16)] * 2),
+        in_specs=[
+            pl.BlockSpec((1, 1, rows, 2, units), lambda e: (layer, e, 0, 0, 0)),
+            pl.BlockSpec((1, 1, rows, units), lambda e: (layer, e, 0, 0)),
+        ],
+        out_specs=tuple(specs),
         compiler_params=kernel_params(),
         cost_estimate=cost(1e6, 5e6),
-        name="prep",
-    )(offs, *pieces_a, *pieces_w)
+        name="pack_wide",
+    )(w_gate_up, w_down_t)
 
 
 def qkv_kernel(with_ffn, *refs):
@@ -109,7 +195,7 @@
 
 def qkv_part(base, ffn, vecs, w_qkv):
     rows, feature_dim = base.shape
-    cols = w_qkv.shape[1]
+    cols = round_up(w_qkv.shape[1], 128)
     row_spec = pl.BlockSpec((TILE, feature_dim), lambda i: (i, 0))
     with_ffn = ffn is not None
     out_shape = [jax.ShapeDtypeStruct((rows, cols), BF16)]
@@ -163,7 +249,7 @@
             out = mm(p_own.astype(BF16), v_own[:width]) + mm(p_oth.astype(BF16), v_oth)
             out = out / total
             rows = slice(tile * TILE, (tile + 1) * TILE)
-            ctx_ref[rows, head * HD : (head + 1) * HD] = out.astype(BF16)
+            ctx_ref[head * TILE : (head + 1) * TILE, tile * HD : (tile + 1) * HD] = out.astype(BF16)
             lse_ref[rows, head : head + 1] = top + jnp.log(total)
 
 
@@ -175,12 +261,12 @@
         functools.partial(attn_fwd_kernel, heads),
         grid=(count,),
         out_shape=(
-            jax.ShapeDtypeStruct((rows, heads * HD), BF16),
+            jax.ShapeDtypeStruct((count * heads * TILE, 2 * HD), BF16),
             jax.ShapeDtypeStruct((rows, 8), F32),
         ),
         in_specs=[SMEM_SPEC, spec, spec],
         out_specs=(
-            pl.BlockSpec((BLOCK, heads * HD), lambda i: (i, 0)),
+            pl.BlockSpec((heads * TILE, 2 * HD), lambda i: (i, 0)),
             pl.BlockSpec((BLOCK, 8), lambda i: (i, 0)),
         ),
         compiler_params=kernel_params(),
@@ -239,14 +325,15 @@
 
 
 def attend_backward(qkv, other, lse, grad_context, info, heads):
-    rows, cols = qkv.shape
-    spec = pl.BlockSpec((BLOCK, cols), lambda i: (i, 0))
+    rows, width = qkv.shape
+    cols = heads * 3 * HD
+    spec = pl.BlockSpec((BLOCK, width), lambda i: (i, 0))
     return pl.pallas_call(
         functools.partial(attn_bwd_kernel, heads),
         grid=(rows // BLOCK,),
         out_shape=(
             jax.ShapeDtypeStruct((rows, cols), F32),
-            jax.ShapeDtypeStruct((rows, cols), BF16),
+            jax.ShapeDtypeStruct((rows, width), BF16),
         ),
         in_specs=[
             SMEM_SPEC,
@@ -255,7 +342,7 @@
             pl.BlockSpec((BLOCK, 8), lambda i: (i, 0)),
             pl.BlockSpec((BLOCK, heads * HD), lambda i: (i, 0)),
         ],
-        out_specs=(spec, spec),
+        out_specs=(pl.BlockSpec((BLOCK, cols), lambda i: (i, 0)), spec),
         compiler_params=kernel_params(),
         cost_estimate=cost(rows * 1024 * heads * HD * 40, rows * cols * 12, rows * heads * 1024),
         name="attend_backward",
@@ -296,7 +383,15 @@
     return pad_rows(list(enumerate(rows)), 128, width).T
 
 
-def middle_kernel(with_prev, *refs):
+def unpack_context(both):
+    heads = both.shape[0] // TILE
+    side = lax.rem(pl.program_id(0), 2) == 0
+    both = jnp.where(side, both[:, :HD], both[:, HD:])
+    parts = [both[head * TILE : (head + 1) * TILE] for head in range(heads)]
+    return jnp.concatenate(parts, axis=1)
+
+
+def middle_kernel(with_prev, rank_ref, *refs):
     if with_prev:
         h_ref, ctx_ref, wo_ref, vec_ref, route_ref, prev_ref, resid_ref = refs[:7]
         refs = refs[7:]
@@ -304,9 +399,11 @@
         h_ref, ctx_ref, wo_ref, vec_ref, route_ref = refs[:5]
         refs = refs[5:]
     mid_ref, base_ref, xm_ref, gate_ref, logit_ref = refs
-    attn_out = mm(ctx_ref[0], wo_ref[0], NT)
-    for rank in range(1, ctx_ref.shape[0]):
-        attn_out += mm(ctx_ref[rank], wo_ref[rank], NT)
+    count = ctx_ref.shape[0]
+    attn_out = mm(unpack_context(ctx_ref[rank_ref[0]]), wo_ref[0], NT)
+    for back in range(1, count):
+        owner = lax.rem(rank_ref[0] + count - back, count)
+        attn_out += mm(unpack_context(ctx_ref[owner]), wo_ref[back], NT)
     middle = h_ref[...].astype(F32) + attn_out
     mid_ref[...] = middle
     vecs = vec_ref[...]
@@ -337,16 +434,18 @@
     )
 
 
-def middle_part(h, ctx_all, wo_all, vecs, routes_t, prev_t, resid):
+def middle_part(h, ctx_all, wo_all, vecs, routes_t, prev_t, resid, rank):
     rows, feature_dim = h.shape
-    tp_count, _, out_cols = ctx_all.shape
+    tp_count, packed, lanes = ctx_all.shape
+    packed = packed * BLOCK // rows
     row_spec = pl.BlockSpec((TILE, feature_dim), lambda i: (i, 0))
     lane8 = pl.BlockSpec((8, TILE), lambda i: (0, i))
     lane16 = pl.BlockSpec((16, TILE), lambda i: (0, i))
-    ins = [h, ctx_all, wo_all, vecs, routes_t]
+    ins = [rank, h, ctx_all, wo_all, vecs, routes_t]
     in_specs = [
+        SMEM_SPEC,
         row_spec,
-        pl.BlockSpec((tp_count, TILE, out_cols), lambda i: (0, i, 0)),
+        pl.BlockSpec((tp_count, packed, lanes), lambda i: (0, i // 2, 0)),
         full_spec(wo_all.shape),
         full_spec(vecs.shape),
         lane8,
@@ -378,8 +477,7 @@
     return high, (value - high.astype(F32)).astype(BF16)
 
 
-def gate_bwd_kernel(with_prev, rank_ref, *refs):
-    del rank_ref
+def gate_bwd_kernel(with_prev, *refs):
     gh_ref, mid_ref, gxm_ref, vec_ref, route_ref, gate_ref, gg_ref, ctx_ref, wo_ref = refs[:9]
     refs = refs[9:]
     if with_prev:
@@ -444,7 +542,7 @@
     gmid_ref[...] = grad_mid
     low_mid = grad_mid.astype(BF16)
     gctx_ref[...] = mm(low_mid, wo_ref[...]).astype(BF16)
-    dwo = mm(low_mid, ctx_ref[...], TN)
+    dwo = mm(low_mid, unpack_context(ctx_ref[...]), TN)
     vec_rows = pad_rows([(ROW_VEC - 16 + j, on_vec[j]) for j in range(2)], 16, TILE)
     vec_hi, vec_lo = split(vec_rows)
     dvec_low = mm(vec_hi, grad_hi) + mm(vec_lo, grad_hi)
@@ -477,15 +575,16 @@
             dres_ref[...] += dres
 
 
-def gate_backward(grad, middle, gxm, vecs, routes_t, gates_t, gg_t, context, wo_all, rank, extra):
+def gate_backward(grad, middle, gxm, vecs, routes_t, gates_t, gg_t, context, wo_all, extra):
     rows, feature_dim = middle.shape
-    out_cols = context.shape[1]
+    out_cols = wo_all.shape[2]
     with_prev = len(extra) == 2
-    row_spec = pl.BlockSpec((TILE, feature_dim), lambda i, r: (i, 0))
-    lane8 = pl.BlockSpec((8, TILE), lambda i, r: (0, i))
-    lane16 = pl.BlockSpec((16, TILE), lambda i, r: (0, i))
-    ctx_spec = pl.BlockSpec((TILE, out_cols), lambda i, r: (i, 0))
-    wo_spec = pl.BlockSpec((pl.Squeezed(), feature_dim, out_cols), lambda i, r: (r[0], 0, 0))
+    row_spec = pl.BlockSpec((TILE, feature_dim), lambda i: (i, 0))
+    lane8 = pl.BlockSpec((8, TILE), lambda i: (0, i))
+    lane16 = pl.BlockSpec((16, TILE), lambda i: (0, i))
+    ctx_spec = pl.BlockSpec((context.shape[0] * BLOCK // rows, 2 * HD), lambda i: (i // 2, 0))
+    out_spec = pl.BlockSpec((TILE, out_cols), lambda i: (i, 0))
+    wo_spec = pl.BlockSpec((pl.Squeezed(), feature_dim, out_cols), lambda i: (0, 0, 0))
     in_specs = [row_spec, row_spec, row_spec, full_spec(vecs.shape), lane8, lane8, lane8]
     in_specs += [ctx_spec, wo_spec, lane16]
     out_shape = [
@@ -494,30 +593,28 @@
         jax.ShapeDtypeStruct((feature_dim, out_cols), F32),
         jax.ShapeDtypeStruct((32, feature_dim), F32),
     ]
-    out_specs = [row_spec, ctx_spec, full_spec((feature_dim, out_cols)), full_spec((32, feature_dim))]
+    out_specs = [row_spec, out_spec, full_spec((feature_dim, out_cols)), full_spec((32, feature_dim))]
     if with_prev:
         in_specs.append(full_spec(extra[1].shape))
         out_shape += [jax.ShapeDtypeStruct((16, rows), F32), jax.ShapeDtypeStruct((16, 16), F32)]
         out_specs += [lane16, full_spec((16, 16))]
     return pl.pallas_call(
         functools.partial(gate_bwd_kernel, with_prev),
-        grid_spec=pltpu.PrefetchScalarGridSpec(
-            num_scalar_prefetch=1,
-            grid=(rows // TILE,),
-            in_specs=in_specs,
-            out_specs=tuple(out_specs),
-        ),
+        grid=(rows // TILE,),
         out_shape=tuple(out_shape),
+        in_specs=in_specs,
+        out_specs=tuple(out_specs),
         compiler_params=kernel_params(),
         cost_estimate=cost(4 * rows * feature_dim * out_cols, rows * feature_dim * 18),
         name="gate_backward",
-    )(rank, grad, middle, gxm, vecs, routes_t, gates_t, gg_t, context, wo_all, *extra)
+    )(grad, middle, gxm, vecs, routes_t, gates_t, gg_t, context, wo_all, *extra)
 
 
 def qkv_bwd_kernel(gown_ref, goth_ref, h_ref, vec_ref, w_ref, part_ref, dw_ref):
     step = pl.program_id(0)
-    grad = (gown_ref[...] + goth_ref[...].astype(F32)).astype(BF16)
-    part_ref[...] = mm(grad, w_ref[...], NT).astype(BF16)
+    cols = gown_ref.shape[1]
+    grad = (gown_ref[...] + goth_ref[:, :cols].astype(F32)).astype(BF16)
+    part_ref[...] = mm(grad, w_ref[:, :cols], NT).astype(BF16)
     hidden = h_ref[...].astype(F32)
     gain = vec_ref[ROW_GA : ROW_GA + 1, :]
     scale = lax.rsqrt(jnp.mean(hidden * hidden, axis=-1, keepdims=True) + EPSILON)
@@ -535,9 +632,10 @@
 
 def qkv_backward(gown, goth, h, vecs, w_qkv):
     rows, feature_dim = h.shape
-    cols = w_qkv.shape[1]
+    cols = gown.shape[1]
     row_spec = pl.BlockSpec((TILE, feature_dim), lambda i: (i, 0))
     col_spec = pl.BlockSpec((TILE, cols), lambda i: (i, 0))
+    oth_spec = pl.BlockSpec((TILE, goth.shape[1]), lambda i: (i, 0))
     return pl.pallas_call(
         qkv_bwd_kernel,
         grid=(rows // TILE,),
@@ -545,7 +643,7 @@
             jax.ShapeDtypeStruct((rows, feature_dim), BF16),
             jax.ShapeDtypeStruct((feature_dim, cols), F32),
         ),
-        in_specs=[col_spec, col_spec, row_spec, full_spec(vecs.shape), full_spec(w_qkv.shape)],
+        in_specs=[col_spec, oth_spec, row_spec, full_spec(vecs.shape), full_spec(w_qkv.shape)],
         out_specs=(row_spec, full_spec((feature_dim, cols))),
         compiler_params=kernel_params(),
         cost_estimate=cost(4 * rows * feature_dim * cols, rows * feature_dim * 10),
@@ -600,16 +698,16 @@
     )(gmid, ga, h, vecs)
 
 
-def experts_kernel(fwd, bwd, blocks, count, halves, rows, offs_ref, *refs):
+def experts_kernel(fwd, bwd, blocks, plan, out_count, rows, offs_ref, *refs):
     refs = list(refs)
     xm_ref = refs.pop(0)
     gh_ref = refs.pop(0) if bwd else None
     route_ref, gate_ref = refs.pop(0), refs.pop(0)
-    w_refs = [refs.pop(0) for _ in range(count * halves)]
+    w_refs = [refs.pop(0) for _ in plan]
     ffn_ref = refs.pop(0) if fwd else None
     if bwd:
         gx_ref = refs.pop(0)
-        dw_refs = [refs.pop(0) for _ in range(count * halves)]
+        dw_refs = [refs.pop(0) for _ in range(out_count)]
     w_scr, place_scr, pick_scr = refs.pop(0), refs.pop(0), refs.pop(0)
     acc_ref = refs.pop(0) if fwd else None
     if bwd:
@@ -618,7 +716,6 @@
     last = pl.num_programs(0) - 1
     width = w_scr.shape[1]
     units = width // 3
-    half = NF // halves
 
     @pl.when(expert == 0)
     def _():
@@ -635,13 +732,17 @@
             gacc_ref[...] = jnp.zeros_like(gacc_ref)
             gg_scr[...] = jnp.zeros_like(gg_scr)
 
-    for part in range(halves):
-
-        @pl.when((expert >= part * half) & (expert < (part + 1) * half))
-        def _(part=part):
-            for piece in range(count):
-                start = pl.multiple_of(offs_ref[piece] * rows, rows)
-                w_scr[pl.ds(start, rows), :] = w_refs[part * count + piece][0]
+    def fill(ref, off):
+        start = pl.multiple_of(offs_ref[off] * rows, rows)
+        w_scr[pl.ds(start, rows), :] = ref[0]
+
+    for ref, (off, first, number) in zip(w_refs, plan):
+        if number == NF:
+            fill(ref, off)
+        else:
+            pl.when((expert >= first) & (expert < first + number))(
+                functools.partial(fill, ref, off)
+            )
 
     hot, gate_cols, masks = [], [], []
     for block in range(blocks):
@@ -675,7 +776,13 @@
 
         @pl.when(expert == last)
         def _():
-            ffn_ref[...] = acc_ref[...].astype(BF16)
+            if bwd:
+                late_rows = ffn_ref.shape[0]
+                ffn_ref[...] = acc_ref[acc_ref.shape[0] - late_rows :, :].astype(BF16)
+                rest = acc_ref.shape[0] - late_rows
+                gx_ref[gx_ref.shape[0] - rest :, :] = acc_ref[:rest, :].astype(BF16)
+            else:
+                ffn_ref[...] = acc_ref[...].astype(BF16)
 
     if bwd:
         raw = raw_scr[...]
@@ -701,48 +808,48 @@
                 hot[block], grad_pick[block * CAP : (block + 1) * CAP], TN
             )
         grad_result = (raw.astype(F32) * gate_col).astype(BF16)
-        dw_scr[:, : 2 * units] = mm(picked, grad_gu, TN).astype(BF16)
-        dw_scr[:, 2 * units :] = mm(grad_result, hidden, TN).astype(BF16)
-        for part in range(halves):
-
-            @pl.when((expert >= part * half) & (expert < (part + 1) * half))
-            def _(part=part):
-                for piece in range(count):
-                    start = pl.multiple_of(offs_ref[piece] * rows, rows)
-                    dw_refs[part * count + piece][0] = dw_scr[pl.ds(start, rows), :]
+        if out_count == 1:
+            dw_refs[0][0, :, : 2 * units] = mm(picked, grad_gu, TN).astype(BF16)
+            dw_refs[0][0, :, 2 * units :] = mm(grad_result, hidden, TN).astype(BF16)
+        else:
+            dw_scr[:, : 2 * units] = mm(picked, grad_gu, TN).astype(BF16)
+            dw_scr[:, 2 * units :] = mm(grad_result, hidden, TN).astype(BF16)
+            half = NF // 2
+            for part in range(2):
+
+                @pl.when((expert >= part * half) & (expert < (part + 1) * half))
+                def _(part=part):
+                    for off in range(8):
+                        start = pl.multiple_of(offs_ref[off] * rows, rows)
+                        dw_refs[2 * part + off % 2][off // 2, 0] = dw_scr[pl.ds(start, rows), :]
 
         @pl.when(expert == last)
         def _():
             total = blocks * BLOCK
             gx_ref[:total, :] = gacc_ref[...].astype(BF16)
-            gx_ref[total:, :] = jnp.zeros((gx_ref.shape[0] - total, gx_ref.shape[1]), BF16)
+            gx_ref[total : total + 16, :] = jnp.zeros((16, gx_ref.shape[1]), BF16)
             gx_ref[total : total + gg_scr.shape[0], :BLOCK] = gg_scr[...].astype(BF16)
 
 
 def experts(fwd, bwd, xm, gh, routes_t, gates_t, pieces, offs):
     rows, feature_dim = xm.shape
     blocks = rows // BLOCK
-    halves, count = len(pieces), len(pieces[0])
-    half = NF // halves
-    piece_rows = pieces[0][0].shape[1]
-    width = pieces[0][0].shape[2]
+    arrays = [item[0] for item in pieces]
+    plan = [item[1:] for item in pieces]
+    _, piece_rows, width = arrays[0].shape
     units = width // 3
-
-    def piece_specs():
-        specs = []
-        for part in range(halves):
-            for _ in range(count):
-                specs.append(
-                    pl.BlockSpec(
-                        (1, piece_rows, width),
-                        lambda e, part=part: (jnp.clip(e - part * half, 0, half - 1), 0, 0),
-                    )
-                )
-        return specs
+    split_out = len(pieces) > 1
+    half = NF // 2
 
     ins = [xm] + ([gh] if bwd else []) + [routes_t, gates_t]
-    in_specs = [SMEM_SPEC] + [full_spec(item.shape) for item in ins] + piece_specs()
-    flat = [piece for part in pieces for piece in part]
+    in_specs = [SMEM_SPEC] + [full_spec(item.shape) for item in ins]
+    for _, first, number in plan:
+        in_specs.append(
+            pl.BlockSpec(
+                (1, piece_rows, width),
+                lambda e, first=first, number=number: (jnp.clip(e - first, 0, number - 1), 0, 0),
+            )
+        )
     out_shape, out_specs, scratch = [], [], []
     scratch += [
         pltpu.VMEM((feature_dim, width), BF16),
@@ -750,26 +857,39 @@
         pltpu.VMEM((blocks * CAP, feature_dim), BF16),
     ]
     flops = 0
+    out_count = 4 if split_out else 1
     if fwd:
-        out_shape.append(jax.ShapeDtypeStruct((rows, feature_dim), BF16))
-        out_specs.append(full_spec((rows, feature_dim)))
+        ffn_rows = LATE if bwd else rows
+        out_shape.append(jax.ShapeDtypeStruct((ffn_rows, feature_dim), BF16))
+        out_specs.append(full_spec((ffn_rows, feature_dim)))
         scratch.append(pltpu.VMEM((rows, feature_dim), F32))
         flops += 1.0e9 * NF * blocks / 2
     if bwd:
-        out_shape.append(jax.ShapeDtypeStruct((rows + 16, feature_dim), BF16))
-        out_specs.append(full_spec((rows + 16, feature_dim)))
-        for piece in flat:
-            out_shape.append(jax.ShapeDtypeStruct(piece.shape, BF16))
-        out_specs += piece_specs()
+        gx_rows = rows + 16 + (rows - LATE if fwd else 0)
+        out_shape.append(jax.ShapeDtypeStruct((gx_rows, feature_dim), BF16))
+        out_specs.append(full_spec((gx_rows, feature_dim)))
+        if split_out:
+            for part in range(2):
+                for _ in range(2):
+                    out_shape.append(jax.ShapeDtypeStruct((4, half, piece_rows, width), BF16))
+                    out_specs.append(
+                        pl.BlockSpec(
+                            (4, 1, piece_rows, width),
+                            lambda e, part=part: (0, jnp.clip(e - part * half, 0, half - 1), 0, 0),
+                        )
+                    )
+        else:
+            out_shape.append(jax.ShapeDtypeStruct((NF, feature_dim, width), BF16))
+            out_specs.append(pl.BlockSpec((1, feature_dim, width), lambda e: (e, 0, 0)))
         scratch += [
             pltpu.VMEM((rows, feature_dim), F32),
             pltpu.VMEM((blocks * CAP, feature_dim), BF16),
             pltpu.VMEM((blocks * 8, BLOCK), F32),
-            pltpu.VMEM((feature_dim, width), BF16),
+            pltpu.VMEM((feature_dim, width) if split_out else (8, 128), BF16),
         ]
         flops += 2.2e9 * NF * blocks / 2
     outs = pl.pallas_call(
-        functools.partial(experts_kernel, fwd, bwd, blocks, count, halves, piece_rows),
+        functools.partial(experts_kernel, fwd, bwd, blocks, plan, out_count, piece_rows),
         grid=(NF,),
         out_shape=tuple(out_shape),
         in_specs=in_specs,
@@ -778,14 +898,75 @@
         compiler_params=kernel_params(),
         cost_estimate=cost(flops, 20e6 * (2 if bwd else 1), rows * units * 8),
         name="experts",
-    )(offs, *ins, *flat)
+    )(offs, *ins, *arrays)
     outs = list(outs)
     ffn = outs.pop(0) if fwd else None
-    if not bwd:
-        return ffn
-    gx = outs.pop(0)
-    grads = [outs[part * count : (part + 1) * count] for part in range(halves)]
-    return ffn, gx, grads
+    return (ffn, outs[0], outs[1:]) if bwd else (ffn, None, None)
+
+
+def final_kernel(with_old, count, *refs):
+    parts = refs[:count]
+    gu_ref, dn_ref = refs[-2:]
+    del with_old
+    half = count // 2
+    units = gu_ref.shape[-1]
+
+    def write(group):
+        total = group[0][...].reshape(group[0].shape[-2:]).astype(F32)
+        for ref in group[1:]:
+            total += ref[...].reshape(ref.shape[-2:]).astype(F32)
+        gu_ref[0, 0, :, 0, :] = total[:, :units]
+        gu_ref[0, 0, :, 1, :] = total[:, units : 2 * units]
+        dn_ref[0, 0] = total[:, 2 * units :]
+
+    @pl.when(pl.program_id(0) < NF // 2)
+    def _():
+        write(parts[:half])
+
+    @pl.when(pl.program_id(0) >= NF // 2)
+    def _():
+        write(parts[half:])
+
+
+def final_sums(lows, highs, old, layer, layer_count):
+    half = NF // 2
+    specs, arrays = [], []
+    for part, group in enumerate((lows, highs)):
+        for item in group:
+            lead = (1,) * (item.ndim - 3)
+            specs.append(
+                pl.BlockSpec(
+                    lead + (1,) + item.shape[-2:],
+                    lambda e, part=part, lead=lead: (0,) * len(lead)
+                    + (jnp.clip(e - part * half, 0, half - 1), 0, 0),
+                )
+            )
+            arrays.append(item)
+    count = len(arrays)
+    rows, width = arrays[0].shape[-2:]
+    units = width // 3
+    aliases = {}
+    if old is not None:
+        specs += [pl.BlockSpec(memory_space=pl.ANY)] * 2
+        arrays += list(old)
+        aliases = {count: 0, count + 1: 1}
+    return pl.pallas_call(
+        functools.partial(final_kernel, old is not None, count),
+        grid=(NF,),
+        out_shape=(
+            jax.ShapeDtypeStruct((layer_count, NF, rows, 2, units), F32),
+            jax.ShapeDtypeStruct((layer_count, NF, rows, units), F32),
+        ),
+        in_specs=specs,
+        out_specs=(
+            pl.BlockSpec((1, 1, rows, 2, units), lambda e: (layer, e, 0, 0, 0)),
+            pl.BlockSpec((1, 1, rows, units), lambda e: (layer, e, 0, 0)),
+        ),
+        input_output_aliases=aliases,
+        compiler_params=kernel_params(),
+        cost_estimate=cost(1e7, NF * rows * width * 12),
+        name="final_sums",
+    )(*arrays)
 
 
 def hop(value, step):
@@ -797,39 +978,56 @@
 
 
 def gather_small(value):
-    by_x, by_y = hop(value, 1), hop(value, 2)
-    by_d = hop(value, 3)
+    by_x, by_y, by_d = hop(value, 1), hop(value, 2), hop(value, 3)
     out = []
     for item in (value, by_x, by_y, by_d):
         out += [item, swap(item)]
     return out
 
 
-def gather_halves(low, high):
+def gather_rest(own, x_high, y_low):
+    low, high = own
     x_low, y_high = hop(low, 1), hop(high, 2)
-    x_high, y_low = hop(high, 1), hop(low, 2)
     d_low, d_high = hop(y_low, 1), hop(x_high, 2)
-    lows, highs = [], []
-    for item in (low, x_low, y_low, d_low):
-        lows += [item, swap(item)]
-    for item in (high, x_high, y_high, d_high):
-        highs += [item, swap(item)]
-    return lows, highs
-
-
-def add_low(first, second):
-    return (first.astype(F32) + second.astype(F32)).astype(BF16)
-
-
-def sum_cores(pieces):
-    return [add_low(pieces[2 * chip], swap(pieces[2 * chip + 1])) for chip in range(4)]
-
-
-def sum_chips(sums, first):
-    second = 3 - first
-    mine = add_low(sums[0], hop(sums[first], first))
-    beside = add_low(sums[second], hop(sums[3], first))
-    return mine.astype(F32) + hop(beside, second).astype(F32)
+    return (low, x_low, y_low, d_low), (high, x_high, y_high, d_high)
+
+
+def gather_cores(lows, highs):
+    half = NF // 2
+    out = []
+    for first, items in ((0, lows), (half, highs)):
+        for chip, item in enumerate(items):
+            out += [(item, 2 * chip, first, half), (swap(item), 2 * chip + 1, first, half)]
+    return out
+
+
+def tie(*values):
+    return lax.optimization_barrier(values)
+
+
+def add_low(*terms):
+    total = terms[0].astype(F32)
+    for term in terms[1:]:
+        total = total + term.astype(F32)
+    return total.astype(BF16)
+
+
+def scatter_cores(keep, send, first):
+    other = swap(send)
+    if first == 1:
+        out = add_low(keep[1::2], other[1::2])
+    else:
+        out = add_low(keep[2:], other[2:])
+    return keep, other, out
+
+
+def scatter_first(keep, other, out, first):
+    got = hop(out, first)
+    return keep[:1], other[:1], got[:1], add_low(keep[3 - first], other[3 - first], got[1])
+
+
+def scatter_second(terms, first):
+    return terms[:3] + (hop(terms[3], 3 - first),)
 
 
 def per_device(
@@ -867,7 +1065,7 @@
     info = jnp.concatenate([ctx.reshape(1), lengths.reshape(-1)]).astype(jnp.int32)
     resid = jnp.zeros((16, 16), F32).at[:NE, :NE].set(w_resid.astype(F32))
 
-    small, wide, outer = [], [], []
+    small, wide = [], []
     for layer in range(layer_count):
         vec = jnp.concatenate(
             [
@@ -878,42 +1076,68 @@
                 v_const[layer].T,
                 norm_attn[layer][:, None],
                 norm_moe[layer][:, None],
-                jnp.zeros((shard_rows, 128 - ROW_GM - 1), BF16),
+                jnp.zeros((shard_rows, PACK - ROW_GM - 1), BF16),
             ],
             axis=1,
         )
-        small.append(jnp.concatenate([w_qkv[layer], vec], axis=1))
-        wide.append(
-            jnp.concatenate(
-                [
-                    w_gate_up[layer].reshape(NF, shard_rows, 2 * units),
-                    jnp.transpose(w_down[layer], (0, 2, 1)),
-                ],
-                axis=2,
-            )
-        )
-    outer = lax.all_gather(jnp.transpose(w_out, (0, 2, 1)), "tp", axis=1)
-
-    weights = []
-    token = None
-    for layer in range(layer_count):
+        pad = jnp.zeros((shard_rows, round_up(qkv_cols, 128) - qkv_cols), BF16)
+        small.append(jnp.concatenate([w_qkv[layer], pad, vec], axis=1))
+        wide.append(pack_wide(w_gate_up, jnp.swapaxes(w_down, 2, 3), layer))
+    tp_count = axes["tp"]
+    outer = jnp.transpose(w_out, (0, 2, 1))
+    outer = [outer] + [
+        lax.ppermute(outer, "tp", [(i, (i + k) % tp_count) for i in range(tp_count)])
+        for k in range(1, tp_count)
+    ]
+    small = [
+        jnp.concatenate([small[layer]] + [item[layer] for item in outer], axis=1)
+        for layer in range(layer_count)
+    ]
+
+    weights, wide_first = [None] * layer_count, [None] * layer_count
+
+    def fetch_small(layer, after):
+        own = small[layer]
         if hyper:
-            low, high = wide[layer][: NF // 2], wide[layer][NF // 2 :]
-            own_small, own_outer = small[layer], outer[layer]
-            if token is not None:
-                own_small, low, high, _ = lax.optimization_barrier((own_small, low, high, token))
-            pieces_small = gather_small(own_small)
-            pieces_outer = gather_small(own_outer)
-            pieces = gather_halves(low, high)
-            token = (pieces[0][6], pieces[1][6])
+            own, _ = tie(own, after)
+            pieces = gather_small(own)
+            first = [pieces[k] for k in (2, 4, 6)]
+            if layer == 0:
+                fetch_first(0, info)
+                pieces, wide_first[0] = tie(pieces, wide_first[0])
+            else:
+                fetch_first(layer, first)
         else:
-            pieces_small = [lax.all_gather(small[layer], groups, axis=0, tiled=True)]
-            pieces_outer = [lax.all_gather(outer[layer], groups, axis=1, tiled=True)]
-            pieces = [[lax.all_gather(wide[layer], groups, axis=1, tiled=True)]]
-        qkv_full, wo_all, vec_cols = prep_weights(
-            pieces_small, pieces_outer, offs, feature_dim, qkv_cols
-        )
-        weights.append((qkv_full, wo_all, vec_cols[:, :32].T.astype(F32), pieces))
+            pieces = [lax.all_gather(own, groups, axis=0, tiled=True)]
+        weights[layer] = list(prep_weights(pieces, offs, feature_dim, qkv_cols, tp_count))
+
+    def fetch_first(layer, after):
+        own, _ = tie(wide[layer], after)
+        wide_first[layer] = (own, hop(own[1], 1), hop(own[0], 2))
+
+    def fetch_rest(layer, value):
+        if hyper:
+            own, x_high, y_low = wide_first[layer]
+            value, own, x_high, y_low = tie(value, own, x_high, y_low)
+            rests[layer] = gather_rest(own, x_high, y_low)
+        return value
+
+    def fetch_cores(layer, after):
+        if hyper:
+            lows, highs = rests[layer]
+            early = (lows[0], lows[2], highs[0], highs[1])
+            early, _ = tie(early, after)
+            lows = (early[0], lows[1], early[1], lows[3])
+            highs = (early[2], early[3], highs[2], highs[3])
+            ends[layer] = (lows[1], lows[3], highs[2], highs[3])
+            weights[layer].append(gather_cores(lows, highs))
+        else:
+            both = jnp.concatenate(wide[layer], axis=0)
+            full = lax.all_gather(both, groups, axis=1, tiled=True)
+            weights[layer].append([(full, 0, 0, NF)])
+
+    ends, rests = [None] * layer_count, [None] * layer_count
+    fetch_small(0, info)
 
     routes_t = jnp.moveaxis(routes.reshape(layer_count, rows, 2), 2, 1)
     routes_t = jnp.concatenate(
@@ -926,23 +1150,29 @@
     base, ffn, prev_t = tokens.reshape(rows, feature_dim), None, None
     saved = []
     for layer in range(layer_count):
-        qkv_full, wo_all, vecs, pieces = weights[layer]
+        qkv_full, wo_all, vecs = weights[layer][:3]
         outs = qkv_part(base, ffn, vecs, qkv_full)
         h_in, qkv = outs if ffn is not None else (base, outs[0])
-        other = swap(qkv)
+        other = fetch_rest(layer, swap(qkv))
         context, lse = attend_forward(qkv, other, info, heads)
         ctx_all = lax.all_gather(context, "tp", axis=0)
+        fetch_cores(layer, context)
+        pieces = weights[layer][3]
         middle, base, xm_low, gates_t, logits_t = middle_part(
-            h_in, ctx_all, wo_all, vecs, routes_t[layer], prev_t, resid
+            h_in, ctx_all, wo_all, vecs, routes_t[layer], prev_t, resid, rank
         )
         saved.append((h_in, qkv, other, context, lse, middle, xm_low, gates_t, prev_t))
         prev_t = logits_t
         if layer < layer_count - 1:
-            part = experts(True, False, xm_low, None, routes_t[layer], gates_t, pieces, offs)
+            fetch_small(layer + 1, ends[layer] if hyper else ctx_all)
+            part, _, _ = experts(True, False, xm_low, None, routes_t[layer], gates_t, pieces, offs)
             ffn = lax.psum(part, "tp")
+            if hyper:
+                ffn, wide_first[layer + 1] = tie(ffn, wide_first[layer + 1])
 
     grad, grad_low = cot, cot
-    grad_logits = None
+    upper_gain = None
+    grad_logits, wide_out, pending, small_terms, late = None, None, None, None, None
     finals = [None] * layer_count
     for layer in reversed(range(layer_count)):
         qkv_full, wo_all, vecs, pieces = weights[layer]
@@ -951,75 +1181,113 @@
         part, gx, grads = experts(
             top, True, xm_low, grad_low, routes_t[layer], gates_t, pieces, offs
         )
+        if not top and late is not None:
+            late = lax.psum(late, "tp")
+            gx, grads, late, pending = tie(gx, grads, late, pending)
+            mixed = (base_top + jnp.concatenate([early, late], axis=0).astype(F32)).astype(BF16)
         gx = lax.psum(gx, "tp")
+        if hyper:
+            sums = [scatter_cores(grads[2 * k], grads[2 * k + 1], k + 1) for k in range(2)]
+            if pending is not None:
+                wide_terms, small_sums, dres = pending
+                terms = [scatter_second(wide_terms[k], k + 1) for k in range(2)]
+                wide_out = final_sums(terms[0], terms[1], wide_out, layer + 1, layer_count)
+                small_terms = scatter_first(*small_sums, 1)
+                gx, sums, wide_out, small_terms = tie(gx, sums, wide_out, small_terms)
+            else:
+                gx, sums = tie(gx, sums)
+            grads = [scatter_first(*sums[k], k + 1) for k in range(2)]
         if top:
-            ffn = lax.psum(part, "tp")
-            mixed = (base + ffn.astype(F32)).astype(BF16)
+            base_top, early = base, gx[rows + 16 :]
         gg_t = gx[rows : rows + 16, :block_len].astype(F32)
         gg_t = jnp.moveaxis(gg_t.reshape(2, 8, block_len)[: rows // BLOCK], 0, 1).reshape(8, rows)
         extra = (prev_t, resid) if prev_t is not None else (grad_logits,)
         outs = gate_backward(
-            grad, middle, gx, vecs, routes_t[layer], gates_t, gg_t, context, wo_all, rank, extra
+            grad, middle, gx, vecs, routes_t[layer], gates_t, gg_t, context, wo_all, extra
         )
         gmid, gctx, dwo, dvec = outs[:4]
         if prev_t is not None:
             grad_logits, dres = outs[4:]
         gown, goth = attend_backward(qkv, other, lse, gctx, info, heads)
-        ga_part, dqkv = qkv_backward(gown, swap(goth), h_in, vecs, qkv_full)
+        goth = swap(goth)
+        if hyper and layer == 0:
+            goth, grads = tie(goth, grads)
+        ga_part, dqkv = qkv_backward(gown, goth, h_in, vecs, qkv_full)
+        if upper_gain is not None:
+            dvec = dvec.at[ROW_UP].set(upper_gain)
+        packed = pack_grads(dqkv, dwo, dvec, offs)
         ga = lax.psum(ga_part, "tp")
+        own = None
+        if hyper:
+            small_sums = scatter_cores(*packed, 1)
+            if layer > 0:
+                dres = dres + swap(dres)
+                dres = dres + hop(dres, 1)
+                ga, grads, small_sums, dres = tie(ga, grads, small_sums, dres)
+                dres = dres + hop(dres, 2)
+                pending = (grads, small_sums, dres)
+            else:
+                small_terms = scatter_second(small_terms, 1)
+                ga, small_terms = tie(ga, small_terms)
+                terms = [scatter_second(grads[k], k + 1) for k in range(2)]
+                wide_out = final_sums(terms[0], terms[1], wide_out, layer, layer_count)
+                own = scatter_second(scatter_first(*small_sums, 1), 1)
+        if top:
+            late, ga = tie(part, ga)
         outs = norm_backward(gmid, ga, h_in, vecs, layer > 0)
         grad, dgain = outs[0], outs[-1]
+        upper_gain = dgain[0]
         grad_low = outs[1]
-        finals[layer] = (grads, dqkv, dwo, dvec, dgain)
-
-    results = []
-    gain_rows = jnp.concatenate([item[4][:1] for item in finals] + [dres[:NE + 4].reshape(1, -1)], axis=1)
+        finals[layer] = (grads, packed, own if hyper else None, dgain)
+
+    gain_first = finals[0][3][:1]
     if hyper:
-        total = gain_rows + swap(gain_rows)
-        total = total + hop(total, 1)
-        total = total + hop(total, 2)
+        gain_first = gain_first + swap(gain_first)
+        gain_first = (
+            gain_first + hop(gain_first, 1) + (hop(gain_first, 2) + hop(gain_first, 3))
+        )
+        resid_total = dres[:NE, :NE]
     else:
-        total = lax.psum(gain_rows, groups)
-    gain_total = total[0, : layer_count * feature_dim].reshape(layer_count, feature_dim)
-    resid_total = total[0, layer_count * feature_dim :].reshape(16, 16)[:NE, :NE]
-    gain_own = lax.dynamic_slice(gain_total, (0, me * shard_rows), (layer_count, shard_rows))
-    for layer in range(layer_count):
-        grads, dqkv, dwo, dvec, _ = finals[layer]
-        packed = jnp.concatenate([dqkv, dwo, dvec.T], axis=1).astype(BF16)
+        gain_first = lax.psum(gain_first, groups)
+        resid_total = lax.psum(dres, groups)[:NE, :NE]
+    gain_first = lax.dynamic_slice(gain_first[0], (me * shard_rows,), (shard_rows,))
+    results = [None] * layer_count
+    for layer in reversed(range(layer_count)):
+        grads, packed, own, _ = finals[layer]
         if hyper:
-            packed = packed.reshape(shard_count, shard_rows, -1)
-            packed = [
-                lax.dynamic_index_in_dim(packed, me ^ off, 0, keepdims=False)
-                for off in range(shard_count)
-            ]
-            own = sum_chips(sum_cores(packed), 1)
-            low = sum_chips(sum_cores(grads[0]), 1)
-            high = sum_chips(sum_cores(grads[1]), 2)
-            wide_own = jnp.concatenate([low, high], axis=0)
+            own = own if layer == 0 else small_terms
+            own = sum(term.reshape(shard_rows, -1).astype(F32) for term in own)
         else:
-            own = lax.psum_scatter(packed, groups, scatter_dimension=0, tiled=True).astype(F32)
+            own = lax.psum_scatter(packed[0], groups, scatter_dimension=0, tiled=True).astype(F32)
             wide_own = lax.psum_scatter(
-                grads[0][0], groups, scatter_dimension=1, tiled=True
+                grads[0], groups, scatter_dimension=1, tiled=True
             ).astype(F32)
-        out_cols = dwo.shape[1]
+            here = (
+                wide_own[:, :, : 2 * units].reshape(NF, shard_rows, 2, units),
+                wide_own[:, :, 2 * units :],
+            )
+            if wide_out is None:
+                wide_out = ([], [])
+            wide_out[0].insert(0, here[0])
+            wide_out[1].insert(0, here[1])
+        out_cols = heads * HD
         vec = own[:, qkv_cols + out_cols :]
-        results.append(
-            (
-                own[:, :qkv_cols],
-                own[:, qkv_cols : qkv_cols + out_cols].T,
-                vec[:, ROW_GM],
-                vec[:, :NE],
-                jnp.stack([vec[:, ROW_CONST : ROW_CONST + 2], vec[:, ROW_CONST + 2 : ROW_CONST + 4]]),
-                vec[:, ROW_VEC : ROW_VEC + 2].T,
-                wide_own[:, :, : 2 * units].reshape(NF, shard_rows, 2, units),
-                jnp.transpose(wide_own[:, :, 2 * units :], (0, 2, 1)),
-            )
+        results[layer] = (
+            own[:, :qkv_cols],
+            own[:, qkv_cols : qkv_cols + out_cols].T,
+            vec[:, ROW_GM],
+            vec[:, :NE],
+            jnp.stack([vec[:, ROW_CONST : ROW_CONST + 2], vec[:, ROW_CONST + 2 : ROW_CONST + 4]]),
+            vec[:, ROW_VEC : ROW_VEC + 2].T,
+            vec[:, ROW_UP],
         )
-    stacked = [jnp.stack([item[member] for item in results]) for member in range(8)]
+    if not hyper:
+        wide_out = (jnp.stack(wide_out[0]), jnp.stack(wide_out[1]))
+    stacked = [jnp.stack([item[member] for item in results]) for member in range(6)]
     return (
         mixed.reshape(tokens.shape),
         grad.reshape(tokens.shape),
-        gain_own,
+        jnp.stack([gain_first] + [item[6] for item in results[: layer_count - 1]]),
         stacked[0],
         stacked[1],
         stacked[2],
@@ -1027,8 +1295,8 @@
         resid_total,
         stacked[4],
         stacked[5],
-        stacked[6],
-        stacked[7],
+        wide_out[0],
+        jnp.swapaxes(wide_out[1], 2, 3),
     )
 
 

time: 958 us -> 891 us (0.930)
  Pallas kernels: 229 us -> 271 us
  waiting for transfers between devices: 466 us -> 429 us
  other arithmetic: 82.1 us -> 51.9 us
  local copies, waits for them, and re-layouts: 77.2 us -> 58.1 us
  blocking collectives: 15.5 us -> 0 us
    psum x2 -> x1, waiting for transfers between devices: 73.6 us -> 19.6 us  [per_device(): ffn = lax.psum(part, 'tp')]
    pallas_call x7 -> x13, Pallas kernels: 126 us -> 167 us  [the longest x3 95.2 us: experts(): pl.pallas_call(functools.partial(experts_kernel, fwd, bwd, blocks, plan,...]
    ppermute x61 -> x36, waiting for transfers between devices: 2.19 us -> 29.8 us  [swap(): return lax.ppermute(value, 'ctx', [(0, 1), (1, 0)])]
    psum x1 -> x2, waiting for transfers between devices: 35.6 us -> 59.8 us  [per_device(): ga = lax.psum(ga_part, 'tp')]
    slice x6 -> x23, local copies, waits for them, and re-layouts: 6.04 us -> 30.1 us  [the longest x5 10.5 us: scatter_first(): keep[:1]]
    psum x2, waiting for transfers between devices: 116 us -> 92.3 us  [per_device(): gx = lax.psum(gx, 'tp')]
    all_gather x1 -> x0, blocking collectives: 15.5 us -> none  [per_device(): outer = lax.all_gather(jnp.transpose(w_out, (0, 2, 1)), 'tp', axis=1)]
    another operation x12 -> x8, other arithmetic: 17.7 us -> 3.23 us  [per_device(): jnp.stack([item[member] for item in results])]
  transfers between devices with their start and end apart: 112 -> 82, of which waited for: 36 -> 38; matrix products, arithmetic and copies ran while one was open for 14% -> 10% of each run, Pallas kernels for 16% -> 18%
where the time goes in v2:
time: 891 us; the launch traced here: 880 us
  waiting for transfers between devices  429 us (48%)
  Pallas kernels  271 us (30%)
  local copies, waits for them, and re-layouts  58.1 us (7%)
  starting transfers between devices  54.7 us (6%)
  other arithmetic  51.9 us (6%)
  between operations  15.4 us (2%)
    ppermute x35, waiting for transfers between devices, hop(): return lax.ppermute(value, 'fsdp', [(i, i ^ step) for i in range(4)])  225 us
    pallas_call x3, Pallas kernels, experts(): pl.pallas_call(functools.partial(experts_kernel, fwd, bwd, blocks, plan,...  95.2 us
    psum x2, waiting for transfers between devices, per_device(): gx = lax.psum(gx, 'tp')  92.3 us
    psum x2, waiting for transfers between devices, per_device(): ga = lax.psum(ga_part, 'tp')  59.8 us
    ppermute x35, starting transfers between devices, hop(): return lax.ppermute(value, 'fsdp', [(i, i ^ step) for i in range(4)])  41.1 us
    convert_element_type x12, other arithmetic, add_low(): return total.astype(BF16)  34.4 us
    ppermute x36, waiting for transfers between devices, swap(): return lax.ppermute(value, 'ctx', [(0, 1), (1, 0)])  29.8 us
    pallas_call x2, Pallas kernels, attend_backward(): pl.pallas_call(functools.partial(attn_bwd_kernel, heads), grid=(rows // B...  29 us
  transfers between devices with their start and end apart: 82, of which 38 were waited for; matrix products, arithmetic and copies ran while one was open for 10% of the time, Pallas kernels for 18%

profile of v2, /device:TPU:0, one launch (start us, length us, event | category | flops | bytes accessed | tf_op | source)
XLA Modules:
  0.0 880.1 jit_solution(15746459493438247542)
XLA Ops:
  8.2 5.1 collective-permute-start.2
  15.6 7.6 pack_wide.2
  36.3 23.9 %collective-permute-done.8.refs_6_ = bf16[96,1536]{1,0:T(8,128)(2,1)S(1)} collective-permute-done((bf16[96,1536]{1,0:T(8,128)(2,1)S(1)}, bf16[96,1536]{1,0:T(8,128)(2,1)S(1)}, u32[]{:S(2)}, u32[]{:S(2)}) %collective-permute-start.8) | collective-permute-done | bytes 294944 | tf_op jit(solution)/shard_map/ppermute | solution.py:973
  66.9 4.3 prep.2
  71.2 5.1 qkv_part.2.own_ref
  80.6 8.4 attend_forward.2
  96.0 23.0 %collective-permute-done.14.refs_5_.refs_6_ = bf16[4,96,1536]{2,1,0:T(8,128)(2,1)} collective-permute-done((bf16[4,96,1536]{2,1,0:T(8,128)(2,1)S(1)}, bf16[4,96,1536]{2,1,0:T(8,128)(2,1)}, u32[]{:S(2)}, u32[]{:S(2)}) %collective-permute-start.14) | collective-permute-done | bytes 1179680 | tf_op jit(solution)/shard_map/ppermute | solution.py:973
  119.0 24.5 %collective-permute-done.17.refs_9_.refs_10_ = bf16[4,96,1536]{2,1,0:T(8,128)(2,1)} collective-permute-done((bf16[4,96,1536]{2,1,0:T(8,128)(2,1)S(1)}, bf16[4,96,1536]{2,1,0:T(8,128)(2,1)}, u32[]{:S(2)}, u32[]{:S(2)}) %collective-permute-start.17) | collective-permute-done | bytes 1179680 | tf_op jit(solution)/shard_map/ppermute | solution.py:973
  147.0 9.5 %middle_part.2 = (f32[1024,768]{1,0:T(8,128)}, f32[1024,768]{1,0:T(8,128)}, bf16[1024,768]{1,0:T(8,128)(2,1)}, f32[8,1024]{1,0:T(8,128)}, f32[16,1024]{1,0:T(8,128)}) custom-call(s32[1]{0:T(128)} %bitcast.rank_ref, bf16[1024,768]{1,0:T(8,128)(2,1)} %bitcast.132, bf16[4,1536,128]{2,1,0:T(8,128)(2,1)} %bitcast.142, ...), custom_call_target="tpu_custom_call" | custom-call | flops 60397976 | bytes 629145 | tf_op jit(solution)/shard_map/middle_part/pallas_call | solution.py:457
  158.3 18.9 %experts.3 = bf16[1024,768]{1,0:T(8,128)(2,1)} custom-call(s32[8]{0:T(128)} %iota_xor_fusion.offs_ref, bf16[1024,768]{1,0:T(8,128)(2,1)} %get-tuple-element.234.refs_0_, s32[8,1024]{1,0:T(8,128)} %get-tuple-element.441.refs_4_.refs_1_.refs_2_, f32[8,1024]{1,0:T(8,128)} %get-tuple-element.235.refs_2_.refs_3_.refs_5_, ...), custom_call_target="tpu_custom_call" | custom-call | flops 400000000 | bytes 1000000 | tf_op jit(solution)/shard_map/experts/pallas_call | solution.py:891
  185.0 7.5 pack_wide.3
  192.5 5.6 collective-permute-done.26.refs_4_
  204.2 3.5 prep.3
  207.7 18.9 %collective-permute-done.29.refs_8_ = bf16[4,96,1536]{2,1,0:T(8,128)(2,1)} collective-permute-done((bf16[4,96,1536]{2,1,0:T(8,128)(2,1)}, bf16[4,96,1536]{2,1,0:T(8,128)(2,1)}, u32[]{:S(2)}, u32[]{:S(2)}) %collective-permute-start.29) | collective-permute-done | bytes 1179680 | tf_op jit(solution)/shard_map/ppermute | solution.py:973
  226.8 19.6 %all-reduce.9.cloned.1.call-done.refs_1_ = bf16[1024,768]{1,0:T(8,128)(2,1)} async-done(((bf16[1024,768]{1,0:T(8,128)(2,1)}), bf16[1024,768]{1,0:T(8,128)(2,1)}) %all-reduce.9.cloned.1.call-update) | async-done | bytes 1572880 | tf_op jit(solution)/shard_map/psum | solution.py:1169
  246.4 6.0 qkv_part.3
  256.8 8.4 attend_forward.3
  273.2 21.8 %collective-permute-done.36.refs_6_ = bf16[4,96,1536]{2,1,0:T(8,128)(2,1)} collective-permute-done((bf16[4,96,1536]{2,1,0:T(8,128)(2,1)S(1)}, bf16[4,96,1536]{2,1,0:T(8,128)(2,1)}, u32[]{:S(2)}, u32[]{:S(2)}) %collective-permute-start.36) | collective-permute-done | bytes 1179680 | tf_op jit(solution)/shard_map/ppermute | solution.py:973
  295.0 24.7 %collective-permute-done.39.refs_10_ = bf16[4,96,1536]{2,1,0:T(8,128)(2,1)} collective-permute-done((bf16[4,96,1536]{2,1,0:T(8,128)(2,1)}, bf16[4,96,1536]{2,1,0:T(8,128)(2,1)}, u32[]{:S(2)}, u32[]{:S(2)}) %collective-permute-start.39) | collective-permute-done | bytes 1179680 | tf_op jit(solution)/shard_map/ppermute | solution.py:973
  324.2 10.3 %middle_part.3 = (f32[1024,768]{1,0:T(8,128)}, f32[1024,768]{1,0:T(8,128)}, bf16[1024,768]{1,0:T(8,128)(2,1)}, f32[8,1024]{1,0:T(8,128)}, f32[16,1024]{1,0:T(8,128)}) custom-call(s32[1]{0:T(128)} %bitcast.rank_ref, f32[1024,768]{1,0:T(8,128)} %get-tuple-element.252.refs_0_.h_ref, bf16[4,1536,128]{2,1,0:T(8,128)(2,1)} %bitcast.144, ...), custom_call_target="tpu_custom_call" | custom-call | flops 60397976 | bytes 629145 | tf_op jit(solution)/shard_map/middle_part/pallas_call | solution.py:457
  335.6 42.0 %experts.4 = (bf16[512,768]{1,0:T(8,128)(2,1)}, bf16[1552,768]{1,0:T(8,128)(2,1)}, bf16[4,4,96,1536]{3,2,1,0:T(8,128)(2,1)}, bf16[4,4,96,1536]{3,2,1,0:T(8,128)(...) custom-call(s32[8]{0:T(128)} %iota_xor_fusion.offs_ref, ...), custom_call_target="tpu_custom_call" | custom-call | flops 1280000000 | bytes 2000000 | tf_op jit(solution)/shard_map/experts/pallas_call | solution.py:891
  378.5 7.6 collective-permute-done.47
  389.2 3.6 collective-permute-done.48
  392.8 3.7 add_convert_fusion.2
  396.6 77.6 %all-reduce.11.cloned.1.call-done.refs_2_ = bf16[1552,768]{1,0:T(8,128)(2,1)} async-done(((bf16[1552,768]{1,0:T(8,128)(2,1)}), bf16[1552,768]{1,0:T(8,128)(2,1)}) %all-reduce.11.cloned.1.call-update) | async-done | bytes 2383888 | tf_op jit(solution)/shard_map/psum | solution.py:1188
  478.4 12.1 %gate_backward.2 = (f32[1024,768]{1,0:T(8,128)}, bf16[1024,192]{1,0:T(8,128)(2,1)}, f32[768,192]{1,0:T(8,128)}, f32[32,768]{1,0:T(8,128)}, f32[16,1024]{1,0:T(8,128)}, /*index=5*/f32[16,16]{1,0:T(8,128)}) custom-call(bf16[1024,768]{1,0:T(8,128)(2,1)} %bitcast.136, f32[1024,768]{1,0:T(8,128)} %get-tuple-element.279.refs_1_, ...), custom_call_target="tpu_custom_call" | custom-call | flops 30198988 | bytes 707788 | tf_op jit(solution)/shard_map/gate_backward/pallas_call | solution.py:601
  490.5 14.5 %attend_backward.2 = (f32[1024,576]{1,0:T(8,128)}, bf16[1024,640]{1,0:T(8,128)(2,1)}) custom-call(s32[3]{0:T(128)} %pad_add_fusion.info_ref, bf16[1024,640]{1,0:T(8,128)(2,1)} %get-tuple-element.253.own_ref, bf16[1024,640]{1,0:T(8,128)(2,1)} %copy-done.1, f32[1024,8]{1,0:T(8,128)} %get-tuple-element.282.lse_ref, bf16[1024,192]{1,0:T(8,128)(2,1)} %get-tuple-element.283.gctx_ref), custom_call_target="tpu_custom_call" | custom-call | flops 402653184 | bytes 353894 | tf_op jit(solution)/shard_map/attend_backward/pallas_call | solution.py:331
  509.4 7.9 qkv_backward.2
  538.8 3.4 fusion
  542.2 3.5 fusion.1
  545.6 41.8 %all-reduce.13.cloned.1.call-done.ga_ref = bf16[1024,768]{1,0:T(8,128)(2,1)} async-done(((bf16[1024,768]{1,0:T(8,128)(2,1)}), bf16[1024,768]{1,0:T(8,128)(2,1)}) %all-reduce.13.cloned.1.call-update) | async-done | bytes 1572880 | tf_op jit(solution)/shard_map/psum | solution.py:1219
  589.1 6.4 norm_backward.2
  595.5 34.4 %experts.5 = (bf16[1040,768]{1,0:T(8,128)(2,1)}, bf16[4,4,96,1536]{3,2,1,0:T(8,128)(2,1)}, bf16[4,4,96,1536]{3,2,1,0:T(8,128)(2,1)}, bf16[4,4,96,1536]{3,2,1,0:T(8,128)(2,1)}, bf16[4,4,96,1536]{3,2,1,0:T(8,128)(2,1)}) custom-call(s32[8]{0:T(128)} %iota_xor_fusion.offs_ref, bf16[1024,768]{1,0:T(8,128)(2,1)} %get-tuple-element.234.refs_0_, ...), custom_call_target="tpu_custom_call" | custom-call | flops 880000000 | bytes 2000000 | tf_op jit(solution)/shard_map/experts/pallas_call | solution.py:891
  637.7 31.9 %collective-permute-done.60 = bf16[2,96,896]{2,1,0:T(8,128)(2,1)S(1)} collective-permute-done((bf16[2,96,896]{2,1,0:T(8,128)(2,1)S(1)}, bf16[2,96,896]{2,1,0:T(8,128)(2,1)S(1)}, u32[]{:S(2)}, u32[]{:S(2)}) %collective-permute-start.60) | collective-permute-done | bytes 344096 | tf_op jit(solution)/shard_map/ppermute | solution.py:973
  673.2 9.0 %final_sums.2 = (f32[2,8,96,2,512]{4,3,2,1,0:T(2,128)}, f32[2,8,96,512]{3,2,1,0:T(8,128)}) custom-call(bf16[1,4,96,1536]{3,2,1,0:T(8,128)(2,1)} %slice.362.refs_0_, bf16[1,4,96,1536]{3,2,1,0:T(8,128)(2,1)} %slice.363.refs_1_, bf16[1,4,96,1536]{3,2,1,0:T(8,128)(2,1)} %slice.434.refs_2_, bf16[4,96,1536]{2,1,0:T(8,128)(2,1)} %copy-done.18, ...), custom_call_target="tpu_custom_call" | custom-call | flops 500000 | bytes 707788 | tf_op jit(solution)/shard_map/final_sums/pallas_call | solution.py:953
  682.2 4.5 add_convert_fusion.1
  686.7 3.7 add_convert_fusion
  690.5 14.7 %all-reduce.17.cloned.1.call-done.refs_2_ = bf16[1040,768]{1,0:T(8,128)(2,1)} async-done(((bf16[1040,768]{1,0:T(8,128)(2,1)}), bf16[1040,768]{1,0:T(8,128)(2,1)}) %all-reduce.17.cloned.1.call-update) | async-done | bytes 1597456 | tf_op jit(solution)/shard_map/psum | solution.py:1188
  709.5 11.8 %gate_backward.3 = (f32[1024,768]{1,0:T(8,128)}, bf16[1024,192]{1,0:T(8,128)(2,1)}, f32[768,192]{1,0:T(8,128)}, f32[32,768]{1,0:T(8,128)}) custom-call(f32[1024,768]{1,0:T(8,128)} %get-tuple-element.321.refs_0_, f32[1024,768]{1,0:T(8,128)} %get-tuple-element.322.refs_1_, bf16[1040,768]{1,0:T(8,128)(2,1)} %all-reduce.17.cloned.1.call-done.refs_2_, ...), custom_call_target="tpu_custom_call" | custom-call | flops 30198988 | bytes 707788 | tf_op jit(solution)/shard_map/gate_backward/pallas_call | solution.py:601
  721.2 14.5 %attend_backward.3 = (f32[1024,576]{1,0:T(8,128)}, bf16[1024,640]{1,0:T(8,128)(2,1)}) custom-call(s32[3]{0:T(128)} %pad_add_fusion.info_ref, bf16[1024,640]{1,0:T(8,128)(2,1)} %qkv_part.2.own_ref, bf16[1024,640]{1,0:T(8,128)(2,1)} %copy-done, f32[1024,8]{1,0:T(8,128)} %get-tuple-element.344.lse_ref, bf16[1024,192]{1,0:T(8,128)(2,1)} %get-tuple-element.345.gctx_ref), custom_call_target="tpu_custom_call" | custom-call | flops 402653184 | bytes 353894 | tf_op jit(solution)/shard_map/attend_backward/pallas_call | solution.py:331
  747.2 10.0 %collective-permute-done.62 = bf16[2,4,96,1536]{3,2,1,0:T(8,128)(2,1)S(1)} collective-permute-done((bf16[2,4,96,1536]{3,2,1,0:T(8,128)(2,1)}, bf16[2,4,96,1536]{3,2,1,0:T(8,128)(2,1)S(1)}, u32[]{:S(2)}, u32[]{:S(2)}) %collective-permute-start.62) | collective-permute-done | bytes 2359328 | tf_op jit(solution)/shard_map/ppermute | solution.py:973
  764.0 3.5 fusion.3
  767.4 8.0 qkv_backward.3
  785.2 30.9 %collective-permute-done.70 = bf16[2,96,896]{2,1,0:T(8,128)(2,1)} collective-permute-done((bf16[2,96,896]{2,1,0:T(8,128)(2,1)}, bf16[2,96,896]{2,1,0:T(8,128)(2,1)}, u32[]{:S(2)}, u32[]{:S(2)}) %collective-permute-start.70) | collective-permute-done | bytes 344096 | tf_op jit(solution)/shard_map/ppermute | solution.py:973
  817.9 3.6 add_convert_fusion.4
  825.0 9.0 %final_sums.3 = (f32[2,8,96,2,512]{4,3,2,1,0:T(2,128)}, f32[2,8,96,512]{3,2,1,0:T(8,128)}) custom-call(bf16[1,4,96,1536]{3,2,1,0:T(8,128)(2,1)} %slice.387.refs_0_, bf16[1,4,96,1536]{3,2,1,0:T(8,128)(2,1)} %slice.388.refs_1_, bf16[1,4,96,1536]{3,2,1,0:T(8,128)(2,1)} %slice.441.refs_2_, ...), custom_call_target="tpu_custom_call", output_to_operand_aliasing={{0}: (8, {}), {1}: (9, {})} | custom-call | flops 500000 | bytes 707788 | tf_op jit(solution)/shard_map/final_sums/pallas_call | solution.py:953
  836.0 18.0 %all-reduce.19.cloned.1.call-done.ga_ref = bf16[1024,768]{1,0:T(8,128)(2,1)} async-done(((bf16[1024,768]{1,0:T(8,128)(2,1)}), bf16[1024,768]{1,0:T(8,128)(2,1)}) %all-reduce.19.cloned.1.call-update) | async-done | bytes 1572880 | tf_op jit(solution)/shard_map/psum | solution.py:1219
  855.4 5.7 norm_backward.3
  (359 shorter events, 171.0 us)
Async XLA Ops:
  7.2 139.8 %all-gather.5.cloned.1.call-start = ((), (), s32[]{:S(2)}) async-start(), calls=%async_computation.6 | async-start | bytes 1966080 | tf_op jit(solution)/shard_map/all_gather | solution.py:1158
  8.2 21.2 %collective-permute-start.2 = (bf16[2,96,192]{2,1,0:T(8,128)(2,1)S(1)}, bf16[2,96,192]{2,1,0:T(8,128)(2,1)S(1)}, u32[]{:S(2)}, u32[]{:S(2)}) collective-permute-start(bf16[2,96,192]{2,1,0:T(8,128)(2,1)S(1)} %bitcast.145), channel_id=1, source_target_pairs={{0,3},{1,0},{2,1},{3,2},{4,7},{5,4},{6,5},{7,6},{8,11},{9,8},{10,9... | collective-permute-start | bytes 221192 | tf_op jit(solution)/shard_map/ppermute | solution.py:1089
  13.3 16.7 %collective-permute-start.1 = (bf16[2,96,192]{2,1,0:T(8,128)(2,1)S(1)}, bf16[2,96,192]{2,1,0:T(8,128)(2,1)S(1)}, u32[]{:S(2)}, u32[]{:S(2)}) collective-permute-start(bf16[2,96,192]{2,1,0:T(8,128)(2,1)S(1)} %bitcast.146), channel_id=1, source_target_pairs={{0,2},{1,3},{2,0},{3,1},{4,6},{5,7},{6,4},{7,5},{8,10},{9,11},{10,... | collective-permute-start | bytes 221192 | tf_op jit(solution)/shard_map/ppermute | solution.py:1089
  13.3 17.3 %collective-permute-start = (bf16[2,96,192]{2,1,0:T(8,128)(2,1)S(1)}, bf16[2,96,192]{2,1,0:T(8,128)(2,1)S(1)}, u32[]{:S(2)}, u32[]{:S(2)}) collective-permute-start(bf16[2,96,192]{2,1,0:T(8,128)(2,1)S(1)} %bitcast.147), channel_id=1, source_target_pairs={{0,1},{1,2},{2,3},{3,0},{4,5},{5,6},{6,7},{7,4},{8,9},{9,10},{10,1... | collective-permute-start | bytes 221192 | tf_op jit(solution)/shard_map/ppermute | solution.py:1089
  23.2 43.6 %collective-permute-start.11 = (bf16[4,96,1536]{2,1,0:T(8,128)(2,1)}, bf16[4,96,1536]{2,1,0:T(8,128)(2,1)S(1)}, u32[]{:S(2)}, u32[]{:S(2)}) collective-permute-start(bf16[4,96,1536]{2,1,0:T(8,128)(2,1)} %get-tuple-element.240.refs_3_.refs_4_), channel_id=1, source_target_pairs={{0,16},{8,24},{16,0},{24,8},{1,17},{9,25},{17,1},{25,9},{2,18},{10... | collective-permute-start | bytes 3538952 | tf_op jit(solution)/shard_map/ppermute | solution.py:973
  24.8 42.1 %collective-permute-start.10 = (bf16[4,96,1536]{2,1,0:T(8,128)(2,1)}, bf16[4,96,1536]{2,1,0:T(8,128)(2,1)S(1)}, u32[]{:S(2)}, u32[]{:S(2)}) collective-permute-start(bf16[4,96,1536]{2,1,0:T(8,128)(2,1)} %get-tuple-element.242.refs_11_.refs_12_), channel_id=1, source_target_pairs={{0,8},{8,0},{16,24},{24,16},{1,9},{9,1},{17,25},{25,17},{2,10},{10... | collective-permute-start | bytes 3538952 | tf_op jit(solution)/shard_map/ppermute | solution.py:973
  32.7 27.5 %collective-permute-start.8 = (bf16[96,1536]{1,0:T(8,128)(2,1)S(1)}, bf16[96,1536]{1,0:T(8,128)(2,1)S(1)}, u32[]{:S(2)}, u32[]{:S(2)}) collective-permute-start(bf16[96,1536]{1,0:T(8,128)(2,1)S(1)} %concatenate.20.refs_0_), channel_id=1, source_target_pairs={{0,24},{8,16},{16,8},{24,0},{1,25},{9,17},{17,9},{25,1},{2,26},{10... | collective-permute-start | bytes 884744 | tf_op jit(solution)/shard_map/ppermute | solution.py:973
  33.3 29.7 %collective-permute-start.6 = (bf16[96,1536]{1,0:T(8,128)(2,1)S(1)}, bf16[96,1536]{1,0:T(8,128)(2,1)S(1)}, u32[]{:S(2)}, u32[]{:S(2)}) collective-permute-start(bf16[96,1536]{1,0:T(8,128)(2,1)S(1)} %concatenate.20.refs_0_), channel_id=1, source_target_pairs={{0,16},{8,24},{16,0},{24,8},{1,17},{9,25},{17,1},{25,9},{2,18},{10... | collective-permute-start | bytes 884744 | tf_op jit(solution)/shard_map/ppermute | solution.py:973
  34.8 29.5 %collective-permute-start.4 = (bf16[96,1536]{1,0:T(8,128)(2,1)S(1)}, bf16[96,1536]{1,0:T(8,128)(2,1)S(1)}, u32[]{:S(2)}, u32[]{:S(2)}) collective-permute-start(bf16[96,1536]{1,0:T(8,128)(2,1)S(1)} %concatenate.20.refs_0_), channel_id=1, source_target_pairs={{0,8},{8,0},{16,24},{24,16},{1,9},{9,1},{17,25},{25,17},{2,10},{10... | collective-permute-start | bytes 884744 | tf_op jit(solution)/shard_map/ppermute | solution.py:973
  89.6 156.8 %all-reduce.9.cloned.1.call-start = ((), (), s32[]{:S(2)}) async-start(), calls=%async_computation | async-start | bytes 3145728 | tf_op jit(solution)/shard_map/psum | solution.py:1169
  90.1 28.9 %collective-permute-start.14 = (bf16[4,96,1536]{2,1,0:T(8,128)(2,1)S(1)}, bf16[4,96,1536]{2,1,0:T(8,128)(2,1)}, u32[]{:S(2)}, u32[]{:S(2)}) collective-permute-start(bf16[4,96,1536]{2,1,0:T(8,128)(2,1)S(1)} %copy-done.2), channel_id=1, source_target_pairs={{0,8},{8,0},{16,24},{24,16},{1,9},{9,1},{17,25},{25,17},{2,10},{10... | collective-permute-start | bytes 3538952 | tf_op jit(solution)/shard_map/ppermute | solution.py:973
  91.6 51.9 %collective-permute-start.17 = (bf16[4,96,1536]{2,1,0:T(8,128)(2,1)S(1)}, bf16[4,96,1536]{2,1,0:T(8,128)(2,1)}, u32[]{:S(2)}, u32[]{:S(2)}) collective-permute-start(bf16[4,96,1536]{2,1,0:T(8,128)(2,1)S(1)} %collective-permute-done.11.refs_7_.refs_8_), channel_id=1, source_target_pairs={{0,8},{8,0},{16,24},{24,16},{1,9},{9,1},{17,25},{25,17},{2,10},{10... | collective-permute-start | bytes 3538952 | tf_op jit(solution)/shard_map/ppermute | solution.py:973
  92.1 51.4 %collective-permute-start.21 = (bf16[4,96,1536]{2,1,0:T(8,128)(2,1)S(1)}, bf16[4,96,1536]{2,1,0:T(8,128)(2,1)}, u32[]{:S(2)}, u32[]{:S(2)}) collective-permute-start(bf16[4,96,1536]{2,1,0:T(8,128)(2,1)S(1)} %copy-done.3), channel_id=1, source_target_pairs={{0,16},{8,24},{16,0},{24,8},{1,17},{9,25},{17,1},{25,9},{2,18},{10... | collective-permute-start | bytes 3538952 | tf_op jit(solution)/shard_map/ppermute | solution.py:973
  95.4 50.3 %collective-permute-start.23 = (bf16[4,96,1536]{2,1,0:T(8,128)(2,1)}, bf16[4,96,1536]{2,1,0:T(8,128)(2,1)}, u32[]{:S(2)}, u32[]{:S(2)}) collective-permute-start(bf16[4,96,1536]{2,1,0:T(8,128)(2,1)} %copy-done.5), channel_id=1, source_target_pairs={{0,16},{8,24},{16,0},{24,8},{1,17},{9,25},{17,1},{25,9},{2,18},{10... | collective-permute-start | bytes 3538952 | tf_op jit(solution)/shard_map/ppermute | solution.py:973
  96.0 60.5 %collective-permute-start.20 = (bf16[4,96,1536]{2,1,0:T(8,128)(2,1)}, bf16[4,96,1536]{2,1,0:T(8,128)(2,1)}, u32[]{:S(2)}, u32[]{:S(2)}) collective-permute-start(bf16[4,96,1536]{2,1,0:T(8,128)(2,1)} %copy-done.5), channel_id=1, source_target_pairs={{0,4},{4,0},{1,5},{5,1},{2,6},{6,2},{3,7},{7,3},{8,12},{12,8},{9,1... | collective-permute-start | bytes 3538952 | tf_op jit(solution)/shard_map/ppermute | solution.py:977
  119.0 37.5 %collective-permute-start.15 = (bf16[4,96,1536]{2,1,0:T(8,128)(2,1)}, bf16[4,96,1536]{2,1,0:T(8,128)(2,1)S(1)}, u32[]{:S(2)}, u32[]{:S(2)}) collective-permute-start(bf16[4,96,1536]{2,1,0:T(8,128)(2,1)} %collective-permute-done.14.refs_5_.refs_6_), channel_id=1, source_target_pairs={{0,4},{4,0},{1,5},{5,1},{2,6},{6,2},{3,7},{7,3},{8,12},{12,8},{9,1... | collective-permute-start | bytes 3538952 | tf_op jit(solution)/shard_map/ppermute | solution.py:977
  177.2 147.0 %all-gather.7.cloned.1.call-start = ((), (), s32[]{:S(2)}) async-start(), calls=%async_computation.7 | async-start | bytes 1966080 | tf_op jit(solution)/shard_map/all_gather | solution.py:1158
  182.9 15.2 %collective-permute-start.26 = (bf16[96,1536]{1,0:T(8,128)(2,1)S(1)}, bf16[96,1536]{1,0:T(8,128)(2,1)S(1)}, u32[]{:S(2)}, u32[]{:S(2)}) collective-permute-start(bf16[96,1536]{1,0:T(8,128)(2,1)S(1)} %concatenate.22.refs_0_), channel_id=1, source_target_pairs={{0,16},{8,24},{16,0},{24,8},{1,17},{9,25},{17,1},{25,9},{2,18},{10... | collective-permute-start | bytes 884744 | tf_op jit(solution)/shard_map/ppermute | solution.py:973
  198.2 28.4 %collective-permute-start.29 = (bf16[4,96,1536]{2,1,0:T(8,128)(2,1)}, bf16[4,96,1536]{2,1,0:T(8,128)(2,1)}, u32[]{:S(2)}, u32[]{:S(2)}) collective-permute-start(bf16[4,96,1536]{2,1,0:T(8,128)(2,1)} %get-tuple-element.269.refs_4_), channel_id=1, source_target_pairs={{0,16},{8,24},{16,0},{24,8},{1,17},{9,25},{17,1},{25,9},{2,18},{10... | collective-permute-start | bytes 3538952 | tf_op jit(solution)/shard_map/ppermute | solution.py:973
  198.8 28.0 %collective-permute-start.28 = (bf16[4,96,1536]{2,1,0:T(8,128)(2,1)}, bf16[4,96,1536]{2,1,0:T(8,128)(2,1)}, u32[]{:S(2)}, u32[]{:S(2)}) collective-permute-start(bf16[4,96,1536]{2,1,0:T(8,128)(2,1)} %get-tuple-element.271.refs_12_), channel_id=1, source_target_pairs={{0,8},{8,0},{16,24},{24,16},{1,9},{9,1},{17,25},{25,17},{2,10},{10... | collective-permute-start | bytes 3538952 | tf_op jit(solution)/shard_map/ppermute | solution.py:973
  265.8 208.3 %all-reduce.11.cloned.1.call-start = ((), (), s32[]{:S(2)}) async-start(), calls=%async_computation.1 | async-start | bytes 4767744 | tf_op jit(solution)/shard_map/psum | solution.py:1188
  266.1 28.9 %collective-permute-start.36 = (bf16[4,96,1536]{2,1,0:T(8,128)(2,1)S(1)}, bf16[4,96,1536]{2,1,0:T(8,128)(2,1)}, u32[]{:S(2)}, u32[]{:S(2)}) collective-permute-start(bf16[4,96,1536]{2,1,0:T(8,128)(2,1)S(1)} %copy-done.13), channel_id=1, source_target_pairs={{0,8},{8,0},{16,24},{24,16},{1,9},{9,1},{17,25},{25,17},{2,10},{10... | collective-permute-start | bytes 3538952 | tf_op jit(solution)/shard_map/ppermute | solution.py:973
  267.5 52.1 %collective-permute-start.39 = (bf16[4,96,1536]{2,1,0:T(8,128)(2,1)}, bf16[4,96,1536]{2,1,0:T(8,128)(2,1)}, u32[]{:S(2)}, u32[]{:S(2)}) collective-permute-start(bf16[4,96,1536]{2,1,0:T(8,128)(2,1)} %collective-permute-done.29.refs_8_), channel_id=1, source_target_pairs={{0,8},{8,0},{16,24},{24,16},{1,9},{9,1},{17,25},{25,17},{2,10},{10... | collective-permute-start | bytes 3538952 | tf_op jit(solution)/shard_map/ppermute | solution.py:973
  268.5 51.2 %collective-permute-start.43 = (bf16[4,96,1536]{2,1,0:T(8,128)(2,1)}, bf16[4,96,1536]{2,1,0:T(8,128)(2,1)}, u32[]{:S(2)}, u32[]{:S(2)}) collective-permute-start(bf16[4,96,1536]{2,1,0:T(8,128)(2,1)} %get-tuple-element.271.refs_12_), channel_id=1, source_target_pairs={{0,16},{8,24},{16,0},{24,8},{1,17},{9,25},{17,1},{25,9},{2,18},{10... | collective-permute-start | bytes 3538952 | tf_op jit(solution)/shard_map/ppermute | solution.py:973
  271.6 50.5 %collective-permute-start.45 = (bf16[4,96,1536]{2,1,0:T(8,128)(2,1)}, bf16[4,96,1536]{2,1,0:T(8,128)(2,1)}, u32[]{:S(2)}, u32[]{:S(2)}) collective-permute-start(bf16[4,96,1536]{2,1,0:T(8,128)(2,1)} %collective-permute-done.28.refs_14_), channel_id=1, source_target_pairs={{0,16},{8,24},{16,0},{24,8},{1,17},{9,25},{17,1},{25,9},{2,18},{10... | collective-permute-start | bytes 3538952 | tf_op jit(solution)/shard_map/ppermute | solution.py:973
  273.1 61.4 %collective-permute-start.42 = (bf16[4,96,1536]{2,1,0:T(8,128)(2,1)}, bf16[4,96,1536]{2,1,0:T(8,128)(2,1)}, u32[]{:S(2)}, u32[]{:S(2)}) collective-permute-start(bf16[4,96,1536]{2,1,0:T(8,128)(2,1)} %collective-permute-done.28.refs_14_), channel_id=1, source_target_pairs={{0,4},{4,0},{1,5},{5,1},{2,6},{6,2},{3,7},{7,3},{8,12},{12,8},{9,1... | collective-permute-start | bytes 3538952 | tf_op jit(solution)/shard_map/ppermute | solution.py:977
  295.0 39.6 %collective-permute-start.37 = (bf16[4,96,1536]{2,1,0:T(8,128)(2,1)}, bf16[4,96,1536]{2,1,0:T(8,128)(2,1)S(1)}, u32[]{:S(2)}, u32[]{:S(2)}) collective-permute-start(bf16[4,96,1536]{2,1,0:T(8,128)(2,1)} %collective-permute-done.36.refs_6_), channel_id=1, source_target_pairs={{0,4},{4,0},{1,5},{5,1},{2,6},{6,2},{3,7},{7,3},{8,12},{12,8},{9,1... | collective-permute-start | bytes 3538952 | tf_op jit(solution)/shard_map/ppermute | solution.py:977
  319.7 14.8 %collective-permute-start.40 = (bf16[4,96,1536]{2,1,0:T(8,128)(2,1)}, bf16[4,96,1536]{2,1,0:T(8,128)(2,1)}, u32[]{:S(2)}, u32[]{:S(2)}) collective-permute-start(bf16[4,96,1536]{2,1,0:T(8,128)(2,1)} %collective-permute-done.39.refs_10_), channel_id=1, source_target_pairs={{0,4},{4,0},{1,5},{5,1},{2,6},{6,2},{3,7},{7,3},{8,12},{12,8},{9,1... | collective-permute-start | bytes 3538952 | tf_op jit(solution)/shard_map/ppermute | solution.py:977
  319.7 14.9 %collective-permute-start.44 = (bf16[4,96,1536]{2,1,0:T(8,128)(2,1)}, bf16[4,96,1536]{2,1,0:T(8,128)(2,1)}, u32[]{:S(2)}, u32[]{:S(2)}) collective-permute-start(bf16[4,96,1536]{2,1,0:T(8,128)(2,1)} %collective-permute-done.43.refs_16_), channel_id=1, source_target_pairs={{0,4},{4,0},{1,5},{5,1},{2,6},{6,2},{3,7},{7,3},{8,12},{12,8},{9,1... | collective-permute-start | bytes 3538952 | tf_op jit(solution)/shard_map/ppermute | solution.py:977
  378.3 209.2 %all-reduce.13.cloned.1.call-start = ((), (), s32[]{:S(2)}) async-start(), calls=%async_computation.2 | async-start | bytes 3145728 | tf_op jit(solution)/shard_map/psum | solution.py:1219
  474.1 59.8 %collective-permute-start.50 = (bf16[2,4,96,1536]{3,2,1,0:T(8,128)(2,1)S(1)}, bf16[2,4,96,1536]{3,2,1,0:T(8,128)(2,1)}, u32[]{:S(2)}, u32[]{:S(2)}) collective-permute-start(bf16[2,4,96,1536]{3,2,1,0:T(8,128)(2,1)S(1)} %add_convert_fusion.3), channel_id=1, source_target_pairs={{0,8},{8,0},{16,24},{24,16},{1,9},{9,1},{17,25},{25,17},{2,10},{10... | collective-permute-start | bytes 7077896 | tf_op jit(solution)/shard_map/ppermute | solution.py:973
  475.6 60.8 %collective-permute-start.51 = (bf16[2,4,96,1536]{3,2,1,0:T(8,128)(2,1)}, bf16[2,4,96,1536]{3,2,1,0:T(8,128)(2,1)}, u32[]{:S(2)}, u32[]{:S(2)}) collective-permute-start(bf16[2,4,96,1536]{3,2,1,0:T(8,128)(2,1)} %add_convert_fusion.2), channel_id=1, source_target_pairs={{0,16},{8,24},{16,0},{24,8},{1,17},{9,25},{17,1},{25,9},{2,18},{10... | collective-permute-start | bytes 7077896 | tf_op jit(solution)/shard_map/ppermute | solution.py:973
  520.9 111.5 %all-reduce.15.cloned.1.call-start = ((), (), s32[]{:S(2)}) async-start(), calls=%async_computation.3 | async-start | bytes 1572864 | tf_op jit(solution)/shard_map/psum | solution.py:1185
  587.5 117.7 %all-reduce.17.cloned.1.call-start = ((), (), s32[]{:S(2)}) async-start(), calls=%async_computation.4 | async-start | bytes 3194880 | tf_op jit(solution)/shard_map/psum | solution.py:1188
  587.5 42.3 %collective-permute-start.55 = (f32[16,16]{1,0:T(8,128)S(1)}, f32[16,16]{1,0:T(8,128)S(1)}, u32[]{:S(2)}, u32[]{:S(2)}) collective-permute-start(f32[16,16]{1,0:T(8,128)S(1)} %add.163), channel_id=1, source_target_pairs={{0,16},{8,24},{16,0},{24,8},{1,17},{9,25},{17,1},{25,9},{2,18},{10... | collective-permute-start | bytes 3080 | tf_op jit(solution)/shard_map/ppermute | solution.py:973
  632.4 49.8 %collective-permute-start.56 = (bf16[4,4,96,1536]{3,2,1,0:T(8,128)(2,1)}, bf16[4,4,96,1536]{3,2,1,0:T(8,128)(2,1)}, u32[]{:S(2)}, u32[]{:S(2)}) collective-permute-start(bf16[4,4,96,1536]{3,2,1,0:T(8,128)(2,1)} %get-tuple-element.325), channel_id=1, source_target_pairs={{0,4},{4,0},{1,5},{5,1},{2,6},{6,2},{3,7},{7,3},{8,12},{12,8},{9,1... | collective-permute-start | bytes 14155784 | tf_op jit(solution)/shard_map/ppermute | solution.py:977
  632.4 54.3 %collective-permute-start.57 = (bf16[4,4,96,1536]{3,2,1,0:T(8,128)(2,1)}, bf16[4,4,96,1536]{3,2,1,0:T(8,128)(2,1)}, u32[]{:S(2)}, u32[]{:S(2)}) collective-permute-start(bf16[4,4,96,1536]{3,2,1,0:T(8,128)(2,1)} %get-tuple-element.327), channel_id=1, source_target_pairs={{0,4},{4,0},{1,5},{5,1},{2,6},{6,2},{3,7},{7,3},{8,12},{12,8},{9,1... | collective-permute-start | bytes 14155784 | tf_op jit(solution)/shard_map/ppermute | solution.py:977
  632.9 39.3 %collective-permute-start.58 = (bf16[4,96,1536]{2,1,0:T(8,128)(2,1)}, bf16[4,96,1536]{2,1,0:T(8,128)(2,1)S(1)}, u32[]{:S(2)}, u32[]{:S(2)}) collective-permute-start(bf16[4,96,1536]{2,1,0:T(8,128)(2,1)} %fusion), channel_id=1, source_target_pairs={{0,16},{8,24},{16,0},{24,8},{1,17},{9,25},{17,1},{25,9},{2,18},{10... | collective-permute-start | bytes 3538952 | tf_op jit(solution)/shard_map/ppermute | solution.py:973
  634.4 37.8 %collective-permute-start.59 = (bf16[4,96,1536]{2,1,0:T(8,128)(2,1)}, bf16[4,96,1536]{2,1,0:T(8,128)(2,1)}, u32[]{:S(2)}, u32[]{:S(2)}) collective-permute-start(bf16[4,96,1536]{2,1,0:T(8,128)(2,1)} %fusion.1), channel_id=1, source_target_pairs={{0,8},{8,0},{16,24},{24,16},{1,9},{9,1},{17,25},{25,17},{2,10},{10... | collective-permute-start | bytes 3538952 | tf_op jit(solution)/shard_map/ppermute | solution.py:973
  635.9 33.7 %collective-permute-start.60 = (bf16[2,96,896]{2,1,0:T(8,128)(2,1)S(1)}, bf16[2,96,896]{2,1,0:T(8,128)(2,1)S(1)}, u32[]{:S(2)}, u32[]{:S(2)}) collective-permute-start(bf16[2,96,896]{2,1,0:T(8,128)(2,1)S(1)} %copy-done.25), channel_id=1, source_target_pairs={{0,8},{8,0},{16,24},{24,16},{1,9},{9,1},{17,25},{25,17},{2,10},{10... | collective-permute-start | bytes 1032200 | tf_op jit(solution)/shard_map/ppermute | solution.py:973
  636.4 217.6 %all-reduce.19.cloned.1.call-start = ((), (), s32[]{:S(2)}) async-start(), calls=%async_computation.5 | async-start | bytes 3145728 | tf_op jit(solution)/shard_map/psum | solution.py:1219
  705.2 52.0 %collective-permute-start.62 = (bf16[2,4,96,1536]{3,2,1,0:T(8,128)(2,1)}, bf16[2,4,96,1536]{3,2,1,0:T(8,128)(2,1)S(1)}, u32[]{:S(2)}, u32[]{:S(2)}) collective-permute-start(bf16[2,4,96,1536]{3,2,1,0:T(8,128)(2,1)} %add_convert_fusion.1), channel_id=1, source_target_pairs={{0,8},{8,0},{16,24},{24,16},{1,9},{9,1},{17,25},{25,17},{2,10},{10... | collective-permute-start | bytes 7077896 | tf_op jit(solution)/shard_map/ppermute | solution.py:973
  706.7 51.8 %collective-permute-start.63 = (bf16[2,4,96,1536]{3,2,1,0:T(8,128)(2,1)}, bf16[2,4,96,1536]{3,2,1,0:T(8,128)(2,1)}, u32[]{:S(2)}, u32[]{:S(2)}) collective-permute-start(bf16[2,4,96,1536]{3,2,1,0:T(8,128)(2,1)} %add_convert_fusion), channel_id=1, source_target_pairs={{0,16},{8,24},{16,0},{24,8},{1,17},{9,25},{17,1},{25,9},{2,18},{10... | collective-permute-start | bytes 7077896 | tf_op jit(solution)/shard_map/ppermute | solution.py:973
  735.7 31.8 %collective-permute-start.61 = (bf16[1024,640]{1,0:T(8,128)(2,1)}, bf16[1024,640]{1,0:T(8,128)(2,1)}, u32[]{:S(2)}, u32[]{:S(2)}) collective-permute-start(bf16[1024,640]{1,0:T(8,128)(2,1)} %get-tuple-element.347), channel_id=1, source_target_pairs={{0,4},{4,0},{1,5},{5,1},{2,6},{6,2},{3,7},{7,3},{8,12},{12,8},{9,1... | collective-permute-start | bytes 3932168 | tf_op jit(solution)/shard_map/ppermute | solution.py:977
  778.8 44.1 %collective-permute-start.72 = (bf16[4,96,1536]{2,1,0:T(8,128)(2,1)}, bf16[4,96,1536]{2,1,0:T(8,128)(2,1)S(1)}, u32[]{:S(2)}, u32[]{:S(2)}) collective-permute-start(bf16[4,96,1536]{2,1,0:T(8,128)(2,1)} %fusion.2), channel_id=1, source_target_pairs={{0,16},{8,24},{16,0},{24,8},{1,17},{9,25},{17,1},{25,9},{2,18},{10... | collective-permute-start | bytes 3538952 | tf_op jit(solution)/shard_map/ppermute | solution.py:973
  780.3 42.6 %collective-permute-start.73 = (bf16[4,96,1536]{2,1,0:T(8,128)(2,1)}, bf16[4,96,1536]{2,1,0:T(8,128)(2,1)S(1)}, u32[]{:S(2)}, u32[]{:S(2)}) collective-permute-start(bf16[4,96,1536]{2,1,0:T(8,128)(2,1)} %fusion.3), channel_id=1, source_target_pairs={{0,8},{8,0},{16,24},{24,16},{1,9},{9,1},{17,25},{25,17},{2,10},{10... | collective-permute-start | bytes 3538952 | tf_op jit(solution)/shard_map/ppermute | solution.py:973
  784.3 31.8 %collective-permute-start.70 = (bf16[2,96,896]{2,1,0:T(8,128)(2,1)}, bf16[2,96,896]{2,1,0:T(8,128)(2,1)}, u32[]{:S(2)}, u32[]{:S(2)}) collective-permute-start(bf16[2,96,896]{2,1,0:T(8,128)(2,1)} %add_convert_fusion.9), channel_id=1, source_target_pairs={{0,8},{8,0},{16,24},{24,16},{1,9},{9,1},{17,25},{25,17},{2,10},{10... | collective-permute-start | bytes 1032200 | tf_op jit(solution)/shard_map/ppermute | solution.py:973
  817.2 16.8 %collective-permute-start.71 = (bf16[96,896]{1,0:T(8,128)(2,1)S(1)}, bf16[96,896]{1,0:T(8,128)(2,1)S(1)}, u32[]{:S(2)}, u32[]{:S(2)}) collective-permute-start(bf16[96,896]{1,0:T(8,128)(2,1)S(1)} %fusion.5), channel_id=1, source_target_pairs={{0,16},{8,24},{16,0},{24,8},{1,17},{9,25},{17,1},{25,9},{2,18},{10... | collective-permute-start | bytes 516104 | tf_op jit(solution)/shard_map/ppermute | solution.py:973
  (88 other events, 918.3 us)
Sparse Core Ops, SparseCore 0:
  89.7 36.9 all-gather.4
  177.3 69.0 all-reduce.8
  265.9 36.1 all-gather.6
  378.4 95.6 all-reduce.10
  521.0 66.3 all-reduce.12
  589.7 42.6 all-reduce.14
  636.6 68.5 all-reduce.16
  785.3 68.6 all-reduce.18

commit v3 on v2

--- a/solution.py
+++ b/solution.py
@@ -18,11 +18,10 @@
 F32 = jnp.float32
 BF16 = jnp.bfloat16
 HIGH = lax.Precision.HIGHEST
-ROW_CONST, ROW_VEC, ROW_GA, ROW_GM, ROW_UP = 16, 20, 22, 23, 24
+ROW_CONST, ROW_VEC, ROW_GA, ROW_GM = 16, 20, 22, 23
 VMEM_LIMIT = 58 * 1024 * 1024
 SCALE = 0.05
 PACK = 128
-LATE = 512
 
 NN = (((1,), (0,)), ((), ()))
 NT = (((1,), (1,)), ((), ()))
@@ -67,47 +66,61 @@
     return -(-value // unit) * unit
 
 
-def prep_kernel(count, rows, offs_ref, *refs):
-    qkv_ref, wo_ref, vec_ref, scr_ref = refs[count:]
-    cols, out_cols = qkv_ref.shape[1], wo_ref.shape[2]
+def prep_kernel(count, rows, out_cols, offs_ref, *refs):
+    qkv_ref, vec_ref, wo_refs = refs[count], refs[count + 1], refs[count + 2 : -2]
+    scr_ref, wo_scr = refs[-2:]
+    cols = qkv_ref.shape[1]
     for piece in range(count):
         start = pl.multiple_of(offs_ref[piece] * rows, rows)
         block = refs[piece][...]
         qkv_ref[pl.ds(start, rows), :] = block[:, :cols]
         scr_ref[pl.ds(start, rows), :] = block[:, cols : cols + PACK].astype(F32)
-        for rank in range(wo_ref.shape[0]):
+        for rank in range(len(wo_refs)):
             first = cols + PACK + rank * out_cols
-            wo_ref[rank, pl.ds(start, rows), :] = block[:, first : first + out_cols]
+            wo_scr[rank, pl.ds(start, rows), :out_cols] = block[:, first : first + out_cols]
     vec_ref[...] = scr_ref[...].T[:32]
-
-
-def prep_weights(pieces, offs, feature_dim, qkv_cols, tp_count):
+    total = wo_scr.shape[1]
+    rest = out_cols - 128
+    for rank, ref in enumerate(wo_refs):
+        ref[:total, :] = wo_scr[rank, :, :128]
+        ref[total:, :rest] = wo_scr[rank, : total // 2, 128:out_cols]
+        ref[total:, rest:] = wo_scr[rank, total // 2 :, 128:out_cols]
+
+
+def prep_weights(pieces, offs, feature_dim, qkv_cols, out_cols, out_count):
     count = len(pieces)
     cols = round_up(qkv_cols, 128)
-    out_cols = (pieces[0].shape[1] - cols - PACK) // tp_count
     vmem = pl.BlockSpec(memory_space=pltpu.VMEM)
-    return pl.pallas_call(
-        functools.partial(prep_kernel, count, feature_dim // count),
-        out_shape=(
-            jax.ShapeDtypeStruct((feature_dim, cols), BF16),
-            jax.ShapeDtypeStruct((tp_count, feature_dim, out_cols), BF16),
-            jax.ShapeDtypeStruct((32, feature_dim), F32),
+    outs = pl.pallas_call(
+        functools.partial(prep_kernel, count, feature_dim // count, out_cols),
+        out_shape=tuple(
+            [
+                jax.ShapeDtypeStruct((feature_dim, cols), BF16),
+                jax.ShapeDtypeStruct((32, feature_dim), F32),
+            ]
+            + [jax.ShapeDtypeStruct((feature_dim * 3 // 2, 128), BF16)] * out_count
         ),
         in_specs=[SMEM_SPEC] + [vmem] * count,
-        out_specs=(vmem, vmem, vmem),
-        scratch_shapes=[pltpu.VMEM((feature_dim, PACK), F32)],
+        out_specs=tuple([vmem] * (2 + out_count)),
+        scratch_shapes=[
+            pltpu.VMEM((feature_dim, PACK), F32),
+            pltpu.VMEM((out_count, feature_dim, 256), BF16),
+        ],
         compiler_params=kernel_params(),
         cost_estimate=cost(1e6, 3e6),
         name="prep",
     )(offs, *pieces)
-
-
-def pack_kernel(count, rows, offs_ref, dqkv_ref, dwo_ref, dvec_ref, *refs):
+    return outs[0], outs[1], list(outs[2:])
+
+
+def pack_kernel(count, rows, offs_ref, dqkv_ref, dwo_ref, dvec_ref, dgain_ref, *refs):
     outs, scr_ref = refs[:-1], refs[-1]
     cols, out_cols = dqkv_ref.shape[1], dwo_ref.shape[1]
     scr_ref[:, :cols] = dqkv_ref[...]
     scr_ref[:, cols : cols + out_cols] = dwo_ref[...]
-    wide = jnp.concatenate([dvec_ref[...], jnp.zeros((96, dvec_ref.shape[1]), F32)], axis=0).T
+    vec = dvec_ref[...]
+    vec = jnp.where(iota(vec.shape, 0) == ROW_GA, dgain_ref[0:1, :], vec)
+    wide = jnp.concatenate([vec, jnp.zeros((PACK - vec.shape[0], vec.shape[1]), F32)], axis=0).T
     scr_ref[:, cols + out_cols :] = wide
     for piece in range(count):
         start = pl.multiple_of(offs_ref[piece] * rows, rows)
@@ -118,7 +131,7 @@
             outs[0][...] = block
 
 
-def pack_grads(dqkv, dwo, dvec, offs):
+def pack_grads(dqkv, dwo, dvec, dgain, offs):
     feature_dim = dqkv.shape[0]
     count = offs.shape[0]
     rows = feature_dim // count
@@ -129,13 +142,13 @@
     return pl.pallas_call(
         functools.partial(pack_kernel, count, rows),
         out_shape=tuple([jax.ShapeDtypeStruct(shape, BF16)] * outs),
-        in_specs=[SMEM_SPEC, vmem, vmem, vmem],
+        in_specs=[SMEM_SPEC, vmem, vmem, vmem, vmem],
         out_specs=tuple([vmem] * outs),
         scratch_shapes=[pltpu.VMEM((feature_dim, width), F32)],
         compiler_params=kernel_params(),
         cost_estimate=cost(1e6, 6e6),
         name="pack_grads",
-    )(offs, dqkv, dwo, dvec)
+    )(offs, dqkv, dwo, dvec, dgain)
 
 
 def pack_wide_kernel(gu_ref, down_ref, low_ref, high_ref):
@@ -392,18 +405,24 @@
 
 
 def middle_kernel(with_prev, rank_ref, *refs):
+    h_ref, ctx_ref, refs = refs[0], refs[1], refs[2:]
+    count = ctx_ref.shape[0]
+    wo_refs, refs = refs[:count], refs[count:]
     if with_prev:
-        h_ref, ctx_ref, wo_ref, vec_ref, route_ref, prev_ref, resid_ref = refs[:7]
-        refs = refs[7:]
+        vec_ref, route_ref, prev_ref, resid_ref = refs[:4]
+        refs = refs[4:]
     else:
-        h_ref, ctx_ref, wo_ref, vec_ref, route_ref = refs[:5]
-        refs = refs[5:]
+        vec_ref, route_ref = refs[:2]
+        refs = refs[2:]
     mid_ref, base_ref, xm_ref, gate_ref, logit_ref = refs
-    count = ctx_ref.shape[0]
-    attn_out = mm(unpack_context(ctx_ref[rank_ref[0]]), wo_ref[0], NT)
-    for back in range(1, count):
-        owner = lax.rem(rank_ref[0] + count - back, count)
-        attn_out += mm(unpack_context(ctx_ref[owner]), wo_ref[back], NT)
+    attn_out = 0.0
+    for back, ref in enumerate(wo_refs):
+        context = unpack_context(ctx_ref[lax.rem(rank_ref[0] + count - back, count)])
+        total = ref.shape[0] * 2 // 3
+        rest = context[:, 128:]
+        attn_out += mm(context[:, :128], ref[:total], NT) + jnp.concatenate(
+            [mm(rest, ref[total:, :HD], NT), mm(rest, ref[total:, HD:], NT)], axis=1
+        )
     middle = h_ref[...].astype(F32) + attn_out
     mid_ref[...] = middle
     vecs = vec_ref[...]
@@ -441,12 +460,12 @@
     row_spec = pl.BlockSpec((TILE, feature_dim), lambda i: (i, 0))
     lane8 = pl.BlockSpec((8, TILE), lambda i: (0, i))
     lane16 = pl.BlockSpec((16, TILE), lambda i: (0, i))
-    ins = [rank, h, ctx_all, wo_all, vecs, routes_t]
+    ins = [rank, h, ctx_all, *wo_all, vecs, routes_t]
     in_specs = [
         SMEM_SPEC,
         row_spec,
         pl.BlockSpec((tp_count, packed, lanes), lambda i: (0, i // 2, 0)),
-        full_spec(wo_all.shape),
+        *[full_spec(item.shape) for item in wo_all],
         full_spec(vecs.shape),
         lane8,
     ]
@@ -541,7 +560,12 @@
     grad_mid = grad + scale * (weighted - unit * mean)
     gmid_ref[...] = grad_mid
     low_mid = grad_mid.astype(BF16)
-    gctx_ref[...] = mm(low_mid, wo_ref[...]).astype(BF16)
+    total = low_mid.shape[1]
+    gctx_ref[:, :128] = mm(low_mid, wo_ref[:total]).astype(BF16)
+    gctx_ref[:, 128:] = (
+        mm(low_mid[:, : total // 2], wo_ref[total:, :HD])
+        + mm(low_mid[:, total // 2 :], wo_ref[total:, HD:])
+    ).astype(BF16)
     dwo = mm(low_mid, unpack_context(ctx_ref[...]), TN)
     vec_rows = pad_rows([(ROW_VEC - 16 + j, on_vec[j]) for j in range(2)], 16, TILE)
     vec_hi, vec_lo = split(vec_rows)
@@ -575,16 +599,16 @@
             dres_ref[...] += dres
 
 
-def gate_backward(grad, middle, gxm, vecs, routes_t, gates_t, gg_t, context, wo_all, extra):
+def gate_backward(grad, middle, gxm, vecs, routes_t, gates_t, gg_t, context, wo_own, extra):
     rows, feature_dim = middle.shape
-    out_cols = wo_all.shape[2]
+    out_cols = context.shape[0] * BLOCK // rows // TILE * HD
     with_prev = len(extra) == 2
     row_spec = pl.BlockSpec((TILE, feature_dim), lambda i: (i, 0))
     lane8 = pl.BlockSpec((8, TILE), lambda i: (0, i))
     lane16 = pl.BlockSpec((16, TILE), lambda i: (0, i))
     ctx_spec = pl.BlockSpec((context.shape[0] * BLOCK // rows, 2 * HD), lambda i: (i // 2, 0))
     out_spec = pl.BlockSpec((TILE, out_cols), lambda i: (i, 0))
-    wo_spec = pl.BlockSpec((pl.Squeezed(), feature_dim, out_cols), lambda i: (0, 0, 0))
+    wo_spec = full_spec(wo_own.shape)
     in_specs = [row_spec, row_spec, row_spec, full_spec(vecs.shape), lane8, lane8, lane8]
     in_specs += [ctx_spec, wo_spec, lane16]
     out_shape = [
@@ -607,27 +631,32 @@
         compiler_params=kernel_params(),
         cost_estimate=cost(4 * rows * feature_dim * out_cols, rows * feature_dim * 18),
         name="gate_backward",
-    )(grad, middle, gxm, vecs, routes_t, gates_t, gg_t, context, wo_all, *extra)
-
-
-def qkv_bwd_kernel(gown_ref, goth_ref, h_ref, vec_ref, w_ref, part_ref, dw_ref):
+    )(grad, middle, gxm, vecs, routes_t, gates_t, gg_t, context, wo_own, *extra)
+
+
+def qkv_bwd_kernel(gown_ref, goth_ref, h_ref, vec_ref, w_ref, part_ref, dw_ref, dgain_ref):
     step = pl.program_id(0)
     cols = gown_ref.shape[1]
     grad = (gown_ref[...] + goth_ref[:, :cols].astype(F32)).astype(BF16)
-    part_ref[...] = mm(grad, w_ref[:, :cols], NT).astype(BF16)
+    part = mm(grad, w_ref[:, :cols], NT)
+    part_ref[...] = part.astype(BF16)
     hidden = h_ref[...].astype(F32)
     gain = vec_ref[ROW_GA : ROW_GA + 1, :]
     scale = lax.rsqrt(jnp.mean(hidden * hidden, axis=-1, keepdims=True) + EPSILON)
-    attn_in = (hidden * scale * gain).astype(BF16)
+    unit = hidden * scale
+    attn_in = (unit * gain).astype(BF16)
     dw = mm(attn_in, grad, TN)
+    dgain = jnp.broadcast_to(jnp.sum(part * unit, axis=0, keepdims=True), dgain_ref.shape)
 
     @pl.when(step == 0)
     def _():
         dw_ref[...] = dw
+        dgain_ref[...] = dgain
 
     @pl.when(step > 0)
     def _():
         dw_ref[...] += dw
+        dgain_ref[...] += dgain
 
 
 def qkv_backward(gown, goth, h, vecs, w_qkv):
@@ -642,9 +671,10 @@
         out_shape=(
             jax.ShapeDtypeStruct((rows, feature_dim), BF16),
             jax.ShapeDtypeStruct((feature_dim, cols), F32),
+            jax.ShapeDtypeStruct((8, feature_dim), F32),
         ),
         in_specs=[col_spec, oth_spec, row_spec, full_spec(vecs.shape), full_spec(w_qkv.shape)],
-        out_specs=(row_spec, full_spec((feature_dim, cols))),
+        out_specs=(row_spec, full_spec((feature_dim, cols)), full_spec((8, feature_dim))),
         compiler_params=kernel_params(),
         cost_estimate=cost(4 * rows * feature_dim * cols, rows * feature_dim * 10),
         name="qkv_backward",
@@ -652,7 +682,6 @@
 
 
 def norm_bwd_kernel(with_low, gmid_ref, ga_ref, h_ref, vec_ref, out_ref, *rest):
-    step = pl.program_id(0)
     hidden = h_ref[...].astype(F32)
     gain = vec_ref[ROW_GA : ROW_GA + 1, :]
     scale = lax.rsqrt(jnp.mean(hidden * hidden, axis=-1, keepdims=True) + EPSILON)
@@ -664,16 +693,6 @@
     out_ref[...] = grad
     if with_low:
         rest[0][...] = grad.astype(BF16)
-    dgain_ref = rest[-1]
-    dgain = jnp.broadcast_to(jnp.sum(grad_y * unit, axis=0, keepdims=True), dgain_ref.shape)
-
-    @pl.when(step == 0)
-    def _():
-        dgain_ref[...] = dgain
-
-    @pl.when(step > 0)
-    def _():
-        dgain_ref[...] += dgain
 
 
 def norm_backward(gmid, ga, h, vecs, with_low):
@@ -684,8 +703,6 @@
     if with_low:
         out_shape.append(jax.ShapeDtypeStruct((rows, feature_dim), BF16))
         out_specs.append(row_spec)
-    out_shape.append(jax.ShapeDtypeStruct((8, feature_dim), F32))
-    out_specs.append(full_spec((8, feature_dim)))
     return pl.pallas_call(
         functools.partial(norm_bwd_kernel, with_low),
         grid=(rows // TILE,),
@@ -708,10 +725,10 @@
     if bwd:
         gx_ref = refs.pop(0)
         dw_refs = [refs.pop(0) for _ in range(out_count)]
-    w_scr, place_scr, pick_scr = refs.pop(0), refs.pop(0), refs.pop(0)
-    acc_ref = refs.pop(0) if fwd else None
+    w_scr, hot_scr, pick_scr = refs.pop(0), refs.pop(0), refs.pop(0)
+    part_scr = refs.pop(0) if fwd else None
     if bwd:
-        gacc_ref, raw_scr, gg_scr, dw_scr = refs
+        gpart_scr, raw_scr, gg_scr, dw_scr = refs
     expert = pl.program_id(0)
     last = pl.num_programs(0) - 1
     width = w_scr.shape[1]
@@ -720,17 +737,28 @@
     @pl.when(expert == 0)
     def _():
         order = (iota((BLOCK, BLOCK), 0) < iota((BLOCK, BLOCK), 1)).astype(BF16)
+        ids = iota((NF, BLOCK), 0)
+        row_ids = iota((CAP, BLOCK), 0).astype(F32)
         for block in range(blocks):
             lanes = slice(block * BLOCK, (block + 1) * BLOCK)
-            ids = iota((8, BLOCK), 0)
             hits = (ids == route_ref[0:1, lanes]) | (ids == route_ref[1:2, lanes])
-            earlier = mm(hits.astype(BF16), order)
-            place_scr[block] = jnp.where(hits, earlier, -1.0)
-        if fwd:
-            acc_ref[...] = jnp.zeros_like(acc_ref)
+            place = jnp.where(hits, mm(hits.astype(BF16), order), -1.0)
+            for each in range(NF):
+                hot_scr[block, each * CAP : (each + 1) * CAP, :] = (
+                    (row_ids == place[each : each + 1]).astype(F32).astype(BF16)
+                )
+            hot = hot_scr[block]
+            for source, target in ((xm_ref, pick_scr),) + (((gh_ref, raw_scr),) if bwd else ()):
+                rows_all = mm(hot, source[lanes, :]).astype(BF16)
+                for each in range(NF):
+                    target[each, block * CAP : (block + 1) * CAP, :] = rows_all[
+                        each * CAP : (each + 1) * CAP
+                    ]
         if bwd:
-            gacc_ref[...] = jnp.zeros_like(gacc_ref)
             gg_scr[...] = jnp.zeros_like(gg_scr)
+
+    def combine(source, block):
+        return mm(hot_scr[block], source[block], TN)
 
     def fill(ref, off):
         start = pl.multiple_of(offs_ref[off] * rows, rows)
@@ -745,23 +773,19 @@
             )
 
     hot, gate_cols, masks = [], [], []
+    first_row = pl.multiple_of(expert * CAP, CAP)
     for block in range(blocks):
         lanes = slice(block * BLOCK, (block + 1) * BLOCK)
-        place = place_scr[block, pl.ds(expert, 1), :]
-        one_hot = (iota((CAP, BLOCK), 0).astype(F32) == place).astype(F32)
+        one_hot = hot_scr[block, pl.ds(first_row, CAP), :].astype(F32)
         mask = [route_ref[slot : slot + 1, lanes] == expert for slot in range(2)]
         gate_row = jnp.where(mask[0], gate_ref[0:1, lanes], 0.0) + jnp.where(
             mask[1], gate_ref[1:2, lanes], 0.0
         )
         gate_cols.append(jnp.sum(one_hot * gate_row, axis=1, keepdims=True))
-        one_hot = one_hot.astype(BF16)
-        pick_scr[block * CAP : (block + 1) * CAP, :] = mm(one_hot, xm_ref[lanes, :]).astype(BF16)
-        if bwd:
-            raw_scr[block * CAP : (block + 1) * CAP, :] = mm(one_hot, gh_ref[lanes, :]).astype(BF16)
         hot.append(one_hot)
         masks.append(mask)
     gate_col = jnp.concatenate(gate_cols, axis=0)
-    picked = pick_scr[...]
+    picked = pick_scr[expert]
     gate_up = mm(picked, w_scr[:, : 2 * units])
     gate_in, up_in = gate_up[:, :units], gate_up[:, units:]
     sigmoid = lax.logistic(gate_in)
@@ -770,27 +794,22 @@
     if fwd:
         scaled = (mm(hidden, w_scr[:, 2 * units :], NT) * gate_col).astype(BF16)
         for block in range(blocks):
-            acc_ref[block * BLOCK : (block + 1) * BLOCK, :] += mm(
-                hot[block], scaled[block * CAP : (block + 1) * CAP], TN
-            )
+            part_scr[block, pl.ds(first_row, CAP), :] = scaled[block * CAP : (block + 1) * CAP]
 
         @pl.when(expert == last)
         def _():
-            if bwd:
-                late_rows = ffn_ref.shape[0]
-                ffn_ref[...] = acc_ref[acc_ref.shape[0] - late_rows :, :].astype(BF16)
-                rest = acc_ref.shape[0] - late_rows
-                gx_ref[gx_ref.shape[0] - rest :, :] = acc_ref[:rest, :].astype(BF16)
-            else:
-                ffn_ref[...] = acc_ref[...].astype(BF16)
+            for block in range(blocks):
+                ffn_ref[block * BLOCK : (block + 1) * BLOCK, :] = combine(part_scr, block).astype(
+                    BF16
+                )
 
     if bwd:
-        raw = raw_scr[...]
+        raw = raw_scr[expert]
         grad_raw = mm(raw, w_scr[:, 2 * units :])
         gate_dot = jnp.sum(hidden.astype(F32) * grad_raw, axis=1, keepdims=True)
         for block in range(blocks):
             row = jnp.sum(
-                hot[block].astype(F32) * gate_dot[block * CAP : (block + 1) * CAP],
+                hot[block] * gate_dot[block * CAP : (block + 1) * CAP],
                 axis=0,
                 keepdims=True,
             )
@@ -804,9 +823,7 @@
         grad_gu = jnp.concatenate([grad_gate.astype(BF16), grad_up.astype(BF16)], axis=1)
         grad_pick = mm(grad_gu, w_scr[:, : 2 * units], NT).astype(BF16)
         for block in range(blocks):
-            gacc_ref[block * BLOCK : (block + 1) * BLOCK, :] += mm(
-                hot[block], grad_pick[block * CAP : (block + 1) * CAP], TN
-            )
+            gpart_scr[block, pl.ds(first_row, CAP), :] = grad_pick[block * CAP : (block + 1) * CAP]
         grad_result = (raw.astype(F32) * gate_col).astype(BF16)
         if out_count == 1:
             dw_refs[0][0, :, : 2 * units] = mm(picked, grad_gu, TN).astype(BF16)
@@ -826,7 +843,10 @@
         @pl.when(expert == last)
         def _():
             total = blocks * BLOCK
-            gx_ref[:total, :] = gacc_ref[...].astype(BF16)
+            for block in range(blocks):
+                gx_ref[block * BLOCK : (block + 1) * BLOCK, :] = combine(gpart_scr, block).astype(
+                    BF16
+                )
             gx_ref[total : total + 16, :] = jnp.zeros((16, gx_ref.shape[1]), BF16)
             gx_ref[total : total + gg_scr.shape[0], :BLOCK] = gg_scr[...].astype(BF16)
 
@@ -853,21 +873,19 @@
     out_shape, out_specs, scratch = [], [], []
     scratch += [
         pltpu.VMEM((feature_dim, width), BF16),
-        pltpu.VMEM((blocks, 8, BLOCK), F32),
-        pltpu.VMEM((blocks * CAP, feature_dim), BF16),
+        pltpu.VMEM((blocks, NF * CAP, BLOCK), BF16),
+        pltpu.VMEM((NF, blocks * CAP, feature_dim), BF16),
     ]
     flops = 0
     out_count = 4 if split_out else 1
     if fwd:
-        ffn_rows = LATE if bwd else rows
-        out_shape.append(jax.ShapeDtypeStruct((ffn_rows, feature_dim), BF16))
-        out_specs.append(full_spec((ffn_rows, feature_dim)))
-        scratch.append(pltpu.VMEM((rows, feature_dim), F32))
+        out_shape.append(jax.ShapeDtypeStruct((rows, feature_dim), BF16))
+        out_specs.append(full_spec((rows, feature_dim)))
+        scratch.append(pltpu.VMEM((blocks, NF * CAP, feature_dim), BF16))
         flops += 1.0e9 * NF * blocks / 2
     if bwd:
-        gx_rows = rows + 16 + (rows - LATE if fwd else 0)
-        out_shape.append(jax.ShapeDtypeStruct((gx_rows, feature_dim), BF16))
-        out_specs.append(full_spec((gx_rows, feature_dim)))
+        out_shape.append(jax.ShapeDtypeStruct((rows + 16, feature_dim), BF16))
+        out_specs.append(full_spec((rows + 16, feature_dim)))
         if split_out:
             for part in range(2):
                 for _ in range(2):
@@ -882,8 +900,8 @@
             out_shape.append(jax.ShapeDtypeStruct((NF, feature_dim, width), BF16))
             out_specs.append(pl.BlockSpec((1, feature_dim, width), lambda e: (e, 0, 0)))
         scratch += [
-            pltpu.VMEM((rows, feature_dim), F32),
-            pltpu.VMEM((blocks * CAP, feature_dim), BF16),
+            pltpu.VMEM((blocks, NF * CAP, feature_dim), BF16),
+            pltpu.VMEM((NF, blocks * CAP, feature_dim), BF16),
             pltpu.VMEM((blocks * 8, BLOCK), F32),
             pltpu.VMEM((feature_dim, width) if split_out else (8, 128), BF16),
         ]
@@ -985,11 +1003,12 @@
     return out
 
 
-def gather_rest(own, x_high, y_low):
-    low, high = own
-    x_low, y_high = hop(low, 1), hop(high, 2)
-    d_low, d_high = hop(y_low, 1), hop(x_high, 2)
-    return (low, x_low, y_low, d_low), (high, x_high, y_high, d_high)
+def turn(value, steps, count):
+    return lax.ppermute(value, "tp", [(i, (i + steps) % count) for i in range(count)])
+
+
+def share(value, count):
+    return [value] + [turn(value, k, count) for k in range(1, count)]
 
 
 def gather_cores(lows, highs):
@@ -1022,7 +1041,10 @@
 
 
 def scatter_first(keep, other, out, first):
-    got = hop(out, first)
+    return scatter_beside(keep, other, hop(out, first), first)
+
+
+def scatter_beside(keep, other, got, first):
     return keep[:1], other[:1], got[:1], add_low(keep[3 - first], other[3 - first], got[1])
 
 
@@ -1065,6 +1087,8 @@
     info = jnp.concatenate([ctx.reshape(1), lengths.reshape(-1)]).astype(jnp.int32)
     resid = jnp.zeros((16, 16), F32).at[:NE, :NE].set(w_resid.astype(F32))
 
+    tp_count = axes["tp"]
+    outer = share(jnp.transpose(w_out, (0, 2, 1)), tp_count)
     small, wide = [], []
     for layer in range(layer_count):
         vec = jnp.concatenate(
@@ -1081,19 +1105,9 @@
             axis=1,
         )
         pad = jnp.zeros((shard_rows, round_up(qkv_cols, 128) - qkv_cols), BF16)
-        small.append(jnp.concatenate([w_qkv[layer], pad, vec], axis=1))
+        turned = [item[layer] for item in outer]
+        small.append(jnp.concatenate([w_qkv[layer], pad, vec] + turned, axis=1))
         wide.append(pack_wide(w_gate_up, jnp.swapaxes(w_down, 2, 3), layer))
-    tp_count = axes["tp"]
-    outer = jnp.transpose(w_out, (0, 2, 1))
-    outer = [outer] + [
-        lax.ppermute(outer, "tp", [(i, (i + k) % tp_count) for i in range(tp_count)])
-        for k in range(1, tp_count)
-    ]
-    small = [
-        jnp.concatenate([small[layer]] + [item[layer] for item in outer], axis=1)
-        for layer in range(layer_count)
-    ]
-
     weights, wide_first = [None] * layer_count, [None] * layer_count
 
     def fetch_small(layer, after):
@@ -1101,25 +1115,29 @@
         if hyper:
             own, _ = tie(own, after)
             pieces = gather_small(own)
-            first = [pieces[k] for k in (2, 4, 6)]
-            if layer == 0:
-                fetch_first(0, info)
-                pieces, wide_first[0] = tie(pieces, wide_first[0])
-            else:
-                fetch_first(layer, first)
+            fetch_first(layer, [pieces[k] for k in (2, 4, 6)])
         else:
             pieces = [lax.all_gather(own, groups, axis=0, tiled=True)]
-        weights[layer] = list(prep_weights(pieces, offs, feature_dim, qkv_cols, tp_count))
+        outs = prep_weights(pieces, offs, feature_dim, qkv_cols, heads * HD, tp_count)
+        weights[layer] = [outs[0], outs[2], outs[1]]
+        if hyper and layer == 0:
+            weights[0][0], wide_first[0] = tie(weights[0][0], wide_first[0])
 
     def fetch_first(layer, after):
-        own, _ = tie(wide[layer], after)
-        wide_first[layer] = (own, hop(own[1], 1), hop(own[0], 2))
+        (low, high), _ = tie(wide[layer], after)
+        lows, highs = [low, None, hop(low, 2)], [high, hop(high, 1), None]
+        if layer > 0:
+            lows[1], highs[2] = hop(low, 1), hop(high, 2)
+        wide_first[layer] = (lows, highs)
 
     def fetch_rest(layer, value):
         if hyper:
-            own, x_high, y_low = wide_first[layer]
-            value, own, x_high, y_low = tie(value, own, x_high, y_low)
-            rests[layer] = gather_rest(own, x_high, y_low)
+            value, (lows, highs) = tie(value, wide_first[layer])
+            if layer == 0:
+                lows[1], highs[2] = hop(lows[0], 1), hop(highs[0], 2)
+            lows.append(hop(lows[2], 1))
+            highs.append(hop(highs[1], 2))
+            rests[layer] = (lows, highs)
         return value
 
     def fetch_cores(layer, after):
@@ -1130,11 +1148,20 @@
             lows = (early[0], lows[1], early[1], lows[3])
             highs = (early[2], early[3], highs[2], highs[3])
             ends[layer] = (lows[1], lows[3], highs[2], highs[3])
-            weights[layer].append(gather_cores(lows, highs))
+            rests[layer] = (lows, highs)
+            if layer + 1 < layer_count:
+                mid, wide[layer + 1] = tie((lows[1], highs[2]), wide[layer + 1])
+                rests[layer] = ((lows[0], mid[0]) + lows[2:], highs[:2] + (mid[1], highs[3]))
         else:
             both = jnp.concatenate(wide[layer], axis=0)
             full = lax.all_gather(both, groups, axis=1, tiled=True)
             weights[layer].append([(full, 0, 0, NF)])
+
+    def fetch_last(layer, after):
+        if hyper:
+            lows, highs = rests[layer]
+            last, _ = tie((lows[3], highs[3]), after)
+            weights[layer].append(gather_cores(lows[:3] + last[:1], highs[:3] + last[1:]))
 
     ends, rests = [None] * layer_count, [None] * layer_count
     fetch_small(0, info)
@@ -1150,17 +1177,19 @@
     base, ffn, prev_t = tokens.reshape(rows, feature_dim), None, None
     saved = []
     for layer in range(layer_count):
-        qkv_full, wo_all, vecs = weights[layer][:3]
+        qkv_full, _, vecs = weights[layer][:3]
         outs = qkv_part(base, ffn, vecs, qkv_full)
         h_in, qkv = outs if ffn is not None else (base, outs[0])
         other = fetch_rest(layer, swap(qkv))
         context, lse = attend_forward(qkv, other, info, heads)
         ctx_all = lax.all_gather(context, "tp", axis=0)
         fetch_cores(layer, context)
-        pieces = weights[layer][3]
+        wo_all = weights[layer][1]
         middle, base, xm_low, gates_t, logits_t = middle_part(
             h_in, ctx_all, wo_all, vecs, routes_t[layer], prev_t, resid, rank
         )
+        fetch_last(layer, xm_low)
+        pieces = weights[layer][3]
         saved.append((h_in, qkv, other, context, lse, middle, xm_low, gates_t, prev_t))
         prev_t = logits_t
         if layer < layer_count - 1:
@@ -1171,7 +1200,6 @@
                 ffn, wide_first[layer + 1] = tie(ffn, wide_first[layer + 1])
 
     grad, grad_low = cot, cot
-    upper_gain = None
     grad_logits, wide_out, pending, small_terms, late = None, None, None, None, None
     finals = [None] * layer_count
     for layer in reversed(range(layer_count)):
@@ -1182,82 +1210,85 @@
             top, True, xm_low, grad_low, routes_t[layer], gates_t, pieces, offs
         )
         if not top and late is not None:
-            late = lax.psum(late, "tp")
+            late[0] = lax.psum(late[0], "tp")
             gx, grads, late, pending = tie(gx, grads, late, pending)
-            mixed = (base_top + jnp.concatenate([early, late], axis=0).astype(F32)).astype(BF16)
         gx = lax.psum(gx, "tp")
         if hyper:
             sums = [scatter_cores(grads[2 * k], grads[2 * k + 1], k + 1) for k in range(2)]
             if pending is not None:
-                wide_terms, small_sums, dres = pending
+                wide_terms, small_parts, dres = pending
                 terms = [scatter_second(wide_terms[k], k + 1) for k in range(2)]
+                terms, sums = tie(terms, sums)
                 wide_out = final_sums(terms[0], terms[1], wide_out, layer + 1, layer_count)
-                small_terms = scatter_first(*small_sums, 1)
-                gx, sums, wide_out, small_terms = tie(gx, sums, wide_out, small_terms)
+                upper = scatter_cores(*pack_grads(*small_parts, offs), 1)
+                gx, sums, wide_out, upper = tie(gx, sums, wide_out, upper)
+                upper_got = hop(upper[2], 1)
             else:
                 gx, sums = tie(gx, sums)
-            grads = [scatter_first(*sums[k], k + 1) for k in range(2)]
+            got = [hop(sums[k][2], k + 1) for k in range(2)]
         if top:
-            base_top, early = base, gx[rows + 16 :]
+            base_top = base
+        else:
+            late[1], gx = tie(late[1], gx)
+            late[1] = lax.psum(late[1], "tp")
         gg_t = gx[rows : rows + 16, :block_len].astype(F32)
         gg_t = jnp.moveaxis(gg_t.reshape(2, 8, block_len)[: rows // BLOCK], 0, 1).reshape(8, rows)
         extra = (prev_t, resid) if prev_t is not None else (grad_logits,)
         outs = gate_backward(
-            grad, middle, gx, vecs, routes_t[layer], gates_t, gg_t, context, wo_all, extra
+            grad, middle, gx, vecs, routes_t[layer], gates_t, gg_t, context, wo_all[0], extra
         )
         gmid, gctx, dwo, dvec = outs[:4]
         if prev_t is not None:
             grad_logits, dres = outs[4:]
         gown, goth = attend_backward(qkv, other, lse, gctx, info, heads)
+        if not top:
+            gown, goth, late = tie(gown, goth, late)
         goth = swap(goth)
-        if hyper and layer == 0:
-            goth, grads = tie(goth, grads)
-        ga_part, dqkv = qkv_backward(gown, goth, h_in, vecs, qkv_full)
-        if upper_gain is not None:
-            dvec = dvec.at[ROW_UP].set(upper_gain)
-        packed = pack_grads(dqkv, dwo, dvec, offs)
+        if hyper:
+            wide_terms = [scatter_beside(*sums[k][:2], got[k], k + 1) for k in range(2)]
+            if layer == 0:
+                goth, wide_terms, upper_got = tie(goth, wide_terms, upper_got)
+        ga_part, dqkv, dgain = qkv_backward(gown, goth, h_in, vecs, qkv_full)
+        small_parts = (dqkv, dwo, dvec, dgain)
+        own = None
         ga = lax.psum(ga_part, "tp")
-        own = None
         if hyper:
-            small_sums = scatter_cores(*packed, 1)
             if layer > 0:
                 dres = dres + swap(dres)
                 dres = dres + hop(dres, 1)
-                ga, grads, small_sums, dres = tie(ga, grads, small_sums, dres)
+                ga, wide_terms, dres, small_parts = tie(ga, wide_terms, dres, small_parts)
                 dres = dres + hop(dres, 2)
-                pending = (grads, small_sums, dres)
+                pending = (wide_terms, small_parts, dres)
             else:
-                small_terms = scatter_second(small_terms, 1)
-                ga, small_terms = tie(ga, small_terms)
-                terms = [scatter_second(grads[k], k + 1) for k in range(2)]
+                small_terms = scatter_second(scatter_beside(*upper[:2], upper_got, 1), 1)
+                terms = [scatter_second(wide_terms[k], k + 1) for k in range(2)]
+                terms, small_parts = tie(terms, small_parts)
                 wide_out = final_sums(terms[0], terms[1], wide_out, layer, layer_count)
-                own = scatter_second(scatter_first(*small_sums, 1), 1)
+                own = scatter_cores(*pack_grads(*small_parts, offs), 1)
+                owns = [scatter_second(scatter_first(*own, 1), 1), small_terms]
+                owns = [
+                    sum(term.reshape(shard_rows, -1).astype(F32) for term in item) for item in owns
+                ]
+                gains = share(jnp.stack([item[:, -PACK + ROW_GA] for item in owns]), tp_count)
         if top:
-            late, ga = tie(part, ga)
+            late = [part[:block_len], part[block_len:]]
+            late[0], ga = tie(late[0], ga)
         outs = norm_backward(gmid, ga, h_in, vecs, layer > 0)
-        grad, dgain = outs[0], outs[-1]
-        upper_gain = dgain[0]
-        grad_low = outs[1]
-        finals[layer] = (grads, packed, own if hyper else None, dgain)
-
-    gain_first = finals[0][3][:1]
-    if hyper:
-        gain_first = gain_first + swap(gain_first)
-        gain_first = (
-            gain_first + hop(gain_first, 1) + (hop(gain_first, 2) + hop(gain_first, 3))
-        )
-        resid_total = dres[:NE, :NE]
-    else:
-        gain_first = lax.psum(gain_first, groups)
-        resid_total = lax.psum(dres, groups)[:NE, :NE]
-    gain_first = lax.dynamic_slice(gain_first[0], (me * shard_rows,), (shard_rows,))
+        grad = outs[0]
+        grad_low = outs[-1]
+        finals[layer] = (grads, small_parts, own)
+
+    late = jnp.concatenate(late, axis=0)
+    mixed = (base_top + late.astype(F32)).astype(BF16)
+
+    resid_total = (dres if hyper else lax.psum(dres, groups))[:NE, :NE]
     results = [None] * layer_count
     for layer in reversed(range(layer_count)):
-        grads, packed, own, _ = finals[layer]
+        grads, small_parts, own = finals[layer]
         if hyper:
-            own = own if layer == 0 else small_terms
-            own = sum(term.reshape(shard_rows, -1).astype(F32) for term in own)
+            own = owns[layer]
         else:
+            packed = pack_grads(*small_parts, offs)
             own = lax.psum_scatter(packed[0], groups, scatter_dimension=0, tiled=True).astype(F32)
             wide_own = lax.psum_scatter(
                 grads[0], groups, scatter_dimension=1, tiled=True
@@ -1279,15 +1310,20 @@
             vec[:, :NE],
             jnp.stack([vec[:, ROW_CONST : ROW_CONST + 2], vec[:, ROW_CONST + 2 : ROW_CONST + 4]]),
             vec[:, ROW_VEC : ROW_VEC + 2].T,
-            vec[:, ROW_UP],
+            vec[:, ROW_GA],
         )
     if not hyper:
         wide_out = (jnp.stack(wide_out[0]), jnp.stack(wide_out[1]))
-    stacked = [jnp.stack([item[member] for item in results]) for member in range(6)]
+    stacked = [jnp.stack([item[member] for item in results]) for member in range(7)]
+    gains = jnp.stack(gains if hyper else share(stacked[6], tp_count))
+    gain_own = sum(
+        lax.dynamic_index_in_dim(gains, (rank[0] + tp_count - j) % tp_count, 0, keepdims=False)
+        for j in range(tp_count)
+    )
     return (
         mixed.reshape(tokens.shape),
         grad.reshape(tokens.shape),
-        jnp.stack([gain_first] + [item[6] for item in results[: layer_count - 1]]),
+        gain_own,
         stacked[0],
         stacked[1],
         stacked[2],

time: 891 us -> 837 us (0.939)
  waiting for transfers between devices: 429 us -> 387 us
    ppermute x35 -> x32, waiting for transfers between devices: 225 us -> 141 us  [hop(): return lax.ppermute(value, 'fsdp', [(i, i ^ step) for i in range(4)])]
    all_gather x2, waiting for transfers between devices: 0.01 us -> 31.1 us  [per_device(): ctx_all = lax.all_gather(context, 'tp', axis=0)]
    psum x1, waiting for transfers between devices: 19.6 us -> 0.01 us  [per_device(): ffn = lax.psum(part, 'tp')]
    ppermute x36 -> x35, waiting for transfers between devices: 29.8 us -> 47.2 us  [swap(): return lax.ppermute(value, 'ctx', [(0, 1), (1, 0)])]
    psum x1 -> x2, waiting for transfers between devices: 1.93 us -> 17.1 us  [the longest x1 13.6 us: per_device(): late[1] = lax.psum(late[1], 'tp')]
    psum x2, waiting for transfers between devices: 92.3 us -> 81 us  [per_device(): gx = lax.psum(gx, 'tp')]
    psum x2, waiting for transfers between devices: 59.8 us -> 70 us  [per_device(): ga = lax.psum(ga_part, 'tp')]
    ppermute x35 -> x32, starting transfers between devices: 41.1 us -> 35.6 us  [hop(): return lax.ppermute(value, 'fsdp', [(i, i ^ step) for i in range(4)])]
  transfers between devices with their start and end apart: 82 -> 82, of which waited for: 38 -> 48; matrix products, arithmetic and copies ran while one was open for 10% -> 11% of each run, Pallas kernels for 18% -> 22%
where the time goes in v3:
time: 837 us; the launch traced here: 829 us
  waiting for transfers between devices  387 us (46%)
  Pallas kernels  268 us (32%)
  local copies, waits for them, and re-layouts  59 us (7%)
  starting transfers between devices  53.1 us (6%)
  other arithmetic  46.4 us (6%)
  between operations  14.7 us (2%)
    ppermute x32, waiting for transfers between devices, hop(): return lax.ppermute(value, 'fsdp', [(i, i ^ step) for i in range(4)])  141 us
    pallas_call x3, Pallas kernels, experts(): pl.pallas_call(functools.partial(experts_kernel, fwd, bwd, blocks, plan,...  89.9 us
    psum x2, waiting for transfers between devices, per_device(): gx = lax.psum(gx, 'tp')  81 us
    psum x2, waiting for transfers between devices, per_device(): ga = lax.psum(ga_part, 'tp')  70 us
    ppermute x35, waiting for transfers between devices, swap(): return lax.ppermute(value, 'ctx', [(0, 1), (1, 0)])  47.2 us
    ppermute x32, starting transfers between devices, hop(): return lax.ppermute(value, 'fsdp', [(i, i ^ step) for i in range(4)])  35.6 us
    convert_element_type x12, other arithmetic, add_low(): return total.astype(BF16)  31.3 us
    all_gather x2, waiting for transfers between devices, per_device(): ctx_all = lax.all_gather(context, 'tp', axis=0)  31.1 us
  transfers between devices with their start and end apart: 82, of which 48 were waited for; matrix products, arithmetic and copies ran while one was open for 11% of the time, Pallas kernels for 22%

profile of v3, /device:TPU:0, one launch (start us, length us, event | category | flops | bytes accessed | tf_op | source)
XLA Modules:
  0.0 828.6 jit_solution(10570707212371175967)
XLA Ops:
  29.9 7.5 pack_wide.2
  37.4 4.4 collective-permute-done.6.refs_4_
  48.9 3.8 prep.2
  52.7 15.0 %collective-permute-done.10.refs_7_.refs_8_ = bf16[4,96,1536]{2,1,0:T(8,128)(2,1)S(1)} collective-permute-done((bf16[4,96,1536]{2,1,0:T(8,128)(2,1)}, bf16[4,96,1536]{2,1,0:T(8,128)(2,1)S(1)}, u32[]{:S(2)}, u32[]{:S(2)}) %collective-permute-start.10) | collective-permute-done | bytes 1179680 | tf_op jit(solution)/shard_map/ppermute | solution.py:991
  69.1 5.0 qkv_part.2.own_ref
  78.5 8.4 %attend_forward.2 = (bf16[1536,128]{1,0:T(8,128)(2,1)}, f32[1024,8]{1,0:T(8,128)}) custom-call(s32[3]{0:T(128)} %pad_add_fusion.info_ref, bf16[1024,640]{1,0:T(8,128)(2,1)} %qkv_part.2.own_ref, bf16[1024,640]{1,0:T(8,128)(2,1)} %copy-done), custom_call_target="tpu_custom_call" | custom-call | flops 161061280 | bytes 196608 | tf_op jit(solution)/shard_map/attend_forward/pallas_call | solution.py:273
  91.6 24.8 %collective-permute-done.14.refs_5_.refs_6_ = bf16[4,96,1536]{2,1,0:T(8,128)(2,1)S(1)} collective-permute-done((bf16[4,96,1536]{2,1,0:T(8,128)(2,1)S(1)}, bf16[4,96,1536]{2,1,0:T(8,128)(2,1)S(1)}, u32[]{:S(2)}, u32[]{:S(2)}) %collective-permute-start.14) | collective-permute-done | bytes 1179680 | tf_op jit(solution)/shard_map/ppermute | solution.py:991
  118.8 7.5 pack_wide.3
  127.7 10.4 %middle_part.2 = (f32[1024,768]{1,0:T(8,128)}, f32[1024,768]{1,0:T(8,128)}, bf16[1024,768]{1,0:T(8,128)(2,1)}, f32[8,1024]{1,0:T(8,128)}, f32[16,1024]{1,0:T(8,128)}) custom-call(s32[1]{0:T(128)} %bitcast.rank_ref, bf16[1024,768]{1,0:T(8,128)(2,1)} %bitcast.140, bf16[4,1536,128]{2,1,0:T(8,128)(2,1)} %bitcast.151, ...), custom_call_target="tpu_custom_call" | custom-call | flops 60397976 | bytes 629145 | tf_op jit(solution)/shard_map/middle_part/pallas_call | solution.py:476
  151.7 18.6 %experts.3 = bf16[1024,768]{1,0:T(8,128)(2,1)} custom-call(s32[8]{0:T(128)} %iota_xor_fusion.offs_ref, bf16[1024,768]{1,0:T(8,128)(2,1)} %get-tuple-element.258.refs_0_, s32[8,1024]{1,0:T(8,128)} %get-tuple-element.513.refs_7_.refs_1_.refs_2_.refs_4_, f32[8,1024]{1,0:T(8,128)} %get-tuple-element.259.refs_2_.refs_3_.refs_5_, ...), custom_call_target="tpu_custom_call" | custom-call | flops 400000000 | bytes 1000000 | tf_op jit(solution)/shard_map/experts/pallas_call | solution.py:909
  178.1 6.4 collective-permute-done.25.refs_2_
  184.5 6.6 collective-permute-done.26.refs_4_
  200.7 3.8 prep.3
  204.5 15.6 %collective-permute-done.28.refs_6_ = bf16[4,96,1536]{2,1,0:T(8,128)(2,1)} collective-permute-done((bf16[4,96,1536]{2,1,0:T(8,128)(2,1)S(1)}, bf16[4,96,1536]{2,1,0:T(8,128)(2,1)}, u32[]{:S(2)}, u32[]{:S(2)}) %collective-permute-start.28) | collective-permute-done | bytes 1179680 | tf_op jit(solution)/shard_map/ppermute | solution.py:991
  221.1 22.3 %collective-permute-done.30.refs_14_ = bf16[4,96,1536]{2,1,0:T(8,128)(2,1)} collective-permute-done((bf16[4,96,1536]{2,1,0:T(8,128)(2,1)}, bf16[4,96,1536]{2,1,0:T(8,128)(2,1)}, u32[]{:S(2)}, u32[]{:S(2)}) %collective-permute-start.30) | collective-permute-done | bytes 1179680 | tf_op jit(solution)/shard_map/ppermute | solution.py:991
  244.5 6.0 qkv_part.3
  254.8 8.4 %attend_forward.3 = (bf16[1536,128]{1,0:T(8,128)(2,1)}, f32[1024,8]{1,0:T(8,128)}) custom-call(s32[3]{0:T(128)} %pad_add_fusion.info_ref, bf16[1024,640]{1,0:T(8,128)(2,1)} %get-tuple-element.283.own_ref, bf16[1024,640]{1,0:T(8,128)(2,1)} %copy-done.1), custom_call_target="tpu_custom_call" | custom-call | flops 161061280 | bytes 196608 | tf_op jit(solution)/shard_map/attend_forward/pallas_call | solution.py:273
  265.9 31.1 %all-gather.7.cloned.1.call-done = bf16[6144,128]{1,0:T(8,128)(2,1)} async-done(((bf16[1536,128]{1,0:T(8,128)(2,1)}), bf16[6144,128]{1,0:T(8,128)(2,1)}) %all-gather.7.cloned.1.call-update) | async-done | bytes 1572880 | tf_op jit(solution)/shard_map/all_gather | solution.py:1185
  297.0 11.0 %middle_part.3 = (f32[1024,768]{1,0:T(8,128)}, f32[1024,768]{1,0:T(8,128)}, bf16[1024,768]{1,0:T(8,128)(2,1)}, f32[8,1024]{1,0:T(8,128)}, f32[16,1024]{1,0:T(8,128)}) custom-call(s32[1]{0:T(128)} %bitcast.rank_ref, f32[1024,768]{1,0:T(8,128)} %get-tuple-element.282.refs_0_.h_ref, bf16[4,1536,128]{2,1,0:T(8,128)(2,1)} %bitcast.153, ...), custom_call_target="tpu_custom_call" | custom-call | flops 60397976 | bytes 629145 | tf_op jit(solution)/shard_map/middle_part/pallas_call | solution.py:476
  311.3 3.4 collective-permute-done.44.refs_15_
  318.1 38.3 %experts.4 = (bf16[1024,768]{1,0:T(8,128)(2,1)}, bf16[1040,768]{1,0:T(8,128)(2,1)}, bf16[4,4,96,1536]{3,2,1,0:T(8,128)(2,1)}, bf16[4,4,96,1536]{3,2,1,0:T(8,128)...) custom-call(s32[8]{0:T(128)} %iota_xor_fusion.offs_ref, ...), custom_call_target="tpu_custom_call" | custom-call | flops 1280000000 | bytes 2000000 | tf_op jit(solution)/shard_map/experts/pallas_call | solution.py:909
  357.4 7.3 collective-permute-done.47
  367.9 3.6 collective-permute-done.48
  371.4 3.8 add_convert_fusion.2
  375.3 50.9 %all-reduce.12.cloned.1.call-done.refs_2_ = bf16[1040,768]{1,0:T(8,128)(2,1)} async-done(((bf16[1040,768]{1,0:T(8,128)(2,1)}), bf16[1040,768]{1,0:T(8,128)(2,1)}) %all-reduce.12.cloned.1.call-update) | async-done | bytes 1597456 | tf_op jit(solution)/shard_map/psum | solution.py:1215
  430.4 13.0 %gate_backward.2 = (f32[1024,768]{1,0:T(8,128)}, bf16[1024,192]{1,0:T(8,128)(2,1)}, f32[768,192]{1,0:T(8,128)}, f32[32,768]{1,0:T(8,128)}, f32[16,1024]{1,0:T(8,128)}, /*index=5*/f32[16,16]{1,0:T(8,128)}) custom-call(bf16[1024,768]{1,0:T(8,128)(2,1)} %bitcast.144, f32[1024,768]{1,0:T(8,128)} %get-tuple-element.299.refs_1_, ...), custom_call_target="tpu_custom_call" | custom-call | flops 30198988 | bytes 707788 | tf_op jit(solution)/shard_map/gate_backward/pallas_call | solution.py:625
  443.4 14.5 %attend_backward.2 = (f32[1024,576]{1,0:T(8,128)}, bf16[1024,640]{1,0:T(8,128)(2,1)}) custom-call(s32[3]{0:T(128)} %pad_add_fusion.info_ref, bf16[1024,640]{1,0:T(8,128)(2,1)} %get-tuple-element.283.own_ref, bf16[1024,640]{1,0:T(8,128)(2,1)} %copy-done.1, f32[1024,8]{1,0:T(8,128)} %get-tuple-element.322.lse_ref, bf16[1024,192]{1,0:T(8,128)(2,1)} %get-tuple-element.323.gctx_ref), custom_call_target="tpu_custom_call" | custom-call | flops 402653184 | bytes 353894 | tf_op jit(solution)/shard_map/attend_backward/pallas_call | solution.py:344
  462.2 8.0 qkv_backward.2
  493.7 43.1 %all-reduce.14.cloned.1.call-done.ga_ref = bf16[1024,768]{1,0:T(8,128)(2,1)} async-done(((bf16[1024,768]{1,0:T(8,128)(2,1)}), bf16[1024,768]{1,0:T(8,128)(2,1)}) %all-reduce.14.cloned.1.call-update) | async-done | bytes 1572880 | tf_op jit(solution)/shard_map/psum | solution.py:1254
  538.4 6.2 norm_backward.2
  544.6 33.0 %experts.5 = (bf16[1040,768]{1,0:T(8,128)(2,1)}, bf16[4,4,96,1536]{3,2,1,0:T(8,128)(2,1)}, bf16[4,4,96,1536]{3,2,1,0:T(8,128)(2,1)}, bf16[4,4,96,1536]{3,2,1,0:T(8,128)(2,1)}, bf16[4,4,96,1536]{3,2,1,0:T(8,128)(2,1)}) custom-call(s32[8]{0:T(128)} %iota_xor_fusion.offs_ref, bf16[1024,768]{1,0:T(8,128)(2,1)} %get-tuple-element.258.refs_0_, ...), custom_call_target="tpu_custom_call" | custom-call | flops 880000000 | bytes 2000000 | tf_op jit(solution)/shard_map/experts/pallas_call | solution.py:909
  578.2 3.5 all-reduce.16.cloned.1.call-done
  597.7 3.7 add_convert_fusion
  601.5 12.6 %collective-permute-done.55.refs_3_ = bf16[4,96,1536]{2,1,0:T(8,128)(2,1)S(1)} collective-permute-done((bf16[4,96,1536]{2,1,0:T(8,128)(2,1)S(1)}, bf16[4,96,1536]{2,1,0:T(8,128)(2,1)S(1)}, u32[]{:S(2)}, u32[]{:S(2)}) %collective-permute-start.55) | collective-permute-done | bytes 1179680 | tf_op jit(solution)/shard_map/ppermute | solution.py:991
  616.5 8.9 %final_sums.2 = (f32[2,8,96,2,512]{4,3,2,1,0:T(2,128)}, f32[2,8,96,512]{3,2,1,0:T(8,128)}) custom-call(bf16[1,4,96,1536]{3,2,1,0:T(8,128)(2,1)} %slice.346.refs_0_, bf16[1,4,96,1536]{3,2,1,0:T(8,128)(2,1)} %slice.347.refs_1_, bf16[1,4,96,1536]{3,2,1,0:T(8,128)(2,1)} %slice.418.refs_2_, bf16[4,96,1536]{2,1,0:T(8,128)(2,1)} %copy-done.22, ...), custom_call_target="tpu_custom_call" | custom-call | flops 500000 | bytes 707788 | tf_op jit(solution)/shard_map/final_sums/pallas_call | solution.py:971
  625.4 30.1 %all-reduce.18.cloned.1.call-done.refs_2_ = bf16[1040,768]{1,0:T(8,128)(2,1)} async-done(((bf16[1040,768]{1,0:T(8,128)(2,1)}), bf16[1040,768]{1,0:T(8,128)(2,1)}) %all-reduce.18.cloned.1.call-update) | async-done | bytes 1597456 | tf_op jit(solution)/shard_map/psum | solution.py:1215
  660.0 12.4 %gate_backward.3 = (f32[1024,768]{1,0:T(8,128)}, bf16[1024,192]{1,0:T(8,128)(2,1)}, f32[768,192]{1,0:T(8,128)}, f32[32,768]{1,0:T(8,128)}) custom-call(f32[1024,768]{1,0:T(8,128)} %get-tuple-element.340.refs_0_, f32[1024,768]{1,0:T(8,128)} %get-tuple-element.341.refs_1_, bf16[1040,768]{1,0:T(8,128)(2,1)} %all-reduce.18.cloned.1.call-done.refs_2_, ...), custom_call_target="tpu_custom_call" | custom-call | flops 30198988 | bytes 707788 | tf_op jit(solution)/shard_map/gate_backward/pallas_call | solution.py:625
  672.4 14.5 %attend_backward.3 = (f32[1024,576]{1,0:T(8,128)}, bf16[1024,640]{1,0:T(8,128)(2,1)}) custom-call(s32[3]{0:T(128)} %pad_add_fusion.info_ref, bf16[1024,640]{1,0:T(8,128)(2,1)} %qkv_part.2.own_ref, bf16[1024,640]{1,0:T(8,128)(2,1)} %copy-done, f32[1024,8]{1,0:T(8,128)} %get-tuple-element.298.lse_ref, bf16[1024,192]{1,0:T(8,128)(2,1)} %get-tuple-element.401.gctx_ref), custom_call_target="tpu_custom_call" | custom-call | flops 402653184 | bytes 353894 | tf_op jit(solution)/shard_map/attend_backward/pallas_call | solution.py:344
  686.9 13.6 %all-reduce.20.cloned.1.call-done = bf16[512,768]{1,0:T(8,128)(2,1)} async-done(((bf16[512,768]{1,0:T(8,128)(2,1)}), bf16[512,768]{1,0:T(8,128)(2,1)}) %all-reduce.20.cloned.1.call-update) | async-done | bytes 786448 | tf_op jit(solution)/shard_map/psum | solution.py:1233
  716.5 3.4 fusion.2
  719.9 3.6 fusion.3
  730.7 8.0 qkv_backward.3
  738.7 13.9 %collective-permute-done.64.refs_3_ = bf16[4,96,1536]{2,1,0:T(8,128)(2,1)} collective-permute-done((bf16[4,96,1536]{2,1,0:T(8,128)(2,1)}, bf16[4,96,1536]{2,1,0:T(8,128)(2,1)}, u32[]{:S(2)}, u32[]{:S(2)}) %collective-permute-start.64) | collective-permute-done | bytes 1179680 | tf_op jit(solution)/shard_map/ppermute | solution.py:991
  753.1 3.4 pack_grads.3
  760.9 9.2 %collective-permute-done.67 = bf16[2,96,896]{2,1,0:T(8,128)(2,1)S(1)} collective-permute-done((bf16[2,96,896]{2,1,0:T(8,128)(2,1)S(1)}, bf16[2,96,896]{2,1,0:T(8,128)(2,1)S(1)}, u32[]{:S(2)}, u32[]{:S(2)}) %collective-permute-start.67) | collective-permute-done | bytes 344096 | tf_op jit(solution)/shard_map/ppermute | solution.py:991
  771.4 9.0 %final_sums.3 = (f32[2,8,96,2,512]{4,3,2,1,0:T(2,128)}, f32[2,8,96,512]{3,2,1,0:T(8,128)}) custom-call(bf16[1,4,96,1536]{3,2,1,0:T(8,128)(2,1)} %slice.366.refs_0_, bf16[1,4,96,1536]{3,2,1,0:T(8,128)(2,1)} %slice.367.refs_1_, bf16[1,4,96,1536]{3,2,1,0:T(8,128)(2,1)} %slice.423.refs_2_, ...), custom_call_target="tpu_custom_call", output_to_operand_aliasing={{0}: (8, {}), {1}: (9, {})} | custom-call | flops 500000 | bytes 707788 | tf_op jit(solution)/shard_map/final_sums/pallas_call | solution.py:971
  780.3 27.0 %all-reduce.22.cloned.1.call-done.ga_ref = bf16[1024,768]{1,0:T(8,128)(2,1)} async-done(((bf16[1024,768]{1,0:T(8,128)(2,1)}), bf16[1024,768]{1,0:T(8,128)(2,1)}) %all-reduce.22.cloned.1.call-update) | async-done | bytes 1572880 | tf_op jit(solution)/shard_map/psum | solution.py:1254
  807.3 5.5 norm_backward.3
  (347 shorter events, 190.2 us)
Async XLA Ops:
  7.2 120.5 %all-gather.5.cloned.1.call-start = ((), (), s32[]{:S(2)}) async-start(), calls=%async_computation.7 | async-start | bytes 1966080 | tf_op jit(solution)/shard_map/all_gather | solution.py:1185
  8.2 15.9 %collective-permute-start = (bf16[2,96,192]{2,1,0:T(8,128)(2,1)S(1)}, bf16[2,96,192]{2,1,0:T(8,128)(2,1)S(1)}, u32[]{:S(2)}, u32[]{:S(2)}) collective-permute-start(bf16[2,96,192]{2,1,0:T(8,128)(2,1)S(1)} %bitcast.154), channel_id=1, source_target_pairs={{0,1},{1,2},{2,3},{3,0},{4,5},{5,6},{6,7},{7,4},{8,9},{9,10},{10,1... | collective-permute-start | bytes 221192 | tf_op jit(solution)/shard_map/ppermute | solution.py:1007
  11.3 13.5 %collective-permute-start.1 = (bf16[2,96,192]{2,1,0:T(8,128)(2,1)S(1)}, bf16[2,96,192]{2,1,0:T(8,128)(2,1)S(1)}, u32[]{:S(2)}, u32[]{:S(2)}) collective-permute-start(bf16[2,96,192]{2,1,0:T(8,128)(2,1)S(1)} %bitcast.155), channel_id=1, source_target_pairs={{0,2},{1,3},{2,0},{3,1},{4,6},{5,7},{6,4},{7,5},{8,10},{9,11},{10,... | collective-permute-start | bytes 221192 | tf_op jit(solution)/shard_map/ppermute | solution.py:1007
  27.9 13.9 %collective-permute-start.6 = (bf16[96,1536]{1,0:T(8,128)(2,1)S(1)}, bf16[96,1536]{1,0:T(8,128)(2,1)S(1)}, u32[]{:S(2)}, u32[]{:S(2)}) collective-permute-start(bf16[96,1536]{1,0:T(8,128)(2,1)S(1)} %concatenate.18.refs_0_), channel_id=1, source_target_pairs={{0,16},{8,24},{16,0},{24,8},{1,17},{9,25},{17,1},{25,9},{2,18},{10... | collective-permute-start | bytes 884744 | tf_op jit(solution)/shard_map/ppermute | solution.py:991
  41.8 25.9 %collective-permute-start.10 = (bf16[4,96,1536]{2,1,0:T(8,128)(2,1)}, bf16[4,96,1536]{2,1,0:T(8,128)(2,1)S(1)}, u32[]{:S(2)}, u32[]{:S(2)}) collective-permute-start(bf16[4,96,1536]{2,1,0:T(8,128)(2,1)} %get-tuple-element.264.refs_3_.refs_4_), channel_id=1, source_target_pairs={{0,16},{8,24},{16,0},{24,8},{1,17},{9,25},{17,1},{25,9},{2,18},{10... | collective-permute-start | bytes 3538952 | tf_op jit(solution)/shard_map/ppermute | solution.py:991
  43.7 24.3 %collective-permute-start.11 = (bf16[4,96,1536]{2,1,0:T(8,128)(2,1)}, bf16[4,96,1536]{2,1,0:T(8,128)(2,1)S(1)}, u32[]{:S(2)}, u32[]{:S(2)}) collective-permute-start(bf16[4,96,1536]{2,1,0:T(8,128)(2,1)} %get-tuple-element.270.refs_11_.refs_12_), channel_id=1, source_target_pairs={{0,8},{8,0},{16,24},{24,16},{1,9},{9,1},{17,25},{25,17},{2,10},{10... | collective-permute-start | bytes 3538952 | tf_op jit(solution)/shard_map/ppermute | solution.py:991
  86.8 157.7 %all-reduce.10.cloned.1.call-start = ((), (), s32[]{:S(2)}) async-start(), calls=%async_computation | async-start | bytes 3145728 | tf_op jit(solution)/shard_map/psum | solution.py:1198
  87.4 28.9 %collective-permute-start.14 = (bf16[4,96,1536]{2,1,0:T(8,128)(2,1)S(1)}, bf16[4,96,1536]{2,1,0:T(8,128)(2,1)S(1)}, u32[]{:S(2)}, u32[]{:S(2)}) collective-permute-start(bf16[4,96,1536]{2,1,0:T(8,128)(2,1)S(1)} %copy-done.2), channel_id=1, source_target_pairs={{0,8},{8,0},{16,24},{24,16},{1,9},{9,1},{17,25},{25,17},{2,10},{10... | collective-permute-start | bytes 3538952 | tf_op jit(solution)/shard_map/ppermute | solution.py:991
  88.9 28.9 %collective-permute-start.15 = (bf16[4,96,1536]{2,1,0:T(8,128)(2,1)S(1)}, bf16[4,96,1536]{2,1,0:T(8,128)(2,1)S(1)}, u32[]{:S(2)}, u32[]{:S(2)}) collective-permute-start(bf16[4,96,1536]{2,1,0:T(8,128)(2,1)S(1)} %copy-done.3), channel_id=1, source_target_pairs={{0,16},{8,24},{16,0},{24,8},{1,17},{9,25},{17,1},{25,9},{2,18},{10... | collective-permute-start | bytes 3538952 | tf_op jit(solution)/shard_map/ppermute | solution.py:991
  90.3 50.6 %collective-permute-start.18 = (bf16[4,96,1536]{2,1,0:T(8,128)(2,1)S(1)}, bf16[4,96,1536]{2,1,0:T(8,128)(2,1)}, u32[]{:S(2)}, u32[]{:S(2)}) collective-permute-start(bf16[4,96,1536]{2,1,0:T(8,128)(2,1)S(1)} %collective-permute-done.10.refs_7_.refs_8_), channel_id=1, source_target_pairs={{0,8},{8,0},{16,24},{24,16},{1,9},{9,1},{17,25},{25,17},{2,10},{10... | collective-permute-start | bytes 3538952 | tf_op jit(solution)/shard_map/ppermute | solution.py:991
  90.9 51.1 %collective-permute-start.19 = (bf16[4,96,1536]{2,1,0:T(8,128)(2,1)}, bf16[4,96,1536]{2,1,0:T(8,128)(2,1)}, u32[]{:S(2)}, u32[]{:S(2)}) collective-permute-start(bf16[4,96,1536]{2,1,0:T(8,128)(2,1)} %copy-done.5), channel_id=1, source_target_pairs={{0,16},{8,24},{16,0},{24,8},{1,17},{9,25},{17,1},{25,9},{2,18},{10... | collective-permute-start | bytes 3538952 | tf_op jit(solution)/shard_map/ppermute | solution.py:991
  91.6 50.5 %collective-permute-start.13 = (bf16[4,96,1536]{2,1,0:T(8,128)(2,1)S(1)}, bf16[4,96,1536]{2,1,0:T(8,128)(2,1)}, u32[]{:S(2)}, u32[]{:S(2)}) collective-permute-start(bf16[4,96,1536]{2,1,0:T(8,128)(2,1)S(1)} %copy-done.2), channel_id=1, source_target_pairs={{0,4},{4,0},{1,5},{5,1},{2,6},{6,2},{3,7},{7,3},{8,12},{12,8},{9,1... | collective-permute-start | bytes 3538952 | tf_op jit(solution)/shard_map/ppermute | solution.py:995
  116.3 26.3 %collective-permute-start.17 = (bf16[4,96,1536]{2,1,0:T(8,128)(2,1)S(1)}, bf16[4,96,1536]{2,1,0:T(8,128)(2,1)}, u32[]{:S(2)}, u32[]{:S(2)}) collective-permute-start(bf16[4,96,1536]{2,1,0:T(8,128)(2,1)S(1)} %collective-permute-done.10.refs_7_.refs_8_), channel_id=1, source_target_pairs={{0,4},{4,0},{1,5},{5,1},{2,6},{6,2},{3,7},{7,3},{8,12},{12,8},{9,1... | collective-permute-start | bytes 3538952 | tf_op jit(solution)/shard_map/ppermute | solution.py:995
  118.8 23.8 %collective-permute-start.21 = (bf16[4,96,1536]{2,1,0:T(8,128)(2,1)S(1)}, bf16[4,96,1536]{2,1,0:T(8,128)(2,1)}, u32[]{:S(2)}, u32[]{:S(2)}) collective-permute-start(bf16[4,96,1536]{2,1,0:T(8,128)(2,1)S(1)} %copy-done.3), channel_id=1, source_target_pairs={{0,4},{4,0},{1,5},{5,1},{2,6},{6,2},{3,7},{7,3},{8,12},{12,8},{9,1... | collective-permute-start | bytes 3538952 | tf_op jit(solution)/shard_map/ppermute | solution.py:995
  170.4 126.7 %all-gather.7.cloned.1.call-start = ((), (), s32[]{:S(2)}) async-start(), calls=%async_computation.8 | async-start | bytes 1966080 | tf_op jit(solution)/shard_map/all_gather | solution.py:1185
  176.0 15.1 %collective-permute-start.26 = (bf16[96,1536]{1,0:T(8,128)(2,1)S(1)}, bf16[96,1536]{1,0:T(8,128)(2,1)S(1)}, u32[]{:S(2)}, u32[]{:S(2)}) collective-permute-start(bf16[96,1536]{1,0:T(8,128)(2,1)S(1)} %concatenate.20.refs_0_), channel_id=1, source_target_pairs={{0,16},{8,24},{16,0},{24,8},{1,17},{9,25},{17,1},{25,9},{2,18},{10... | collective-permute-start | bytes 884744 | tf_op jit(solution)/shard_map/ppermute | solution.py:991
  177.3 13.7 %collective-permute-start.27 = (bf16[96,1536]{1,0:T(8,128)(2,1)S(1)}, bf16[96,1536]{1,0:T(8,128)(2,1)S(1)}, u32[]{:S(2)}, u32[]{:S(2)}) collective-permute-start(bf16[96,1536]{1,0:T(8,128)(2,1)S(1)} %concatenate.20.refs_0_), channel_id=1, source_target_pairs={{0,24},{8,16},{16,8},{24,0},{1,25},{9,17},{17,9},{25,1},{2,26},{10... | collective-permute-start | bytes 884744 | tf_op jit(solution)/shard_map/ppermute | solution.py:991
  178.1 17.1 %collective-permute-start.32 = (bf16[96,1536]{1,0:T(8,128)(2,1)S(1)}, bf16[96,1536]{1,0:T(8,128)(2,1)S(1)}, u32[]{:S(2)}, u32[]{:S(2)}) collective-permute-start(bf16[96,1536]{1,0:T(8,128)(2,1)S(1)} %concatenate.20.refs_0_), channel_id=1, source_target_pairs={{0,4},{4,0},{1,5},{5,1},{2,6},{6,2},{3,7},{7,3},{8,12},{12,8},{9,1... | collective-permute-start | bytes 884744 | tf_op jit(solution)/shard_map/ppermute | solution.py:995
  191.1 29.1 %collective-permute-start.28 = (bf16[4,96,1536]{2,1,0:T(8,128)(2,1)S(1)}, bf16[4,96,1536]{2,1,0:T(8,128)(2,1)}, u32[]{:S(2)}, u32[]{:S(2)}) collective-permute-start(bf16[4,96,1536]{2,1,0:T(8,128)(2,1)S(1)} %copy-done.20), channel_id=1, source_target_pairs={{0,8},{8,0},{16,24},{24,16},{1,9},{9,1},{17,25},{25,17},{2,10},{10... | collective-permute-start | bytes 3538952 | tf_op jit(solution)/shard_map/ppermute | solution.py:991
  192.1 29.0 %collective-permute-start.29 = (bf16[4,96,1536]{2,1,0:T(8,128)(2,1)S(1)}, bf16[4,96,1536]{2,1,0:T(8,128)(2,1)}, u32[]{:S(2)}, u32[]{:S(2)}) collective-permute-start(bf16[4,96,1536]{2,1,0:T(8,128)(2,1)S(1)} %copy-done.20), channel_id=1, source_target_pairs={{0,16},{8,24},{16,0},{24,8},{1,17},{9,25},{17,1},{25,9},{2,18},{10... | collective-permute-start | bytes 3538952 | tf_op jit(solution)/shard_map/ppermute | solution.py:991
  193.1 50.3 %collective-permute-start.30 = (bf16[4,96,1536]{2,1,0:T(8,128)(2,1)}, bf16[4,96,1536]{2,1,0:T(8,128)(2,1)}, u32[]{:S(2)}, u32[]{:S(2)}) collective-permute-start(bf16[4,96,1536]{2,1,0:T(8,128)(2,1)} %get-tuple-element.310.refs_12_), channel_id=1, source_target_pairs={{0,8},{8,0},{16,24},{24,16},{1,9},{9,1},{17,25},{25,17},{2,10},{10... | collective-permute-start | bytes 3538952 | tf_op jit(solution)/shard_map/ppermute | solution.py:991
  194.5 50.0 %collective-permute-start.31 = (bf16[4,96,1536]{2,1,0:T(8,128)(2,1)}, bf16[4,96,1536]{2,1,0:T(8,128)(2,1)}, u32[]{:S(2)}, u32[]{:S(2)}) collective-permute-start(bf16[4,96,1536]{2,1,0:T(8,128)(2,1)} %get-tuple-element.310.refs_12_), channel_id=1, source_target_pairs={{0,16},{8,24},{16,0},{24,8},{1,17},{9,25},{17,1},{25,9},{2,18},{10... | collective-permute-start | bytes 3538952 | tf_op jit(solution)/shard_map/ppermute | solution.py:991
  263.2 163.0 %all-reduce.12.cloned.1.call-start = ((), (), s32[]{:S(2)}) async-start(), calls=%async_computation.1 | async-start | bytes 3194880 | tf_op jit(solution)/shard_map/psum | solution.py:1215
  263.5 44.6 %collective-permute-start.40 = (bf16[4,96,1536]{2,1,0:T(8,128)(2,1)}, bf16[4,96,1536]{2,1,0:T(8,128)(2,1)}, u32[]{:S(2)}, u32[]{:S(2)}) collective-permute-start(bf16[4,96,1536]{2,1,0:T(8,128)(2,1)} %collective-permute-done.29.refs_8_), channel_id=1, source_target_pairs={{0,8},{8,0},{16,24},{24,16},{1,9},{9,1},{17,25},{25,17},{2,10},{10... | collective-permute-start | bytes 3538952 | tf_op jit(solution)/shard_map/ppermute | solution.py:991
  264.1 44.0 %collective-permute-start.41 = (bf16[4,96,1536]{2,1,0:T(8,128)(2,1)}, bf16[4,96,1536]{2,1,0:T(8,128)(2,1)}, u32[]{:S(2)}, u32[]{:S(2)}) collective-permute-start(bf16[4,96,1536]{2,1,0:T(8,128)(2,1)} %collective-permute-done.30.refs_14_), channel_id=1, source_target_pairs={{0,16},{8,24},{16,0},{24,8},{1,17},{9,25},{17,1},{25,9},{2,18},{10... | collective-permute-start | bytes 3538952 | tf_op jit(solution)/shard_map/ppermute | solution.py:991
  264.8 43.9 %collective-permute-start.37 = (bf16[4,96,1536]{2,1,0:T(8,128)(2,1)S(1)}, bf16[4,96,1536]{2,1,0:T(8,128)(2,1)}, u32[]{:S(2)}, u32[]{:S(2)}) collective-permute-start(bf16[4,96,1536]{2,1,0:T(8,128)(2,1)S(1)} %copy-done.20), channel_id=1, source_target_pairs={{0,4},{4,0},{1,5},{5,1},{2,6},{6,2},{3,7},{7,3},{8,12},{12,8},{9,1... | collective-permute-start | bytes 3538952 | tf_op jit(solution)/shard_map/ppermute | solution.py:995
  264.8 44.0 %collective-permute-start.38 = (bf16[4,96,1536]{2,1,0:T(8,128)(2,1)}, bf16[4,96,1536]{2,1,0:T(8,128)(2,1)}, u32[]{:S(2)}, u32[]{:S(2)}) collective-permute-start(bf16[4,96,1536]{2,1,0:T(8,128)(2,1)} %collective-permute-done.28.refs_6_), channel_id=1, source_target_pairs={{0,4},{4,0},{1,5},{5,1},{2,6},{6,2},{3,7},{7,3},{8,12},{12,8},{9,1... | collective-permute-start | bytes 3538952 | tf_op jit(solution)/shard_map/ppermute | solution.py:995
  265.3 43.9 %collective-permute-start.39 = (bf16[4,96,1536]{2,1,0:T(8,128)(2,1)}, bf16[4,96,1536]{2,1,0:T(8,128)(2,1)}, u32[]{:S(2)}, u32[]{:S(2)}) collective-permute-start(bf16[4,96,1536]{2,1,0:T(8,128)(2,1)} %collective-permute-done.29.refs_8_), channel_id=1, source_target_pairs={{0,4},{4,0},{1,5},{5,1},{2,6},{6,2},{3,7},{7,3},{8,12},{12,8},{9,1... | collective-permute-start | bytes 3538952 | tf_op jit(solution)/shard_map/ppermute | solution.py:995
  356.6 14.9 %collective-permute-start.48 = (bf16[4,4,96,1536]{3,2,1,0:T(8,128)(2,1)}, bf16[4,4,96,1536]{3,2,1,0:T(8,128)(2,1)}, u32[]{:S(2)}, u32[]{:S(2)}) collective-permute-start(bf16[4,4,96,1536]{3,2,1,0:T(8,128)(2,1)} %get-tuple-element.318), channel_id=1, source_target_pairs={{0,4},{4,0},{1,5},{5,1},{2,6},{6,2},{3,7},{7,3},{8,12},{12,8},{9,1... | collective-permute-start | bytes 14155784 | tf_op jit(solution)/shard_map/ppermute | solution.py:995
  357.0 179.8 %all-reduce.14.cloned.1.call-start = ((), (), s32[]{:S(2)}) async-start(), calls=%async_computation.2 | async-start | bytes 3145728 | tf_op jit(solution)/shard_map/psum | solution.py:1254
  426.1 57.3 %collective-permute-start.50 = (bf16[2,4,96,1536]{3,2,1,0:T(8,128)(2,1)S(1)}, bf16[2,4,96,1536]{3,2,1,0:T(8,128)(2,1)}, u32[]{:S(2)}, u32[]{:S(2)}) collective-permute-start(bf16[2,4,96,1536]{3,2,1,0:T(8,128)(2,1)S(1)} %add_convert_fusion.3), channel_id=1, source_target_pairs={{0,8},{8,0},{16,24},{24,16},{1,9},{9,1},{17,25},{25,17},{2,10},{10... | collective-permute-start | bytes 7077896 | tf_op jit(solution)/shard_map/ppermute | solution.py:991
  427.6 58.2 %collective-permute-start.51 = (bf16[2,4,96,1536]{3,2,1,0:T(8,128)(2,1)}, bf16[2,4,96,1536]{3,2,1,0:T(8,128)(2,1)}, u32[]{:S(2)}, u32[]{:S(2)}) collective-permute-start(bf16[2,4,96,1536]{3,2,1,0:T(8,128)(2,1)} %add_convert_fusion.2), channel_id=1, source_target_pairs={{0,16},{8,24},{16,0},{24,8},{1,17},{9,25},{17,1},{25,9},{2,18},{10... | collective-permute-start | bytes 7077896 | tf_op jit(solution)/shard_map/ppermute | solution.py:991
  470.3 111.5 %all-reduce.16.cloned.1.call-start = ((), (), s32[]{:S(2)}) async-start(), calls=%async_computation.3 | async-start | bytes 1572864 | tf_op jit(solution)/shard_map/psum | solution.py:1213
  536.8 118.7 %all-reduce.18.cloned.1.call-start = ((), (), s32[]{:S(2)}) async-start(), calls=%async_computation.4 | async-start | bytes 3194880 | tf_op jit(solution)/shard_map/psum | solution.py:1215
  536.8 40.8 %collective-permute-start.54 = (f32[16,16]{1,0:T(8,128)S(1)}, f32[16,16]{1,0:T(8,128)S(1)}, u32[]{:S(2)}, u32[]{:S(2)}) collective-permute-start(f32[16,16]{1,0:T(8,128)S(1)} %add.202), channel_id=1, source_target_pairs={{0,16},{8,24},{16,0},{24,8},{1,17},{9,25},{17,1},{25,9},{2,18},{10... | collective-permute-start | bytes 3080 | tf_op jit(solution)/shard_map/ppermute | solution.py:991
  581.7 16.0 %collective-permute-start.58 = (bf16[4,4,96,1536]{3,2,1,0:T(8,128)(2,1)}, bf16[4,4,96,1536]{3,2,1,0:T(8,128)(2,1)}, u32[]{:S(2)}, u32[]{:S(2)}) collective-permute-start(bf16[4,4,96,1536]{3,2,1,0:T(8,128)(2,1)} %get-tuple-element.375), channel_id=1, source_target_pairs={{0,4},{4,0},{1,5},{5,1},{2,6},{6,2},{3,7},{7,3},{8,12},{12,8},{9,1... | collective-permute-start | bytes 14155784 | tf_op jit(solution)/shard_map/ppermute | solution.py:995
  585.6 114.9 %all-reduce.20.cloned.1.call-start = ((), (), s32[]{:S(2)}) async-start(), calls=%async_computation.5 | async-start | bytes 1572864 | tf_op jit(solution)/shard_map/psum | solution.py:1233
  585.7 28.4 %collective-permute-start.55 = (bf16[4,96,1536]{2,1,0:T(8,128)(2,1)S(1)}, bf16[4,96,1536]{2,1,0:T(8,128)(2,1)S(1)}, u32[]{:S(2)}, u32[]{:S(2)}) collective-permute-start(bf16[4,96,1536]{2,1,0:T(8,128)(2,1)S(1)} %fusion), channel_id=1, source_target_pairs={{0,16},{8,24},{16,0},{24,8},{1,17},{9,25},{17,1},{25,9},{2,18},{10... | collective-permute-start | bytes 3538952 | tf_op jit(solution)/shard_map/ppermute | solution.py:991
  587.2 28.3 %collective-permute-start.56 = (bf16[4,96,1536]{2,1,0:T(8,128)(2,1)}, bf16[4,96,1536]{2,1,0:T(8,128)(2,1)S(1)}, u32[]{:S(2)}, u32[]{:S(2)}) collective-permute-start(bf16[4,96,1536]{2,1,0:T(8,128)(2,1)} %fusion.1), channel_id=1, source_target_pairs={{0,8},{8,0},{16,24},{24,16},{1,9},{9,1},{17,25},{25,17},{2,10},{10... | collective-permute-start | bytes 3538952 | tf_op jit(solution)/shard_map/ppermute | solution.py:991
  655.5 56.2 %collective-permute-start.61 = (bf16[2,4,96,1536]{3,2,1,0:T(8,128)(2,1)S(1)}, bf16[2,4,96,1536]{3,2,1,0:T(8,128)(2,1)}, u32[]{:S(2)}, u32[]{:S(2)}) collective-permute-start(bf16[2,4,96,1536]{3,2,1,0:T(8,128)(2,1)S(1)} %add_convert_fusion.1), channel_id=1, source_target_pairs={{0,8},{8,0},{16,24},{24,16},{1,9},{9,1},{17,25},{25,17},{2,10},{10... | collective-permute-start | bytes 7077896 | tf_op jit(solution)/shard_map/ppermute | solution.py:991
  656.9 57.1 %collective-permute-start.62 = (bf16[2,4,96,1536]{3,2,1,0:T(8,128)(2,1)}, bf16[2,4,96,1536]{3,2,1,0:T(8,128)(2,1)}, u32[]{:S(2)}, u32[]{:S(2)}) collective-permute-start(bf16[2,4,96,1536]{3,2,1,0:T(8,128)(2,1)} %add_convert_fusion), channel_id=1, source_target_pairs={{0,16},{8,24},{16,0},{24,8},{1,17},{9,25},{17,1},{25,9},{2,18},{10... | collective-permute-start | bytes 7077896 | tf_op jit(solution)/shard_map/ppermute | solution.py:991
  658.4 148.9 %all-reduce.22.cloned.1.call-start = ((), (), s32[]{:S(2)}) async-start(), calls=%async_computation.6 | async-start | bytes 3145728 | tf_op jit(solution)/shard_map/psum | solution.py:1254
  700.5 23.0 %collective-permute-start.60 = (bf16[1024,640]{1,0:T(8,128)(2,1)}, bf16[1024,640]{1,0:T(8,128)(2,1)}, u32[]{:S(2)}, u32[]{:S(2)}) collective-permute-start(bf16[1024,640]{1,0:T(8,128)(2,1)} %get-tuple-element.410), channel_id=1, source_target_pairs={{0,4},{4,0},{1,5},{5,1},{2,6},{6,2},{3,7},{7,3},{8,12},{12,8},{9,1... | collective-permute-start | bytes 3932168 | tf_op jit(solution)/shard_map/ppermute | solution.py:995
  710.2 13.3 %collective-permute-start.63 = (bf16[2,96,896]{2,1,0:T(8,128)(2,1)S(1)}, bf16[2,96,896]{2,1,0:T(8,128)(2,1)S(1)}, u32[]{:S(2)}, u32[]{:S(2)}) collective-permute-start(bf16[2,96,896]{2,1,0:T(8,128)(2,1)S(1)} %copy-done.28), channel_id=1, source_target_pairs={{0,8},{8,0},{16,24},{24,16},{1,9},{9,1},{17,25},{25,17},{2,10},{10... | collective-permute-start | bytes 1032200 | tf_op jit(solution)/shard_map/ppermute | solution.py:991
  723.5 29.1 %collective-permute-start.64 = (bf16[4,96,1536]{2,1,0:T(8,128)(2,1)}, bf16[4,96,1536]{2,1,0:T(8,128)(2,1)}, u32[]{:S(2)}, u32[]{:S(2)}) collective-permute-start(bf16[4,96,1536]{2,1,0:T(8,128)(2,1)} %fusion.2), channel_id=1, source_target_pairs={{0,16},{8,24},{16,0},{24,8},{1,17},{9,25},{17,1},{25,9},{2,18},{10... | collective-permute-start | bytes 3538952 | tf_op jit(solution)/shard_map/ppermute | solution.py:991
  725.0 28.1 %collective-permute-start.65 = (bf16[4,96,1536]{2,1,0:T(8,128)(2,1)}, bf16[4,96,1536]{2,1,0:T(8,128)(2,1)}, u32[]{:S(2)}, u32[]{:S(2)}) collective-permute-start(bf16[4,96,1536]{2,1,0:T(8,128)(2,1)} %fusion.3), channel_id=1, source_target_pairs={{0,8},{8,0},{16,24},{24,16},{1,9},{9,1},{17,25},{25,17},{2,10},{10... | collective-permute-start | bytes 3538952 | tf_op jit(solution)/shard_map/ppermute | solution.py:991
  727.3 29.2 %collective-permute-start.69 = (bf16[96,896]{1,0:T(8,128)(2,1)}, bf16[96,896]{1,0:T(8,128)(2,1)}, u32[]{:S(2)}, u32[]{:S(2)}) collective-permute-start(bf16[96,896]{1,0:T(8,128)(2,1)} %fusion.5), channel_id=1, source_target_pairs={{0,16},{8,24},{16,0},{24,8},{1,17},{9,25},{17,1},{25,9},{2,18},{10... | collective-permute-start | bytes 516104 | tf_op jit(solution)/shard_map/ppermute | solution.py:991
  770.1 42.7 %collective-permute-start.68 = (bf16[96,896]{1,0:T(8,128)(2,1)S(1)}, bf16[96,896]{1,0:T(8,128)(2,1)S(1)}, u32[]{:S(2)}, u32[]{:S(2)}) collective-permute-start(bf16[96,896]{1,0:T(8,128)(2,1)S(1)} %fusion.4), channel_id=1, source_target_pairs={{0,16},{8,24},{16,0},{24,8},{1,17},{9,25},{17,1},{25,9},{2,18},{10... | collective-permute-start | bytes 516104 | tf_op jit(solution)/shard_map/ppermute | solution.py:991
  (83 other events, 599.1 us)
Sparse Core Ops, SparseCore 0:
  87.0 35.2 all-gather.4
  170.5 67.2 all-reduce.9
  263.3 33.6 all-gather.6
  357.1 69.0 all-reduce.11
  470.4 66.3 all-reduce.13
  539.0 42.6 all-reduce.15
  585.7 69.6 all-reduce.17
  658.5 41.9 all-reduce.19
  738.8 68.4 all-reduce.21

commit v4 on v3

--- a/solution.py
+++ b/solution.py
@@ -1011,12 +1011,13 @@
     return [value] + [turn(value, k, count) for k in range(1, count)]
 
 
-def gather_cores(lows, highs):
+def gather_cores(lows, highs, swapped):
     half = NF // 2
     out = []
-    for first, items in ((0, lows), (half, highs)):
+    for first, items, done in ((0, lows, swapped[0]), (half, highs, swapped[1])):
         for chip, item in enumerate(items):
-            out += [(item, 2 * chip, first, half), (swap(item), 2 * chip + 1, first, half)]
+            other = done[chip] if chip in done else swap(item)
+            out += [(item, 2 * chip, first, half), (other, 2 * chip + 1, first, half)]
     return out
 
 
@@ -1045,7 +1046,7 @@
 
 
 def scatter_beside(keep, other, got, first):
-    return keep[:1], other[:1], got[:1], add_low(keep[3 - first], other[3 - first], got[1])
+    return keep, other, got, add_low(keep[3 - first], other[3 - first], got[1])
 
 
 def scatter_second(terms, first):
@@ -1120,50 +1121,54 @@
             pieces = [lax.all_gather(own, groups, axis=0, tiled=True)]
         outs = prep_weights(pieces, offs, feature_dim, qkv_cols, heads * HD, tp_count)
         weights[layer] = [outs[0], outs[2], outs[1]]
-        if hyper and layer == 0:
-            weights[0][0], wide_first[0] = tie(weights[0][0], wide_first[0])
 
     def fetch_first(layer, after):
         (low, high), _ = tie(wide[layer], after)
         lows, highs = [low, None, hop(low, 2)], [high, hop(high, 1), None]
         if layer > 0:
             lows[1], highs[2] = hop(low, 1), hop(high, 2)
-        wide_first[layer] = (lows, highs)
+        wide_first[layer] = (lows, highs, [swap(low), swap(high)] if layer == 0 else [])
 
     def fetch_rest(layer, value):
         if hyper:
-            value, (lows, highs) = tie(value, wide_first[layer])
+            value, (lows, highs, own) = tie(value, wide_first[layer])
+            swapped[layer] = ({0: own[0]}, {0: own[1]}) if own else ({}, {})
+            value = swap(value)
             if layer == 0:
                 lows[1], highs[2] = hop(lows[0], 1), hop(highs[0], 2)
             lows.append(hop(lows[2], 1))
             highs.append(hop(highs[1], 2))
             rests[layer] = (lows, highs)
+        else:
+            value = swap(value)
         return value
 
     def fetch_cores(layer, after):
         if hyper:
             lows, highs = rests[layer]
-            early = (lows[0], lows[2], highs[0], highs[1])
-            early, _ = tie(early, after)
-            lows = (early[0], lows[1], early[1], lows[3])
-            highs = (early[2], early[3], highs[2], highs[3])
-            ends[layer] = (lows[1], lows[3], highs[2], highs[3])
+            if layer == 0:
+                swapped[0][0][2], swapped[0][1][1] = swap(lows[2]), swap(highs[1])
+                after, swapped[0] = tie(after, swapped[0])
+                if layer + 1 < layer_count:
+                    mid, wide[layer + 1] = tie((lows[1], highs[2]), wide[layer + 1])
+                    lows[1], highs[2] = mid
+            else:
+                (lows, highs), _ = tie((lows, highs), after)
             rests[layer] = (lows, highs)
-            if layer + 1 < layer_count:
-                mid, wide[layer + 1] = tie((lows[1], highs[2]), wide[layer + 1])
-                rests[layer] = ((lows[0], mid[0]) + lows[2:], highs[:2] + (mid[1], highs[3]))
         else:
             both = jnp.concatenate(wide[layer], axis=0)
             full = lax.all_gather(both, groups, axis=1, tiled=True)
             weights[layer].append([(full, 0, 0, NF)])
+        return after
 
     def fetch_last(layer, after):
         if hyper:
             lows, highs = rests[layer]
-            last, _ = tie((lows[3], highs[3]), after)
-            weights[layer].append(gather_cores(lows[:3] + last[:1], highs[:3] + last[1:]))
-
-    ends, rests = [None] * layer_count, [None] * layer_count
+            if layer == 0:
+                (lows[3], highs[3]), _ = tie((lows[3], highs[3]), after)
+            weights[layer].append(gather_cores(lows, highs, swapped[layer]))
+
+    rests, swapped = [None] * layer_count, [None] * layer_count
     fetch_small(0, info)
 
     routes_t = jnp.moveaxis(routes.reshape(layer_count, rows, 2), 2, 1)
@@ -1180,10 +1185,9 @@
         qkv_full, _, vecs = weights[layer][:3]
         outs = qkv_part(base, ffn, vecs, qkv_full)
         h_in, qkv = outs if ffn is not None else (base, outs[0])
-        other = fetch_rest(layer, swap(qkv))
+        other = fetch_rest(layer, qkv)
         context, lse = attend_forward(qkv, other, info, heads)
-        ctx_all = lax.all_gather(context, "tp", axis=0)
-        fetch_cores(layer, context)
+        ctx_all = lax.all_gather(fetch_cores(layer, context), "tp", axis=0)
         wo_all = weights[layer][1]
         middle, base, xm_low, gates_t, logits_t = middle_part(
             h_in, ctx_all, wo_all, vecs, routes_t[layer], prev_t, resid, rank
@@ -1193,8 +1197,8 @@
         saved.append((h_in, qkv, other, context, lse, middle, xm_low, gates_t, prev_t))
         prev_t = logits_t
         if layer < layer_count - 1:
-            fetch_small(layer + 1, ends[layer] if hyper else ctx_all)
             part, _, _ = experts(True, False, xm_low, None, routes_t[layer], gates_t, pieces, offs)
+            fetch_small(layer + 1, part)
             ffn = lax.psum(part, "tp")
             if hyper:
                 ffn, wide_first[layer + 1] = tie(ffn, wide_first[layer + 1])
@@ -1215,6 +1219,7 @@
         gx = lax.psum(gx, "tp")
         if hyper:
             sums = [scatter_cores(grads[2 * k], grads[2 * k + 1], k + 1) for k in range(2)]
+            got = [hop(sums[k][2], k + 1) for k in range(2)]
             if pending is not None:
                 wide_terms, small_parts, dres = pending
                 terms = [scatter_second(wide_terms[k], k + 1) for k in range(2)]
@@ -1225,7 +1230,6 @@
                 upper_got = hop(upper[2], 1)
             else:
                 gx, sums = tie(gx, sums)
-            got = [hop(sums[k][2], k + 1) for k in range(2)]
         if top:
             base_top = base
         else:
@@ -1241,13 +1245,13 @@
         if prev_t is not None:
             grad_logits, dres = outs[4:]
         gown, goth = attend_backward(qkv, other, lse, gctx, info, heads)
+        if hyper:
+            wide_terms = [scatter_beside(*sums[k][:2], got[k], k + 1) for k in range(2)]
         if not top:
             gown, goth, late = tie(gown, goth, late)
+            if hyper:
+                gown, wide_terms, upper_got = tie(gown, wide_terms, upper_got)
         goth = swap(goth)
-        if hyper:
-            wide_terms = [scatter_beside(*sums[k][:2], got[k], k + 1) for k in range(2)]
-            if layer == 0:
-                goth, wide_terms, upper_got = tie(goth, wide_terms, upper_got)
         ga_part, dqkv, dgain = qkv_backward(gown, goth, h_in, vecs, qkv_full)
         small_parts = (dqkv, dwo, dvec, dgain)
         own = None
@@ -1262,12 +1266,13 @@
             else:
                 small_terms = scatter_second(scatter_beside(*upper[:2], upper_got, 1), 1)
                 terms = [scatter_second(wide_terms[k], k + 1) for k in range(2)]
-                terms, small_parts = tie(terms, small_parts)
+                terms, small_parts, late = tie(terms, small_parts, late)
                 wide_out = final_sums(terms[0], terms[1], wide_out, layer, layer_count)
                 own = scatter_cores(*pack_grads(*small_parts, offs), 1)
                 owns = [scatter_second(scatter_first(*own, 1), 1), small_terms]
                 owns = [
-                    sum(term.reshape(shard_rows, -1).astype(F32) for term in item) for item in owns
+                    sum((term[0] if term.ndim == 3 else term).astype(F32) for term in item)
+                    for item in owns
                 ]
                 gains = share(jnp.stack([item[:, -PACK + ROW_GA] for item in owns]), tp_count)
         if top:

time: 837 us -> 799 us (0.955)
  waiting for transfers between devices: 387 us -> 359 us
  local copies, waits for them, and re-layouts: 59 us -> 38.7 us
    slice x12 -> x0, local copies, waits for them, and re-layouts: 27.4 us -> none  [the longest x4 9.51 us: scatter_beside(): got[:1]]
    all_gather x2, waiting for transfers between devices: 31.1 us -> 12.6 us  [per_device(): ctx_all = lax.all_gather(fetch_cores(layer, context), 'tp', axis=0)]
    ppermute x32, waiting for transfers between devices: 141 us -> 132 us  [hop(): return lax.ppermute(value, 'fsdp', [(i, i ^ step) for i in range(4)])]
  transfers between devices with their start and end apart: 82 -> 82, of which waited for: 48 -> 44; matrix products, arithmetic and copies ran while one was open for 11% -> 10% of each run, Pallas kernels for 22% -> 26%
where the time goes in v4:
time: 799 us; the launch traced here: 791 us
  waiting for transfers between devices  359 us (45%)
  Pallas kernels  270 us (34%)
  starting transfers between devices  57.6 us (7%)
  other arithmetic  51.3 us (6%)
  local copies, waits for them, and re-layouts  38.7 us (5%)
  between operations  14.7 us (2%)
    ppermute x32, waiting for transfers between devices, hop(): return lax.ppermute(value, 'fsdp', [(i, i ^ step) for i in range(4)])  132 us
    pallas_call x3, Pallas kernels, experts(): pl.pallas_call(functools.partial(experts_kernel, fwd, bwd, blocks, plan,...  89.9 us
    psum x2, waiting for transfers between devices, per_device(): gx = lax.psum(gx, 'tp')  80.2 us
    psum x2, waiting for transfers between devices, per_device(): ga = lax.psum(ga_part, 'tp')  77.1 us
    ppermute x32, starting transfers between devices, hop(): return lax.ppermute(value, 'fsdp', [(i, i ^ step) for i in range(4)])  39.5 us
    ppermute x35, waiting for transfers between devices, swap(): return lax.ppermute(value, 'ctx', [(0, 1), (1, 0)])  39.3 us
    convert_element_type x12, other arithmetic, add_low(): return total.astype(BF16)  36.7 us
    pallas_call x2, Pallas kernels, attend_backward(): pl.pallas_call(functools.partial(attn_bwd_kernel, heads), grid=(rows // B...  29 us
  transfers between devices with their start and end apart: 82, of which 44 were waited for; matrix products, arithmetic and copies ran while one was open for 10% of the time, Pallas kernels for 26%

profile of v4, /device:TPU:0, one launch (start us, length us, event | category | flops | bytes accessed | tf_op | source)
XLA Modules:
  0.0 791.1 jit_solution(16844480466025822714)
XLA Ops:
  29.9 7.5 pack_wide.2
  37.4 4.4 collective-permute-done.6.refs_4_
  51.6 3.8 prep.2
  55.5 5.0 qkv_part.2.own_ref
  60.5 7.3 collective-permute-done.10.refs_7_.refs_8_
  68.7 3.8 collective-permute-done.14.other_ref
  73.6 8.4 %attend_forward.2 = (bf16[1536,128]{1,0:T(8,128)(2,1)}, f32[1024,8]{1,0:T(8,128)}) custom-call(s32[3]{0:T(128)} %pad_add_fusion.info_ref, bf16[1024,640]{1,0:T(8,128)(2,1)} %qkv_part.2.own_ref, bf16[1024,640]{1,0:T(8,128)(2,1)} %copy-done.4), custom_call_target="tpu_custom_call" | custom-call | flops 161061280 | bytes 196608 | tf_op jit(solution)/shard_map/attend_forward/pallas_call | solution.py:273
  87.6 7.5 pack_wide.3
  96.5 16.0 %collective-permute-done.17.refs_5_.refs_6_ = bf16[4,96,1536]{2,1,0:T(8,128)(2,1)} collective-permute-done((bf16[4,96,1536]{2,1,0:T(8,128)(2,1)S(1)}, bf16[4,96,1536]{2,1,0:T(8,128)(2,1)}, u32[]{:S(2)}, u32[]{:S(2)}) %collective-permute-start.17) | collective-permute-done | bytes 1179680 | tf_op jit(solution)/shard_map/ppermute | solution.py:991
  114.6 4.0 all-gather.5.cloned.1.call-done
  118.5 10.2 %middle_part.2 = (f32[1024,768]{1,0:T(8,128)}, f32[1024,768]{1,0:T(8,128)}, bf16[1024,768]{1,0:T(8,128)(2,1)}, f32[8,1024]{1,0:T(8,128)}, f32[16,1024]{1,0:T(8,128)}) custom-call(s32[1]{0:T(128)} %bitcast.rank_ref, bf16[1024,768]{1,0:T(8,128)(2,1)} %bitcast.140, bf16[4,1536,128]{2,1,0:T(8,128)(2,1)} %bitcast.149, ...), custom_call_target="tpu_custom_call" | custom-call | flops 60397976 | bytes 629145 | tf_op jit(solution)/shard_map/middle_part/pallas_call | solution.py:476
  128.7 8.3 %collective-permute-done.20.refs_9_.refs_10_ = bf16[4,96,1536]{2,1,0:T(8,128)(2,1)} collective-permute-done((bf16[4,96,1536]{2,1,0:T(8,128)(2,1)S(1)}, bf16[4,96,1536]{2,1,0:T(8,128)(2,1)}, u32[]{:S(2)}, u32[]{:S(2)}) %collective-permute-start.20) | collective-permute-done | bytes 1179680 | tf_op jit(solution)/shard_map/ppermute | solution.py:991
  148.2 18.6 %experts.3 = bf16[1024,768]{1,0:T(8,128)(2,1)} custom-call(s32[8]{0:T(128)} %iota_xor_fusion.offs_ref, bf16[1024,768]{1,0:T(8,128)(2,1)} %get-tuple-element.254.refs_0_, s32[8,1024]{1,0:T(8,128)} %get-tuple-element.505.refs_7_.refs_1_.refs_2_.refs_4_, f32[8,1024]{1,0:T(8,128)} %get-tuple-element.255.refs_2_.refs_3_.refs_5_, ...), custom_call_target="tpu_custom_call" | custom-call | flops 400000000 | bytes 1000000 | tf_op jit(solution)/shard_map/experts/pallas_call | solution.py:909
  170.5 6.6 collective-permute-done.25.refs_2_
  177.1 4.8 collective-permute-done.26.refs_4_
  192.9 3.8 prep.3
  196.7 15.9 %collective-permute-done.28.refs_6_ = bf16[4,96,1536]{2,1,0:T(8,128)(2,1)} collective-permute-done((bf16[4,96,1536]{2,1,0:T(8,128)(2,1)}, bf16[4,96,1536]{2,1,0:T(8,128)(2,1)}, u32[]{:S(2)}, u32[]{:S(2)}) %collective-permute-start.28) | collective-permute-done | bytes 1179680 | tf_op jit(solution)/shard_map/ppermute | solution.py:991
  213.5 22.6 %collective-permute-done.30.refs_14_ = bf16[4,96,1536]{2,1,0:T(8,128)(2,1)} collective-permute-done((bf16[4,96,1536]{2,1,0:T(8,128)(2,1)}, bf16[4,96,1536]{2,1,0:T(8,128)(2,1)}, u32[]{:S(2)}, u32[]{:S(2)}) %collective-permute-start.30) | collective-permute-done | bytes 1179680 | tf_op jit(solution)/shard_map/ppermute | solution.py:991
  236.4 5.9 qkv_part.3
  246.8 8.4 %attend_forward.3 = (bf16[1536,128]{1,0:T(8,128)(2,1)}, f32[1024,8]{1,0:T(8,128)}) custom-call(s32[3]{0:T(128)} %pad_add_fusion.info_ref, bf16[1024,640]{1,0:T(8,128)(2,1)} %get-tuple-element.284.own_ref, bf16[1024,640]{1,0:T(8,128)(2,1)} %copy-done.5), custom_call_target="tpu_custom_call" | custom-call | flops 161061280 | bytes 196608 | tf_op jit(solution)/shard_map/attend_forward/pallas_call | solution.py:273
  255.4 15.8 %collective-permute-done.37.refs_10_ = bf16[4,96,1536]{2,1,0:T(8,128)(2,1)} collective-permute-done((bf16[4,96,1536]{2,1,0:T(8,128)(2,1)}, bf16[4,96,1536]{2,1,0:T(8,128)(2,1)}, u32[]{:S(2)}, u32[]{:S(2)}) %collective-permute-start.37) | collective-permute-done | bytes 1179680 | tf_op jit(solution)/shard_map/ppermute | solution.py:991
  281.1 8.6 %all-gather.7.cloned.1.call-done = bf16[6144,128]{1,0:T(8,128)(2,1)} async-done(((bf16[1536,128]{1,0:T(8,128)(2,1)}), bf16[6144,128]{1,0:T(8,128)(2,1)}) %all-gather.7.cloned.1.call-update) | async-done | bytes 1572880 | tf_op jit(solution)/shard_map/all_gather | solution.py:1190
  289.7 10.9 %middle_part.3 = (f32[1024,768]{1,0:T(8,128)}, f32[1024,768]{1,0:T(8,128)}, bf16[1024,768]{1,0:T(8,128)(2,1)}, f32[8,1024]{1,0:T(8,128)}, f32[16,1024]{1,0:T(8,128)}) custom-call(s32[1]{0:T(128)} %bitcast.rank_ref, f32[1024,768]{1,0:T(8,128)} %get-tuple-element.276.refs_0_.h_ref, bf16[4,1536,128]{2,1,0:T(8,128)(2,1)} %bitcast.151, ...), custom_call_target="tpu_custom_call" | custom-call | flops 60397976 | bytes 629145 | tf_op jit(solution)/shard_map/middle_part/pallas_call | solution.py:476
  301.7 38.3 %experts.4 = (bf16[1024,768]{1,0:T(8,128)(2,1)}, bf16[1040,768]{1,0:T(8,128)(2,1)}, bf16[4,4,96,1536]{3,2,1,0:T(8,128)(2,1)}, bf16[4,4,96,1536]{3,2,1,0:T(8,128)...) custom-call(s32[8]{0:T(128)} %iota_xor_fusion.offs_ref, ...), custom_call_target="tpu_custom_call" | custom-call | flops 1280000000 | bytes 2000000 | tf_op jit(solution)/shard_map/experts/pallas_call | solution.py:909
  340.9 7.4 collective-permute-done.47.refs_1_
  348.3 4.6 add_convert_fusion.3
  360.3 49.5 %all-reduce.12.cloned.1.call-done.refs_2_ = bf16[1040,768]{1,0:T(8,128)(2,1)} async-done(((bf16[1040,768]{1,0:T(8,128)(2,1)}), bf16[1040,768]{1,0:T(8,128)(2,1)}) %all-reduce.12.cloned.1.call-update) | async-done | bytes 1597456 | tf_op jit(solution)/shard_map/psum | solution.py:1219
  411.1 13.0 %gate_backward.2 = (f32[1024,768]{1,0:T(8,128)}, bf16[1024,192]{1,0:T(8,128)(2,1)}, f32[768,192]{1,0:T(8,128)}, f32[32,768]{1,0:T(8,128)}, f32[16,1024]{1,0:T(8,128)}, /*index=5*/f32[16,16]{1,0:T(8,128)}) custom-call(bf16[1024,768]{1,0:T(8,128)(2,1)} %bitcast.144, f32[1024,768]{1,0:T(8,128)} %get-tuple-element.293.refs_1_, ...), custom_call_target="tpu_custom_call" | custom-call | flops 30198988 | bytes 707788 | tf_op jit(solution)/shard_map/gate_backward/pallas_call | solution.py:625
  424.1 14.5 %attend_backward.2 = (f32[1024,576]{1,0:T(8,128)}, bf16[1024,640]{1,0:T(8,128)(2,1)}) custom-call(s32[3]{0:T(128)} %pad_add_fusion.info_ref, bf16[1024,640]{1,0:T(8,128)(2,1)} %get-tuple-element.284.own_ref, bf16[1024,640]{1,0:T(8,128)(2,1)} %copy-done.5, f32[1024,8]{1,0:T(8,128)} %get-tuple-element.318.lse_ref, bf16[1024,192]{1,0:T(8,128)(2,1)} %get-tuple-element.319.gctx_ref), custom_call_target="tpu_custom_call" | custom-call | flops 402653184 | bytes 353894 | tf_op jit(solution)/shard_map/attend_backward/pallas_call | solution.py:344
  442.9 8.1 %qkv_backward.2 = (bf16[1024,768]{1,0:T(8,128)(2,1)}, f32[768,576]{1,0:T(8,128)}, f32[8,768]{1,0:T(8,128)}) custom-call(f32[1024,576]{1,0:T(8,128)} %get-tuple-element.320.gown_ref, bf16[1024,640]{1,0:T(8,128)(2,1)} %copy-done.14, f32[1024,768]{1,0:T(8,128)} %get-tuple-element.276.refs_0_.h_ref, ...), custom_call_target="tpu_custom_call" | custom-call | flops 90596968 | bytes 393216 | tf_op jit(solution)/shard_map/qkv_backward/pallas_call | solution.py:668
  462.9 56.4 %all-reduce.14.cloned.1.call-done.ga_ref = bf16[1024,768]{1,0:T(8,128)(2,1)} async-done(((bf16[1024,768]{1,0:T(8,128)(2,1)}), bf16[1024,768]{1,0:T(8,128)(2,1)}) %all-reduce.14.cloned.1.call-update) | async-done | bytes 1572880 | tf_op jit(solution)/shard_map/psum | solution.py:1258
  521.4 6.3 norm_backward.2
  527.7 33.0 %experts.5 = (bf16[1040,768]{1,0:T(8,128)(2,1)}, bf16[4,4,96,1536]{3,2,1,0:T(8,128)(2,1)}, bf16[4,4,96,1536]{3,2,1,0:T(8,128)(2,1)}, bf16[4,4,96,1536]{3,2,1,0:T(8,128)(2,1)}, bf16[4,4,96,1536]{3,2,1,0:T(8,128)(2,1)}) custom-call(s32[8]{0:T(128)} %iota_xor_fusion.offs_ref, bf16[1024,768]{1,0:T(8,128)(2,1)} %get-tuple-element.254.refs_0_, ...), custom_call_target="tpu_custom_call" | custom-call | flops 880000000 | bytes 2000000 | tf_op jit(solution)/shard_map/experts/pallas_call | solution.py:909
  567.8 4.7 collective-permute-done.57.refs_1_
  572.5 4.4 add_convert_fusion.1
  579.2 3.9 add_convert_fusion
  596.5 8.9 %final_sums.2 = (f32[2,8,96,2,512]{4,3,2,1,0:T(2,128)}, f32[2,8,96,512]{3,2,1,0:T(8,128)}) custom-call(bf16[4,4,96,1536]{3,2,1,0:T(8,128)(2,1)} %get-tuple-element.374.refs_0_, bf16[4,4,96,1536]{3,2,1,0:T(8,128)(2,1)} %collective-permute-done.47.refs_1_, bf16[2,4,96,1536]{3,2,1,0:T(8,128)(2,1)} %copy-done.3, bf16[4,96,1536]{2,1,0:T(8,128)(2,1)} %copy-done.20, ...), custom_call_target="tpu_custom_call" | custom-call | flops 500000 | bytes 707788 | tf_op jit(solution)/shard_map/final_sums/pallas_call | solution.py:971
  605.4 30.7 %all-reduce.18.cloned.1.call-done.refs_2_ = bf16[1040,768]{1,0:T(8,128)(2,1)} async-done(((bf16[1040,768]{1,0:T(8,128)(2,1)}), bf16[1040,768]{1,0:T(8,128)(2,1)}) %all-reduce.18.cloned.1.call-update) | async-done | bytes 1597456 | tf_op jit(solution)/shard_map/psum | solution.py:1219
  639.2 12.4 %gate_backward.3 = (f32[1024,768]{1,0:T(8,128)}, bf16[1024,192]{1,0:T(8,128)(2,1)}, f32[768,192]{1,0:T(8,128)}, f32[32,768]{1,0:T(8,128)}) custom-call(f32[1024,768]{1,0:T(8,128)} %get-tuple-element.334.refs_0_, f32[1024,768]{1,0:T(8,128)} %get-tuple-element.335.refs_1_, bf16[1040,768]{1,0:T(8,128)(2,1)} %all-reduce.18.cloned.1.call-done.refs_2_, ...), custom_call_target="tpu_custom_call" | custom-call | flops 30198988 | bytes 707788 | tf_op jit(solution)/shard_map/gate_backward/pallas_call | solution.py:625
  651.6 14.5 %attend_backward.3 = (f32[1024,576]{1,0:T(8,128)}, bf16[1024,640]{1,0:T(8,128)(2,1)}) custom-call(s32[3]{0:T(128)} %pad_add_fusion.info_ref, bf16[1024,640]{1,0:T(8,128)(2,1)} %qkv_part.2.own_ref, bf16[1024,640]{1,0:T(8,128)(2,1)} %copy-done.4, f32[1024,8]{1,0:T(8,128)} %get-tuple-element.292.lse_ref, bf16[1024,192]{1,0:T(8,128)(2,1)} %get-tuple-element.393.gctx_ref), custom_call_target="tpu_custom_call" | custom-call | flops 402653184 | bytes 353894 | tf_op jit(solution)/shard_map/attend_backward/pallas_call | solution.py:344
  666.1 15.1 %all-reduce.20.cloned.1.call-done = bf16[512,768]{1,0:T(8,128)(2,1)} async-done(((bf16[512,768]{1,0:T(8,128)(2,1)}), bf16[512,768]{1,0:T(8,128)(2,1)}) %all-reduce.20.cloned.1.call-update) | async-done | bytes 786448 | tf_op jit(solution)/shard_map/psum | solution.py:1237
  681.3 4.0 fusion.2
  693.4 7.8 qkv_backward.3
  701.2 19.9 %collective-permute-done.69 = bf16[96,896]{1,0:T(8,128)(2,1)} collective-permute-done((bf16[96,896]{1,0:T(8,128)(2,1)S(1)}, bf16[96,896]{1,0:T(8,128)(2,1)}, u32[]{:S(2)}, u32[]{:S(2)}) %collective-permute-start.69) | collective-permute-done | bytes 172064 | tf_op jit(solution)/shard_map/ppermute | solution.py:991
  722.3 4.2 pack_grads.3
  734.3 9.8 %final_sums.3 = (f32[2,8,96,2,512]{4,3,2,1,0:T(2,128)}, f32[2,8,96,512]{3,2,1,0:T(8,128)}) custom-call(bf16[4,4,96,1536]{3,2,1,0:T(8,128)(2,1)} %get-tuple-element.434.refs_0_, bf16[4,4,96,1536]{3,2,1,0:T(8,128)(2,1)} %collective-permute-done.57.refs_1_, bf16[2,4,96,1536]{3,2,1,0:T(8,128)(2,1)} %copy-done.2, ...), custom_call_target="tpu_custom_call", output_to_operand_aliasing={{0}: (8, {}), {1}: (9, {})} | custom-call | flops 500000 | bytes 707788 | tf_op jit(solution)/shard_map/final_sums/pallas_call | solution.py:971
  748.2 20.7 %all-reduce.22.cloned.1.call-done.ga_ref = bf16[1024,768]{1,0:T(8,128)(2,1)} async-done(((bf16[1024,768]{1,0:T(8,128)(2,1)}), bf16[1024,768]{1,0:T(8,128)(2,1)}) %all-reduce.22.cloned.1.call-update) | async-done | bytes 1572880 | tf_op jit(solution)/shard_map/psum | solution.py:1258
  768.9 5.5 norm_backward.3
  (338 shorter events, 170.8 us)
Async XLA Ops:
  7.2 111.4 %all-gather.5.cloned.1.call-start = ((), (), s32[]{:S(2)}) async-start(), calls=%async_computation.7 | async-start | bytes 1966080 | tf_op jit(solution)/shard_map/all_gather | solution.py:1190
  8.2 15.9 %collective-permute-start = (bf16[2,96,192]{2,1,0:T(8,128)(2,1)S(1)}, bf16[2,96,192]{2,1,0:T(8,128)(2,1)S(1)}, u32[]{:S(2)}, u32[]{:S(2)}) collective-permute-start(bf16[2,96,192]{2,1,0:T(8,128)(2,1)S(1)} %bitcast.152), channel_id=1, source_target_pairs={{0,1},{1,2},{2,3},{3,0},{4,5},{5,6},{6,7},{7,4},{8,9},{9,10},{10,1... | collective-permute-start | bytes 221192 | tf_op jit(solution)/shard_map/ppermute | solution.py:1007
  29.8 14.6 %collective-permute-start.3 = (bf16[96,1536]{1,0:T(8,128)(2,1)S(1)}, bf16[96,1536]{1,0:T(8,128)(2,1)S(1)}, u32[]{:S(2)}, u32[]{:S(2)}) collective-permute-start(bf16[96,1536]{1,0:T(8,128)(2,1)S(1)} %concatenate.18.refs_0_), channel_id=1, source_target_pairs={{0,4},{4,0},{1,5},{5,1},{2,6},{6,2},{3,7},{7,3},{8,12},{12,8},{9,1... | collective-permute-start | bytes 884744 | tf_op jit(solution)/shard_map/ppermute | solution.py:995
  41.8 25.9 %collective-permute-start.10 = (bf16[4,96,1536]{2,1,0:T(8,128)(2,1)}, bf16[4,96,1536]{2,1,0:T(8,128)(2,1)S(1)}, u32[]{:S(2)}, u32[]{:S(2)}) collective-permute-start(bf16[4,96,1536]{2,1,0:T(8,128)(2,1)} %get-tuple-element.256.refs_3_.refs_4_), channel_id=1, source_target_pairs={{0,16},{8,24},{16,0},{24,8},{1,17},{9,25},{17,1},{25,9},{2,18},{10... | collective-permute-start | bytes 3538952 | tf_op jit(solution)/shard_map/ppermute | solution.py:991
  43.7 24.4 %collective-permute-start.11 = (bf16[4,96,1536]{2,1,0:T(8,128)(2,1)}, bf16[4,96,1536]{2,1,0:T(8,128)(2,1)}, u32[]{:S(2)}, u32[]{:S(2)}) collective-permute-start(bf16[4,96,1536]{2,1,0:T(8,128)(2,1)} %get-tuple-element.258.refs_11_.refs_12_), channel_id=1, source_target_pairs={{0,8},{8,0},{16,24},{24,16},{1,9},{9,1},{17,25},{25,17},{2,10},{10... | collective-permute-start | bytes 3538952 | tf_op jit(solution)/shard_map/ppermute | solution.py:991
  43.9 24.2 %collective-permute-start.12 = (bf16[4,96,1536]{2,1,0:T(8,128)(2,1)}, bf16[4,96,1536]{2,1,0:T(8,128)(2,1)}, u32[]{:S(2)}, u32[]{:S(2)}) collective-permute-start(bf16[4,96,1536]{2,1,0:T(8,128)(2,1)} %get-tuple-element.256.refs_3_.refs_4_), channel_id=1, source_target_pairs={{0,4},{4,0},{1,5},{5,1},{2,6},{6,2},{3,7},{7,3},{8,12},{12,8},{9,1... | collective-permute-start | bytes 3538952 | tf_op jit(solution)/shard_map/ppermute | solution.py:995
  43.9 24.2 %collective-permute-start.13 = (bf16[4,96,1536]{2,1,0:T(8,128)(2,1)}, bf16[4,96,1536]{2,1,0:T(8,128)(2,1)}, u32[]{:S(2)}, u32[]{:S(2)}) collective-permute-start(bf16[4,96,1536]{2,1,0:T(8,128)(2,1)} %get-tuple-element.258.refs_11_.refs_12_), channel_id=1, source_target_pairs={{0,4},{4,0},{1,5},{5,1},{2,6},{6,2},{3,7},{7,3},{8,12},{12,8},{9,1... | collective-permute-start | bytes 3538952 | tf_op jit(solution)/shard_map/ppermute | solution.py:995
  68.6 14.4 %collective-permute-start.16 = (bf16[4,96,1536]{2,1,0:T(8,128)(2,1)}, bf16[4,96,1536]{2,1,0:T(8,128)(2,1)}, u32[]{:S(2)}, u32[]{:S(2)}) collective-permute-start(bf16[4,96,1536]{2,1,0:T(8,128)(2,1)} %collective-permute-done.11.refs_13_.refs_14_), channel_id=1, source_target_pairs={{0,4},{4,0},{1,5},{5,1},{2,6},{6,2},{3,7},{7,3},{8,12},{12,8},{9,1... | collective-permute-start | bytes 3538952 | tf_op jit(solution)/shard_map/ppermute | solution.py:995
  83.0 153.4 %all-reduce.10.cloned.1.call-start = ((), (), s32[]{:S(2)}) async-start(), calls=%async_computation | async-start | bytes 3145728 | tf_op jit(solution)/shard_map/psum | solution.py:1202
  83.5 29.0 %collective-permute-start.17 = (bf16[4,96,1536]{2,1,0:T(8,128)(2,1)S(1)}, bf16[4,96,1536]{2,1,0:T(8,128)(2,1)}, u32[]{:S(2)}, u32[]{:S(2)}) collective-permute-start(bf16[4,96,1536]{2,1,0:T(8,128)(2,1)S(1)} %copy-done.6), channel_id=1, source_target_pairs={{0,8},{8,0},{16,24},{24,16},{1,9},{9,1},{17,25},{25,17},{2,10},{10... | collective-permute-start | bytes 3538952 | tf_op jit(solution)/shard_map/ppermute | solution.py:991
  85.1 29.0 %collective-permute-start.18 = (bf16[4,96,1536]{2,1,0:T(8,128)(2,1)S(1)}, bf16[4,96,1536]{2,1,0:T(8,128)(2,1)}, u32[]{:S(2)}, u32[]{:S(2)}) collective-permute-start(bf16[4,96,1536]{2,1,0:T(8,128)(2,1)S(1)} %copy-done.7), channel_id=1, source_target_pairs={{0,16},{8,24},{16,0},{24,8},{1,17},{9,25},{17,1},{25,9},{2,18},{10... | collective-permute-start | bytes 3538952 | tf_op jit(solution)/shard_map/ppermute | solution.py:991
  86.6 50.4 %collective-permute-start.20 = (bf16[4,96,1536]{2,1,0:T(8,128)(2,1)S(1)}, bf16[4,96,1536]{2,1,0:T(8,128)(2,1)}, u32[]{:S(2)}, u32[]{:S(2)}) collective-permute-start(bf16[4,96,1536]{2,1,0:T(8,128)(2,1)S(1)} %collective-permute-done.10.refs_7_.refs_8_), channel_id=1, source_target_pairs={{0,8},{8,0},{16,24},{24,16},{1,9},{9,1},{17,25},{25,17},{2,10},{10... | collective-permute-start | bytes 3538952 | tf_op jit(solution)/shard_map/ppermute | solution.py:991
  87.1 51.1 %collective-permute-start.21 = (bf16[4,96,1536]{2,1,0:T(8,128)(2,1)}, bf16[4,96,1536]{2,1,0:T(8,128)(2,1)}, u32[]{:S(2)}, u32[]{:S(2)}) collective-permute-start(bf16[4,96,1536]{2,1,0:T(8,128)(2,1)} %collective-permute-done.11.refs_13_.refs_14_), channel_id=1, source_target_pairs={{0,16},{8,24},{16,0},{24,8},{1,17},{9,25},{17,1},{25,9},{2,18},{10... | collective-permute-start | bytes 3538952 | tf_op jit(solution)/shard_map/ppermute | solution.py:991
  114.0 32.8 %collective-permute-start.19 = (bf16[4,96,1536]{2,1,0:T(8,128)(2,1)}, bf16[4,96,1536]{2,1,0:T(8,128)(2,1)S(1)}, u32[]{:S(2)}, u32[]{:S(2)}) collective-permute-start(bf16[4,96,1536]{2,1,0:T(8,128)(2,1)} %collective-permute-done.17.refs_5_.refs_6_), channel_id=1, source_target_pairs={{0,4},{4,0},{1,5},{5,1},{2,6},{6,2},{3,7},{7,3},{8,12},{12,8},{9,1... | collective-permute-start | bytes 3538952 | tf_op jit(solution)/shard_map/ppermute | solution.py:995
  114.1 32.8 %collective-permute-start.23 = (bf16[4,96,1536]{2,1,0:T(8,128)(2,1)}, bf16[4,96,1536]{2,1,0:T(8,128)(2,1)S(1)}, u32[]{:S(2)}, u32[]{:S(2)}) collective-permute-start(bf16[4,96,1536]{2,1,0:T(8,128)(2,1)} %collective-permute-done.18.refs_15_.refs_16_), channel_id=1, source_target_pairs={{0,4},{4,0},{1,5},{5,1},{2,6},{6,2},{3,7},{7,3},{8,12},{12,8},{9,1... | collective-permute-start | bytes 3538952 | tf_op jit(solution)/shard_map/ppermute | solution.py:995
  166.9 122.8 %all-gather.7.cloned.1.call-start = ((), (), s32[]{:S(2)}) async-start(), calls=%async_computation.8 | async-start | bytes 1966080 | tf_op jit(solution)/shard_map/all_gather | solution.py:1190
  170.5 16.9 %collective-permute-start.32 = (bf16[96,1536]{1,0:T(8,128)(2,1)}, bf16[96,1536]{1,0:T(8,128)(2,1)S(1)}, u32[]{:S(2)}, u32[]{:S(2)}) collective-permute-start(bf16[96,1536]{1,0:T(8,128)(2,1)} %concatenate.20.refs_0_), channel_id=1, source_target_pairs={{0,4},{4,0},{1,5},{5,1},{2,6},{6,2},{3,7},{7,3},{8,12},{12,8},{9,1... | collective-permute-start | bytes 884744 | tf_op jit(solution)/shard_map/ppermute | solution.py:995
  183.4 29.2 %collective-permute-start.28 = (bf16[4,96,1536]{2,1,0:T(8,128)(2,1)}, bf16[4,96,1536]{2,1,0:T(8,128)(2,1)}, u32[]{:S(2)}, u32[]{:S(2)}) collective-permute-start(bf16[4,96,1536]{2,1,0:T(8,128)(2,1)} %get-tuple-element.302.refs_4_), channel_id=1, source_target_pairs={{0,8},{8,0},{16,24},{24,16},{1,9},{9,1},{17,25},{25,17},{2,10},{10... | collective-permute-start | bytes 3538952 | tf_op jit(solution)/shard_map/ppermute | solution.py:991
  184.3 29.2 %collective-permute-start.29 = (bf16[4,96,1536]{2,1,0:T(8,128)(2,1)}, bf16[4,96,1536]{2,1,0:T(8,128)(2,1)}, u32[]{:S(2)}, u32[]{:S(2)}) collective-permute-start(bf16[4,96,1536]{2,1,0:T(8,128)(2,1)} %get-tuple-element.302.refs_4_), channel_id=1, source_target_pairs={{0,16},{8,24},{16,0},{24,8},{1,17},{9,25},{17,1},{25,9},{2,18},{10... | collective-permute-start | bytes 3538952 | tf_op jit(solution)/shard_map/ppermute | solution.py:991
  185.8 50.3 %collective-permute-start.30 = (bf16[4,96,1536]{2,1,0:T(8,128)(2,1)}, bf16[4,96,1536]{2,1,0:T(8,128)(2,1)}, u32[]{:S(2)}, u32[]{:S(2)}) collective-permute-start(bf16[4,96,1536]{2,1,0:T(8,128)(2,1)} %get-tuple-element.306.refs_12_), channel_id=1, source_target_pairs={{0,8},{8,0},{16,24},{24,16},{1,9},{9,1},{17,25},{25,17},{2,10},{10... | collective-permute-start | bytes 3538952 | tf_op jit(solution)/shard_map/ppermute | solution.py:991
  186.3 50.1 %collective-permute-start.31 = (bf16[4,96,1536]{2,1,0:T(8,128)(2,1)}, bf16[4,96,1536]{2,1,0:T(8,128)(2,1)}, u32[]{:S(2)}, u32[]{:S(2)}) collective-permute-start(bf16[4,96,1536]{2,1,0:T(8,128)(2,1)} %get-tuple-element.306.refs_12_), channel_id=1, source_target_pairs={{0,16},{8,24},{16,0},{24,8},{1,17},{9,25},{17,1},{25,9},{2,18},{10... | collective-permute-start | bytes 3538952 | tf_op jit(solution)/shard_map/ppermute | solution.py:991
  242.5 28.7 %collective-permute-start.37 = (bf16[4,96,1536]{2,1,0:T(8,128)(2,1)}, bf16[4,96,1536]{2,1,0:T(8,128)(2,1)}, u32[]{:S(2)}, u32[]{:S(2)}) collective-permute-start(bf16[4,96,1536]{2,1,0:T(8,128)(2,1)} %collective-permute-done.29.refs_8_), channel_id=1, source_target_pairs={{0,8},{8,0},{16,24},{24,16},{1,9},{9,1},{17,25},{25,17},{2,10},{10... | collective-permute-start | bytes 3538952 | tf_op jit(solution)/shard_map/ppermute | solution.py:991
  244.0 28.4 %collective-permute-start.38 = (bf16[4,96,1536]{2,1,0:T(8,128)(2,1)}, bf16[4,96,1536]{2,1,0:T(8,128)(2,1)}, u32[]{:S(2)}, u32[]{:S(2)}) collective-permute-start(bf16[4,96,1536]{2,1,0:T(8,128)(2,1)} %collective-permute-done.30.refs_14_), channel_id=1, source_target_pairs={{0,16},{8,24},{16,0},{24,8},{1,17},{9,25},{17,1},{25,9},{2,18},{10... | collective-permute-start | bytes 3538952 | tf_op jit(solution)/shard_map/ppermute | solution.py:991
  255.2 154.6 %all-reduce.12.cloned.1.call-start = ((), (), s32[]{:S(2)}) async-start(), calls=%async_computation.1 | async-start | bytes 3194880 | tf_op jit(solution)/shard_map/psum | solution.py:1219
  272.8 27.8 %collective-permute-start.42 = (bf16[4,96,1536]{2,1,0:T(8,128)(2,1)}, bf16[4,96,1536]{2,1,0:T(8,128)(2,1)}, u32[]{:S(2)}, u32[]{:S(2)}) collective-permute-start(bf16[4,96,1536]{2,1,0:T(8,128)(2,1)} %collective-permute-done.37.refs_10_), channel_id=1, source_target_pairs={{0,4},{4,0},{1,5},{5,1},{2,6},{6,2},{3,7},{7,3},{8,12},{12,8},{9,1... | collective-permute-start | bytes 3538952 | tf_op jit(solution)/shard_map/ppermute | solution.py:995
  273.3 27.3 %collective-permute-start.43 = (bf16[4,96,1536]{2,1,0:T(8,128)(2,1)}, bf16[4,96,1536]{2,1,0:T(8,128)(2,1)}, u32[]{:S(2)}, u32[]{:S(2)}) collective-permute-start(bf16[4,96,1536]{2,1,0:T(8,128)(2,1)} %get-tuple-element.306.refs_12_), channel_id=1, source_target_pairs={{0,4},{4,0},{1,5},{5,1},{2,6},{6,2},{3,7},{7,3},{8,12},{12,8},{9,1... | collective-permute-start | bytes 3538952 | tf_op jit(solution)/shard_map/ppermute | solution.py:995
  277.8 22.8 %collective-permute-start.44 = (bf16[4,96,1536]{2,1,0:T(8,128)(2,1)}, bf16[4,96,1536]{2,1,0:T(8,128)(2,1)S(1)}, u32[]{:S(2)}, u32[]{:S(2)}) collective-permute-start(bf16[4,96,1536]{2,1,0:T(8,128)(2,1)} %collective-permute-done.30.refs_14_), channel_id=1, source_target_pairs={{0,4},{4,0},{1,5},{5,1},{2,6},{6,2},{3,7},{7,3},{8,12},{12,8},{9,1... | collective-permute-start | bytes 3538952 | tf_op jit(solution)/shard_map/ppermute | solution.py:995
  278.0 22.7 %collective-permute-start.45 = (bf16[4,96,1536]{2,1,0:T(8,128)(2,1)}, bf16[4,96,1536]{2,1,0:T(8,128)(2,1)}, u32[]{:S(2)}, u32[]{:S(2)}) collective-permute-start(bf16[4,96,1536]{2,1,0:T(8,128)(2,1)} %collective-permute-done.31.refs_16_), channel_id=1, source_target_pairs={{0,4},{4,0},{1,5},{5,1},{2,6},{6,2},{3,7},{7,3},{8,12},{12,8},{9,1... | collective-permute-start | bytes 3538952 | tf_op jit(solution)/shard_map/ppermute | solution.py:995
  278.9 21.8 %collective-permute-start.46 = (bf16[4,96,1536]{2,1,0:T(8,128)(2,1)}, bf16[4,96,1536]{2,1,0:T(8,128)(2,1)}, u32[]{:S(2)}, u32[]{:S(2)}) collective-permute-start(bf16[4,96,1536]{2,1,0:T(8,128)(2,1)} %collective-permute-done.38.refs_18_), channel_id=1, source_target_pairs={{0,4},{4,0},{1,5},{5,1},{2,6},{6,2},{3,7},{7,3},{8,12},{12,8},{9,1... | collective-permute-start | bytes 3538952 | tf_op jit(solution)/shard_map/ppermute | solution.py:995
  340.1 15.0 %collective-permute-start.48 = (bf16[4,4,96,1536]{3,2,1,0:T(8,128)(2,1)}, bf16[4,4,96,1536]{3,2,1,0:T(8,128)(2,1)}, u32[]{:S(2)}, u32[]{:S(2)}) collective-permute-start(bf16[4,4,96,1536]{3,2,1,0:T(8,128)(2,1)} %get-tuple-element.314), channel_id=1, source_target_pairs={{0,4},{4,0},{1,5},{5,1},{2,6},{6,2},{3,7},{7,3},{8,12},{12,8},{9,1... | collective-permute-start | bytes 14155784 | tf_op jit(solution)/shard_map/ppermute | solution.py:995
  340.6 178.7 %all-reduce.14.cloned.1.call-start = ((), (), s32[]{:S(2)}) async-start(), calls=%async_computation.2 | async-start | bytes 3145728 | tf_op jit(solution)/shard_map/psum | solution.py:1258
  352.9 103.5 %collective-permute-start.50 = (bf16[2,4,96,1536]{3,2,1,0:T(8,128)(2,1)}, bf16[2,4,96,1536]{3,2,1,0:T(8,128)(2,1)S(1)}, u32[]{:S(2)}, u32[]{:S(2)}) collective-permute-start(bf16[2,4,96,1536]{3,2,1,0:T(8,128)(2,1)} %add_convert_fusion.3), channel_id=1, source_target_pairs={{0,8},{8,0},{16,24},{24,16},{1,9},{9,1},{17,25},{25,17},{2,10},{10... | collective-permute-start | bytes 7077896 | tf_op jit(solution)/shard_map/ppermute | solution.py:991
  358.8 100.6 %collective-permute-start.51 = (bf16[2,4,96,1536]{3,2,1,0:T(8,128)(2,1)}, bf16[2,4,96,1536]{3,2,1,0:T(8,128)(2,1)}, u32[]{:S(2)}, u32[]{:S(2)}) collective-permute-start(bf16[2,4,96,1536]{3,2,1,0:T(8,128)(2,1)} %add_convert_fusion.2), channel_id=1, source_target_pairs={{0,16},{8,24},{16,0},{24,8},{1,17},{9,25},{17,1},{25,9},{2,18},{10... | collective-permute-start | bytes 7077896 | tf_op jit(solution)/shard_map/ppermute | solution.py:991
  451.0 113.3 %all-reduce.16.cloned.1.call-start = ((), (), s32[]{:S(2)}) async-start(), calls=%async_computation.3 | async-start | bytes 1572864 | tf_op jit(solution)/shard_map/psum | solution.py:1217
  519.3 116.8 %all-reduce.18.cloned.1.call-start = ((), (), s32[]{:S(2)}) async-start(), calls=%async_computation.4 | async-start | bytes 3194880 | tf_op jit(solution)/shard_map/psum | solution.py:1219
  519.8 40.9 %collective-permute-start.54 = (f32[16,16]{1,0:T(8,128)S(1)}, f32[16,16]{1,0:T(8,128)S(1)}, u32[]{:S(2)}, u32[]{:S(2)}) collective-permute-start(f32[16,16]{1,0:T(8,128)S(1)} %add.202), channel_id=1, source_target_pairs={{0,16},{8,24},{16,0},{24,8},{1,17},{9,25},{17,1},{25,9},{2,18},{10... | collective-permute-start | bytes 3080 | tf_op jit(solution)/shard_map/ppermute | solution.py:991
  564.2 15.0 %collective-permute-start.58 = (bf16[4,4,96,1536]{3,2,1,0:T(8,128)(2,1)}, bf16[4,4,96,1536]{3,2,1,0:T(8,128)(2,1)}, u32[]{:S(2)}, u32[]{:S(2)}) collective-permute-start(bf16[4,4,96,1536]{3,2,1,0:T(8,128)(2,1)} %get-tuple-element.369), channel_id=1, source_target_pairs={{0,4},{4,0},{1,5},{5,1},{2,6},{6,2},{3,7},{7,3},{8,12},{12,8},{9,1... | collective-permute-start | bytes 14155784 | tf_op jit(solution)/shard_map/ppermute | solution.py:995
  564.8 116.5 %all-reduce.20.cloned.1.call-start = ((), (), s32[]{:S(2)}) async-start(), calls=%async_computation.5 | async-start | bytes 1572864 | tf_op jit(solution)/shard_map/psum | solution.py:1237
  564.8 28.9 %collective-permute-start.55 = (bf16[4,96,1536]{2,1,0:T(8,128)(2,1)S(1)}, bf16[4,96,1536]{2,1,0:T(8,128)(2,1)S(1)}, u32[]{:S(2)}, u32[]{:S(2)}) collective-permute-start(bf16[4,96,1536]{2,1,0:T(8,128)(2,1)S(1)} %fusion), channel_id=1, source_target_pairs={{0,16},{8,24},{16,0},{24,8},{1,17},{9,25},{17,1},{25,9},{2,18},{10... | collective-permute-start | bytes 3538952 | tf_op jit(solution)/shard_map/ppermute | solution.py:991
  566.4 29.1 %collective-permute-start.56 = (bf16[4,96,1536]{2,1,0:T(8,128)(2,1)}, bf16[4,96,1536]{2,1,0:T(8,128)(2,1)S(1)}, u32[]{:S(2)}, u32[]{:S(2)}) collective-permute-start(bf16[4,96,1536]{2,1,0:T(8,128)(2,1)} %fusion.1), channel_id=1, source_target_pairs={{0,8},{8,0},{16,24},{24,16},{1,9},{9,1},{17,25},{25,17},{2,10},{10... | collective-permute-start | bytes 3538952 | tf_op jit(solution)/shard_map/ppermute | solution.py:991
  576.9 104.3 %collective-permute-start.60 = (bf16[2,4,96,1536]{3,2,1,0:T(8,128)(2,1)}, bf16[2,4,96,1536]{3,2,1,0:T(8,128)(2,1)S(1)}, u32[]{:S(2)}, u32[]{:S(2)}) collective-permute-start(bf16[2,4,96,1536]{3,2,1,0:T(8,128)(2,1)} %add_convert_fusion.1), channel_id=1, source_target_pairs={{0,8},{8,0},{16,24},{24,16},{1,9},{9,1},{17,25},{25,17},{2,10},{10... | collective-permute-start | bytes 7077896 | tf_op jit(solution)/shard_map/ppermute | solution.py:991
  583.1 102.1 %collective-permute-start.61 = (bf16[2,4,96,1536]{3,2,1,0:T(8,128)(2,1)}, bf16[2,4,96,1536]{3,2,1,0:T(8,128)(2,1)}, u32[]{:S(2)}, u32[]{:S(2)}) collective-permute-start(bf16[2,4,96,1536]{3,2,1,0:T(8,128)(2,1)} %add_convert_fusion), channel_id=1, source_target_pairs={{0,16},{8,24},{16,0},{24,8},{1,17},{9,25},{17,1},{25,9},{2,18},{10... | collective-permute-start | bytes 7077896 | tf_op jit(solution)/shard_map/ppermute | solution.py:991
  636.1 132.7 %all-reduce.22.cloned.1.call-start = ((), (), s32[]{:S(2)}) async-start(), calls=%async_computation.6 | async-start | bytes 3145728 | tf_op jit(solution)/shard_map/psum | solution.py:1258
  636.4 52.4 %collective-permute-start.62 = (bf16[2,96,896]{2,1,0:T(8,128)(2,1)S(1)}, bf16[2,96,896]{2,1,0:T(8,128)(2,1)}, u32[]{:S(2)}, u32[]{:S(2)}) collective-permute-start(bf16[2,96,896]{2,1,0:T(8,128)(2,1)S(1)} %copy-done.30), channel_id=1, source_target_pairs={{0,8},{8,0},{16,24},{24,16},{1,9},{9,1},{17,25},{25,17},{2,10},{10... | collective-permute-start | bytes 1032200 | tf_op jit(solution)/shard_map/ppermute | solution.py:991
  688.7 33.6 %collective-permute-start.63 = (bf16[4,96,1536]{2,1,0:T(8,128)(2,1)}, bf16[4,96,1536]{2,1,0:T(8,128)(2,1)S(1)}, u32[]{:S(2)}, u32[]{:S(2)}) collective-permute-start(bf16[4,96,1536]{2,1,0:T(8,128)(2,1)} %fusion.2), channel_id=1, source_target_pairs={{0,16},{8,24},{16,0},{24,8},{1,17},{9,25},{17,1},{25,9},{2,18},{10... | collective-permute-start | bytes 3538952 | tf_op jit(solution)/shard_map/ppermute | solution.py:991
  690.2 32.1 %collective-permute-start.64 = (bf16[4,96,1536]{2,1,0:T(8,128)(2,1)}, bf16[4,96,1536]{2,1,0:T(8,128)(2,1)S(1)}, u32[]{:S(2)}, u32[]{:S(2)}) collective-permute-start(bf16[4,96,1536]{2,1,0:T(8,128)(2,1)} %fusion.3), channel_id=1, source_target_pairs={{0,8},{8,0},{16,24},{24,16},{1,9},{9,1},{17,25},{25,17},{2,10},{10... | collective-permute-start | bytes 3538952 | tf_op jit(solution)/shard_map/ppermute | solution.py:991
  692.7 28.4 %collective-permute-start.69 = (bf16[96,896]{1,0:T(8,128)(2,1)S(1)}, bf16[96,896]{1,0:T(8,128)(2,1)}, u32[]{:S(2)}, u32[]{:S(2)}) collective-permute-start(bf16[96,896]{1,0:T(8,128)(2,1)S(1)} %fusion.5), channel_id=1, source_target_pairs={{0,16},{8,24},{16,0},{24,8},{1,17},{9,25},{17,1},{25,9},{2,18},{10... | collective-permute-start | bytes 516104 | tf_op jit(solution)/shard_map/ppermute | solution.py:991
  745.1 29.3 %collective-permute-start.68 = (bf16[96,896]{1,0:T(8,128)(2,1)S(1)}, bf16[96,896]{1,0:T(8,128)(2,1)S(1)}, u32[]{:S(2)}, u32[]{:S(2)}) collective-permute-start(bf16[96,896]{1,0:T(8,128)(2,1)S(1)} %fusion.4), channel_id=1, source_target_pairs={{0,16},{8,24},{16,0},{24,8},{1,17},{9,25},{17,1},{25,9},{2,18},{10... | collective-permute-start | bytes 516104 | tf_op jit(solution)/shard_map/ppermute | solution.py:991
  (85 other events, 822.7 us)
Sparse Core Ops, SparseCore 0:
  83.1 35.3 all-gather.4
  167.0 66.4 all-reduce.9
  255.3 34.3 all-gather.6
  340.7 69.0 all-reduce.11
  451.1 68.1 all-reduce.13
  521.5 42.6 all-reduce.15
  566.6 69.4 all-reduce.17
  638.5 42.7 all-reduce.19
  701.3 67.5 all-reduce.21

commit v5 on v4

--- a/solution.py
+++ b/solution.py
@@ -725,14 +725,43 @@
     if bwd:
         gx_ref = refs.pop(0)
         dw_refs = [refs.pop(0) for _ in range(out_count)]
-    w_scr, hot_scr, pick_scr = refs.pop(0), refs.pop(0), refs.pop(0)
+    w_scr, sem_ref, hot_scr, pick_scr = (refs.pop(0) for _ in range(4))
     part_scr = refs.pop(0) if fwd else None
     if bwd:
         gpart_scr, raw_scr, gg_scr, dw_scr = refs
     expert = pl.program_id(0)
     last = pl.num_programs(0) - 1
-    width = w_scr.shape[1]
+    depth, width = w_scr.shape[0] // 2, w_scr.shape[1]
     units = width // 3
+
+    def move(each, target, start):
+        for ref, (off, first, number) in zip(w_refs, plan):
+
+            def one(ref=ref, off=off, first=first):
+                row = pl.multiple_of(offs_ref[off] * rows + target * depth, rows)
+                copy = pltpu.make_async_copy(
+                    ref.at[each - first], w_scr.at[pl.ds(row, rows)], sem_ref.at[target, off]
+                )
+                if start:
+                    copy.start()
+                else:
+                    copy.wait()
+
+            if number == NF:
+                one()
+            else:
+                pl.when((each >= first) & (each < first + number))(one)
+
+    slot = lax.rem(expert, 2)
+    here = pl.ds(pl.multiple_of(slot * depth, depth), depth)
+
+    @pl.when(expert == 0)
+    def _():
+        move(0 * expert, 0, True)
+
+    @pl.when(expert < last)
+    def _():
+        move(expert + 1, 1 - slot, True)
 
     @pl.when(expert == 0)
     def _():
@@ -760,18 +789,7 @@
     def combine(source, block):
         return mm(hot_scr[block], source[block], TN)
 
-    def fill(ref, off):
-        start = pl.multiple_of(offs_ref[off] * rows, rows)
-        w_scr[pl.ds(start, rows), :] = ref[0]
-
-    for ref, (off, first, number) in zip(w_refs, plan):
-        if number == NF:
-            fill(ref, off)
-        else:
-            pl.when((expert >= first) & (expert < first + number))(
-                functools.partial(fill, ref, off)
-            )
-
+    move(expert, slot, False)
     hot, gate_cols, masks = [], [], []
     first_row = pl.multiple_of(expert * CAP, CAP)
     for block in range(blocks):
@@ -786,13 +804,13 @@
         masks.append(mask)
     gate_col = jnp.concatenate(gate_cols, axis=0)
     picked = pick_scr[expert]
-    gate_up = mm(picked, w_scr[:, : 2 * units])
+    gate_up = mm(picked, w_scr[here, : 2 * units])
     gate_in, up_in = gate_up[:, :units], gate_up[:, units:]
     sigmoid = lax.logistic(gate_in)
     silu = gate_in * sigmoid
     hidden = (silu * up_in).astype(BF16)
     if fwd:
-        scaled = (mm(hidden, w_scr[:, 2 * units :], NT) * gate_col).astype(BF16)
+        scaled = (mm(hidden, w_scr[here, 2 * units :], NT) * gate_col).astype(BF16)
         for block in range(blocks):
             part_scr[block, pl.ds(first_row, CAP), :] = scaled[block * CAP : (block + 1) * CAP]
 
@@ -805,7 +823,7 @@
 
     if bwd:
         raw = raw_scr[expert]
-        grad_raw = mm(raw, w_scr[:, 2 * units :])
+        grad_raw = mm(raw, w_scr[here, 2 * units :])
         gate_dot = jnp.sum(hidden.astype(F32) * grad_raw, axis=1, keepdims=True)
         for block in range(blocks):
             row = jnp.sum(
@@ -821,7 +839,7 @@
         grad_gate = grad_hidden * up_in * sigmoid * (1.0 + gate_in * (1.0 - sigmoid))
         grad_up = grad_hidden * silu
         grad_gu = jnp.concatenate([grad_gate.astype(BF16), grad_up.astype(BF16)], axis=1)
-        grad_pick = mm(grad_gu, w_scr[:, : 2 * units], NT).astype(BF16)
+        grad_pick = mm(grad_gu, w_scr[here, : 2 * units], NT).astype(BF16)
         for block in range(blocks):
             gpart_scr[block, pl.ds(first_row, CAP), :] = grad_pick[block * CAP : (block + 1) * CAP]
         grad_result = (raw.astype(F32) * gate_col).astype(BF16)
@@ -863,16 +881,11 @@
 
     ins = [xm] + ([gh] if bwd else []) + [routes_t, gates_t]
     in_specs = [SMEM_SPEC] + [full_spec(item.shape) for item in ins]
-    for _, first, number in plan:
-        in_specs.append(
-            pl.BlockSpec(
-                (1, piece_rows, width),
-                lambda e, first=first, number=number: (jnp.clip(e - first, 0, number - 1), 0, 0),
-            )
-        )
+    in_specs += [pl.BlockSpec(memory_space=pl.ANY)] * len(plan)
     out_shape, out_specs, scratch = [], [], []
     scratch += [
-        pltpu.VMEM((feature_dim, width), BF16),
+        pltpu.VMEM((2 * feature_dim, width), BF16),
+        pltpu.SemaphoreType.DMA((2, offs.shape[0])),
         pltpu.VMEM((blocks, NF * CAP, BLOCK), BF16),
         pltpu.VMEM((NF, blocks * CAP, feature_dim), BF16),
     ]
@@ -1150,7 +1163,9 @@
                 swapped[0][0][2], swapped[0][1][1] = swap(lows[2]), swap(highs[1])
                 after, swapped[0] = tie(after, swapped[0])
                 if layer + 1 < layer_count:
-                    mid, wide[layer + 1] = tie((lows[1], highs[2]), wide[layer + 1])
+                    mid, wide[layer + 1], small[layer + 1] = tie(
+                        (lows[1], highs[2]), wide[layer + 1], small[layer + 1]
+                    )
                     lows[1], highs[2] = mid
             else:
                 (lows, highs), _ = tie((lows, highs), after)

time: 799 us -> 791 us (0.990)
    ppermute x32, waiting for transfers between devices: 132 us -> 123 us  [hop(): return lax.ppermute(value, 'fsdp', [(i, i ^ step) for i in range(4)])]
    unnamed x112 -> x116, local copies, waits for them, and re-layouts: 16.6 us -> 16.3 us
  transfers between devices with their start and end apart: 82 -> 82, of which waited for: 44 -> 46; matrix products, arithmetic and copies ran while one was open for 10% -> 10% of each run, Pallas kernels for 26% -> 26%
where the time goes in v5:
time: 791 us; the launch traced here: 783 us
  waiting for transfers between devices  357 us (45%)
  Pallas kernels  263 us (33%)
  starting transfers between devices  57.8 us (7%)
  other arithmetic  51.3 us (6%)
  local copies, waits for them, and re-layouts  38.6 us (5%)
  between operations  14.7 us (2%)
    ppermute x32, waiting for transfers between devices, hop(): return lax.ppermute(value, 'fsdp', [(i, i ^ step) for i in range(4)])  123 us
    pallas_call x3, Pallas kernels, experts(): pl.pallas_call(functools.partial(experts_kernel, fwd, bwd, blocks, plan,...  83.4 us
    psum x2, waiting for transfers between devices, per_device(): gx = lax.psum(gx, 'tp')  80.2 us
    psum x2, waiting for transfers between devices, per_device(): ga = lax.psum(ga_part, 'tp')  77.1 us
    ppermute x35, waiting for transfers between devices, swap(): return lax.ppermute(value, 'ctx', [(0, 1), (1, 0)])  43.4 us
    ppermute x32, starting transfers between devices, hop(): return lax.ppermute(value, 'fsdp', [(i, i ^ step) for i in range(4)])  39.6 us
    convert_element_type x12, other arithmetic, add_low(): return total.astype(BF16)  36.7 us
    pallas_call x2, Pallas kernels, attend_backward(): pl.pallas_call(functools.partial(attn_bwd_kernel, heads), grid=(rows // B...  29 us
  transfers between devices with their start and end apart: 82, of which 46 were waited for; matrix products, arithmetic and copies ran while one was open for 10% of the time, Pallas kernels for 26%

profile of v5, /device:TPU:0, one launch (start us, length us, event | category | flops | bytes accessed | tf_op | source)
XLA Modules:
  0.0 782.7 jit_solution(12000774694065665649)
XLA Ops:
  29.9 7.5 pack_wide.2
  37.5 4.4 collective-permute-done.6.refs_4_
  55.5 5.0 qkv_part.2.own_ref
  60.5 7.3 collective-permute-done.10.refs_7_.refs_8_
  68.8 3.8 collective-permute-done.14.other_ref
  73.7 8.4 %attend_forward.2 = (bf16[1536,128]{1,0:T(8,128)(2,1)}, f32[1024,8]{1,0:T(8,128)}) custom-call(s32[3]{0:T(128)} %pad_add_fusion.info_ref, bf16[1024,640]{1,0:T(8,128)(2,1)} %qkv_part.2.own_ref, bf16[1024,640]{1,0:T(8,128)(2,1)} %copy-done.4), custom_call_target="tpu_custom_call" | custom-call | flops 161061280 | bytes 196608 | tf_op jit(solution)/shard_map/attend_forward/pallas_call | solution.py:273
  87.5 7.5 pack_wide.3
  104.6 7.8 collective-permute-done.17.refs_5_.refs_6_
  114.4 4.2 all-gather.5.cloned.1.call-done
  118.6 10.2 %middle_part.2 = (f32[1024,768]{1,0:T(8,128)}, f32[1024,768]{1,0:T(8,128)}, bf16[1024,768]{1,0:T(8,128)(2,1)}, f32[8,1024]{1,0:T(8,128)}, f32[16,1024]{1,0:T(8,128)}) custom-call(s32[1]{0:T(128)} %bitcast.rank_ref, bf16[1024,768]{1,0:T(8,128)(2,1)} %bitcast.140, bf16[4,1536,128]{2,1,0:T(8,128)(2,1)} %bitcast.149, ...), custom_call_target="tpu_custom_call" | custom-call | flops 60397976 | bytes 629145 | tf_op jit(solution)/shard_map/middle_part/pallas_call | solution.py:476
  128.8 8.1 %collective-permute-done.20.refs_9_.refs_10_ = bf16[4,96,1536]{2,1,0:T(8,128)(2,1)} collective-permute-done((bf16[4,96,1536]{2,1,0:T(8,128)(2,1)S(1)}, bf16[4,96,1536]{2,1,0:T(8,128)(2,1)}, u32[]{:S(2)}, u32[]{:S(2)}) %collective-permute-start.20) | collective-permute-done | bytes 1179680 | tf_op jit(solution)/shard_map/ppermute | solution.py:1004
  143.8 16.8 %experts.3 = bf16[1024,768]{1,0:T(8,128)(2,1)} custom-call(s32[8]{0:T(128)} %iota_xor_fusion.offs_ref, bf16[1024,768]{1,0:T(8,128)(2,1)} %get-tuple-element.255.refs_0_, s32[8,1024]{1,0:T(8,128)} %get-tuple-element.507.refs_7_.refs_1_.refs_2_.refs_4_, f32[8,1024]{1,0:T(8,128)} %get-tuple-element.256.refs_2_.refs_3_.refs_5_, ...), custom_call_target="tpu_custom_call" | custom-call | flops 400000000 | bytes 1000000 | tf_op jit(solution)/shard_map/experts/pallas_call | solution.py:922
  164.2 6.6 collective-permute-done.25.refs_2_
  170.8 5.0 collective-permute-done.26.refs_4_
  186.8 3.8 prep.3
  190.6 15.8 %collective-permute-done.28.refs_6_ = bf16[4,96,1536]{2,1,0:T(8,128)(2,1)} collective-permute-done((bf16[4,96,1536]{2,1,0:T(8,128)(2,1)}, bf16[4,96,1536]{2,1,0:T(8,128)(2,1)}, u32[]{:S(2)}, u32[]{:S(2)}) %collective-permute-start.28) | collective-permute-done | bytes 1179680 | tf_op jit(solution)/shard_map/ppermute | solution.py:1004
  207.4 22.8 %collective-permute-done.30.refs_14_ = bf16[4,96,1536]{2,1,0:T(8,128)(2,1)} collective-permute-done((bf16[4,96,1536]{2,1,0:T(8,128)(2,1)}, bf16[4,96,1536]{2,1,0:T(8,128)(2,1)}, u32[]{:S(2)}, u32[]{:S(2)}) %collective-permute-start.30) | collective-permute-done | bytes 1179680 | tf_op jit(solution)/shard_map/ppermute | solution.py:1004
  230.5 5.9 qkv_part.3
  240.8 8.4 %attend_forward.3 = (bf16[1536,128]{1,0:T(8,128)(2,1)}, f32[1024,8]{1,0:T(8,128)}) custom-call(s32[3]{0:T(128)} %pad_add_fusion.info_ref, bf16[1024,640]{1,0:T(8,128)(2,1)} %get-tuple-element.286.own_ref, bf16[1024,640]{1,0:T(8,128)(2,1)} %copy-done.5), custom_call_target="tpu_custom_call" | custom-call | flops 161061280 | bytes 196608 | tf_op jit(solution)/shard_map/attend_forward/pallas_call | solution.py:273
  249.8 15.4 %collective-permute-done.37.refs_10_ = bf16[4,96,1536]{2,1,0:T(8,128)(2,1)} collective-permute-done((bf16[4,96,1536]{2,1,0:T(8,128)(2,1)}, bf16[4,96,1536]{2,1,0:T(8,128)(2,1)}, u32[]{:S(2)}, u32[]{:S(2)}) %collective-permute-start.37) | collective-permute-done | bytes 1179680 | tf_op jit(solution)/shard_map/ppermute | solution.py:1004
  275.1 8.6 %all-gather.7.cloned.1.call-done = bf16[6144,128]{1,0:T(8,128)(2,1)} async-done(((bf16[1536,128]{1,0:T(8,128)(2,1)}), bf16[6144,128]{1,0:T(8,128)(2,1)}) %all-gather.7.cloned.1.call-update) | async-done | bytes 1572880 | tf_op jit(solution)/shard_map/all_gather | solution.py:1205
  283.7 10.9 %middle_part.3 = (f32[1024,768]{1,0:T(8,128)}, f32[1024,768]{1,0:T(8,128)}, bf16[1024,768]{1,0:T(8,128)(2,1)}, f32[8,1024]{1,0:T(8,128)}, f32[16,1024]{1,0:T(8,128)}) custom-call(s32[1]{0:T(128)} %bitcast.rank_ref, f32[1024,768]{1,0:T(8,128)} %get-tuple-element.278.refs_0_.h_ref, bf16[4,1536,128]{2,1,0:T(8,128)(2,1)} %bitcast.151, ...), custom_call_target="tpu_custom_call" | custom-call | flops 60397976 | bytes 629145 | tf_op jit(solution)/shard_map/middle_part/pallas_call | solution.py:476
  295.7 35.8 %experts.4 = (bf16[1024,768]{1,0:T(8,128)(2,1)}, bf16[1040,768]{1,0:T(8,128)(2,1)}, bf16[4,4,96,1536]{3,2,1,0:T(8,128)(2,1)}, bf16[4,4,96,1536]{3,2,1,0:T(8,128)...) custom-call(s32[8]{0:T(128)} %iota_xor_fusion.offs_ref, ...), custom_call_target="tpu_custom_call" | custom-call | flops 1280000000 | bytes 2000000 | tf_op jit(solution)/shard_map/experts/pallas_call | solution.py:922
  332.4 7.5 collective-permute-done.47.refs_1_
  339.9 4.6 add_convert_fusion.3
  351.8 49.5 %all-reduce.12.cloned.1.call-done.refs_2_ = bf16[1040,768]{1,0:T(8,128)(2,1)} async-done(((bf16[1040,768]{1,0:T(8,128)(2,1)}), bf16[1040,768]{1,0:T(8,128)(2,1)}) %all-reduce.12.cloned.1.call-update) | async-done | bytes 1597456 | tf_op jit(solution)/shard_map/psum | solution.py:1234
  402.6 13.0 %gate_backward.2 = (f32[1024,768]{1,0:T(8,128)}, bf16[1024,192]{1,0:T(8,128)(2,1)}, f32[768,192]{1,0:T(8,128)}, f32[32,768]{1,0:T(8,128)}, f32[16,1024]{1,0:T(8,128)}, /*index=5*/f32[16,16]{1,0:T(8,128)}) custom-call(bf16[1024,768]{1,0:T(8,128)(2,1)} %bitcast.144, f32[1024,768]{1,0:T(8,128)} %get-tuple-element.295.refs_1_, ...), custom_call_target="tpu_custom_call" | custom-call | flops 30198988 | bytes 707788 | tf_op jit(solution)/shard_map/gate_backward/pallas_call | solution.py:625
  415.6 14.5 %attend_backward.2 = (f32[1024,576]{1,0:T(8,128)}, bf16[1024,640]{1,0:T(8,128)(2,1)}) custom-call(s32[3]{0:T(128)} %pad_add_fusion.info_ref, bf16[1024,640]{1,0:T(8,128)(2,1)} %get-tuple-element.286.own_ref, bf16[1024,640]{1,0:T(8,128)(2,1)} %copy-done.5, f32[1024,8]{1,0:T(8,128)} %get-tuple-element.320.lse_ref, bf16[1024,192]{1,0:T(8,128)(2,1)} %get-tuple-element.321.gctx_ref), custom_call_target="tpu_custom_call" | custom-call | flops 402653184 | bytes 353894 | tf_op jit(solution)/shard_map/attend_backward/pallas_call | solution.py:344
  434.5 8.0 %qkv_backward.2 = (bf16[1024,768]{1,0:T(8,128)(2,1)}, f32[768,576]{1,0:T(8,128)}, f32[8,768]{1,0:T(8,128)}) custom-call(f32[1024,576]{1,0:T(8,128)} %get-tuple-element.322.gown_ref, bf16[1024,640]{1,0:T(8,128)(2,1)} %copy-done.16, f32[1024,768]{1,0:T(8,128)} %get-tuple-element.278.refs_0_.h_ref, ...), custom_call_target="tpu_custom_call" | custom-call | flops 90596968 | bytes 393216 | tf_op jit(solution)/shard_map/qkv_backward/pallas_call | solution.py:668
  454.4 56.4 %all-reduce.14.cloned.1.call-done.ga_ref = bf16[1024,768]{1,0:T(8,128)(2,1)} async-done(((bf16[1024,768]{1,0:T(8,128)(2,1)}), bf16[1024,768]{1,0:T(8,128)(2,1)}) %all-reduce.14.cloned.1.call-update) | async-done | bytes 1572880 | tf_op jit(solution)/shard_map/psum | solution.py:1273
  512.7 6.3 norm_backward.2
  518.9 30.8 %experts.5 = (bf16[1040,768]{1,0:T(8,128)(2,1)}, bf16[4,4,96,1536]{3,2,1,0:T(8,128)(2,1)}, bf16[4,4,96,1536]{3,2,1,0:T(8,128)(2,1)}, bf16[4,4,96,1536]{3,2,1,0:T(8,128)(2,1)}, bf16[4,4,96,1536]{3,2,1,0:T(8,128)(2,1)}) custom-call(s32[8]{0:T(128)} %iota_xor_fusion.offs_ref, bf16[1024,768]{1,0:T(8,128)(2,1)} %get-tuple-element.255.refs_0_, ...), custom_call_target="tpu_custom_call" | custom-call | flops 880000000 | bytes 2000000 | tf_op jit(solution)/shard_map/experts/pallas_call | solution.py:922
  550.4 5.4 all-reduce.16.cloned.1.call-done
  559.4 4.7 collective-permute-done.57.refs_1_
  564.0 4.5 add_convert_fusion.1
  570.8 3.8 add_convert_fusion
  588.0 8.9 %final_sums.2 = (f32[2,8,96,2,512]{4,3,2,1,0:T(2,128)}, f32[2,8,96,512]{3,2,1,0:T(8,128)}) custom-call(bf16[4,4,96,1536]{3,2,1,0:T(8,128)(2,1)} %get-tuple-element.376.refs_0_, bf16[4,4,96,1536]{3,2,1,0:T(8,128)(2,1)} %collective-permute-done.47.refs_1_, bf16[2,4,96,1536]{3,2,1,0:T(8,128)(2,1)} %copy-done.3, bf16[4,96,1536]{2,1,0:T(8,128)(2,1)} %copy-done.22, ...), custom_call_target="tpu_custom_call" | custom-call | flops 500000 | bytes 707788 | tf_op jit(solution)/shard_map/final_sums/pallas_call | solution.py:984
  596.9 30.7 %all-reduce.18.cloned.1.call-done.refs_2_ = bf16[1040,768]{1,0:T(8,128)(2,1)} async-done(((bf16[1040,768]{1,0:T(8,128)(2,1)}), bf16[1040,768]{1,0:T(8,128)(2,1)}) %all-reduce.18.cloned.1.call-update) | async-done | bytes 1597456 | tf_op jit(solution)/shard_map/psum | solution.py:1234
  631.0 12.4 %gate_backward.3 = (f32[1024,768]{1,0:T(8,128)}, bf16[1024,192]{1,0:T(8,128)(2,1)}, f32[768,192]{1,0:T(8,128)}, f32[32,768]{1,0:T(8,128)}) custom-call(f32[1024,768]{1,0:T(8,128)} %get-tuple-element.336.refs_0_, f32[1024,768]{1,0:T(8,128)} %get-tuple-element.337.refs_1_, bf16[1040,768]{1,0:T(8,128)(2,1)} %all-reduce.18.cloned.1.call-done.refs_2_, ...), custom_call_target="tpu_custom_call" | custom-call | flops 30198988 | bytes 707788 | tf_op jit(solution)/shard_map/gate_backward/pallas_call | solution.py:625
  643.4 14.5 %attend_backward.3 = (f32[1024,576]{1,0:T(8,128)}, bf16[1024,640]{1,0:T(8,128)(2,1)}) custom-call(s32[3]{0:T(128)} %pad_add_fusion.info_ref, bf16[1024,640]{1,0:T(8,128)(2,1)} %qkv_part.2.own_ref, bf16[1024,640]{1,0:T(8,128)(2,1)} %copy-done.4, f32[1024,8]{1,0:T(8,128)} %get-tuple-element.294.lse_ref, bf16[1024,192]{1,0:T(8,128)(2,1)} %get-tuple-element.395.gctx_ref), custom_call_target="tpu_custom_call" | custom-call | flops 402653184 | bytes 353894 | tf_op jit(solution)/shard_map/attend_backward/pallas_call | solution.py:344
  657.9 14.9 %all-reduce.20.cloned.1.call-done = bf16[512,768]{1,0:T(8,128)(2,1)} async-done(((bf16[512,768]{1,0:T(8,128)(2,1)}), bf16[512,768]{1,0:T(8,128)(2,1)}) %all-reduce.20.cloned.1.call-update) | async-done | bytes 786448 | tf_op jit(solution)/shard_map/psum | solution.py:1252
  672.8 3.9 fusion.2
  684.9 7.8 qkv_backward.3
  692.7 19.9 %collective-permute-done.69 = bf16[96,896]{1,0:T(8,128)(2,1)} collective-permute-done((bf16[96,896]{1,0:T(8,128)(2,1)S(1)}, bf16[96,896]{1,0:T(8,128)(2,1)}, u32[]{:S(2)}, u32[]{:S(2)}) %collective-permute-start.69) | collective-permute-done | bytes 172064 | tf_op jit(solution)/shard_map/ppermute | solution.py:1004
  713.8 4.2 pack_grads.3
  725.8 9.8 %final_sums.3 = (f32[2,8,96,2,512]{4,3,2,1,0:T(2,128)}, f32[2,8,96,512]{3,2,1,0:T(8,128)}) custom-call(bf16[4,4,96,1536]{3,2,1,0:T(8,128)(2,1)} %get-tuple-element.436.refs_0_, bf16[4,4,96,1536]{3,2,1,0:T(8,128)(2,1)} %collective-permute-done.57.refs_1_, bf16[2,4,96,1536]{3,2,1,0:T(8,128)(2,1)} %copy-done.2, ...), custom_call_target="tpu_custom_call", output_to_operand_aliasing={{0}: (8, {}), {1}: (9, {})} | custom-call | flops 500000 | bytes 707788 | tf_op jit(solution)/shard_map/final_sums/pallas_call | solution.py:984
  739.7 20.7 %all-reduce.22.cloned.1.call-done.ga_ref = bf16[1024,768]{1,0:T(8,128)(2,1)} async-done(((bf16[1024,768]{1,0:T(8,128)(2,1)}), bf16[1024,768]{1,0:T(8,128)(2,1)}) %all-reduce.22.cloned.1.call-update) | async-done | bytes 1572880 | tf_op jit(solution)/shard_map/psum | solution.py:1273
  760.4 5.5 norm_backward.3
  (342 shorter events, 175.8 us)
Async XLA Ops:
  7.2 111.4 %all-gather.5.cloned.1.call-start = ((), (), s32[]{:S(2)}) async-start(), calls=%async_computation.7 | async-start | bytes 1966080 | tf_op jit(solution)/shard_map/all_gather | solution.py:1205
  8.2 16.0 %collective-permute-start = (bf16[2,96,192]{2,1,0:T(8,128)(2,1)S(1)}, bf16[2,96,192]{2,1,0:T(8,128)(2,1)S(1)}, u32[]{:S(2)}, u32[]{:S(2)}) collective-permute-start(bf16[2,96,192]{2,1,0:T(8,128)(2,1)S(1)} %bitcast.152), channel_id=1, source_target_pairs={{0,1},{1,2},{2,3},{3,0},{4,5},{5,6},{6,7},{7,4},{8,9},{9,10},{10,1... | collective-permute-start | bytes 221192 | tf_op jit(solution)/shard_map/ppermute | solution.py:1020
  29.9 14.6 %collective-permute-start.3 = (bf16[96,1536]{1,0:T(8,128)(2,1)S(1)}, bf16[96,1536]{1,0:T(8,128)(2,1)S(1)}, u32[]{:S(2)}, u32[]{:S(2)}) collective-permute-start(bf16[96,1536]{1,0:T(8,128)(2,1)S(1)} %concatenate.18.refs_0_), channel_id=1, source_target_pairs={{0,4},{4,0},{1,5},{5,1},{2,6},{6,2},{3,7},{7,3},{8,12},{12,8},{9,1... | collective-permute-start | bytes 884744 | tf_op jit(solution)/shard_map/ppermute | solution.py:1008
  41.9 25.9 %collective-permute-start.10 = (bf16[4,96,1536]{2,1,0:T(8,128)(2,1)}, bf16[4,96,1536]{2,1,0:T(8,128)(2,1)S(1)}, u32[]{:S(2)}, u32[]{:S(2)}) collective-permute-start(bf16[4,96,1536]{2,1,0:T(8,128)(2,1)} %get-tuple-element.257.refs_3_.refs_4_), channel_id=1, source_target_pairs={{0,16},{8,24},{16,0},{24,8},{1,17},{9,25},{17,1},{25,9},{2,18},{10... | collective-permute-start | bytes 3538952 | tf_op jit(solution)/shard_map/ppermute | solution.py:1004
  43.8 24.4 %collective-permute-start.11 = (bf16[4,96,1536]{2,1,0:T(8,128)(2,1)}, bf16[4,96,1536]{2,1,0:T(8,128)(2,1)}, u32[]{:S(2)}, u32[]{:S(2)}) collective-permute-start(bf16[4,96,1536]{2,1,0:T(8,128)(2,1)} %get-tuple-element.259.refs_11_.refs_12_), channel_id=1, source_target_pairs={{0,8},{8,0},{16,24},{24,16},{1,9},{9,1},{17,25},{25,17},{2,10},{10... | collective-permute-start | bytes 3538952 | tf_op jit(solution)/shard_map/ppermute | solution.py:1004
  44.0 24.2 %collective-permute-start.12 = (bf16[4,96,1536]{2,1,0:T(8,128)(2,1)}, bf16[4,96,1536]{2,1,0:T(8,128)(2,1)}, u32[]{:S(2)}, u32[]{:S(2)}) collective-permute-start(bf16[4,96,1536]{2,1,0:T(8,128)(2,1)} %get-tuple-element.257.refs_3_.refs_4_), channel_id=1, source_target_pairs={{0,4},{4,0},{1,5},{5,1},{2,6},{6,2},{3,7},{7,3},{8,12},{12,8},{9,1... | collective-permute-start | bytes 3538952 | tf_op jit(solution)/shard_map/ppermute | solution.py:1008
  44.0 24.2 %collective-permute-start.13 = (bf16[4,96,1536]{2,1,0:T(8,128)(2,1)}, bf16[4,96,1536]{2,1,0:T(8,128)(2,1)}, u32[]{:S(2)}, u32[]{:S(2)}) collective-permute-start(bf16[4,96,1536]{2,1,0:T(8,128)(2,1)} %get-tuple-element.259.refs_11_.refs_12_), channel_id=1, source_target_pairs={{0,4},{4,0},{1,5},{5,1},{2,6},{6,2},{3,7},{7,3},{8,12},{12,8},{9,1... | collective-permute-start | bytes 3538952 | tf_op jit(solution)/shard_map/ppermute | solution.py:1008
  83.1 147.4 %all-reduce.10.cloned.1.call-start = ((), (), s32[]{:S(2)}) async-start(), calls=%async_computation | async-start | bytes 3145728 | tf_op jit(solution)/shard_map/psum | solution.py:1217
  83.4 29.0 %collective-permute-start.17 = (bf16[4,96,1536]{2,1,0:T(8,128)(2,1)S(1)}, bf16[4,96,1536]{2,1,0:T(8,128)(2,1)}, u32[]{:S(2)}, u32[]{:S(2)}) collective-permute-start(bf16[4,96,1536]{2,1,0:T(8,128)(2,1)S(1)} %copy-done.6), channel_id=1, source_target_pairs={{0,8},{8,0},{16,24},{24,16},{1,9},{9,1},{17,25},{25,17},{2,10},{10... | collective-permute-start | bytes 3538952 | tf_op jit(solution)/shard_map/ppermute | solution.py:1004
  85.0 29.0 %collective-permute-start.18 = (bf16[4,96,1536]{2,1,0:T(8,128)(2,1)S(1)}, bf16[4,96,1536]{2,1,0:T(8,128)(2,1)}, u32[]{:S(2)}, u32[]{:S(2)}) collective-permute-start(bf16[4,96,1536]{2,1,0:T(8,128)(2,1)S(1)} %copy-done.7), channel_id=1, source_target_pairs={{0,16},{8,24},{16,0},{24,8},{1,17},{9,25},{17,1},{25,9},{2,18},{10... | collective-permute-start | bytes 3538952 | tf_op jit(solution)/shard_map/ppermute | solution.py:1004
  86.5 50.4 %collective-permute-start.20 = (bf16[4,96,1536]{2,1,0:T(8,128)(2,1)S(1)}, bf16[4,96,1536]{2,1,0:T(8,128)(2,1)}, u32[]{:S(2)}, u32[]{:S(2)}) collective-permute-start(bf16[4,96,1536]{2,1,0:T(8,128)(2,1)S(1)} %collective-permute-done.10.refs_7_.refs_8_), channel_id=1, source_target_pairs={{0,8},{8,0},{16,24},{24,16},{1,9},{9,1},{17,25},{25,17},{2,10},{10... | collective-permute-start | bytes 3538952 | tf_op jit(solution)/shard_map/ppermute | solution.py:1004
  87.0 51.1 %collective-permute-start.21 = (bf16[4,96,1536]{2,1,0:T(8,128)(2,1)}, bf16[4,96,1536]{2,1,0:T(8,128)(2,1)}, u32[]{:S(2)}, u32[]{:S(2)}) collective-permute-start(bf16[4,96,1536]{2,1,0:T(8,128)(2,1)} %collective-permute-done.11.refs_13_.refs_14_), channel_id=1, source_target_pairs={{0,16},{8,24},{16,0},{24,8},{1,17},{9,25},{17,1},{25,9},{2,18},{10... | collective-permute-start | bytes 3538952 | tf_op jit(solution)/shard_map/ppermute | solution.py:1004
  113.9 24.7 %collective-permute-start.19 = (bf16[4,96,1536]{2,1,0:T(8,128)(2,1)}, bf16[4,96,1536]{2,1,0:T(8,128)(2,1)S(1)}, u32[]{:S(2)}, u32[]{:S(2)}) collective-permute-start(bf16[4,96,1536]{2,1,0:T(8,128)(2,1)} %collective-permute-done.17.refs_5_.refs_6_), channel_id=1, source_target_pairs={{0,4},{4,0},{1,5},{5,1},{2,6},{6,2},{3,7},{7,3},{8,12},{12,8},{9,1... | collective-permute-start | bytes 3538952 | tf_op jit(solution)/shard_map/ppermute | solution.py:1008
  113.9 24.7 %collective-permute-start.23 = (bf16[4,96,1536]{2,1,0:T(8,128)(2,1)}, bf16[4,96,1536]{2,1,0:T(8,128)(2,1)S(1)}, u32[]{:S(2)}, u32[]{:S(2)}) collective-permute-start(bf16[4,96,1536]{2,1,0:T(8,128)(2,1)} %collective-permute-done.18.refs_15_.refs_16_), channel_id=1, source_target_pairs={{0,4},{4,0},{1,5},{5,1},{2,6},{6,2},{3,7},{7,3},{8,12},{12,8},{9,1... | collective-permute-start | bytes 3538952 | tf_op jit(solution)/shard_map/ppermute | solution.py:1008
  160.6 123.1 %all-gather.7.cloned.1.call-start = ((), (), s32[]{:S(2)}) async-start(), calls=%async_computation.8 | async-start | bytes 1966080 | tf_op jit(solution)/shard_map/all_gather | solution.py:1205
  161.3 14.5 %collective-permute-start.26 = (bf16[96,1536]{1,0:T(8,128)(2,1)}, bf16[96,1536]{1,0:T(8,128)(2,1)S(1)}, u32[]{:S(2)}, u32[]{:S(2)}) collective-permute-start(bf16[96,1536]{1,0:T(8,128)(2,1)} %concatenate.20.refs_0_), channel_id=1, source_target_pairs={{0,16},{8,24},{16,0},{24,8},{1,17},{9,25},{17,1},{25,9},{2,18},{10... | collective-permute-start | bytes 884744 | tf_op jit(solution)/shard_map/ppermute | solution.py:1004
  164.2 17.1 %collective-permute-start.32 = (bf16[96,1536]{1,0:T(8,128)(2,1)}, bf16[96,1536]{1,0:T(8,128)(2,1)S(1)}, u32[]{:S(2)}, u32[]{:S(2)}) collective-permute-start(bf16[96,1536]{1,0:T(8,128)(2,1)} %concatenate.20.refs_0_), channel_id=1, source_target_pairs={{0,4},{4,0},{1,5},{5,1},{2,6},{6,2},{3,7},{7,3},{8,12},{12,8},{9,1... | collective-permute-start | bytes 884744 | tf_op jit(solution)/shard_map/ppermute | solution.py:1008
  177.3 29.2 %collective-permute-start.28 = (bf16[4,96,1536]{2,1,0:T(8,128)(2,1)}, bf16[4,96,1536]{2,1,0:T(8,128)(2,1)}, u32[]{:S(2)}, u32[]{:S(2)}) collective-permute-start(bf16[4,96,1536]{2,1,0:T(8,128)(2,1)} %get-tuple-element.304.refs_4_), channel_id=1, source_target_pairs={{0,8},{8,0},{16,24},{24,16},{1,9},{9,1},{17,25},{25,17},{2,10},{10... | collective-permute-start | bytes 3538952 | tf_op jit(solution)/shard_map/ppermute | solution.py:1004
  178.1 29.2 %collective-permute-start.29 = (bf16[4,96,1536]{2,1,0:T(8,128)(2,1)}, bf16[4,96,1536]{2,1,0:T(8,128)(2,1)}, u32[]{:S(2)}, u32[]{:S(2)}) collective-permute-start(bf16[4,96,1536]{2,1,0:T(8,128)(2,1)} %get-tuple-element.304.refs_4_), channel_id=1, source_target_pairs={{0,16},{8,24},{16,0},{24,8},{1,17},{9,25},{17,1},{25,9},{2,18},{10... | collective-permute-start | bytes 3538952 | tf_op jit(solution)/shard_map/ppermute | solution.py:1004
  179.6 50.5 %collective-permute-start.30 = (bf16[4,96,1536]{2,1,0:T(8,128)(2,1)}, bf16[4,96,1536]{2,1,0:T(8,128)(2,1)}, u32[]{:S(2)}, u32[]{:S(2)}) collective-permute-start(bf16[4,96,1536]{2,1,0:T(8,128)(2,1)} %get-tuple-element.308.refs_12_), channel_id=1, source_target_pairs={{0,8},{8,0},{16,24},{24,16},{1,9},{9,1},{17,25},{25,17},{2,10},{10... | collective-permute-start | bytes 3538952 | tf_op jit(solution)/shard_map/ppermute | solution.py:1004
  180.2 50.2 %collective-permute-start.31 = (bf16[4,96,1536]{2,1,0:T(8,128)(2,1)}, bf16[4,96,1536]{2,1,0:T(8,128)(2,1)}, u32[]{:S(2)}, u32[]{:S(2)}) collective-permute-start(bf16[4,96,1536]{2,1,0:T(8,128)(2,1)} %get-tuple-element.308.refs_12_), channel_id=1, source_target_pairs={{0,16},{8,24},{16,0},{24,8},{1,17},{9,25},{17,1},{25,9},{2,18},{10... | collective-permute-start | bytes 3538952 | tf_op jit(solution)/shard_map/ppermute | solution.py:1004
  236.5 28.7 %collective-permute-start.37 = (bf16[4,96,1536]{2,1,0:T(8,128)(2,1)}, bf16[4,96,1536]{2,1,0:T(8,128)(2,1)}, u32[]{:S(2)}, u32[]{:S(2)}) collective-permute-start(bf16[4,96,1536]{2,1,0:T(8,128)(2,1)} %collective-permute-done.29.refs_8_), channel_id=1, source_target_pairs={{0,8},{8,0},{16,24},{24,16},{1,9},{9,1},{17,25},{25,17},{2,10},{10... | collective-permute-start | bytes 3538952 | tf_op jit(solution)/shard_map/ppermute | solution.py:1004
  238.0 28.4 %collective-permute-start.38 = (bf16[4,96,1536]{2,1,0:T(8,128)(2,1)}, bf16[4,96,1536]{2,1,0:T(8,128)(2,1)}, u32[]{:S(2)}, u32[]{:S(2)}) collective-permute-start(bf16[4,96,1536]{2,1,0:T(8,128)(2,1)} %collective-permute-done.30.refs_14_), channel_id=1, source_target_pairs={{0,16},{8,24},{16,0},{24,8},{1,17},{9,25},{17,1},{25,9},{2,18},{10... | collective-permute-start | bytes 3538952 | tf_op jit(solution)/shard_map/ppermute | solution.py:1004
  249.2 152.1 %all-reduce.12.cloned.1.call-start = ((), (), s32[]{:S(2)}) async-start(), calls=%async_computation.1 | async-start | bytes 3194880 | tf_op jit(solution)/shard_map/psum | solution.py:1234
  266.9 27.8 %collective-permute-start.42 = (bf16[4,96,1536]{2,1,0:T(8,128)(2,1)}, bf16[4,96,1536]{2,1,0:T(8,128)(2,1)}, u32[]{:S(2)}, u32[]{:S(2)}) collective-permute-start(bf16[4,96,1536]{2,1,0:T(8,128)(2,1)} %collective-permute-done.37.refs_10_), channel_id=1, source_target_pairs={{0,4},{4,0},{1,5},{5,1},{2,6},{6,2},{3,7},{7,3},{8,12},{12,8},{9,1... | collective-permute-start | bytes 3538952 | tf_op jit(solution)/shard_map/ppermute | solution.py:1008
  267.4 27.3 %collective-permute-start.43 = (bf16[4,96,1536]{2,1,0:T(8,128)(2,1)}, bf16[4,96,1536]{2,1,0:T(8,128)(2,1)}, u32[]{:S(2)}, u32[]{:S(2)}) collective-permute-start(bf16[4,96,1536]{2,1,0:T(8,128)(2,1)} %get-tuple-element.308.refs_12_), channel_id=1, source_target_pairs={{0,4},{4,0},{1,5},{5,1},{2,6},{6,2},{3,7},{7,3},{8,12},{12,8},{9,1... | collective-permute-start | bytes 3538952 | tf_op jit(solution)/shard_map/ppermute | solution.py:1008
  271.9 22.8 %collective-permute-start.44 = (bf16[4,96,1536]{2,1,0:T(8,128)(2,1)}, bf16[4,96,1536]{2,1,0:T(8,128)(2,1)S(1)}, u32[]{:S(2)}, u32[]{:S(2)}) collective-permute-start(bf16[4,96,1536]{2,1,0:T(8,128)(2,1)} %collective-permute-done.30.refs_14_), channel_id=1, source_target_pairs={{0,4},{4,0},{1,5},{5,1},{2,6},{6,2},{3,7},{7,3},{8,12},{12,8},{9,1... | collective-permute-start | bytes 3538952 | tf_op jit(solution)/shard_map/ppermute | solution.py:1008
  272.0 22.7 %collective-permute-start.45 = (bf16[4,96,1536]{2,1,0:T(8,128)(2,1)}, bf16[4,96,1536]{2,1,0:T(8,128)(2,1)}, u32[]{:S(2)}, u32[]{:S(2)}) collective-permute-start(bf16[4,96,1536]{2,1,0:T(8,128)(2,1)} %collective-permute-done.31.refs_16_), channel_id=1, source_target_pairs={{0,4},{4,0},{1,5},{5,1},{2,6},{6,2},{3,7},{7,3},{8,12},{12,8},{9,1... | collective-permute-start | bytes 3538952 | tf_op jit(solution)/shard_map/ppermute | solution.py:1008
  272.9 21.8 %collective-permute-start.46 = (bf16[4,96,1536]{2,1,0:T(8,128)(2,1)}, bf16[4,96,1536]{2,1,0:T(8,128)(2,1)}, u32[]{:S(2)}, u32[]{:S(2)}) collective-permute-start(bf16[4,96,1536]{2,1,0:T(8,128)(2,1)} %collective-permute-done.38.refs_18_), channel_id=1, source_target_pairs={{0,4},{4,0},{1,5},{5,1},{2,6},{6,2},{3,7},{7,3},{8,12},{12,8},{9,1... | collective-permute-start | bytes 3538952 | tf_op jit(solution)/shard_map/ppermute | solution.py:1008
  331.6 15.0 %collective-permute-start.48 = (bf16[4,4,96,1536]{3,2,1,0:T(8,128)(2,1)}, bf16[4,4,96,1536]{3,2,1,0:T(8,128)(2,1)}, u32[]{:S(2)}, u32[]{:S(2)}) collective-permute-start(bf16[4,4,96,1536]{3,2,1,0:T(8,128)(2,1)} %get-tuple-element.316), channel_id=1, source_target_pairs={{0,4},{4,0},{1,5},{5,1},{2,6},{6,2},{3,7},{7,3},{8,12},{12,8},{9,1... | collective-permute-start | bytes 14155784 | tf_op jit(solution)/shard_map/ppermute | solution.py:1008
  332.2 178.7 %all-reduce.14.cloned.1.call-start = ((), (), s32[]{:S(2)}) async-start(), calls=%async_computation.2 | async-start | bytes 3145728 | tf_op jit(solution)/shard_map/psum | solution.py:1273
  344.4 103.6 %collective-permute-start.50 = (bf16[2,4,96,1536]{3,2,1,0:T(8,128)(2,1)}, bf16[2,4,96,1536]{3,2,1,0:T(8,128)(2,1)S(1)}, u32[]{:S(2)}, u32[]{:S(2)}) collective-permute-start(bf16[2,4,96,1536]{3,2,1,0:T(8,128)(2,1)} %add_convert_fusion.3), channel_id=1, source_target_pairs={{0,8},{8,0},{16,24},{24,16},{1,9},{9,1},{17,25},{25,17},{2,10},{10... | collective-permute-start | bytes 7077896 | tf_op jit(solution)/shard_map/ppermute | solution.py:1004
  350.4 100.6 %collective-permute-start.51 = (bf16[2,4,96,1536]{3,2,1,0:T(8,128)(2,1)}, bf16[2,4,96,1536]{3,2,1,0:T(8,128)(2,1)}, u32[]{:S(2)}, u32[]{:S(2)}) collective-permute-start(bf16[2,4,96,1536]{3,2,1,0:T(8,128)(2,1)} %add_convert_fusion.2), channel_id=1, source_target_pairs={{0,16},{8,24},{16,0},{24,8},{1,17},{9,25},{17,1},{25,9},{2,18},{10... | collective-permute-start | bytes 7077896 | tf_op jit(solution)/shard_map/ppermute | solution.py:1004
  442.5 113.2 %all-reduce.16.cloned.1.call-start = ((), (), s32[]{:S(2)}) async-start(), calls=%async_computation.3 | async-start | bytes 1572864 | tf_op jit(solution)/shard_map/psum | solution.py:1232
  510.9 116.8 %all-reduce.18.cloned.1.call-start = ((), (), s32[]{:S(2)}) async-start(), calls=%async_computation.4 | async-start | bytes 3194880 | tf_op jit(solution)/shard_map/psum | solution.py:1234
  511.1 38.6 %collective-permute-start.54 = (f32[16,16]{1,0:T(8,128)S(1)}, f32[16,16]{1,0:T(8,128)S(1)}, u32[]{:S(2)}, u32[]{:S(2)}) collective-permute-start(f32[16,16]{1,0:T(8,128)S(1)} %add.202), channel_id=1, source_target_pairs={{0,16},{8,24},{16,0},{24,8},{1,17},{9,25},{17,1},{25,9},{2,18},{10... | collective-permute-start | bytes 3080 | tf_op jit(solution)/shard_map/ppermute | solution.py:1004
  555.8 15.0 %collective-permute-start.58 = (bf16[4,4,96,1536]{3,2,1,0:T(8,128)(2,1)}, bf16[4,4,96,1536]{3,2,1,0:T(8,128)(2,1)}, u32[]{:S(2)}, u32[]{:S(2)}) collective-permute-start(bf16[4,4,96,1536]{3,2,1,0:T(8,128)(2,1)} %get-tuple-element.371), channel_id=1, source_target_pairs={{0,4},{4,0},{1,5},{5,1},{2,6},{6,2},{3,7},{7,3},{8,12},{12,8},{9,1... | collective-permute-start | bytes 14155784 | tf_op jit(solution)/shard_map/ppermute | solution.py:1008
  556.3 116.5 %all-reduce.20.cloned.1.call-start = ((), (), s32[]{:S(2)}) async-start(), calls=%async_computation.5 | async-start | bytes 1572864 | tf_op jit(solution)/shard_map/psum | solution.py:1252
  556.4 28.9 %collective-permute-start.55 = (bf16[4,96,1536]{2,1,0:T(8,128)(2,1)S(1)}, bf16[4,96,1536]{2,1,0:T(8,128)(2,1)S(1)}, u32[]{:S(2)}, u32[]{:S(2)}) collective-permute-start(bf16[4,96,1536]{2,1,0:T(8,128)(2,1)S(1)} %fusion), channel_id=1, source_target_pairs={{0,16},{8,24},{16,0},{24,8},{1,17},{9,25},{17,1},{25,9},{2,18},{10... | collective-permute-start | bytes 3538952 | tf_op jit(solution)/shard_map/ppermute | solution.py:1004
  557.9 29.1 %collective-permute-start.56 = (bf16[4,96,1536]{2,1,0:T(8,128)(2,1)}, bf16[4,96,1536]{2,1,0:T(8,128)(2,1)S(1)}, u32[]{:S(2)}, u32[]{:S(2)}) collective-permute-start(bf16[4,96,1536]{2,1,0:T(8,128)(2,1)} %fusion.1), channel_id=1, source_target_pairs={{0,8},{8,0},{16,24},{24,16},{1,9},{9,1},{17,25},{25,17},{2,10},{10... | collective-permute-start | bytes 3538952 | tf_op jit(solution)/shard_map/ppermute | solution.py:1004
  568.6 104.2 %collective-permute-start.60 = (bf16[2,4,96,1536]{3,2,1,0:T(8,128)(2,1)}, bf16[2,4,96,1536]{3,2,1,0:T(8,128)(2,1)S(1)}, u32[]{:S(2)}, u32[]{:S(2)}) collective-permute-start(bf16[2,4,96,1536]{3,2,1,0:T(8,128)(2,1)} %add_convert_fusion.1), channel_id=1, source_target_pairs={{0,8},{8,0},{16,24},{24,16},{1,9},{9,1},{17,25},{25,17},{2,10},{10... | collective-permute-start | bytes 7077896 | tf_op jit(solution)/shard_map/ppermute | solution.py:1004
  574.6 102.1 %collective-permute-start.61 = (bf16[2,4,96,1536]{3,2,1,0:T(8,128)(2,1)}, bf16[2,4,96,1536]{3,2,1,0:T(8,128)(2,1)}, u32[]{:S(2)}, u32[]{:S(2)}) collective-permute-start(bf16[2,4,96,1536]{3,2,1,0:T(8,128)(2,1)} %add_convert_fusion), channel_id=1, source_target_pairs={{0,16},{8,24},{16,0},{24,8},{1,17},{9,25},{17,1},{25,9},{2,18},{10... | collective-permute-start | bytes 7077896 | tf_op jit(solution)/shard_map/ppermute | solution.py:1004
  627.7 132.7 %all-reduce.22.cloned.1.call-start = ((), (), s32[]{:S(2)}) async-start(), calls=%async_computation.6 | async-start | bytes 3145728 | tf_op jit(solution)/shard_map/psum | solution.py:1273
  628.2 52.1 %collective-permute-start.62 = (bf16[2,96,896]{2,1,0:T(8,128)(2,1)S(1)}, bf16[2,96,896]{2,1,0:T(8,128)(2,1)}, u32[]{:S(2)}, u32[]{:S(2)}) collective-permute-start(bf16[2,96,896]{2,1,0:T(8,128)(2,1)S(1)} %copy-done.32), channel_id=1, source_target_pairs={{0,8},{8,0},{16,24},{24,16},{1,9},{9,1},{17,25},{25,17},{2,10},{10... | collective-permute-start | bytes 1032200 | tf_op jit(solution)/shard_map/ppermute | solution.py:1004
  680.2 33.6 %collective-permute-start.63 = (bf16[4,96,1536]{2,1,0:T(8,128)(2,1)}, bf16[4,96,1536]{2,1,0:T(8,128)(2,1)S(1)}, u32[]{:S(2)}, u32[]{:S(2)}) collective-permute-start(bf16[4,96,1536]{2,1,0:T(8,128)(2,1)} %fusion.2), channel_id=1, source_target_pairs={{0,16},{8,24},{16,0},{24,8},{1,17},{9,25},{17,1},{25,9},{2,18},{10... | collective-permute-start | bytes 3538952 | tf_op jit(solution)/shard_map/ppermute | solution.py:1004
  681.7 32.1 %collective-permute-start.64 = (bf16[4,96,1536]{2,1,0:T(8,128)(2,1)}, bf16[4,96,1536]{2,1,0:T(8,128)(2,1)S(1)}, u32[]{:S(2)}, u32[]{:S(2)}) collective-permute-start(bf16[4,96,1536]{2,1,0:T(8,128)(2,1)} %fusion.3), channel_id=1, source_target_pairs={{0,8},{8,0},{16,24},{24,16},{1,9},{9,1},{17,25},{25,17},{2,10},{10... | collective-permute-start | bytes 3538952 | tf_op jit(solution)/shard_map/ppermute | solution.py:1004
  684.2 28.4 %collective-permute-start.69 = (bf16[96,896]{1,0:T(8,128)(2,1)S(1)}, bf16[96,896]{1,0:T(8,128)(2,1)}, u32[]{:S(2)}, u32[]{:S(2)}) collective-permute-start(bf16[96,896]{1,0:T(8,128)(2,1)S(1)} %fusion.5), channel_id=1, source_target_pairs={{0,16},{8,24},{16,0},{24,8},{1,17},{9,25},{17,1},{25,9},{2,18},{10... | collective-permute-start | bytes 516104 | tf_op jit(solution)/shard_map/ppermute | solution.py:1004
  736.6 29.3 %collective-permute-start.68 = (bf16[96,896]{1,0:T(8,128)(2,1)S(1)}, bf16[96,896]{1,0:T(8,128)(2,1)S(1)}, u32[]{:S(2)}, u32[]{:S(2)}) collective-permute-start(bf16[96,896]{1,0:T(8,128)(2,1)S(1)} %fusion.4), channel_id=1, source_target_pairs={{0,16},{8,24},{16,0},{24,8},{1,17},{9,25},{17,1},{25,9},{2,18},{10... | collective-permute-start | bytes 516104 | tf_op jit(solution)/shard_map/ppermute | solution.py:1004
  (87 other events, 818.3 us)
Sparse Core Ops, SparseCore 0:
  83.2 35.3 all-gather.4
  160.8 66.4 all-reduce.9
  249.3 34.3 all-gather.6
  332.3 68.9 all-reduce.11
  442.7 68.1 all-reduce.13
  513.1 42.6 all-reduce.15
  558.2 69.4 all-reduce.17
  630.0 42.6 all-reduce.19
  692.8 67.5 all-reduce.21

commit v6 on v5

--- a/solution.py
+++ b/solution.py
@@ -1203,6 +1203,10 @@
         other = fetch_rest(layer, qkv)
         context, lse = attend_forward(qkv, other, info, heads)
         ctx_all = lax.all_gather(fetch_cores(layer, context), "tp", axis=0)
+        if hyper and layer == 0:
+            lows, highs = rests[0]
+            swapped[0][0][1], swapped[0][1][2] = swap(lows[1]), swap(highs[2])
+            ctx_all, swapped[0] = tie(ctx_all, swapped[0])
         wo_all = weights[layer][1]
         middle, base, xm_low, gates_t, logits_t = middle_part(
             h_in, ctx_all, wo_all, vecs, routes_t[layer], prev_t, resid, rank

time: 791 us -> 782 us (0.989)
  waiting for transfers between devices: 357 us -> 347 us
    ppermute x32, waiting for transfers between devices: 123 us -> 105 us  [hop(): return lax.ppermute(value, 'fsdp', [(i, i ^ step) for i in range(4)])]
    all_gather x2, waiting for transfers between devices: 12.8 us -> 23.4 us  [per_device(): ctx_all = lax.all_gather(fetch_cores(layer, context), 'tp', axis=0)]
  transfers between devices with their start and end apart: 82 -> 82, of which waited for: 46 -> 43; matrix products, arithmetic and copies ran while one was open for 10% -> 10% of each run, Pallas kernels for 26% -> 26%
where the time goes in v6:
time: 782 us; the launch traced here: 774 us
  waiting for transfers between devices  347 us (44%)
  Pallas kernels  263 us (34%)
  starting transfers between devices  59.2 us (8%)
  other arithmetic  51.3 us (7%)
  local copies, waits for them, and re-layouts  38.4 us (5%)
  between operations  14.7 us (2%)
    ppermute x32, waiting for transfers between devices, hop(): return lax.ppermute(value, 'fsdp', [(i, i ^ step) for i in range(4)])  105 us
    pallas_call x3, Pallas kernels, experts(): pl.pallas_call(functools.partial(experts_kernel, fwd, bwd, blocks, plan,...  83.4 us
    psum x2, waiting for transfers between devices, per_device(): gx = lax.psum(gx, 'tp')  80.2 us
    psum x2, waiting for transfers between devices, per_device(): ga = lax.psum(ga_part, 'tp')  77.2 us
    ppermute x35, waiting for transfers between devices, swap(): return lax.ppermute(value, 'ctx', [(0, 1), (1, 0)])  41 us
    ppermute x32, starting transfers between devices, hop(): return lax.ppermute(value, 'fsdp', [(i, i ^ step) for i in range(4)])  40.9 us
    convert_element_type x12, other arithmetic, add_low(): return total.astype(BF16)  36.7 us
    pallas_call x2, Pallas kernels, attend_backward(): pl.pallas_call(functools.partial(attn_bwd_kernel, heads), grid=(rows // B...  29 us
  transfers between devices with their start and end apart: 82, of which 43 were waited for; matrix products, arithmetic and copies ran while one was open for 10% of the time, Pallas kernels for 26%

profile of v6, /device:TPU:0, one launch (start us, length us, event | category | flops | bytes accessed | tf_op | source)
XLA Modules:
  0.0 774.0 jit_solution(3451375310618577288)
XLA Ops:
  29.9 7.5 pack_wide.2
  37.4 4.4 collective-permute-done.6.refs_4_
  51.6 3.8 prep.2
  55.4 5.1 qkv_part.2.own_ref
  60.5 7.2 collective-permute-done.10.refs_7_.refs_8_
  73.6 8.4 %attend_forward.2 = (bf16[1536,128]{1,0:T(8,128)(2,1)}, f32[1024,8]{1,0:T(8,128)}) custom-call(s32[3]{0:T(128)} %pad_add_fusion.info_ref, bf16[1024,640]{1,0:T(8,128)(2,1)} %qkv_part.2.own_ref, bf16[1024,640]{1,0:T(8,128)(2,1)} %copy-done.4), custom_call_target="tpu_custom_call" | custom-call | flops 161061280 | bytes 196608 | tf_op jit(solution)/shard_map/attend_forward/pallas_call | solution.py:273
  83.3 7.6 pack_wide.3
  104.0 14.5 %all-gather.5.cloned.1.call-done = bf16[6144,128]{1,0:T(8,128)(2,1)} async-done(((bf16[1536,128]{1,0:T(8,128)(2,1)}), bf16[6144,128]{1,0:T(8,128)(2,1)}) %all-gather.5.cloned.1.call-update) | async-done | bytes 1572880 | tf_op jit(solution)/shard_map/all_gather | solution.py:1205
  118.5 10.2 %middle_part.2 = (f32[1024,768]{1,0:T(8,128)}, f32[1024,768]{1,0:T(8,128)}, bf16[1024,768]{1,0:T(8,128)(2,1)}, f32[8,1024]{1,0:T(8,128)}, f32[16,1024]{1,0:T(8,128)}) custom-call(s32[1]{0:T(128)} %bitcast.rank_ref, bf16[1024,768]{1,0:T(8,128)(2,1)} %bitcast.140, bf16[4,1536,128]{2,1,0:T(8,128)(2,1)} %bitcast.149, ...), custom_call_target="tpu_custom_call" | custom-call | flops 60397976 | bytes 629145 | tf_op jit(solution)/shard_map/middle_part/pallas_call | solution.py:476
  135.0 16.8 %experts.3 = bf16[1024,768]{1,0:T(8,128)(2,1)} custom-call(s32[8]{0:T(128)} %iota_xor_fusion.offs_ref, bf16[1024,768]{1,0:T(8,128)(2,1)} %get-tuple-element.273.refs_0_, s32[8,1024]{1,0:T(8,128)} %get-tuple-element.521.refs_7_.refs_1_.refs_2_.refs_4_, f32[8,1024]{1,0:T(8,128)} %get-tuple-element.274.refs_2_.refs_3_.refs_5_, ...), custom_call_target="tpu_custom_call" | custom-call | flops 400000000 | bytes 1000000 | tf_op jit(solution)/shard_map/experts/pallas_call | solution.py:922
  155.4 6.6 collective-permute-done.25.refs_2_
  162.0 5.4 collective-permute-done.26.refs_4_
  177.9 3.8 prep.3
  181.8 15.8 %collective-permute-done.28.refs_6_ = bf16[4,96,1536]{2,1,0:T(8,128)(2,1)} collective-permute-done((bf16[4,96,1536]{2,1,0:T(8,128)(2,1)}, bf16[4,96,1536]{2,1,0:T(8,128)(2,1)}, u32[]{:S(2)}, u32[]{:S(2)}) %collective-permute-start.28) | collective-permute-done | bytes 1179680 | tf_op jit(solution)/shard_map/ppermute | solution.py:1004
  198.6 22.6 %collective-permute-done.30.refs_14_ = bf16[4,96,1536]{2,1,0:T(8,128)(2,1)} collective-permute-done((bf16[4,96,1536]{2,1,0:T(8,128)(2,1)}, bf16[4,96,1536]{2,1,0:T(8,128)(2,1)}, u32[]{:S(2)}, u32[]{:S(2)}) %collective-permute-start.30) | collective-permute-done | bytes 1179680 | tf_op jit(solution)/shard_map/ppermute | solution.py:1004
  222.0 6.0 qkv_part.3
  232.4 8.4 %attend_forward.3 = (bf16[1536,128]{1,0:T(8,128)(2,1)}, f32[1024,8]{1,0:T(8,128)}) custom-call(s32[3]{0:T(128)} %pad_add_fusion.info_ref, bf16[1024,640]{1,0:T(8,128)(2,1)} %get-tuple-element.300.own_ref, bf16[1024,640]{1,0:T(8,128)(2,1)} %copy-done.5), custom_call_target="tpu_custom_call" | custom-call | flops 161061280 | bytes 196608 | tf_op jit(solution)/shard_map/attend_forward/pallas_call | solution.py:273
  241.4 15.4 %collective-permute-done.37.refs_10_ = bf16[4,96,1536]{2,1,0:T(8,128)(2,1)} collective-permute-done((bf16[4,96,1536]{2,1,0:T(8,128)(2,1)}, bf16[4,96,1536]{2,1,0:T(8,128)(2,1)}, u32[]{:S(2)}, u32[]{:S(2)}) %collective-permute-start.37) | collective-permute-done | bytes 1179680 | tf_op jit(solution)/shard_map/ppermute | solution.py:1004
  266.2 8.9 %all-gather.7.cloned.1.call-done = bf16[6144,128]{1,0:T(8,128)(2,1)} async-done(((bf16[1536,128]{1,0:T(8,128)(2,1)}), bf16[6144,128]{1,0:T(8,128)(2,1)}) %all-gather.7.cloned.1.call-update) | async-done | bytes 1572880 | tf_op jit(solution)/shard_map/all_gather | solution.py:1205
  275.1 10.9 %middle_part.3 = (f32[1024,768]{1,0:T(8,128)}, f32[1024,768]{1,0:T(8,128)}, bf16[1024,768]{1,0:T(8,128)(2,1)}, f32[8,1024]{1,0:T(8,128)}, f32[16,1024]{1,0:T(8,128)}) custom-call(s32[1]{0:T(128)} %bitcast.rank_ref, f32[1024,768]{1,0:T(8,128)} %get-tuple-element.292.refs_0_.h_ref, bf16[4,1536,128]{2,1,0:T(8,128)(2,1)} %bitcast.151, ...), custom_call_target="tpu_custom_call" | custom-call | flops 60397976 | bytes 629145 | tf_op jit(solution)/shard_map/middle_part/pallas_call | solution.py:476
  287.1 35.9 %experts.4 = (bf16[1024,768]{1,0:T(8,128)(2,1)}, bf16[1040,768]{1,0:T(8,128)(2,1)}, bf16[4,4,96,1536]{3,2,1,0:T(8,128)(2,1)}, bf16[4,4,96,1536]{3,2,1,0:T(8,128)...) custom-call(s32[8]{0:T(128)} %iota_xor_fusion.offs_ref, ...), custom_call_target="tpu_custom_call" | custom-call | flops 1280000000 | bytes 2000000 | tf_op jit(solution)/shard_map/experts/pallas_call | solution.py:922
  323.8 7.5 collective-permute-done.47.refs_1_
  331.3 4.6 add_convert_fusion.3
  338.0 3.7 add_convert_fusion.2
  343.3 49.4 %all-reduce.12.cloned.1.call-done.refs_2_ = bf16[1040,768]{1,0:T(8,128)(2,1)} async-done(((bf16[1040,768]{1,0:T(8,128)(2,1)}), bf16[1040,768]{1,0:T(8,128)(2,1)}) %all-reduce.12.cloned.1.call-update) | async-done | bytes 1597456 | tf_op jit(solution)/shard_map/psum | solution.py:1238
  394.0 13.0 %gate_backward.2 = (f32[1024,768]{1,0:T(8,128)}, bf16[1024,192]{1,0:T(8,128)(2,1)}, f32[768,192]{1,0:T(8,128)}, f32[32,768]{1,0:T(8,128)}, f32[16,1024]{1,0:T(8,128)}, /*index=5*/f32[16,16]{1,0:T(8,128)}) custom-call(bf16[1024,768]{1,0:T(8,128)(2,1)} %bitcast.144, f32[1024,768]{1,0:T(8,128)} %get-tuple-element.309.refs_1_, ...), custom_call_target="tpu_custom_call" | custom-call | flops 30198988 | bytes 707788 | tf_op jit(solution)/shard_map/gate_backward/pallas_call | solution.py:625
  407.0 14.5 %attend_backward.2 = (f32[1024,576]{1,0:T(8,128)}, bf16[1024,640]{1,0:T(8,128)(2,1)}) custom-call(s32[3]{0:T(128)} %pad_add_fusion.info_ref, bf16[1024,640]{1,0:T(8,128)(2,1)} %get-tuple-element.300.own_ref, bf16[1024,640]{1,0:T(8,128)(2,1)} %copy-done.5, f32[1024,8]{1,0:T(8,128)} %get-tuple-element.334.lse_ref, bf16[1024,192]{1,0:T(8,128)(2,1)} %get-tuple-element.335.gctx_ref), custom_call_target="tpu_custom_call" | custom-call | flops 402653184 | bytes 353894 | tf_op jit(solution)/shard_map/attend_backward/pallas_call | solution.py:344
  425.8 8.0 %qkv_backward.2 = (bf16[1024,768]{1,0:T(8,128)(2,1)}, f32[768,576]{1,0:T(8,128)}, f32[8,768]{1,0:T(8,128)}) custom-call(f32[1024,576]{1,0:T(8,128)} %get-tuple-element.336.gown_ref, bf16[1024,640]{1,0:T(8,128)(2,1)} %copy-done.16, f32[1024,768]{1,0:T(8,128)} %get-tuple-element.292.refs_0_.h_ref, ...), custom_call_target="tpu_custom_call" | custom-call | flops 90596968 | bytes 393216 | tf_op jit(solution)/shard_map/qkv_backward/pallas_call | solution.py:668
  445.8 56.4 %all-reduce.14.cloned.1.call-done.ga_ref = bf16[1024,768]{1,0:T(8,128)(2,1)} async-done(((bf16[1024,768]{1,0:T(8,128)(2,1)}), bf16[1024,768]{1,0:T(8,128)(2,1)}) %all-reduce.14.cloned.1.call-update) | async-done | bytes 1572880 | tf_op jit(solution)/shard_map/psum | solution.py:1277
  504.0 6.3 norm_backward.2
  510.3 30.8 %experts.5 = (bf16[1040,768]{1,0:T(8,128)(2,1)}, bf16[4,4,96,1536]{3,2,1,0:T(8,128)(2,1)}, bf16[4,4,96,1536]{3,2,1,0:T(8,128)(2,1)}, bf16[4,4,96,1536]{3,2,1,0:T(8,128)(2,1)}, bf16[4,4,96,1536]{3,2,1,0:T(8,128)(2,1)}) custom-call(s32[8]{0:T(128)} %iota_xor_fusion.offs_ref, bf16[1024,768]{1,0:T(8,128)(2,1)} %get-tuple-element.273.refs_0_, ...), custom_call_target="tpu_custom_call" | custom-call | flops 880000000 | bytes 2000000 | tf_op jit(solution)/shard_map/experts/pallas_call | solution.py:922
  541.7 5.5 all-reduce.16.cloned.1.call-done
  550.8 4.6 collective-permute-done.57.refs_1_
  555.4 4.5 add_convert_fusion.1
  562.2 3.8 add_convert_fusion
  579.4 8.9 %final_sums.2 = (f32[2,8,96,2,512]{4,3,2,1,0:T(2,128)}, f32[2,8,96,512]{3,2,1,0:T(8,128)}) custom-call(bf16[4,4,96,1536]{3,2,1,0:T(8,128)(2,1)} %get-tuple-element.390.refs_0_, bf16[4,4,96,1536]{3,2,1,0:T(8,128)(2,1)} %collective-permute-done.47.refs_1_, bf16[2,4,96,1536]{3,2,1,0:T(8,128)(2,1)} %copy-done.3, bf16[4,96,1536]{2,1,0:T(8,128)(2,1)} %copy-done.22, ...), custom_call_target="tpu_custom_call" | custom-call | flops 500000 | bytes 707788 | tf_op jit(solution)/shard_map/final_sums/pallas_call | solution.py:984
  588.3 30.7 %all-reduce.18.cloned.1.call-done.refs_2_ = bf16[1040,768]{1,0:T(8,128)(2,1)} async-done(((bf16[1040,768]{1,0:T(8,128)(2,1)}), bf16[1040,768]{1,0:T(8,128)(2,1)}) %all-reduce.18.cloned.1.call-update) | async-done | bytes 1597456 | tf_op jit(solution)/shard_map/psum | solution.py:1238
  622.4 12.4 %gate_backward.3 = (f32[1024,768]{1,0:T(8,128)}, bf16[1024,192]{1,0:T(8,128)(2,1)}, f32[768,192]{1,0:T(8,128)}, f32[32,768]{1,0:T(8,128)}) custom-call(f32[1024,768]{1,0:T(8,128)} %get-tuple-element.350.refs_0_, f32[1024,768]{1,0:T(8,128)} %get-tuple-element.351.refs_1_, bf16[1040,768]{1,0:T(8,128)(2,1)} %all-reduce.18.cloned.1.call-done.refs_2_, ...), custom_call_target="tpu_custom_call" | custom-call | flops 30198988 | bytes 707788 | tf_op jit(solution)/shard_map/gate_backward/pallas_call | solution.py:625
  634.8 14.5 %attend_backward.3 = (f32[1024,576]{1,0:T(8,128)}, bf16[1024,640]{1,0:T(8,128)(2,1)}) custom-call(s32[3]{0:T(128)} %pad_add_fusion.info_ref, bf16[1024,640]{1,0:T(8,128)(2,1)} %qkv_part.2.own_ref, bf16[1024,640]{1,0:T(8,128)(2,1)} %copy-done.4, f32[1024,8]{1,0:T(8,128)} %get-tuple-element.308.lse_ref, bf16[1024,192]{1,0:T(8,128)(2,1)} %get-tuple-element.409.gctx_ref), custom_call_target="tpu_custom_call" | custom-call | flops 402653184 | bytes 353894 | tf_op jit(solution)/shard_map/attend_backward/pallas_call | solution.py:344
  649.3 14.8 %all-reduce.20.cloned.1.call-done = bf16[512,768]{1,0:T(8,128)(2,1)} async-done(((bf16[512,768]{1,0:T(8,128)(2,1)}), bf16[512,768]{1,0:T(8,128)(2,1)}) %all-reduce.20.cloned.1.call-update) | async-done | bytes 786448 | tf_op jit(solution)/shard_map/psum | solution.py:1256
  664.2 3.9 fusion.2
  668.1 3.5 fusion.3
  676.2 7.8 %qkv_backward.3 = (bf16[1024,768]{1,0:T(8,128)(2,1)}, f32[768,576]{1,0:T(8,128)}, f32[8,768]{1,0:T(8,128)}) custom-call(f32[1024,576]{1,0:T(8,128)} %get-tuple-element.428.gown_ref, bf16[1024,640]{1,0:T(8,128)(2,1)} %collective-permute-done.65.goth_ref, bf16[1024,768]{1,0:T(8,128)(2,1)} %bitcast.141, ...), custom_call_target="tpu_custom_call" | custom-call | flops 90596968 | bytes 393216 | tf_op jit(solution)/shard_map/qkv_backward/pallas_call | solution.py:668
  684.1 19.9 %collective-permute-done.69 = bf16[96,896]{1,0:T(8,128)(2,1)} collective-permute-done((bf16[96,896]{1,0:T(8,128)(2,1)S(1)}, bf16[96,896]{1,0:T(8,128)(2,1)}, u32[]{:S(2)}, u32[]{:S(2)}) %collective-permute-start.69) | collective-permute-done | bytes 172064 | tf_op jit(solution)/shard_map/ppermute | solution.py:1004
  705.2 4.2 pack_grads.3
  717.1 9.8 %final_sums.3 = (f32[2,8,96,2,512]{4,3,2,1,0:T(2,128)}, f32[2,8,96,512]{3,2,1,0:T(8,128)}) custom-call(bf16[4,4,96,1536]{3,2,1,0:T(8,128)(2,1)} %get-tuple-element.450.refs_0_, bf16[4,4,96,1536]{3,2,1,0:T(8,128)(2,1)} %collective-permute-done.57.refs_1_, bf16[2,4,96,1536]{3,2,1,0:T(8,128)(2,1)} %copy-done.2, ...), custom_call_target="tpu_custom_call", output_to_operand_aliasing={{0}: (8, {}), {1}: (9, {})} | custom-call | flops 500000 | bytes 707788 | tf_op jit(solution)/shard_map/final_sums/pallas_call | solution.py:984
  731.0 20.7 %all-reduce.22.cloned.1.call-done.ga_ref = bf16[1024,768]{1,0:T(8,128)(2,1)} async-done(((bf16[1024,768]{1,0:T(8,128)(2,1)}), bf16[1024,768]{1,0:T(8,128)(2,1)}) %all-reduce.22.cloned.1.call-update) | async-done | bytes 1572880 | tf_op jit(solution)/shard_map/psum | solution.py:1277
  751.8 5.5 norm_backward.3
  (342 shorter events, 164.8 us)
Async XLA Ops:
  7.2 111.3 %all-gather.5.cloned.1.call-start = ((), (), s32[]{:S(2)}) async-start(), calls=%async_computation.7 | async-start | bytes 1966080 | tf_op jit(solution)/shard_map/all_gather | solution.py:1205
  8.2 15.9 %collective-permute-start = (bf16[2,96,192]{2,1,0:T(8,128)(2,1)S(1)}, bf16[2,96,192]{2,1,0:T(8,128)(2,1)S(1)}, u32[]{:S(2)}, u32[]{:S(2)}) collective-permute-start(bf16[2,96,192]{2,1,0:T(8,128)(2,1)S(1)} %bitcast.152), channel_id=1, source_target_pairs={{0,1},{1,2},{2,3},{3,0},{4,5},{5,6},{6,7},{7,4},{8,9},{9,10},{10,1... | collective-permute-start | bytes 221192 | tf_op jit(solution)/shard_map/ppermute | solution.py:1020
  29.8 14.6 %collective-permute-start.3 = (bf16[96,1536]{1,0:T(8,128)(2,1)S(1)}, bf16[96,1536]{1,0:T(8,128)(2,1)S(1)}, u32[]{:S(2)}, u32[]{:S(2)}) collective-permute-start(bf16[96,1536]{1,0:T(8,128)(2,1)S(1)} %concatenate.18.refs_0_), channel_id=1, source_target_pairs={{0,4},{4,0},{1,5},{5,1},{2,6},{6,2},{3,7},{7,3},{8,12},{12,8},{9,1... | collective-permute-start | bytes 884744 | tf_op jit(solution)/shard_map/ppermute | solution.py:1008
  41.8 25.9 %collective-permute-start.10 = (bf16[4,96,1536]{2,1,0:T(8,128)(2,1)}, bf16[4,96,1536]{2,1,0:T(8,128)(2,1)S(1)}, u32[]{:S(2)}, u32[]{:S(2)}) collective-permute-start(bf16[4,96,1536]{2,1,0:T(8,128)(2,1)} %get-tuple-element.258.refs_3_.refs_4_), channel_id=1, source_target_pairs={{0,16},{8,24},{16,0},{24,8},{1,17},{9,25},{17,1},{25,9},{2,18},{10... | collective-permute-start | bytes 3538952 | tf_op jit(solution)/shard_map/ppermute | solution.py:1004
  43.7 24.4 %collective-permute-start.11 = (bf16[4,96,1536]{2,1,0:T(8,128)(2,1)}, bf16[4,96,1536]{2,1,0:T(8,128)(2,1)}, u32[]{:S(2)}, u32[]{:S(2)}) collective-permute-start(bf16[4,96,1536]{2,1,0:T(8,128)(2,1)} %get-tuple-element.259.refs_11_.refs_12_), channel_id=1, source_target_pairs={{0,8},{8,0},{16,24},{24,16},{1,9},{9,1},{17,25},{25,17},{2,10},{10... | collective-permute-start | bytes 3538952 | tf_op jit(solution)/shard_map/ppermute | solution.py:1004
  43.9 24.2 %collective-permute-start.12 = (bf16[4,96,1536]{2,1,0:T(8,128)(2,1)}, bf16[4,96,1536]{2,1,0:T(8,128)(2,1)}, u32[]{:S(2)}, u32[]{:S(2)}) collective-permute-start(bf16[4,96,1536]{2,1,0:T(8,128)(2,1)} %get-tuple-element.258.refs_3_.refs_4_), channel_id=1, source_target_pairs={{0,4},{4,0},{1,5},{5,1},{2,6},{6,2},{3,7},{7,3},{8,12},{12,8},{9,1... | collective-permute-start | bytes 3538952 | tf_op jit(solution)/shard_map/ppermute | solution.py:1008
  43.9 24.2 %collective-permute-start.13 = (bf16[4,96,1536]{2,1,0:T(8,128)(2,1)}, bf16[4,96,1536]{2,1,0:T(8,128)(2,1)}, u32[]{:S(2)}, u32[]{:S(2)}) collective-permute-start(bf16[4,96,1536]{2,1,0:T(8,128)(2,1)} %get-tuple-element.259.refs_11_.refs_12_), channel_id=1, source_target_pairs={{0,4},{4,0},{1,5},{5,1},{2,6},{6,2},{3,7},{7,3},{8,12},{12,8},{9,1... | collective-permute-start | bytes 3538952 | tf_op jit(solution)/shard_map/ppermute | solution.py:1008
  68.6 14.4 %collective-permute-start.16 = (bf16[4,96,1536]{2,1,0:T(8,128)(2,1)}, bf16[4,96,1536]{2,1,0:T(8,128)(2,1)}, u32[]{:S(2)}, u32[]{:S(2)}) collective-permute-start(bf16[4,96,1536]{2,1,0:T(8,128)(2,1)} %collective-permute-done.11.refs_13_.refs_14_), channel_id=1, source_target_pairs={{0,4},{4,0},{1,5},{5,1},{2,6},{6,2},{3,7},{7,3},{8,12},{12,8},{9,1... | collective-permute-start | bytes 3538952 | tf_op jit(solution)/shard_map/ppermute | solution.py:1008
  68.7 30.4 %collective-permute-start.17 = (bf16[4,96,1536]{2,1,0:T(8,128)(2,1)S(1)}, bf16[4,96,1536]{2,1,0:T(8,128)(2,1)}, u32[]{:S(2)}, u32[]{:S(2)}) collective-permute-start(bf16[4,96,1536]{2,1,0:T(8,128)(2,1)S(1)} %copy-done.6), channel_id=1, source_target_pairs={{0,8},{8,0},{16,24},{24,16},{1,9},{9,1},{17,25},{25,17},{2,10},{10... | collective-permute-start | bytes 3538952 | tf_op jit(solution)/shard_map/ppermute | solution.py:1004
  70.2 28.9 %collective-permute-start.18 = (bf16[4,96,1536]{2,1,0:T(8,128)(2,1)S(1)}, bf16[4,96,1536]{2,1,0:T(8,128)(2,1)}, u32[]{:S(2)}, u32[]{:S(2)}) collective-permute-start(bf16[4,96,1536]{2,1,0:T(8,128)(2,1)S(1)} %copy-done.7), channel_id=1, source_target_pairs={{0,16},{8,24},{16,0},{24,8},{1,17},{9,25},{17,1},{25,9},{2,18},{10... | collective-permute-start | bytes 3538952 | tf_op jit(solution)/shard_map/ppermute | solution.py:1004
  83.0 139.0 %all-reduce.10.cloned.1.call-start = ((), (), s32[]{:S(2)}) async-start(), calls=%async_computation | async-start | bytes 3145728 | tf_op jit(solution)/shard_map/psum | solution.py:1221
  99.7 29.0 %collective-permute-start.21 = (bf16[4,96,1536]{2,1,0:T(8,128)(2,1)S(1)}, bf16[4,96,1536]{2,1,0:T(8,128)(2,1)}, u32[]{:S(2)}, u32[]{:S(2)}) collective-permute-start(bf16[4,96,1536]{2,1,0:T(8,128)(2,1)S(1)} %collective-permute-done.10.refs_7_.refs_8_), channel_id=1, source_target_pairs={{0,8},{8,0},{16,24},{24,16},{1,9},{9,1},{17,25},{25,17},{2,10},{10... | collective-permute-start | bytes 3538952 | tf_op jit(solution)/shard_map/ppermute | solution.py:1004
  101.2 28.1 %collective-permute-start.22 = (bf16[4,96,1536]{2,1,0:T(8,128)(2,1)}, bf16[4,96,1536]{2,1,0:T(8,128)(2,1)}, u32[]{:S(2)}, u32[]{:S(2)}) collective-permute-start(bf16[4,96,1536]{2,1,0:T(8,128)(2,1)} %collective-permute-done.11.refs_13_.refs_14_), channel_id=1, source_target_pairs={{0,16},{8,24},{16,0},{24,8},{1,17},{9,25},{17,1},{25,9},{2,18},{10... | collective-permute-start | bytes 3538952 | tf_op jit(solution)/shard_map/ppermute | solution.py:1004
  151.8 123.3 %all-gather.7.cloned.1.call-start = ((), (), s32[]{:S(2)}) async-start(), calls=%async_computation.8 | async-start | bytes 1966080 | tf_op jit(solution)/shard_map/all_gather | solution.py:1205
  152.9 14.4 %collective-permute-start.26 = (bf16[96,1536]{1,0:T(8,128)(2,1)}, bf16[96,1536]{1,0:T(8,128)(2,1)S(1)}, u32[]{:S(2)}, u32[]{:S(2)}) collective-permute-start(bf16[96,1536]{1,0:T(8,128)(2,1)} %concatenate.19.refs_0_), channel_id=1, source_target_pairs={{0,16},{8,24},{16,0},{24,8},{1,17},{9,25},{17,1},{25,9},{2,18},{10... | collective-permute-start | bytes 884744 | tf_op jit(solution)/shard_map/ppermute | solution.py:1004
  154.4 14.0 %collective-permute-start.27 = (bf16[96,1536]{1,0:T(8,128)(2,1)}, bf16[96,1536]{1,0:T(8,128)(2,1)S(1)}, u32[]{:S(2)}, u32[]{:S(2)}) collective-permute-start(bf16[96,1536]{1,0:T(8,128)(2,1)} %concatenate.19.refs_0_), channel_id=1, source_target_pairs={{0,24},{8,16},{16,8},{24,0},{1,25},{9,17},{17,9},{25,1},{2,26},{10... | collective-permute-start | bytes 884744 | tf_op jit(solution)/shard_map/ppermute | solution.py:1004
  155.4 17.1 %collective-permute-start.32 = (bf16[96,1536]{1,0:T(8,128)(2,1)}, bf16[96,1536]{1,0:T(8,128)(2,1)S(1)}, u32[]{:S(2)}, u32[]{:S(2)}) collective-permute-start(bf16[96,1536]{1,0:T(8,128)(2,1)} %concatenate.19.refs_0_), channel_id=1, source_target_pairs={{0,4},{4,0},{1,5},{5,1},{2,6},{6,2},{3,7},{7,3},{8,12},{12,8},{9,1... | collective-permute-start | bytes 884744 | tf_op jit(solution)/shard_map/ppermute | solution.py:1008
  168.4 29.2 %collective-permute-start.28 = (bf16[4,96,1536]{2,1,0:T(8,128)(2,1)}, bf16[4,96,1536]{2,1,0:T(8,128)(2,1)}, u32[]{:S(2)}, u32[]{:S(2)}) collective-permute-start(bf16[4,96,1536]{2,1,0:T(8,128)(2,1)} %get-tuple-element.318.refs_4_), channel_id=1, source_target_pairs={{0,8},{8,0},{16,24},{24,16},{1,9},{9,1},{17,25},{25,17},{2,10},{10... | collective-permute-start | bytes 3538952 | tf_op jit(solution)/shard_map/ppermute | solution.py:1004
  169.4 29.2 %collective-permute-start.29 = (bf16[4,96,1536]{2,1,0:T(8,128)(2,1)}, bf16[4,96,1536]{2,1,0:T(8,128)(2,1)}, u32[]{:S(2)}, u32[]{:S(2)}) collective-permute-start(bf16[4,96,1536]{2,1,0:T(8,128)(2,1)} %get-tuple-element.318.refs_4_), channel_id=1, source_target_pairs={{0,16},{8,24},{16,0},{24,8},{1,17},{9,25},{17,1},{25,9},{2,18},{10... | collective-permute-start | bytes 3538952 | tf_op jit(solution)/shard_map/ppermute | solution.py:1004
  170.8 50.5 %collective-permute-start.30 = (bf16[4,96,1536]{2,1,0:T(8,128)(2,1)}, bf16[4,96,1536]{2,1,0:T(8,128)(2,1)}, u32[]{:S(2)}, u32[]{:S(2)}) collective-permute-start(bf16[4,96,1536]{2,1,0:T(8,128)(2,1)} %get-tuple-element.322.refs_12_), channel_id=1, source_target_pairs={{0,8},{8,0},{16,24},{24,16},{1,9},{9,1},{17,25},{25,17},{2,10},{10... | collective-permute-start | bytes 3538952 | tf_op jit(solution)/shard_map/ppermute | solution.py:1004
  171.8 50.2 %collective-permute-start.31 = (bf16[4,96,1536]{2,1,0:T(8,128)(2,1)}, bf16[4,96,1536]{2,1,0:T(8,128)(2,1)}, u32[]{:S(2)}, u32[]{:S(2)}) collective-permute-start(bf16[4,96,1536]{2,1,0:T(8,128)(2,1)} %get-tuple-element.322.refs_12_), channel_id=1, source_target_pairs={{0,16},{8,24},{16,0},{24,8},{1,17},{9,25},{17,1},{25,9},{2,18},{10... | collective-permute-start | bytes 3538952 | tf_op jit(solution)/shard_map/ppermute | solution.py:1004
  228.1 28.7 %collective-permute-start.37 = (bf16[4,96,1536]{2,1,0:T(8,128)(2,1)}, bf16[4,96,1536]{2,1,0:T(8,128)(2,1)}, u32[]{:S(2)}, u32[]{:S(2)}) collective-permute-start(bf16[4,96,1536]{2,1,0:T(8,128)(2,1)} %collective-permute-done.29.refs_8_), channel_id=1, source_target_pairs={{0,8},{8,0},{16,24},{24,16},{1,9},{9,1},{17,25},{25,17},{2,10},{10... | collective-permute-start | bytes 3538952 | tf_op jit(solution)/shard_map/ppermute | solution.py:1004
  229.1 28.4 %collective-permute-start.38 = (bf16[4,96,1536]{2,1,0:T(8,128)(2,1)}, bf16[4,96,1536]{2,1,0:T(8,128)(2,1)}, u32[]{:S(2)}, u32[]{:S(2)}) collective-permute-start(bf16[4,96,1536]{2,1,0:T(8,128)(2,1)} %collective-permute-done.30.refs_14_), channel_id=1, source_target_pairs={{0,16},{8,24},{16,0},{24,8},{1,17},{9,25},{17,1},{25,9},{2,18},{10... | collective-permute-start | bytes 3538952 | tf_op jit(solution)/shard_map/ppermute | solution.py:1004
  240.8 151.9 %all-reduce.12.cloned.1.call-start = ((), (), s32[]{:S(2)}) async-start(), calls=%async_computation.1 | async-start | bytes 3194880 | tf_op jit(solution)/shard_map/psum | solution.py:1238
  258.0 28.1 %collective-permute-start.42 = (bf16[4,96,1536]{2,1,0:T(8,128)(2,1)}, bf16[4,96,1536]{2,1,0:T(8,128)(2,1)}, u32[]{:S(2)}, u32[]{:S(2)}) collective-permute-start(bf16[4,96,1536]{2,1,0:T(8,128)(2,1)} %collective-permute-done.37.refs_10_), channel_id=1, source_target_pairs={{0,4},{4,0},{1,5},{5,1},{2,6},{6,2},{3,7},{7,3},{8,12},{12,8},{9,1... | collective-permute-start | bytes 3538952 | tf_op jit(solution)/shard_map/ppermute | solution.py:1008
  258.5 27.6 %collective-permute-start.43 = (bf16[4,96,1536]{2,1,0:T(8,128)(2,1)}, bf16[4,96,1536]{2,1,0:T(8,128)(2,1)}, u32[]{:S(2)}, u32[]{:S(2)}) collective-permute-start(bf16[4,96,1536]{2,1,0:T(8,128)(2,1)} %get-tuple-element.322.refs_12_), channel_id=1, source_target_pairs={{0,4},{4,0},{1,5},{5,1},{2,6},{6,2},{3,7},{7,3},{8,12},{12,8},{9,1... | collective-permute-start | bytes 3538952 | tf_op jit(solution)/shard_map/ppermute | solution.py:1008
  263.0 23.1 %collective-permute-start.44 = (bf16[4,96,1536]{2,1,0:T(8,128)(2,1)}, bf16[4,96,1536]{2,1,0:T(8,128)(2,1)S(1)}, u32[]{:S(2)}, u32[]{:S(2)}) collective-permute-start(bf16[4,96,1536]{2,1,0:T(8,128)(2,1)} %collective-permute-done.30.refs_14_), channel_id=1, source_target_pairs={{0,4},{4,0},{1,5},{5,1},{2,6},{6,2},{3,7},{7,3},{8,12},{12,8},{9,1... | collective-permute-start | bytes 3538952 | tf_op jit(solution)/shard_map/ppermute | solution.py:1008
  263.1 23.0 %collective-permute-start.45 = (bf16[4,96,1536]{2,1,0:T(8,128)(2,1)}, bf16[4,96,1536]{2,1,0:T(8,128)(2,1)}, u32[]{:S(2)}, u32[]{:S(2)}) collective-permute-start(bf16[4,96,1536]{2,1,0:T(8,128)(2,1)} %collective-permute-done.31.refs_16_), channel_id=1, source_target_pairs={{0,4},{4,0},{1,5},{5,1},{2,6},{6,2},{3,7},{7,3},{8,12},{12,8},{9,1... | collective-permute-start | bytes 3538952 | tf_op jit(solution)/shard_map/ppermute | solution.py:1008
  264.1 22.1 %collective-permute-start.46 = (bf16[4,96,1536]{2,1,0:T(8,128)(2,1)}, bf16[4,96,1536]{2,1,0:T(8,128)(2,1)}, u32[]{:S(2)}, u32[]{:S(2)}) collective-permute-start(bf16[4,96,1536]{2,1,0:T(8,128)(2,1)} %collective-permute-done.38.refs_18_), channel_id=1, source_target_pairs={{0,4},{4,0},{1,5},{5,1},{2,6},{6,2},{3,7},{7,3},{8,12},{12,8},{9,1... | collective-permute-start | bytes 3538952 | tf_op jit(solution)/shard_map/ppermute | solution.py:1008
  323.0 15.0 %collective-permute-start.48 = (bf16[4,4,96,1536]{3,2,1,0:T(8,128)(2,1)}, bf16[4,4,96,1536]{3,2,1,0:T(8,128)(2,1)}, u32[]{:S(2)}, u32[]{:S(2)}) collective-permute-start(bf16[4,4,96,1536]{3,2,1,0:T(8,128)(2,1)} %get-tuple-element.330), channel_id=1, source_target_pairs={{0,4},{4,0},{1,5},{5,1},{2,6},{6,2},{3,7},{7,3},{8,12},{12,8},{9,1... | collective-permute-start | bytes 14155784 | tf_op jit(solution)/shard_map/ppermute | solution.py:1008
  323.6 178.6 %all-reduce.14.cloned.1.call-start = ((), (), s32[]{:S(2)}) async-start(), calls=%async_computation.2 | async-start | bytes 3145728 | tf_op jit(solution)/shard_map/psum | solution.py:1277
  335.9 103.5 %collective-permute-start.50 = (bf16[2,4,96,1536]{3,2,1,0:T(8,128)(2,1)}, bf16[2,4,96,1536]{3,2,1,0:T(8,128)(2,1)S(1)}, u32[]{:S(2)}, u32[]{:S(2)}) collective-permute-start(bf16[2,4,96,1536]{3,2,1,0:T(8,128)(2,1)} %add_convert_fusion.3), channel_id=1, source_target_pairs={{0,8},{8,0},{16,24},{24,16},{1,9},{9,1},{17,25},{25,17},{2,10},{10... | collective-permute-start | bytes 7077896 | tf_op jit(solution)/shard_map/ppermute | solution.py:1004
  341.8 100.5 %collective-permute-start.51 = (bf16[2,4,96,1536]{3,2,1,0:T(8,128)(2,1)}, bf16[2,4,96,1536]{3,2,1,0:T(8,128)(2,1)}, u32[]{:S(2)}, u32[]{:S(2)}) collective-permute-start(bf16[2,4,96,1536]{3,2,1,0:T(8,128)(2,1)} %add_convert_fusion.2), channel_id=1, source_target_pairs={{0,16},{8,24},{16,0},{24,8},{1,17},{9,25},{17,1},{25,9},{2,18},{10... | collective-permute-start | bytes 7077896 | tf_op jit(solution)/shard_map/ppermute | solution.py:1004
  433.9 113.3 %all-reduce.16.cloned.1.call-start = ((), (), s32[]{:S(2)}) async-start(), calls=%async_computation.3 | async-start | bytes 1572864 | tf_op jit(solution)/shard_map/psum | solution.py:1236
  502.2 116.8 %all-reduce.18.cloned.1.call-start = ((), (), s32[]{:S(2)}) async-start(), calls=%async_computation.4 | async-start | bytes 3194880 | tf_op jit(solution)/shard_map/psum | solution.py:1238
  502.5 38.6 %collective-permute-start.54 = (f32[16,16]{1,0:T(8,128)S(1)}, f32[16,16]{1,0:T(8,128)S(1)}, u32[]{:S(2)}, u32[]{:S(2)}) collective-permute-start(f32[16,16]{1,0:T(8,128)S(1)} %add.202), channel_id=1, source_target_pairs={{0,16},{8,24},{16,0},{24,8},{1,17},{9,25},{17,1},{25,9},{2,18},{10... | collective-permute-start | bytes 3080 | tf_op jit(solution)/shard_map/ppermute | solution.py:1004
  547.2 15.0 %collective-permute-start.58 = (bf16[4,4,96,1536]{3,2,1,0:T(8,128)(2,1)}, bf16[4,4,96,1536]{3,2,1,0:T(8,128)(2,1)}, u32[]{:S(2)}, u32[]{:S(2)}) collective-permute-start(bf16[4,4,96,1536]{3,2,1,0:T(8,128)(2,1)} %get-tuple-element.385), channel_id=1, source_target_pairs={{0,4},{4,0},{1,5},{5,1},{2,6},{6,2},{3,7},{7,3},{8,12},{12,8},{9,1... | collective-permute-start | bytes 14155784 | tf_op jit(solution)/shard_map/ppermute | solution.py:1008
  547.7 116.5 %all-reduce.20.cloned.1.call-start = ((), (), s32[]{:S(2)}) async-start(), calls=%async_computation.5 | async-start | bytes 1572864 | tf_op jit(solution)/shard_map/psum | solution.py:1256
  547.8 28.9 %collective-permute-start.55 = (bf16[4,96,1536]{2,1,0:T(8,128)(2,1)S(1)}, bf16[4,96,1536]{2,1,0:T(8,128)(2,1)S(1)}, u32[]{:S(2)}, u32[]{:S(2)}) collective-permute-start(bf16[4,96,1536]{2,1,0:T(8,128)(2,1)S(1)} %fusion), channel_id=1, source_target_pairs={{0,16},{8,24},{16,0},{24,8},{1,17},{9,25},{17,1},{25,9},{2,18},{10... | collective-permute-start | bytes 3538952 | tf_op jit(solution)/shard_map/ppermute | solution.py:1004
  549.3 29.1 %collective-permute-start.56 = (bf16[4,96,1536]{2,1,0:T(8,128)(2,1)}, bf16[4,96,1536]{2,1,0:T(8,128)(2,1)S(1)}, u32[]{:S(2)}, u32[]{:S(2)}) collective-permute-start(bf16[4,96,1536]{2,1,0:T(8,128)(2,1)} %fusion.1), channel_id=1, source_target_pairs={{0,8},{8,0},{16,24},{24,16},{1,9},{9,1},{17,25},{25,17},{2,10},{10... | collective-permute-start | bytes 3538952 | tf_op jit(solution)/shard_map/ppermute | solution.py:1004
  559.9 104.2 %collective-permute-start.60 = (bf16[2,4,96,1536]{3,2,1,0:T(8,128)(2,1)}, bf16[2,4,96,1536]{3,2,1,0:T(8,128)(2,1)S(1)}, u32[]{:S(2)}, u32[]{:S(2)}) collective-permute-start(bf16[2,4,96,1536]{3,2,1,0:T(8,128)(2,1)} %add_convert_fusion.1), channel_id=1, source_target_pairs={{0,8},{8,0},{16,24},{24,16},{1,9},{9,1},{17,25},{25,17},{2,10},{10... | collective-permute-start | bytes 7077896 | tf_op jit(solution)/shard_map/ppermute | solution.py:1004
  566.0 102.1 %collective-permute-start.61 = (bf16[2,4,96,1536]{3,2,1,0:T(8,128)(2,1)}, bf16[2,4,96,1536]{3,2,1,0:T(8,128)(2,1)}, u32[]{:S(2)}, u32[]{:S(2)}) collective-permute-start(bf16[2,4,96,1536]{3,2,1,0:T(8,128)(2,1)} %add_convert_fusion), channel_id=1, source_target_pairs={{0,16},{8,24},{16,0},{24,8},{1,17},{9,25},{17,1},{25,9},{2,18},{10... | collective-permute-start | bytes 7077896 | tf_op jit(solution)/shard_map/ppermute | solution.py:1004
  619.1 132.7 %all-reduce.22.cloned.1.call-start = ((), (), s32[]{:S(2)}) async-start(), calls=%async_computation.6 | async-start | bytes 3145728 | tf_op jit(solution)/shard_map/psum | solution.py:1277
  619.5 52.0 %collective-permute-start.62 = (bf16[2,96,896]{2,1,0:T(8,128)(2,1)S(1)}, bf16[2,96,896]{2,1,0:T(8,128)(2,1)}, u32[]{:S(2)}, u32[]{:S(2)}) collective-permute-start(bf16[2,96,896]{2,1,0:T(8,128)(2,1)S(1)} %copy-done.32), channel_id=1, source_target_pairs={{0,8},{8,0},{16,24},{24,16},{1,9},{9,1},{17,25},{25,17},{2,10},{10... | collective-permute-start | bytes 1032200 | tf_op jit(solution)/shard_map/ppermute | solution.py:1004
  671.6 33.6 %collective-permute-start.63 = (bf16[4,96,1536]{2,1,0:T(8,128)(2,1)}, bf16[4,96,1536]{2,1,0:T(8,128)(2,1)S(1)}, u32[]{:S(2)}, u32[]{:S(2)}) collective-permute-start(bf16[4,96,1536]{2,1,0:T(8,128)(2,1)} %fusion.2), channel_id=1, source_target_pairs={{0,16},{8,24},{16,0},{24,8},{1,17},{9,25},{17,1},{25,9},{2,18},{10... | collective-permute-start | bytes 3538952 | tf_op jit(solution)/shard_map/ppermute | solution.py:1004
  673.1 32.1 %collective-permute-start.64 = (bf16[4,96,1536]{2,1,0:T(8,128)(2,1)}, bf16[4,96,1536]{2,1,0:T(8,128)(2,1)S(1)}, u32[]{:S(2)}, u32[]{:S(2)}) collective-permute-start(bf16[4,96,1536]{2,1,0:T(8,128)(2,1)} %fusion.3), channel_id=1, source_target_pairs={{0,8},{8,0},{16,24},{24,16},{1,9},{9,1},{17,25},{25,17},{2,10},{10... | collective-permute-start | bytes 3538952 | tf_op jit(solution)/shard_map/ppermute | solution.py:1004
  675.6 28.4 %collective-permute-start.69 = (bf16[96,896]{1,0:T(8,128)(2,1)S(1)}, bf16[96,896]{1,0:T(8,128)(2,1)}, u32[]{:S(2)}, u32[]{:S(2)}) collective-permute-start(bf16[96,896]{1,0:T(8,128)(2,1)S(1)} %fusion.5), channel_id=1, source_target_pairs={{0,16},{8,24},{16,0},{24,8},{1,17},{9,25},{17,1},{25,9},{2,18},{10... | collective-permute-start | bytes 516104 | tf_op jit(solution)/shard_map/ppermute | solution.py:1004
  728.0 29.3 %collective-permute-start.68 = (bf16[96,896]{1,0:T(8,128)(2,1)S(1)}, bf16[96,896]{1,0:T(8,128)(2,1)S(1)}, u32[]{:S(2)}, u32[]{:S(2)}) collective-permute-start(bf16[96,896]{1,0:T(8,128)(2,1)S(1)} %fusion.4), channel_id=1, source_target_pairs={{0,16},{8,24},{16,0},{24,8},{1,17},{9,25},{17,1},{25,9},{2,18},{10... | collective-permute-start | bytes 516104 | tf_op jit(solution)/shard_map/ppermute | solution.py:1004
  (87 other events, 819.9 us)
Sparse Core Ops, SparseCore 0:
  83.1 35.3 all-gather.4
  151.9 67.5 all-reduce.9
  240.9 34.1 all-gather.6
  323.7 68.9 all-reduce.11
  434.0 68.1 all-reduce.13
  504.4 42.6 all-reduce.15
  549.5 69.4 all-reduce.17
  621.4 42.6 all-reduce.19
  684.2 67.5 all-reduce.21

commit v7 on v6

--- a/solution.py
+++ b/solution.py
@@ -1163,9 +1163,7 @@
                 swapped[0][0][2], swapped[0][1][1] = swap(lows[2]), swap(highs[1])
                 after, swapped[0] = tie(after, swapped[0])
                 if layer + 1 < layer_count:
-                    mid, wide[layer + 1], small[layer + 1] = tie(
-                        (lows[1], highs[2]), wide[layer + 1], small[layer + 1]
-                    )
+                    mid, wide[layer + 1] = tie((lows[1], highs[2]), wide[layer + 1])
                     lows[1], highs[2] = mid
             else:
                 (lows, highs), _ = tie((lows, highs), after)
@@ -1206,7 +1204,7 @@
         if hyper and layer == 0:
             lows, highs = rests[0]
             swapped[0][0][1], swapped[0][1][2] = swap(lows[1]), swap(highs[2])
-            ctx_all, swapped[0] = tie(ctx_all, swapped[0])
+            ctx_all, swapped[0], small[1:] = tie(ctx_all, swapped[0], small[1:])
         wo_all = weights[layer][1]
         middle, base, xm_low, gates_t, logits_t = middle_part(
             h_in, ctx_all, wo_all, vecs, routes_t[layer], prev_t, resid, rank

time: 782 us -> 782 us (level)
  no operation moved by 1% of the time
where the time goes in v7:
time: 782 us; the launch traced here: 774 us
  waiting for transfers between devices  348 us (45%)
  Pallas kernels  263 us (34%)
  starting transfers between devices  58 us (7%)
  other arithmetic  51.3 us (7%)
  local copies, waits for them, and re-layouts  38.6 us (5%)
  between operations  14.7 us (2%)
    ppermute x32, waiting for transfers between devices, hop(): return lax.ppermute(value, 'fsdp', [(i, i ^ step) for i in range(4)])  112 us
    pallas_call x3, Pallas kernels, experts(): pl.pallas_call(functools.partial(experts_kernel, fwd, bwd, blocks, plan,...  83.4 us
    psum x2, waiting for transfers between devices, per_device(): gx = lax.psum(gx, 'tp')  80.2 us
    psum x2, waiting for transfers between devices, per_device(): ga = lax.psum(ga_part, 'tp')  77.2 us
    ppermute x35, waiting for transfers between devices, swap(): return lax.ppermute(value, 'ctx', [(0, 1), (1, 0)])  41.3 us
    ppermute x32, starting transfers between devices, hop(): return lax.ppermute(value, 'fsdp', [(i, i ^ step) for i in range(4)])  39.7 us
    convert_element_type x12, other arithmetic, add_low(): return total.astype(BF16)  36.7 us
    pallas_call x2, Pallas kernels, attend_backward(): pl.pallas_call(functools.partial(attn_bwd_kernel, heads), grid=(rows // B...  29 us
  transfers between devices with their start and end apart: 82, of which 43 were waited for; matrix products, arithmetic and copies ran while one was open for 10% of the time, Pallas kernels for 26%

profile of v7, /device:TPU:0, one launch (start us, length us, event | category | flops | bytes accessed | tf_op | source)
XLA Modules:
  0.0 774.1 jit_solution(15651090429582194817)
XLA Ops:
  29.9 7.5 pack_wide.2
  37.5 4.4 collective-permute-done.6.refs_4_
  51.7 3.8 prep.2
  55.5 5.1 qkv_part.2.own_ref
  60.7 7.2 collective-permute-done.10.refs_7_.refs_8_
  73.7 8.4 %attend_forward.2 = (bf16[1536,128]{1,0:T(8,128)(2,1)}, f32[1024,8]{1,0:T(8,128)}) custom-call(s32[3]{0:T(128)} %pad_add_fusion.info_ref, bf16[1024,640]{1,0:T(8,128)(2,1)} %qkv_part.2.own_ref, bf16[1024,640]{1,0:T(8,128)(2,1)} %copy-done.4), custom_call_target="tpu_custom_call" | custom-call | flops 161061280 | bytes 196608 | tf_op jit(solution)/shard_map/attend_forward/pallas_call | solution.py:273
  83.4 7.6 pack_wide.3
  91.0 6.2 collective-permute-done.17.refs_5_.refs_6_
  110.6 8.1 %all-gather.5.cloned.1.call-done = bf16[6144,128]{1,0:T(8,128)(2,1)} async-done(((bf16[1536,128]{1,0:T(8,128)(2,1)}), bf16[6144,128]{1,0:T(8,128)(2,1)}) %all-gather.5.cloned.1.call-update) | async-done | bytes 1572880 | tf_op jit(solution)/shard_map/all_gather | solution.py:1203
  118.6 10.2 %middle_part.2 = (f32[1024,768]{1,0:T(8,128)}, f32[1024,768]{1,0:T(8,128)}, bf16[1024,768]{1,0:T(8,128)(2,1)}, f32[8,1024]{1,0:T(8,128)}, f32[16,1024]{1,0:T(8,128)}) custom-call(s32[1]{0:T(128)} %bitcast.rank_ref, bf16[1024,768]{1,0:T(8,128)(2,1)} %bitcast.140, bf16[4,1536,128]{2,1,0:T(8,128)(2,1)} %bitcast.149, ...), custom_call_target="tpu_custom_call" | custom-call | flops 60397976 | bytes 629145 | tf_op jit(solution)/shard_map/middle_part/pallas_call | solution.py:476
  134.6 16.8 %experts.3 = bf16[1024,768]{1,0:T(8,128)(2,1)} custom-call(s32[8]{0:T(128)} %iota_xor_fusion.offs_ref, bf16[1024,768]{1,0:T(8,128)(2,1)} %get-tuple-element.273.refs_0_, s32[8,1024]{1,0:T(8,128)} %get-tuple-element.521.refs_7_.refs_1_.refs_2_.refs_4_, f32[8,1024]{1,0:T(8,128)} %get-tuple-element.274.refs_2_.refs_3_.refs_5_, ...), custom_call_target="tpu_custom_call" | custom-call | flops 400000000 | bytes 1000000 | tf_op jit(solution)/shard_map/experts/pallas_call | solution.py:922
  155.0 6.6 collective-permute-done.25.refs_2_
  161.6 6.7 collective-permute-done.26.refs_4_
  178.0 3.8 prep.3
  181.8 15.8 %collective-permute-done.28.refs_6_ = bf16[4,96,1536]{2,1,0:T(8,128)(2,1)} collective-permute-done((bf16[4,96,1536]{2,1,0:T(8,128)(2,1)}, bf16[4,96,1536]{2,1,0:T(8,128)(2,1)}, u32[]{:S(2)}, u32[]{:S(2)}) %collective-permute-start.28) | collective-permute-done | bytes 1179680 | tf_op jit(solution)/shard_map/ppermute | solution.py:1004
  198.7 22.2 %collective-permute-done.30.refs_14_ = bf16[4,96,1536]{2,1,0:T(8,128)(2,1)} collective-permute-done((bf16[4,96,1536]{2,1,0:T(8,128)(2,1)}, bf16[4,96,1536]{2,1,0:T(8,128)(2,1)}, u32[]{:S(2)}, u32[]{:S(2)}) %collective-permute-start.30) | collective-permute-done | bytes 1179680 | tf_op jit(solution)/shard_map/ppermute | solution.py:1004
  222.1 5.9 qkv_part.3
  232.5 8.4 %attend_forward.3 = (bf16[1536,128]{1,0:T(8,128)(2,1)}, f32[1024,8]{1,0:T(8,128)}) custom-call(s32[3]{0:T(128)} %pad_add_fusion.info_ref, bf16[1024,640]{1,0:T(8,128)(2,1)} %get-tuple-element.300.own_ref, bf16[1024,640]{1,0:T(8,128)(2,1)} %copy-done.5), custom_call_target="tpu_custom_call" | custom-call | flops 161061280 | bytes 196608 | tf_op jit(solution)/shard_map/attend_forward/pallas_call | solution.py:273
  241.4 15.4 %collective-permute-done.37.refs_10_ = bf16[4,96,1536]{2,1,0:T(8,128)(2,1)} collective-permute-done((bf16[4,96,1536]{2,1,0:T(8,128)(2,1)}, bf16[4,96,1536]{2,1,0:T(8,128)(2,1)}, u32[]{:S(2)}, u32[]{:S(2)}) %collective-permute-start.37) | collective-permute-done | bytes 1179680 | tf_op jit(solution)/shard_map/ppermute | solution.py:1004
  266.0 9.3 %all-gather.7.cloned.1.call-done = bf16[6144,128]{1,0:T(8,128)(2,1)} async-done(((bf16[1536,128]{1,0:T(8,128)(2,1)}), bf16[6144,128]{1,0:T(8,128)(2,1)}) %all-gather.7.cloned.1.call-update) | async-done | bytes 1572880 | tf_op jit(solution)/shard_map/all_gather | solution.py:1203
  275.2 10.9 %middle_part.3 = (f32[1024,768]{1,0:T(8,128)}, f32[1024,768]{1,0:T(8,128)}, bf16[1024,768]{1,0:T(8,128)(2,1)}, f32[8,1024]{1,0:T(8,128)}, f32[16,1024]{1,0:T(8,128)}) custom-call(s32[1]{0:T(128)} %bitcast.rank_ref, f32[1024,768]{1,0:T(8,128)} %get-tuple-element.292.refs_0_.h_ref, bf16[4,1536,128]{2,1,0:T(8,128)(2,1)} %bitcast.151, ...), custom_call_target="tpu_custom_call" | custom-call | flops 60397976 | bytes 629145 | tf_op jit(solution)/shard_map/middle_part/pallas_call | solution.py:476
  287.2 35.8 %experts.4 = (bf16[1024,768]{1,0:T(8,128)(2,1)}, bf16[1040,768]{1,0:T(8,128)(2,1)}, bf16[4,4,96,1536]{3,2,1,0:T(8,128)(2,1)}, bf16[4,4,96,1536]{3,2,1,0:T(8,128)...) custom-call(s32[8]{0:T(128)} %iota_xor_fusion.offs_ref, ...), custom_call_target="tpu_custom_call" | custom-call | flops 1280000000 | bytes 2000000 | tf_op jit(solution)/shard_map/experts/pallas_call | solution.py:922
  323.8 7.5 collective-permute-done.47.refs_1_
  331.3 4.6 add_convert_fusion.3
  338.1 3.8 add_convert_fusion.2
  343.3 49.5 %all-reduce.12.cloned.1.call-done.refs_2_ = bf16[1040,768]{1,0:T(8,128)(2,1)} async-done(((bf16[1040,768]{1,0:T(8,128)(2,1)}), bf16[1040,768]{1,0:T(8,128)(2,1)}) %all-reduce.12.cloned.1.call-update) | async-done | bytes 1597456 | tf_op jit(solution)/shard_map/psum | solution.py:1236
  394.1 13.0 %gate_backward.2 = (f32[1024,768]{1,0:T(8,128)}, bf16[1024,192]{1,0:T(8,128)(2,1)}, f32[768,192]{1,0:T(8,128)}, f32[32,768]{1,0:T(8,128)}, f32[16,1024]{1,0:T(8,128)}, /*index=5*/f32[16,16]{1,0:T(8,128)}) custom-call(bf16[1024,768]{1,0:T(8,128)(2,1)} %bitcast.144, f32[1024,768]{1,0:T(8,128)} %get-tuple-element.309.refs_1_, ...), custom_call_target="tpu_custom_call" | custom-call | flops 30198988 | bytes 707788 | tf_op jit(solution)/shard_map/gate_backward/pallas_call | solution.py:625
  407.1 14.5 %attend_backward.2 = (f32[1024,576]{1,0:T(8,128)}, bf16[1024,640]{1,0:T(8,128)(2,1)}) custom-call(s32[3]{0:T(128)} %pad_add_fusion.info_ref, bf16[1024,640]{1,0:T(8,128)(2,1)} %get-tuple-element.300.own_ref, bf16[1024,640]{1,0:T(8,128)(2,1)} %copy-done.5, f32[1024,8]{1,0:T(8,128)} %get-tuple-element.334.lse_ref, bf16[1024,192]{1,0:T(8,128)(2,1)} %get-tuple-element.335.gctx_ref), custom_call_target="tpu_custom_call" | custom-call | flops 402653184 | bytes 353894 | tf_op jit(solution)/shard_map/attend_backward/pallas_call | solution.py:344
  426.0 8.0 %qkv_backward.2 = (bf16[1024,768]{1,0:T(8,128)(2,1)}, f32[768,576]{1,0:T(8,128)}, f32[8,768]{1,0:T(8,128)}) custom-call(f32[1024,576]{1,0:T(8,128)} %get-tuple-element.336.gown_ref, bf16[1024,640]{1,0:T(8,128)(2,1)} %copy-done.16, f32[1024,768]{1,0:T(8,128)} %get-tuple-element.292.refs_0_.h_ref, ...), custom_call_target="tpu_custom_call" | custom-call | flops 90596968 | bytes 393216 | tf_op jit(solution)/shard_map/qkv_backward/pallas_call | solution.py:668
  445.9 56.4 %all-reduce.14.cloned.1.call-done.ga_ref = bf16[1024,768]{1,0:T(8,128)(2,1)} async-done(((bf16[1024,768]{1,0:T(8,128)(2,1)}), bf16[1024,768]{1,0:T(8,128)(2,1)}) %all-reduce.14.cloned.1.call-update) | async-done | bytes 1572880 | tf_op jit(solution)/shard_map/psum | solution.py:1275
  504.1 6.3 norm_backward.2
  510.4 30.8 %experts.5 = (bf16[1040,768]{1,0:T(8,128)(2,1)}, bf16[4,4,96,1536]{3,2,1,0:T(8,128)(2,1)}, bf16[4,4,96,1536]{3,2,1,0:T(8,128)(2,1)}, bf16[4,4,96,1536]{3,2,1,0:T(8,128)(2,1)}, bf16[4,4,96,1536]{3,2,1,0:T(8,128)(2,1)}) custom-call(s32[8]{0:T(128)} %iota_xor_fusion.offs_ref, bf16[1024,768]{1,0:T(8,128)(2,1)} %get-tuple-element.273.refs_0_, ...), custom_call_target="tpu_custom_call" | custom-call | flops 880000000 | bytes 2000000 | tf_op jit(solution)/shard_map/experts/pallas_call | solution.py:922
  541.8 5.5 all-reduce.16.cloned.1.call-done
  550.9 4.7 collective-permute-done.57.refs_1_
  555.5 4.5 add_convert_fusion.1
  562.3 3.8 add_convert_fusion
  579.5 8.9 %final_sums.2 = (f32[2,8,96,2,512]{4,3,2,1,0:T(2,128)}, f32[2,8,96,512]{3,2,1,0:T(8,128)}) custom-call(bf16[4,4,96,1536]{3,2,1,0:T(8,128)(2,1)} %get-tuple-element.390.refs_0_, bf16[4,4,96,1536]{3,2,1,0:T(8,128)(2,1)} %collective-permute-done.47.refs_1_, bf16[2,4,96,1536]{3,2,1,0:T(8,128)(2,1)} %copy-done.3, bf16[4,96,1536]{2,1,0:T(8,128)(2,1)} %copy-done.22, ...), custom_call_target="tpu_custom_call" | custom-call | flops 500000 | bytes 707788 | tf_op jit(solution)/shard_map/final_sums/pallas_call | solution.py:984
  588.4 30.7 %all-reduce.18.cloned.1.call-done.refs_2_ = bf16[1040,768]{1,0:T(8,128)(2,1)} async-done(((bf16[1040,768]{1,0:T(8,128)(2,1)}), bf16[1040,768]{1,0:T(8,128)(2,1)}) %all-reduce.18.cloned.1.call-update) | async-done | bytes 1597456 | tf_op jit(solution)/shard_map/psum | solution.py:1236
  622.5 12.4 %gate_backward.3 = (f32[1024,768]{1,0:T(8,128)}, bf16[1024,192]{1,0:T(8,128)(2,1)}, f32[768,192]{1,0:T(8,128)}, f32[32,768]{1,0:T(8,128)}) custom-call(f32[1024,768]{1,0:T(8,128)} %get-tuple-element.350.refs_0_, f32[1024,768]{1,0:T(8,128)} %get-tuple-element.351.refs_1_, bf16[1040,768]{1,0:T(8,128)(2,1)} %all-reduce.18.cloned.1.call-done.refs_2_, ...), custom_call_target="tpu_custom_call" | custom-call | flops 30198988 | bytes 707788 | tf_op jit(solution)/shard_map/gate_backward/pallas_call | solution.py:625
  634.9 14.5 %attend_backward.3 = (f32[1024,576]{1,0:T(8,128)}, bf16[1024,640]{1,0:T(8,128)(2,1)}) custom-call(s32[3]{0:T(128)} %pad_add_fusion.info_ref, bf16[1024,640]{1,0:T(8,128)(2,1)} %qkv_part.2.own_ref, bf16[1024,640]{1,0:T(8,128)(2,1)} %copy-done.4, f32[1024,8]{1,0:T(8,128)} %get-tuple-element.308.lse_ref, bf16[1024,192]{1,0:T(8,128)(2,1)} %get-tuple-element.409.gctx_ref), custom_call_target="tpu_custom_call" | custom-call | flops 402653184 | bytes 353894 | tf_op jit(solution)/shard_map/attend_backward/pallas_call | solution.py:344
  649.4 14.9 %all-reduce.20.cloned.1.call-done = bf16[512,768]{1,0:T(8,128)(2,1)} async-done(((bf16[512,768]{1,0:T(8,128)(2,1)}), bf16[512,768]{1,0:T(8,128)(2,1)}) %all-reduce.20.cloned.1.call-update) | async-done | bytes 786448 | tf_op jit(solution)/shard_map/psum | solution.py:1254
  664.3 3.9 fusion.2
  676.3 7.8 %qkv_backward.3 = (bf16[1024,768]{1,0:T(8,128)(2,1)}, f32[768,576]{1,0:T(8,128)}, f32[8,768]{1,0:T(8,128)}) custom-call(f32[1024,576]{1,0:T(8,128)} %get-tuple-element.428.gown_ref, bf16[1024,640]{1,0:T(8,128)(2,1)} %collective-permute-done.65.goth_ref, bf16[1024,768]{1,0:T(8,128)(2,1)} %bitcast.141, ...), custom_call_target="tpu_custom_call" | custom-call | flops 90596968 | bytes 393216 | tf_op jit(solution)/shard_map/qkv_backward/pallas_call | solution.py:668
  684.2 19.9 %collective-permute-done.69 = bf16[96,896]{1,0:T(8,128)(2,1)} collective-permute-done((bf16[96,896]{1,0:T(8,128)(2,1)S(1)}, bf16[96,896]{1,0:T(8,128)(2,1)}, u32[]{:S(2)}, u32[]{:S(2)}) %collective-permute-start.69) | collective-permute-done | bytes 172064 | tf_op jit(solution)/shard_map/ppermute | solution.py:1004
  705.3 4.2 pack_grads.3
  717.3 9.8 %final_sums.3 = (f32[2,8,96,2,512]{4,3,2,1,0:T(2,128)}, f32[2,8,96,512]{3,2,1,0:T(8,128)}) custom-call(bf16[4,4,96,1536]{3,2,1,0:T(8,128)(2,1)} %get-tuple-element.450.refs_0_, bf16[4,4,96,1536]{3,2,1,0:T(8,128)(2,1)} %collective-permute-done.57.refs_1_, bf16[2,4,96,1536]{3,2,1,0:T(8,128)(2,1)} %copy-done.2, ...), custom_call_target="tpu_custom_call", output_to_operand_aliasing={{0}: (8, {}), {1}: (9, {})} | custom-call | flops 500000 | bytes 707788 | tf_op jit(solution)/shard_map/final_sums/pallas_call | solution.py:984
  731.1 20.7 %all-reduce.22.cloned.1.call-done.ga_ref = bf16[1024,768]{1,0:T(8,128)(2,1)} async-done(((bf16[1024,768]{1,0:T(8,128)(2,1)}), bf16[1024,768]{1,0:T(8,128)(2,1)}) %all-reduce.22.cloned.1.call-update) | async-done | bytes 1572880 | tf_op jit(solution)/shard_map/psum | solution.py:1275
  751.9 5.5 norm_backward.3
  (342 shorter events, 167.3 us)
Async XLA Ops:
  7.2 111.4 %all-gather.5.cloned.1.call-start = ((), (), s32[]{:S(2)}) async-start(), calls=%async_computation.7 | async-start | bytes 1966080 | tf_op jit(solution)/shard_map/all_gather | solution.py:1203
  8.2 16.0 %collective-permute-start = (bf16[2,96,192]{2,1,0:T(8,128)(2,1)S(1)}, bf16[2,96,192]{2,1,0:T(8,128)(2,1)S(1)}, u32[]{:S(2)}, u32[]{:S(2)}) collective-permute-start(bf16[2,96,192]{2,1,0:T(8,128)(2,1)S(1)} %bitcast.152), channel_id=1, source_target_pairs={{0,1},{1,2},{2,3},{3,0},{4,5},{5,6},{6,7},{7,4},{8,9},{9,10},{10,1... | collective-permute-start | bytes 221192 | tf_op jit(solution)/shard_map/ppermute | solution.py:1020
  27.9 13.9 %collective-permute-start.6 = (bf16[96,1536]{1,0:T(8,128)(2,1)S(1)}, bf16[96,1536]{1,0:T(8,128)(2,1)S(1)}, u32[]{:S(2)}, u32[]{:S(2)}) collective-permute-start(bf16[96,1536]{1,0:T(8,128)(2,1)S(1)} %concatenate.18.refs_0_), channel_id=1, source_target_pairs={{0,16},{8,24},{16,0},{24,8},{1,17},{9,25},{17,1},{25,9},{2,18},{10... | collective-permute-start | bytes 884744 | tf_op jit(solution)/shard_map/ppermute | solution.py:1004
  29.9 14.6 %collective-permute-start.3 = (bf16[96,1536]{1,0:T(8,128)(2,1)S(1)}, bf16[96,1536]{1,0:T(8,128)(2,1)S(1)}, u32[]{:S(2)}, u32[]{:S(2)}) collective-permute-start(bf16[96,1536]{1,0:T(8,128)(2,1)S(1)} %concatenate.18.refs_0_), channel_id=1, source_target_pairs={{0,4},{4,0},{1,5},{5,1},{2,6},{6,2},{3,7},{7,3},{8,12},{12,8},{9,1... | collective-permute-start | bytes 884744 | tf_op jit(solution)/shard_map/ppermute | solution.py:1008
  41.9 25.9 %collective-permute-start.10 = (bf16[4,96,1536]{2,1,0:T(8,128)(2,1)}, bf16[4,96,1536]{2,1,0:T(8,128)(2,1)S(1)}, u32[]{:S(2)}, u32[]{:S(2)}) collective-permute-start(bf16[4,96,1536]{2,1,0:T(8,128)(2,1)} %get-tuple-element.258.refs_3_.refs_4_), channel_id=1, source_target_pairs={{0,16},{8,24},{16,0},{24,8},{1,17},{9,25},{17,1},{25,9},{2,18},{10... | collective-permute-start | bytes 3538952 | tf_op jit(solution)/shard_map/ppermute | solution.py:1004
  43.8 24.4 %collective-permute-start.11 = (bf16[4,96,1536]{2,1,0:T(8,128)(2,1)}, bf16[4,96,1536]{2,1,0:T(8,128)(2,1)}, u32[]{:S(2)}, u32[]{:S(2)}) collective-permute-start(bf16[4,96,1536]{2,1,0:T(8,128)(2,1)} %get-tuple-element.259.refs_11_.refs_12_), channel_id=1, source_target_pairs={{0,8},{8,0},{16,24},{24,16},{1,9},{9,1},{17,25},{25,17},{2,10},{10... | collective-permute-start | bytes 3538952 | tf_op jit(solution)/shard_map/ppermute | solution.py:1004
  44.0 24.2 %collective-permute-start.12 = (bf16[4,96,1536]{2,1,0:T(8,128)(2,1)}, bf16[4,96,1536]{2,1,0:T(8,128)(2,1)}, u32[]{:S(2)}, u32[]{:S(2)}) collective-permute-start(bf16[4,96,1536]{2,1,0:T(8,128)(2,1)} %get-tuple-element.258.refs_3_.refs_4_), channel_id=1, source_target_pairs={{0,4},{4,0},{1,5},{5,1},{2,6},{6,2},{3,7},{7,3},{8,12},{12,8},{9,1... | collective-permute-start | bytes 3538952 | tf_op jit(solution)/shard_map/ppermute | solution.py:1008
  44.0 24.2 %collective-permute-start.13 = (bf16[4,96,1536]{2,1,0:T(8,128)(2,1)}, bf16[4,96,1536]{2,1,0:T(8,128)(2,1)}, u32[]{:S(2)}, u32[]{:S(2)}) collective-permute-start(bf16[4,96,1536]{2,1,0:T(8,128)(2,1)} %get-tuple-element.259.refs_11_.refs_12_), channel_id=1, source_target_pairs={{0,4},{4,0},{1,5},{5,1},{2,6},{6,2},{3,7},{7,3},{8,12},{12,8},{9,1... | collective-permute-start | bytes 3538952 | tf_op jit(solution)/shard_map/ppermute | solution.py:1008
  68.7 14.4 %collective-permute-start.16 = (bf16[4,96,1536]{2,1,0:T(8,128)(2,1)}, bf16[4,96,1536]{2,1,0:T(8,128)(2,1)}, u32[]{:S(2)}, u32[]{:S(2)}) collective-permute-start(bf16[4,96,1536]{2,1,0:T(8,128)(2,1)} %collective-permute-done.11.refs_13_.refs_14_), channel_id=1, source_target_pairs={{0,4},{4,0},{1,5},{5,1},{2,6},{6,2},{3,7},{7,3},{8,12},{12,8},{9,1... | collective-permute-start | bytes 3538952 | tf_op jit(solution)/shard_map/ppermute | solution.py:1008
  68.8 28.4 %collective-permute-start.17 = (bf16[4,96,1536]{2,1,0:T(8,128)(2,1)S(1)}, bf16[4,96,1536]{2,1,0:T(8,128)(2,1)}, u32[]{:S(2)}, u32[]{:S(2)}) collective-permute-start(bf16[4,96,1536]{2,1,0:T(8,128)(2,1)S(1)} %copy-done.6), channel_id=1, source_target_pairs={{0,8},{8,0},{16,24},{24,16},{1,9},{9,1},{17,25},{25,17},{2,10},{10... | collective-permute-start | bytes 3538952 | tf_op jit(solution)/shard_map/ppermute | solution.py:1004
  70.3 28.1 %collective-permute-start.18 = (bf16[4,96,1536]{2,1,0:T(8,128)(2,1)S(1)}, bf16[4,96,1536]{2,1,0:T(8,128)(2,1)}, u32[]{:S(2)}, u32[]{:S(2)}) collective-permute-start(bf16[4,96,1536]{2,1,0:T(8,128)(2,1)S(1)} %copy-done.7), channel_id=1, source_target_pairs={{0,16},{8,24},{16,0},{24,8},{1,17},{9,25},{17,1},{25,9},{2,18},{10... | collective-permute-start | bytes 3538952 | tf_op jit(solution)/shard_map/ppermute | solution.py:1004
  83.1 139.0 %all-reduce.10.cloned.1.call-start = ((), (), s32[]{:S(2)}) async-start(), calls=%async_computation | async-start | bytes 3145728 | tf_op jit(solution)/shard_map/psum | solution.py:1219
  98.9 29.9 %collective-permute-start.21 = (bf16[4,96,1536]{2,1,0:T(8,128)(2,1)S(1)}, bf16[4,96,1536]{2,1,0:T(8,128)(2,1)}, u32[]{:S(2)}, u32[]{:S(2)}) collective-permute-start(bf16[4,96,1536]{2,1,0:T(8,128)(2,1)S(1)} %collective-permute-done.10.refs_7_.refs_8_), channel_id=1, source_target_pairs={{0,8},{8,0},{16,24},{24,16},{1,9},{9,1},{17,25},{25,17},{2,10},{10... | collective-permute-start | bytes 3538952 | tf_op jit(solution)/shard_map/ppermute | solution.py:1004
  99.4 29.4 %collective-permute-start.22 = (bf16[4,96,1536]{2,1,0:T(8,128)(2,1)}, bf16[4,96,1536]{2,1,0:T(8,128)(2,1)}, u32[]{:S(2)}, u32[]{:S(2)}) collective-permute-start(bf16[4,96,1536]{2,1,0:T(8,128)(2,1)} %collective-permute-done.11.refs_13_.refs_14_), channel_id=1, source_target_pairs={{0,16},{8,24},{16,0},{24,8},{1,17},{9,25},{17,1},{25,9},{2,18},{10... | collective-permute-start | bytes 3538952 | tf_op jit(solution)/shard_map/ppermute | solution.py:1004
  151.4 123.8 %all-gather.7.cloned.1.call-start = ((), (), s32[]{:S(2)}) async-start(), calls=%async_computation.8 | async-start | bytes 1966080 | tf_op jit(solution)/shard_map/all_gather | solution.py:1203
  153.0 15.3 %collective-permute-start.26 = (bf16[96,1536]{1,0:T(8,128)(2,1)}, bf16[96,1536]{1,0:T(8,128)(2,1)S(1)}, u32[]{:S(2)}, u32[]{:S(2)}) collective-permute-start(bf16[96,1536]{1,0:T(8,128)(2,1)} %concatenate.19.refs_0_), channel_id=1, source_target_pairs={{0,16},{8,24},{16,0},{24,8},{1,17},{9,25},{17,1},{25,9},{2,18},{10... | collective-permute-start | bytes 884744 | tf_op jit(solution)/shard_map/ppermute | solution.py:1004
  155.0 17.4 %collective-permute-start.32 = (bf16[96,1536]{1,0:T(8,128)(2,1)}, bf16[96,1536]{1,0:T(8,128)(2,1)S(1)}, u32[]{:S(2)}, u32[]{:S(2)}) collective-permute-start(bf16[96,1536]{1,0:T(8,128)(2,1)} %concatenate.19.refs_0_), channel_id=1, source_target_pairs={{0,4},{4,0},{1,5},{5,1},{2,6},{6,2},{3,7},{7,3},{8,12},{12,8},{9,1... | collective-permute-start | bytes 884744 | tf_op jit(solution)/shard_map/ppermute | solution.py:1008
  168.3 29.3 %collective-permute-start.28 = (bf16[4,96,1536]{2,1,0:T(8,128)(2,1)}, bf16[4,96,1536]{2,1,0:T(8,128)(2,1)}, u32[]{:S(2)}, u32[]{:S(2)}) collective-permute-start(bf16[4,96,1536]{2,1,0:T(8,128)(2,1)} %get-tuple-element.318.refs_4_), channel_id=1, source_target_pairs={{0,8},{8,0},{16,24},{24,16},{1,9},{9,1},{17,25},{25,17},{2,10},{10... | collective-permute-start | bytes 3538952 | tf_op jit(solution)/shard_map/ppermute | solution.py:1004
  169.5 29.2 %collective-permute-start.29 = (bf16[4,96,1536]{2,1,0:T(8,128)(2,1)}, bf16[4,96,1536]{2,1,0:T(8,128)(2,1)}, u32[]{:S(2)}, u32[]{:S(2)}) collective-permute-start(bf16[4,96,1536]{2,1,0:T(8,128)(2,1)} %get-tuple-element.318.refs_4_), channel_id=1, source_target_pairs={{0,16},{8,24},{16,0},{24,8},{1,17},{9,25},{17,1},{25,9},{2,18},{10... | collective-permute-start | bytes 3538952 | tf_op jit(solution)/shard_map/ppermute | solution.py:1004
  170.4 50.6 %collective-permute-start.30 = (bf16[4,96,1536]{2,1,0:T(8,128)(2,1)}, bf16[4,96,1536]{2,1,0:T(8,128)(2,1)}, u32[]{:S(2)}, u32[]{:S(2)}) collective-permute-start(bf16[4,96,1536]{2,1,0:T(8,128)(2,1)} %get-tuple-element.322.refs_12_), channel_id=1, source_target_pairs={{0,8},{8,0},{16,24},{24,16},{1,9},{9,1},{17,25},{25,17},{2,10},{10... | collective-permute-start | bytes 3538952 | tf_op jit(solution)/shard_map/ppermute | solution.py:1004
  171.9 50.2 %collective-permute-start.31 = (bf16[4,96,1536]{2,1,0:T(8,128)(2,1)}, bf16[4,96,1536]{2,1,0:T(8,128)(2,1)}, u32[]{:S(2)}, u32[]{:S(2)}) collective-permute-start(bf16[4,96,1536]{2,1,0:T(8,128)(2,1)} %get-tuple-element.322.refs_12_), channel_id=1, source_target_pairs={{0,16},{8,24},{16,0},{24,8},{1,17},{9,25},{17,1},{25,9},{2,18},{10... | collective-permute-start | bytes 3538952 | tf_op jit(solution)/shard_map/ppermute | solution.py:1004
  228.2 28.7 %collective-permute-start.37 = (bf16[4,96,1536]{2,1,0:T(8,128)(2,1)}, bf16[4,96,1536]{2,1,0:T(8,128)(2,1)}, u32[]{:S(2)}, u32[]{:S(2)}) collective-permute-start(bf16[4,96,1536]{2,1,0:T(8,128)(2,1)} %collective-permute-done.29.refs_8_), channel_id=1, source_target_pairs={{0,8},{8,0},{16,24},{24,16},{1,9},{9,1},{17,25},{25,17},{2,10},{10... | collective-permute-start | bytes 3538952 | tf_op jit(solution)/shard_map/ppermute | solution.py:1004
  228.8 28.4 %collective-permute-start.38 = (bf16[4,96,1536]{2,1,0:T(8,128)(2,1)}, bf16[4,96,1536]{2,1,0:T(8,128)(2,1)}, u32[]{:S(2)}, u32[]{:S(2)}) collective-permute-start(bf16[4,96,1536]{2,1,0:T(8,128)(2,1)} %collective-permute-done.30.refs_14_), channel_id=1, source_target_pairs={{0,16},{8,24},{16,0},{24,8},{1,17},{9,25},{17,1},{25,9},{2,18},{10... | collective-permute-start | bytes 3538952 | tf_op jit(solution)/shard_map/ppermute | solution.py:1004
  240.9 151.9 %all-reduce.12.cloned.1.call-start = ((), (), s32[]{:S(2)}) async-start(), calls=%async_computation.1 | async-start | bytes 3194880 | tf_op jit(solution)/shard_map/psum | solution.py:1236
  257.7 28.4 %collective-permute-start.42 = (bf16[4,96,1536]{2,1,0:T(8,128)(2,1)}, bf16[4,96,1536]{2,1,0:T(8,128)(2,1)}, u32[]{:S(2)}, u32[]{:S(2)}) collective-permute-start(bf16[4,96,1536]{2,1,0:T(8,128)(2,1)} %collective-permute-done.37.refs_10_), channel_id=1, source_target_pairs={{0,4},{4,0},{1,5},{5,1},{2,6},{6,2},{3,7},{7,3},{8,12},{12,8},{9,1... | collective-permute-start | bytes 3538952 | tf_op jit(solution)/shard_map/ppermute | solution.py:1008
  258.2 27.9 %collective-permute-start.43 = (bf16[4,96,1536]{2,1,0:T(8,128)(2,1)}, bf16[4,96,1536]{2,1,0:T(8,128)(2,1)}, u32[]{:S(2)}, u32[]{:S(2)}) collective-permute-start(bf16[4,96,1536]{2,1,0:T(8,128)(2,1)} %get-tuple-element.322.refs_12_), channel_id=1, source_target_pairs={{0,4},{4,0},{1,5},{5,1},{2,6},{6,2},{3,7},{7,3},{8,12},{12,8},{9,1... | collective-permute-start | bytes 3538952 | tf_op jit(solution)/shard_map/ppermute | solution.py:1008
  262.7 23.5 %collective-permute-start.44 = (bf16[4,96,1536]{2,1,0:T(8,128)(2,1)}, bf16[4,96,1536]{2,1,0:T(8,128)(2,1)S(1)}, u32[]{:S(2)}, u32[]{:S(2)}) collective-permute-start(bf16[4,96,1536]{2,1,0:T(8,128)(2,1)} %collective-permute-done.30.refs_14_), channel_id=1, source_target_pairs={{0,4},{4,0},{1,5},{5,1},{2,6},{6,2},{3,7},{7,3},{8,12},{12,8},{9,1... | collective-permute-start | bytes 3538952 | tf_op jit(solution)/shard_map/ppermute | solution.py:1008
  262.8 23.3 %collective-permute-start.45 = (bf16[4,96,1536]{2,1,0:T(8,128)(2,1)}, bf16[4,96,1536]{2,1,0:T(8,128)(2,1)}, u32[]{:S(2)}, u32[]{:S(2)}) collective-permute-start(bf16[4,96,1536]{2,1,0:T(8,128)(2,1)} %collective-permute-done.31.refs_16_), channel_id=1, source_target_pairs={{0,4},{4,0},{1,5},{5,1},{2,6},{6,2},{3,7},{7,3},{8,12},{12,8},{9,1... | collective-permute-start | bytes 3538952 | tf_op jit(solution)/shard_map/ppermute | solution.py:1008
  263.8 22.4 %collective-permute-start.46 = (bf16[4,96,1536]{2,1,0:T(8,128)(2,1)}, bf16[4,96,1536]{2,1,0:T(8,128)(2,1)}, u32[]{:S(2)}, u32[]{:S(2)}) collective-permute-start(bf16[4,96,1536]{2,1,0:T(8,128)(2,1)} %collective-permute-done.38.refs_18_), channel_id=1, source_target_pairs={{0,4},{4,0},{1,5},{5,1},{2,6},{6,2},{3,7},{7,3},{8,12},{12,8},{9,1... | collective-permute-start | bytes 3538952 | tf_op jit(solution)/shard_map/ppermute | solution.py:1008
  323.1 15.0 %collective-permute-start.48 = (bf16[4,4,96,1536]{3,2,1,0:T(8,128)(2,1)}, bf16[4,4,96,1536]{3,2,1,0:T(8,128)(2,1)}, u32[]{:S(2)}, u32[]{:S(2)}) collective-permute-start(bf16[4,4,96,1536]{3,2,1,0:T(8,128)(2,1)} %get-tuple-element.330), channel_id=1, source_target_pairs={{0,4},{4,0},{1,5},{5,1},{2,6},{6,2},{3,7},{7,3},{8,12},{12,8},{9,1... | collective-permute-start | bytes 14155784 | tf_op jit(solution)/shard_map/ppermute | solution.py:1008
  323.6 178.7 %all-reduce.14.cloned.1.call-start = ((), (), s32[]{:S(2)}) async-start(), calls=%async_computation.2 | async-start | bytes 3145728 | tf_op jit(solution)/shard_map/psum | solution.py:1275
  335.9 103.5 %collective-permute-start.50 = (bf16[2,4,96,1536]{3,2,1,0:T(8,128)(2,1)}, bf16[2,4,96,1536]{3,2,1,0:T(8,128)(2,1)S(1)}, u32[]{:S(2)}, u32[]{:S(2)}) collective-permute-start(bf16[2,4,96,1536]{3,2,1,0:T(8,128)(2,1)} %add_convert_fusion.3), channel_id=1, source_target_pairs={{0,8},{8,0},{16,24},{24,16},{1,9},{9,1},{17,25},{25,17},{2,10},{10... | collective-permute-start | bytes 7077896 | tf_op jit(solution)/shard_map/ppermute | solution.py:1004
  341.8 100.6 %collective-permute-start.51 = (bf16[2,4,96,1536]{3,2,1,0:T(8,128)(2,1)}, bf16[2,4,96,1536]{3,2,1,0:T(8,128)(2,1)}, u32[]{:S(2)}, u32[]{:S(2)}) collective-permute-start(bf16[2,4,96,1536]{3,2,1,0:T(8,128)(2,1)} %add_convert_fusion.2), channel_id=1, source_target_pairs={{0,16},{8,24},{16,0},{24,8},{1,17},{9,25},{17,1},{25,9},{2,18},{10... | collective-permute-start | bytes 7077896 | tf_op jit(solution)/shard_map/ppermute | solution.py:1004
  434.0 113.2 %all-reduce.16.cloned.1.call-start = ((), (), s32[]{:S(2)}) async-start(), calls=%async_computation.3 | async-start | bytes 1572864 | tf_op jit(solution)/shard_map/psum | solution.py:1234
  502.3 116.8 %all-reduce.18.cloned.1.call-start = ((), (), s32[]{:S(2)}) async-start(), calls=%async_computation.4 | async-start | bytes 3194880 | tf_op jit(solution)/shard_map/psum | solution.py:1236
  502.6 38.6 %collective-permute-start.54 = (f32[16,16]{1,0:T(8,128)S(1)}, f32[16,16]{1,0:T(8,128)S(1)}, u32[]{:S(2)}, u32[]{:S(2)}) collective-permute-start(f32[16,16]{1,0:T(8,128)S(1)} %add.202), channel_id=1, source_target_pairs={{0,16},{8,24},{16,0},{24,8},{1,17},{9,25},{17,1},{25,9},{2,18},{10... | collective-permute-start | bytes 3080 | tf_op jit(solution)/shard_map/ppermute | solution.py:1004
  547.3 15.0 %collective-permute-start.58 = (bf16[4,4,96,1536]{3,2,1,0:T(8,128)(2,1)}, bf16[4,4,96,1536]{3,2,1,0:T(8,128)(2,1)}, u32[]{:S(2)}, u32[]{:S(2)}) collective-permute-start(bf16[4,4,96,1536]{3,2,1,0:T(8,128)(2,1)} %get-tuple-element.385), channel_id=1, source_target_pairs={{0,4},{4,0},{1,5},{5,1},{2,6},{6,2},{3,7},{7,3},{8,12},{12,8},{9,1... | collective-permute-start | bytes 14155784 | tf_op jit(solution)/shard_map/ppermute | solution.py:1008
  547.8 116.5 %all-reduce.20.cloned.1.call-start = ((), (), s32[]{:S(2)}) async-start(), calls=%async_computation.5 | async-start | bytes 1572864 | tf_op jit(solution)/shard_map/psum | solution.py:1254
  547.9 28.9 %collective-permute-start.55 = (bf16[4,96,1536]{2,1,0:T(8,128)(2,1)S(1)}, bf16[4,96,1536]{2,1,0:T(8,128)(2,1)S(1)}, u32[]{:S(2)}, u32[]{:S(2)}) collective-permute-start(bf16[4,96,1536]{2,1,0:T(8,128)(2,1)S(1)} %fusion), channel_id=1, source_target_pairs={{0,16},{8,24},{16,0},{24,8},{1,17},{9,25},{17,1},{25,9},{2,18},{10... | collective-permute-start | bytes 3538952 | tf_op jit(solution)/shard_map/ppermute | solution.py:1004
  549.4 29.1 %collective-permute-start.56 = (bf16[4,96,1536]{2,1,0:T(8,128)(2,1)}, bf16[4,96,1536]{2,1,0:T(8,128)(2,1)S(1)}, u32[]{:S(2)}, u32[]{:S(2)}) collective-permute-start(bf16[4,96,1536]{2,1,0:T(8,128)(2,1)} %fusion.1), channel_id=1, source_target_pairs={{0,8},{8,0},{16,24},{24,16},{1,9},{9,1},{17,25},{25,17},{2,10},{10... | collective-permute-start | bytes 3538952 | tf_op jit(solution)/shard_map/ppermute | solution.py:1004
  560.0 104.2 %collective-permute-start.60 = (bf16[2,4,96,1536]{3,2,1,0:T(8,128)(2,1)}, bf16[2,4,96,1536]{3,2,1,0:T(8,128)(2,1)S(1)}, u32[]{:S(2)}, u32[]{:S(2)}) collective-permute-start(bf16[2,4,96,1536]{3,2,1,0:T(8,128)(2,1)} %add_convert_fusion.1), channel_id=1, source_target_pairs={{0,8},{8,0},{16,24},{24,16},{1,9},{9,1},{17,25},{25,17},{2,10},{10... | collective-permute-start | bytes 7077896 | tf_op jit(solution)/shard_map/ppermute | solution.py:1004
  566.1 102.1 %collective-permute-start.61 = (bf16[2,4,96,1536]{3,2,1,0:T(8,128)(2,1)}, bf16[2,4,96,1536]{3,2,1,0:T(8,128)(2,1)}, u32[]{:S(2)}, u32[]{:S(2)}) collective-permute-start(bf16[2,4,96,1536]{3,2,1,0:T(8,128)(2,1)} %add_convert_fusion), channel_id=1, source_target_pairs={{0,16},{8,24},{16,0},{24,8},{1,17},{9,25},{17,1},{25,9},{2,18},{10... | collective-permute-start | bytes 7077896 | tf_op jit(solution)/shard_map/ppermute | solution.py:1004
  619.2 132.7 %all-reduce.22.cloned.1.call-start = ((), (), s32[]{:S(2)}) async-start(), calls=%async_computation.6 | async-start | bytes 3145728 | tf_op jit(solution)/shard_map/psum | solution.py:1275
  619.6 52.1 %collective-permute-start.62 = (bf16[2,96,896]{2,1,0:T(8,128)(2,1)S(1)}, bf16[2,96,896]{2,1,0:T(8,128)(2,1)}, u32[]{:S(2)}, u32[]{:S(2)}) collective-permute-start(bf16[2,96,896]{2,1,0:T(8,128)(2,1)S(1)} %copy-done.32), channel_id=1, source_target_pairs={{0,8},{8,0},{16,24},{24,16},{1,9},{9,1},{17,25},{25,17},{2,10},{10... | collective-permute-start | bytes 1032200 | tf_op jit(solution)/shard_map/ppermute | solution.py:1004
  671.7 33.6 %collective-permute-start.63 = (bf16[4,96,1536]{2,1,0:T(8,128)(2,1)}, bf16[4,96,1536]{2,1,0:T(8,128)(2,1)S(1)}, u32[]{:S(2)}, u32[]{:S(2)}) collective-permute-start(bf16[4,96,1536]{2,1,0:T(8,128)(2,1)} %fusion.2), channel_id=1, source_target_pairs={{0,16},{8,24},{16,0},{24,8},{1,17},{9,25},{17,1},{25,9},{2,18},{10... | collective-permute-start | bytes 3538952 | tf_op jit(solution)/shard_map/ppermute | solution.py:1004
  673.2 32.1 %collective-permute-start.64 = (bf16[4,96,1536]{2,1,0:T(8,128)(2,1)}, bf16[4,96,1536]{2,1,0:T(8,128)(2,1)S(1)}, u32[]{:S(2)}, u32[]{:S(2)}) collective-permute-start(bf16[4,96,1536]{2,1,0:T(8,128)(2,1)} %fusion.3), channel_id=1, source_target_pairs={{0,8},{8,0},{16,24},{24,16},{1,9},{9,1},{17,25},{25,17},{2,10},{10... | collective-permute-start | bytes 3538952 | tf_op jit(solution)/shard_map/ppermute | solution.py:1004
  675.7 28.4 %collective-permute-start.69 = (bf16[96,896]{1,0:T(8,128)(2,1)S(1)}, bf16[96,896]{1,0:T(8,128)(2,1)}, u32[]{:S(2)}, u32[]{:S(2)}) collective-permute-start(bf16[96,896]{1,0:T(8,128)(2,1)S(1)} %fusion.5), channel_id=1, source_target_pairs={{0,16},{8,24},{16,0},{24,8},{1,17},{9,25},{17,1},{25,9},{2,18},{10... | collective-permute-start | bytes 516104 | tf_op jit(solution)/shard_map/ppermute | solution.py:1004
  728.1 29.3 %collective-permute-start.68 = (bf16[96,896]{1,0:T(8,128)(2,1)S(1)}, bf16[96,896]{1,0:T(8,128)(2,1)S(1)}, u32[]{:S(2)}, u32[]{:S(2)}) collective-permute-start(bf16[96,896]{1,0:T(8,128)(2,1)S(1)} %fusion.4), channel_id=1, source_target_pairs={{0,16},{8,24},{16,0},{24,8},{1,17},{9,25},{17,1},{25,9},{2,18},{10... | collective-permute-start | bytes 516104 | tf_op jit(solution)/shard_map/ppermute | solution.py:1004
  (87 other events, 818.4 us)
Sparse Core Ops, SparseCore 0:
  83.2 35.3 all-gather.4
  151.6 67.9 all-reduce.9
  241.0 34.1 all-gather.6
  323.7 68.9 all-reduce.11
  434.1 68.1 all-reduce.13
  504.5 42.6 all-reduce.15
  549.6 69.4 all-reduce.17
  621.5 42.6 all-reduce.19
  684.3 67.5 all-reduce.21
